TPU v7x, 256 devices: a whole 4x4x8 slice. The times are simulated.
256 devices in a mesh: tile: 32 (over z, x_hi, core), group: 8 (over y, x_lo).
Axes of the slice: x: 4 (x_hi: 2, x_lo: 2; x = x_hi * 2 + x_lo), y: 4, z: 8, core: 2. Of those that a mesh axis runs over, the one named last changes fastest.
Arguments:
- object_field: float32 [2, 320, 4096], P(None, 'group', 'tile'), may hold values from -6 to 6
- probe_field: float32 [2, 256, 256], replicated, may hold values from -6 to 6
- amplitudes: float32 [256, 256, 256], P(('tile', 'group')), may hold values from 0 to 4
- row_start: int32 [256], P(('tile', 'group')), may hold values from 0 to 64
- column_start: int32 [256], P(('tile', 'group')), may hold values from 0 to 128
- live_slots: int32 [256], P(('tile', 'group')), may hold values 0 or 1
Outputs:
- new_object: float32 [2, 320, 4096], P(None, 'group', 'tile')
- new_probe: float32 [2, 256, 256], replicated
All inputs are finite; a program needn't handle non-finite values. No bound on the sum of `live_slots` on one device may be relied on, other than what follows from the above.
Results may differ from a plain program's by a relative error of at most 0.0001.
Values sent between devices are 32-bit elements; how exact they have to be, the bound alone decides.
No kernel may reach another device: no remote copies, remote signals or barrier semaphores. Data moves between devices by JAX's collectives and lax.ppermute only.
A program may use at most 64 MiB of HBM per device.

v0:
```python
import math

import jax
import jax.numpy as jnp
from jax import lax
from jax.sharding import PartitionSpec as P

WIN = 256
HALO = 128


def padded_2(value, sides, width):
    for axis, dim in sides:
        count, length = (lax.axis_size(axis), value.shape[dim])
        up = [(i, (i + 1) % count) for i in range(count - 1)]
        down = [(j, i) for i, j in up]
        last = lax.slice_in_dim(value, length - width, length, axis=dim)
        initial = lax.slice_in_dim(value, 0, width, axis=dim)
        before = lax.ppermute(last, axis, up)
        after = lax.ppermute(initial, axis, down)
        value = jnp.concatenate([before, value, after], axis=dim)
    return value


def dft_tables(length):
    counter = jnp.arange(length, dtype=jnp.int32)
    product = counter[:, None] * counter[None, :] % length
    angles = 2.0 * math.pi / length * product.astype(jnp.float32)
    factor = 1.0 / math.sqrt(length)
    return (jnp.cos(angles) * factor, jnp.sin(angles) * factor)


def apply_left(matrix, values):
    return jnp.einsum("jk,pkl->pjl", matrix, values, precision=lax.Precision.HIGHEST)


def apply_right(values, matrix):
    return jnp.einsum("pjk,kl->pjl", values, matrix, precision=lax.Precision.HIGHEST)


def transform(real_part, imag_part, cos_table, sin_table, sign):
    left_real = apply_left(cos_table, real_part) - sign * apply_left(sin_table, imag_part)
    left_imag = apply_left(cos_table, imag_part) + sign * apply_left(sin_table, real_part)
    right_real = apply_right(left_real, cos_table) - sign * apply_right(left_imag, sin_table)
    right_imag = apply_right(left_imag, cos_table) + sign * apply_right(left_real, sin_table)
    return (right_real, right_imag)


def window_terms(windows, probe_field, amplitudes, live_slots, cos_table, sin_table):
    sample_real = windows[:, 0]
    sample_imag = windows[:, 1]
    probe_real = probe_field[0]
    probe_imag = probe_field[1]
    exit_real = probe_real * sample_real - probe_imag * sample_imag
    exit_imag = probe_real * sample_imag + probe_imag * sample_real
    far_real, far_imag = transform(exit_real, exit_imag, cos_table, sin_table, -1.0)
    modulus = jnp.maximum(jnp.sqrt(far_real * far_real + far_imag * far_imag), 0.25)
    factor = 1.0 - amplitudes / modulus
    miss_real, miss_imag = transform(
        far_real * factor, far_imag * factor, cos_table, sin_table, 1.0
    )
    weight = live_slots.astype(jnp.float32)[:, None, None]
    miss_real = miss_real * weight
    miss_imag = miss_imag * weight
    grad_real = probe_real * miss_real + probe_imag * miss_imag
    grad_imag = probe_real * miss_imag - probe_imag * miss_real
    probe_light = weight * (probe_real * probe_real + probe_imag * probe_imag)
    terms = jnp.stack([grad_real, grad_imag, probe_light], axis=1)
    probe_grad = jnp.stack(
        [
            jnp.sum(sample_real * miss_real + sample_imag * miss_imag, axis=0),
            jnp.sum(sample_real * miss_imag - sample_imag * miss_real, axis=0),
        ],
        axis=0,
    )
    window_light = jnp.sum(weight * (sample_real * sample_real + sample_imag * sample_imag), axis=0)
    return (terms, probe_grad, window_light)


def add_windows(accum, terms, top_rows, left_edges):
    zero_index = jnp.zeros((), jnp.int32)
    channels = terms.shape[1]

    def place(slot, current):
        corner = (zero_index, top_rows[slot], left_edges[slot])
        piece = lax.dynamic_slice(current, corner, (channels, WIN, WIN))
        return lax.dynamic_update_slice(current, piece + terms[slot], corner)

    return lax.fori_loop(0, terms.shape[0], place, accum)


def cut_windows(padded, top_rows, left_edges):
    zero_index = jnp.zeros((), jnp.int32)

    def single(top_row, left_edge):
        return lax.dynamic_slice(padded, (zero_index, top_row, left_edge), (2, WIN, WIN))

    return jax.vmap(single)(top_rows, left_edges)


def edge_strips(accum):
    return jnp.concatenate([accum[:, :, :HALO], accum[:, :, accum.shape[2] - HALO :]], axis=2)


def add_edges(inner, arrived):
    width = inner.shape[2]
    inner = inner.at[:, :, :HALO].add(arrived[:, :, :HALO])
    return inner.at[:, :, width - HALO :].add(arrived[:, :, arrived.shape[2] - HALO :])


def apply_updates(object_field, probe_field, share, probe_grad, window_light):
    light_max = jnp.max(probe_field[0] * probe_field[0] + probe_field[1] * probe_field[1]) + 1e-06
    new_object = object_field - share[0:2] / (share[2:3] + 0.25 * light_max)
    new_probe = (
        probe_field - probe_grad / (window_light + 0.25 * jnp.mean(window_light) + 1e-05)[None]
    )
    return (new_object, new_probe)


def local(object_field, probe_field, amplitudes, row_start, column_start, live_slots):
    cos_table, sin_table = dft_tables(WIN)
    full_rows = lax.all_gather(object_field, "group", axis=1, tiled=True)
    padded = padded_2(full_rows, (("tile", 2),), HALO)
    windows = cut_windows(padded, row_start, column_start)
    terms, probe_grad, window_light = window_terms(
        windows, probe_field, amplitudes, live_slots, cos_table, sin_table
    )
    accum = jnp.zeros((terms.shape[1], padded.shape[1], padded.shape[2]), jnp.float32)
    accum = add_windows(accum, terms, row_start, column_start)
    arrived = padded_2(edge_strips(accum), (("tile", 2),), HALO)
    summed = add_edges(accum[:, :, HALO : accum.shape[2] - HALO], arrived)
    share = lax.psum_scatter(summed, "group", scatter_dimension=1, tiled=True)
    probe_grad, window_light = lax.psum((probe_grad, window_light), ("tile", "group"))
    object_field, probe_field = apply_updates(
        object_field, probe_field, share, probe_grad, window_light
    )
    return (object_field, probe_field)


def solution(mesh):
    return jax.shard_map(
        local,
        mesh=mesh,
        in_specs=(
            P(None, "group", "tile"),
            P(),
            P(("tile", "group"), None, None),
            P(("tile", "group")),
            P(("tile", "group")),
            P(("tile", "group")),
        ),
        out_specs=(P(None, "group", "tile"), P()),
        check_vma=False,
    )
```

profile of v0, /device:TPU:1, one launch (start us, length us, event | category | flops | bytes accessed | tf_op | source)
XLA Modules:
  0.0 369.9 jit_solution(3378128131235949026)
XLA Ops:
  8.0 0.0 all-reduce.3.cloned.1.call-start
  8.1 24.9 %all_gather.3 = f32[2,320,128]{2,1,0:T(8,128)S(1)} all-gather(f32[2,40,128]{2,1,0:T(8,128)} %param.14), channel_id=1, replica_groups=mesh['tile'=32,'group'=8] {'group'}, dimensions={1}, use_global_device_ids=true | all-gather | bytes 368640 | tf_op jit(solution)/shard_map/all_gather | solution.py:122
  33.0 9.6 %collective-permute-start.1 = (f32[2,320,128]{2,1,0:T(8,128)S(1)}, f32[2,320,128]{2,1,0:T(8,128)S(1)}, u32[]{:S(2)}, u32[]{:S(2)}) collective-permute-start(f32[2,320,128]{2,1,0:T(8,128)S(1)} %all_gather.3), channel_id=1, source_target_pairs={{8,0},{16,8},{24,16},{32,24},{40,32},{48,40},{56,48},{64,56},{72,6... | collective-permute-start | bytes 983048 | tf_op jit(solution)/shard_map/ppermute | solution.py:20
  42.6 3.2 collective-permute-start
  47.8 0.9 collective-permute-done.1
  48.6 1.6 collective-permute-done
  50.2 0.4 fusion.12
  50.7 0.1 fusion.40
  50.7 1.5 fusion.38
  52.2 1.5 fusion.34
  53.7 1.5 fusion.9
  55.2 1.5 fusion.7
  56.7 1.5 fusion.47
  58.2 0.0 copy-start.6
  58.2 1.5 fusion.48
  59.7 1.5 fusion.4
  61.2 1.7 bitcast_multiply_fusion.11
  62.9 1.5 fusion.31
  64.4 1.5 fusion.27
  65.9 1.5 fusion.3
  67.4 1.5 fusion.2
  68.8 1.5 fusion.45
  70.3 1.5 fusion.46
  71.8 1.5 fusion
  73.3 0.0 copy-start.1
  73.3 1.7 fusion.1
  75.0 0.7 fusion.24
  75.7 0.1 maximum_bitcast_fusion
  75.8 0.1 broadcast_in_dim.6
  75.9 11.1 %dynamic_update_slice.4 = f32[3,320,384]{2,1,0:T(8,128)S(1)} dynamic-update-slice(f32[3,320,384]{2,1,0:T(8,128)S(1)} %broadcast_in_dim.6, f32[3,256,256]{2,1,0:T(8,128)S(1)} %maximum_bitcast_fusion, s32[]{:T(128)} %constant.112.clone.1, s32[]{:T(128)S(6)} %select_n.60, s32[]{:T(128)S(6)} %select_n.61) | dynamic-update-slice | bytes 1572868 | tf_op jit(solution)/shard_map/while/body/eval_jaxpr/dynamic_update_slice | solution.py:87
  87.0 0.0 copy-start.2
  87.0 0.9 fusion.132
  87.9 5.9 %collective-permute-start.2 = (f32[3,320,128]{2,1,0:T(8,128)}, f32[3,320,128]{2,1,0:T(8,128)S(1)}, u32[]{:S(2)}, u32[]{:S(2)}) collective-permute-start(f32[3,320,128]{2,1,0:T(8,128)} %get-tuple-element.73), channel_id=1, source_target_pairs={{0,8},{8,16},{16,24},{24,32},{32,40},{40,48},{48,56},{56,64},{64,7... | collective-permute-start | bytes 1474568 | tf_op jit(solution)/shard_map/ppermute | solution.py:19
  93.8 1.9 collective-permute-start.3
  95.8 0.8 fusion.18
  96.5 0.8 pad_maximum_fusion
  97.4 0.0 all-reduce.3.cloned.1.call-update
  97.4 0.0 reduce-scatter.2.cloned.1.call-start
  97.4 7.7 %collective-permute-done.2 = f32[3,320,128]{2,1,0:T(8,128)S(1)} collective-permute-done((f32[3,320,128]{2,1,0:T(8,128)}, f32[3,320,128]{2,1,0:T(8,128)S(1)}, u32[]{:S(2)}, u32[]{:S(2)}) %collective-permute-start.2) | collective-permute-done | bytes 491552 | tf_op jit(solution)/shard_map/ppermute | solution.py:19
  105.2 0.4 collective-permute-done.3
  105.6 1.9 fusion.13
  107.5 0.0 reduce-scatter.2.cloned.1.call-update
  108.1 247.0 %all-reduce.3.cloned.1.call-done = (f32[2,256,256]{2,1,0:T(8,128)}, f32[256,256]{1,0:T(8,128)}) async-done(((f32[2,256,256]{2,1,0:T(8,128)}, f32[256,256]{1,0:T(8,128)}), (f32[2,256,256]{2,1,0:T(8,128)}, f32[256,256]{1,0:T(8,128)})) %all-reduce.3.cloned.1.call-update) | async-done | bytes 786448 | tf_op jit(solution)/shard_map/psum | solution.py:133
  355.2 1.6 reduce_sum.8
  357.4 1.0 add_add_fusion
  358.4 1.9 divide_subtract_fusion
  360.3 0.7 fusion.51
  361.1 1.4 fusion.50
  (12 shorter events, 0.0 us)
Async XLA Ops:
  8.0 42.7 %copy-start = (f32[2,256,256]{2,1,0:T(8,128)S(1)}, f32[2,256,256]{2,1,0:T(8,128)}, u32[]{:S(2)}) copy-start(f32[2,256,256]{2,1,0:T(8,128)} %param.15) | copy-start | bytes 1572868
  8.0 347.1 %all-reduce.3.cloned.1.call-start = ((), (), s32[]{:S(2)}) async-start(), calls=%async_computation.2 | async-start | bytes 1572864 | tf_op jit(solution)/shard_map/psum | solution.py:133
  33.0 15.6 %collective-permute-start.1 = (f32[2,320,128]{2,1,0:T(8,128)S(1)}, f32[2,320,128]{2,1,0:T(8,128)S(1)}, u32[]{:S(2)}, u32[]{:S(2)}) collective-permute-start(f32[2,320,128]{2,1,0:T(8,128)S(1)} %all_gather.3), channel_id=1, source_target_pairs={{8,0},{16,8},{24,16},{32,24},{40,32},{48,40},{56,48},{64,56},{72,6... | collective-permute-start | bytes 983048 | tf_op jit(solution)/shard_map/ppermute | solution.py:20
  42.6 7.6 %collective-permute-start = (f32[2,320,128]{2,1,0:T(8,128)S(1)}, f32[2,320,128]{2,1,0:T(8,128)S(1)}, u32[]{:S(2)}, u32[]{:S(2)}) collective-permute-start(f32[2,320,128]{2,1,0:T(8,128)S(1)} %all_gather.3), channel_id=1, source_target_pairs={{0,8},{8,16},{16,24},{24,32},{32,40},{40,48},{48,56},{56,64},{64,7... | collective-permute-start | bytes 983048 | tf_op jit(solution)/shard_map/ppermute | solution.py:19
  58.2 3.0 copy-start.6
  73.3 2.4 copy-start.1
  75.0 0.8 copy-start.3
  87.0 8.7 %copy-start.2 = (f32[256,256]{1,0:T(8,128)S(1)}, f32[256,256]{1,0:T(8,128)}, u32[]{:S(2)}) copy-start(f32[256,256]{1,0:T(8,128)} %copy-done.1) | copy-start | bytes 786436
  87.0 8.7 %copy-start.4 = (f32[256,256]{1,0:T(8,128)S(1)}, f32[256,256]{1,0:T(8,128)}, u32[]{:S(2)}) copy-start(f32[256,256]{1,0:T(8,128)} %copy-done.3) | copy-start | bytes 786436
  87.9 17.3 %collective-permute-start.2 = (f32[3,320,128]{2,1,0:T(8,128)}, f32[3,320,128]{2,1,0:T(8,128)S(1)}, u32[]{:S(2)}, u32[]{:S(2)}) collective-permute-start(f32[3,320,128]{2,1,0:T(8,128)} %get-tuple-element.73), channel_id=1, source_target_pairs={{0,8},{8,16},{16,24},{24,32},{32,40},{40,48},{48,56},{56,64},{64,7... | collective-permute-start | bytes 1474568 | tf_op jit(solution)/shard_map/ppermute | solution.py:19
  93.8 11.8 %collective-permute-start.3 = (f32[3,320,128]{2,1,0:T(8,128)S(1)}, f32[3,320,128]{2,1,0:T(8,128)}, u32[]{:S(2)}, u32[]{:S(2)}) collective-permute-start(f32[3,320,128]{2,1,0:T(8,128)S(1)} %get-tuple-element.74), channel_id=1, source_target_pairs={{8,0},{16,8},{24,16},{32,24},{40,32},{48,40},{56,48},{64,56},{72,6... | collective-permute-start | bytes 1474568 | tf_op jit(solution)/shard_map/ppermute | solution.py:20
  97.4 262.9 %reduce-scatter.2.cloned.1.call-start = ((), (), s32[]{:S(2)}) async-start(), calls=%async_computation.1 | async-start | bytes 552960 | tf_op jit(solution)/shard_map/reduce_scatter | solution.py:132
  107.5 253.6 %copy-start.5 = (f32[2,40,128]{2,1,0:T(8,128)S(1)}, f32[2,40,128]{2,1,0:T(8,128)}, u32[]{:S(2)}) copy-start(f32[2,40,128]{2,1,0:T(8,128)} %param.14) | copy-start | bytes 122884
Sparse Core Ops, SparseCore 0:
  97.5 257.5 all-reduce.2
Sparse Core Ops, SparseCore 1:
  107.6 39.6 reduce-scatter.1
where the time goes:
time: 371 us; the launch traced here: 370 us
  waiting for transfers between devices  258 us (70%)
  blocking collectives  24.9 us (7%)
  matrix products  24.1 us (6%)
  starting transfers between devices  20.7 us (6%)
  between operations  19 us (5%)
  local copies, waits for them, and re-layouts  12.1 us (3%)
  other arithmetic  11.4 us (3%)
    psum x1, waiting for transfers between devices, local(): lax.psum((probe_grad, window_light), ('tile', 'group'))  247 us
    all_gather x1, blocking collectives, local(): full_rows = lax.all_gather(object_field, 'group', axis=1, tiled=True)  24.9 us
    dot_general x8, matrix products, apply_right(): jnp.einsum('pjk,kl->pjl', values, matrix, precision=lax.Precision.HIGHEST)  12.3 us
    dot_general x8, matrix products, apply_left(): jnp.einsum('jk,pkl->pjl', matrix, values, precision=lax.Precision.HIGHEST)  11.8 us
    ppermute x2, starting transfers between devices, padded_2(): after = lax.ppermute(initial, axis, down)  11.6 us
    dynamic_update_slice x1, local copies, waits for them, and re-layouts, place(): return lax.dynamic_update_slice(current, piece + terms[slot], corner)  11.1 us
    ppermute x2, waiting for transfers between devices, padded_2(): before = lax.ppermute(last, axis, up)  9.32 us
    ppermute x2, starting transfers between devices, padded_2(): before = lax.ppermute(last, axis, up)  9.06 us
  transfers between devices with their start and end apart: 6, of which 5 were waited for; matrix products, arithmetic and copies ran while one was open for 2% of the time, Pallas kernels for 0%

commit v1 on v0

v1 whole, which is shorter than its diff:
```python
import jax
import jax.numpy as jnp
import ml_dtypes
import numpy as np
from jax import lax
from jax.experimental import pallas as pl
from jax.experimental.pallas import tpu as pltpu
from jax.sharding import PartitionSpec as P

WIN = 256
LANES = 128
X_LO, Y_A, Y_B = 1, 2, 6
SMEM = pltpu.MemorySpace.SMEM
VMEM = pltpu.MemorySpace.VMEM


def split_tables():
    counter = np.arange(WIN)
    angles = 2.0 * np.pi / WIN * (counter[:, None] * counter[None, :] % WIN)
    cos, sin = np.cos(angles) / np.sqrt(WIN), np.sin(angles) / np.sqrt(WIN)
    both = np.concatenate([cos, sin], axis=0)
    high = both.astype(ml_dtypes.bfloat16)
    low = (both - high.astype(np.float64)).astype(ml_dtypes.bfloat16)
    return high, low


def member(position):
    offset = 0
    for bit, mask in ((4, X_LO), (2, Y_A), (1, Y_B)):
        if position & bit:
            offset ^= mask
    return offset


def halves(value):
    high = value.astype(jnp.bfloat16)
    low = (value - high.astype(jnp.float32)).astype(jnp.bfloat16)
    return high, low


def product(left, right):
    def dot(a, b):
        return jnp.dot(a, b, preferred_element_type=jnp.float32)

    return dot(left[0], right[0]) + dot(left[0], right[1]) + dot(left[1], right[0])


def transform(real, imag, tall, wide, sign):
    cols = product(tall, halves(jnp.concatenate([real, imag], axis=1)))
    left_real = cols[:WIN, :WIN] - sign * cols[WIN:, WIN:]
    left_imag = cols[:WIN, WIN:] + sign * cols[WIN:, :WIN]
    rows = product(halves(jnp.concatenate([left_real, left_imag], axis=0)), wide)
    right_real = rows[:WIN, :WIN] - sign * rows[WIN:, WIN:]
    right_imag = rows[WIN:, :WIN] + sign * rows[:WIN, WIN:]
    return right_real, right_imag


def piece_of(tile, group):
    y_b = (group >> 2) & 1
    y_a = ((group >> 1) & 1) ^ y_b
    return (tile & 1) * 8 + (group & 1) * 4 + y_a * 2 + y_b


def window_kernel(
    place, row_ref, col_ref, live_ref, mid, near, far, probe, amps, high, low,
    send, keep, near_out, far_out, mid_out, peak, field, grads,
):
    tile, group = place[0], place[1]
    row, col = row_ref[0], col_ref[0]
    live = live_ref[0].astype(jnp.float32)
    odd = tile & 1
    for position in range(8):
        top = pl.multiple_of((group ^ member(position)) * 40, 8)
        for part in range(2):
            field[part, 1, pl.ds(top, 40), :] = mid[position, part]
            field[part, 2 - 2 * odd, pl.ds(top, 40), :] = near[position, part]
            field[part, 2 * odd, pl.ds(top, 40), :] = far[position, part]
    lane = lax.broadcasted_iota(jnp.int32, (WIN, LANES), 1)
    back = lax.rem(LANES - col, LANES)
    ahead = lax.rem(col, LANES)
    first = lane < LANES - col

    def cut(part):
        turned = [
            pltpu.roll(field[part, block, pl.ds(row, WIN), :], back, 1) for block in range(3)
        ]
        return jnp.concatenate(
            [jnp.where(first, turned[0], turned[1]), jnp.where(first, turned[1], turned[2])], axis=1
        )

    sample_real, sample_imag = cut(0), cut(1)
    probe_real, probe_imag = probe[0], probe[1]
    exit_real = probe_real * sample_real - probe_imag * sample_imag
    exit_imag = probe_real * sample_imag + probe_imag * sample_real
    tall = (high[...], low[...])
    wide = tuple(jnp.concatenate([table[:WIN], table[WIN:]], axis=1) for table in tall)
    far_real, far_imag = transform(exit_real, exit_imag, tall, wide, -1.0)
    power = far_real * far_real + far_imag * far_imag
    factor = 1.0 - amps[0] * lax.rsqrt(jnp.maximum(power, 0.0625))
    miss_real, miss_imag = transform(far_real * factor, far_imag * factor, tall, wide, 1.0)
    miss_real = miss_real * live
    miss_imag = miss_imag * live
    light = probe_real * probe_real + probe_imag * probe_imag
    peak[...] = jnp.full((8, LANES), jnp.max(light), jnp.float32)

    terms = (
        probe_real * miss_real + probe_imag * miss_imag,
        probe_real * miss_imag - probe_imag * miss_real,
        live * light,
    )
    wrapped = lane < col
    zero = jnp.zeros((WIN, LANES), jnp.float32)
    grads[...] = jnp.zeros_like(grads)
    for part in range(3):
        start = pltpu.roll(terms[part][:, :LANES], ahead, 1)
        end = pltpu.roll(terms[part][:, LANES:], ahead, 1)
        grads[part, 0, pl.ds(row, WIN), :] = jnp.where(wrapped, zero, start)
        grads[part, 1, pl.ds(row, WIN), :] = jnp.where(wrapped, start, end)
        grads[part, 2, pl.ds(row, WIN), :] = jnp.where(wrapped, end, zero)
    for position in range(8):
        top = pl.multiple_of((group ^ member(position)) * 40, 8)
        for part in range(3):
            mid_out[position, part] = grads[part, 1, pl.ds(top, 40), :]
            near_out[position, part] = grads[part, 2 - 2 * odd, pl.ds(top, 40), :]
            far_out[position, part] = grads[part, 2 * odd, pl.ds(top, 40), :]

    window_light = live * (sample_real * sample_real + sample_imag * sample_imag)
    sums = (
        sample_real * miss_real + sample_imag * miss_imag,
        sample_real * miss_imag - sample_imag * miss_real,
        window_light,
    )
    total = jnp.zeros((8, LANES), jnp.float32)
    for line in range(0, WIN, 8):
        total = total + window_light[line : line + 8, :LANES] + window_light[line : line + 8, LANES:]
    mine = piece_of(tile, group)
    keep_top = mine >> 3
    for piece in range(16):
        entry = piece ^ (mine & 7)
        slot = entry & 7
        for part in range(3):
            for side in range(2):
                lines = pl.ds(part * 32 + side * 16, 16)
                value = sums[part][piece * 16 : piece * 16 + 16, side * LANES : (side + 1) * LANES]
                grads_store(send, keep, (piece >> 3) == keep_top, slot, lines, value)
        grads_store(send, keep, (piece >> 3) == keep_top, slot, pl.ds(96, 8), total)


def grads_store(send, keep, stays, slot, lines, value):
    @pl.when(stays)
    def _():
        keep[slot, lines, :] = value

    @pl.when(jnp.logical_not(stays))
    def _():
        send[slot, lines, :] = value


def probe_kernel(place, one, two, probe, out):
    piece = piece_of(place[0], place[1])
    summed = one[0] + two[0]
    mean = jnp.sum(summed[96:104]) * (1.0 / (WIN * WIN))
    for side in range(2):
        bottom = summed[64 + side * 16 : 80 + side * 16] + 0.25 * mean + 1e-05
        for part in range(2):
            lines = part * 32 + side * 16
            top = pl.multiple_of(piece * 16, 16)
            old = probe[part, pl.ds(top, 16), side * LANES : (side + 1) * LANES]
            out[0, lines : lines + 16, :] = old - summed[lines : lines + 16] / bottom


def gather_kernel(place, one, two, out):
    piece = piece_of(place[0], place[1])
    for entry in range(16):
        source, slot = (one, entry) if entry < 8 else (two, entry - 8)
        top = pl.multiple_of((piece ^ entry) * 16, 16)
        for part in range(2):
            for side in range(2):
                lines = part * 32 + side * 16
                out[part, pl.ds(top, 16), side * LANES : (side + 1) * LANES] = source[
                    slot, lines : lines + 16, :
                ]


def object_kernel(one, two, old, peak, out):
    summed = one[0] + two[0]
    bottom = summed[2] + 0.25 * (peak[0:1, :] + 1e-06)
    out[0] = old[0] - summed[0] / bottom
    out[1] = old[1] - summed[1] / bottom


def pair_up(axis, mask):
    return [(i, i ^ mask) for i in range(lax.axis_size(axis))]


def swap(value, axis, mask):
    return lax.ppermute(value, axis, pair_up(axis, mask))


def swap_far(value):
    count = lax.axis_size("tile")
    pairs = []
    for i in range(1, count - 1, 2):
        pairs += [(i, i + 1), (i + 1, i)]
    return lax.ppermute(value, "tile", pairs)


def local(object_field, probe_field, amplitudes, row_start, column_start, live_slots):
    f32 = jnp.float32
    smem, vmem = pl.BlockSpec(memory_space=SMEM), pl.BlockSpec(memory_space=VMEM)
    place = jnp.stack([lax.axis_index("tile"), lax.axis_index("group")]).astype(jnp.int32)
    high, low = split_tables()

    held = object_field[None]
    for mask in (Y_B, Y_A, X_LO):
        held = jnp.concatenate([held, swap(held, "group", mask)], axis=0)
    near, far = swap(held, "tile", 1), swap_far(held)

    shape = jax.ShapeDtypeStruct
    send, keep, near_out, far_out, mid_out, peak = pl.pallas_call(
        window_kernel,
        out_shape=(
            shape((8, 104, LANES), f32),
            shape((8, 104, LANES), f32),
            shape((8, 3, 40, LANES), f32),
            shape((8, 3, 40, LANES), f32),
            shape((8, 3, 40, LANES), f32),
            shape((8, LANES), f32),
        ),
        in_specs=[smem] * 4 + [vmem] * 7,
        out_specs=(vmem,) * 6,
        scratch_shapes=[
            pltpu.VMEM((2, 3, 320, LANES), f32),
            pltpu.VMEM((3, 3, 320, LANES), f32),
        ],
        name="window",
    )(
        place, row_start, column_start, live_slots, held, near, far,
        probe_field, amplitudes, jnp.asarray(high), jnp.asarray(low),
    )

    got = swap(send, "tile", 1)
    for count, mask in ((4, X_LO), (2, Y_A), (1, Y_B)):
        send, keep = keep[count:] + got[count:], keep[:count] + got[:count]
        got = swap(send, "group", mask)
    for mask in (2, 4, 8):
        keep = keep + got
        got = swap(keep, "tile", mask)
    keep = keep + got
    got = swap(keep, "tile", 28)
    piece = pl.pallas_call(
        probe_kernel,
        out_shape=shape((1, 64, LANES), f32),
        in_specs=[smem] + [vmem] * 3,
        out_specs=vmem,
        name="probe",
    )(place, keep, got, probe_field)

    mine = mid_out + swap(near_out, "tile", 1) + swap_far(far_out)
    for count, mask in ((4, X_LO), (2, Y_A), (1, Y_B)):
        got = swap(mine[count:], "group", mask)
        if count > 1:
            mine = mine[:count] + got
    new_object = pl.pallas_call(
        object_kernel,
        out_shape=shape((2, 40, LANES), f32),
        in_specs=[vmem] * 4,
        out_specs=vmem,
        name="object",
    )(mine[:1], got, object_field, peak)

    for mask in (Y_B, Y_A, X_LO):
        piece = jnp.concatenate([piece, swap(piece, "group", mask)], axis=0)
    new_probe = pl.pallas_call(
        gather_kernel,
        out_shape=shape((2, WIN, WIN), f32),
        in_specs=[smem] + [vmem] * 2,
        out_specs=vmem,
        name="gather",
    )(place, piece, swap(piece, "tile", 1))
    return new_object, new_probe


def solution(mesh):
    return jax.shard_map(
        local,
        mesh=mesh,
        in_specs=(
            P(None, "group", "tile"),
            P(),
            P(("tile", "group"), None, None),
            P(("tile", "group")),
            P(("tile", "group")),
            P(("tile", "group")),
        ),
        out_specs=(P(None, "group", "tile"), P()),
        check_vma=False,
    )
```

time: 371 us -> 118 us (0.32)
  waiting for transfers between devices: 258 us -> 39.2 us
  starting transfers between devices: 20.7 us -> 54.9 us
  blocking collectives: 24.9 us -> 0 us
  matrix products: 24.1 us -> 0 us
  between operations: 19 us -> 2.76 us
  Pallas kernels: 0 us -> 12.6 us
  local copies, waits for them, and re-layouts: 12.1 us -> 4.09 us
  other arithmetic: 11.4 us -> 3.55 us
    psum x1 -> x0, waiting for transfers between devices: 247 us -> none  [local(): lax.psum((probe_grad, window_light), ('tile', 'group'))]
    ppermute x4 -> x22, starting transfers between devices: 20.6 us -> 54.9 us  [the longest x20 40.4 us: swap(): return lax.ppermute(value, axis, pair_up(axis, mask))]
    ppermute x4 -> x22, waiting for transfers between devices: 10.6 us -> 39.2 us  [the longest x20 35.4 us: swap(): return lax.ppermute(value, axis, pair_up(axis, mask))]
    all_gather x1 -> x0, blocking collectives: 24.9 us -> none  [local(): full_rows = lax.all_gather(object_field, 'group', axis=1, tiled=True)]
    dot_general x16 -> x0, matrix products: 24.1 us -> none  [the longest x8 12.3 us: apply_right(): jnp.einsum('pjk,kl->pjl', values, matrix, precision=lax.Precision.HIGHEST)]
    pallas_call x0 -> x4, Pallas kernels: none -> 12.6 us  [the longest x1 7.41 us: local(): pl.pallas_call(window_kernel, out_shape=(shape((8, 104, LANES), f32), sha...]
    dynamic_update_slice x1 -> x0, local copies, waits for them, and re-layouts: 11.1 us -> none  [place(): return lax.dynamic_update_slice(current, piece + terms[slot], corner)]
  transfers between devices with their start and end apart: 6 -> 22, of which waited for: 5 -> 16; matrix products, arithmetic and copies ran while one was open for 2% -> 2% of each run, Pallas kernels for 0% -> 3%
where the time goes in v1:
time: 118 us; the launch traced here: 117 us
  starting transfers between devices  54.9 us (47%)
  waiting for transfers between devices  39.2 us (33%)
  Pallas kernels  12.6 us (11%)
  local copies, waits for them, and re-layouts  4.09 us (3%)
  other arithmetic  3.55 us (3%)
  between operations  2.76 us (2%)
    ppermute x20, starting transfers between devices, swap(): return lax.ppermute(value, axis, pair_up(axis, mask))  40.4 us
    ppermute x20, waiting for transfers between devices, swap(): return lax.ppermute(value, axis, pair_up(axis, mask))  35.4 us
    ppermute x2, starting transfers between devices, swap_far(): return lax.ppermute(value, 'tile', pairs)  14.5 us
    pallas_call x1, Pallas kernels, local(): pl.pallas_call(window_kernel, out_shape=(shape((8, 104, LANES), f32), sha...  7.41 us
    ppermute x2, waiting for transfers between devices, swap_far(): return lax.ppermute(value, 'tile', pairs)  3.79 us
    unnamed x26, local copies, waits for them, and re-layouts  3.43 us
  transfers between devices with their start and end apart: 22, of which 16 were waited for; matrix products, arithmetic and copies ran while one was open for 2% of the time, Pallas kernels for 3%

profile of v1, /device:TPU:1, one launch (start us, length us, event | category | flops | bytes accessed | tf_op | source)
XLA Modules:
  0.0 117.1 jit_solution(6554380957722827805)
XLA Ops:
  0.6 3.7 %collective-permute-start = (f32[1,2,40,128]{3,2,1,0:T(8,128)}, f32[1,2,40,128]{3,2,1,0:T(8,128)S(1)}, u32[]{:S(2)}, u32[]{:S(2)}) collective-permute-start(f32[1,2,40,128]{3,2,1,0:T(8,128)} %bitcast.3), channel_id=1, source_target_pairs={{0,6},{1,7},{2,4},{3,5},{4,2},{5,3},{6,0},{7,1},{8,14},{9,15},{10,... | collective-permute-start | bytes 122888 | tf_op jit(solution)/shard_map/ppermute | solution.py:197
  4.3 1.6 %collective-permute-done = f32[1,2,40,128]{3,2,1,0:T(8,128)S(1)} collective-permute-done((f32[1,2,40,128]{3,2,1,0:T(8,128)}, f32[1,2,40,128]{3,2,1,0:T(8,128)S(1)}, u32[]{:S(2)}, u32[]{:S(2)}) %collective-permute-start) | collective-permute-done | bytes 40992 | tf_op jit(solution)/shard_map/ppermute | solution.py:197
  5.9 0.8 pad_maximum_fusion.4
  6.7 3.3 %collective-permute-done.1 = f32[2,2,40,128]{3,2,1,0:T(8,128)S(1)} collective-permute-done((f32[2,2,40,128]{3,2,1,0:T(8,128)S(1)}, f32[2,2,40,128]{3,2,1,0:T(8,128)S(1)}, u32[]{:S(2)}, u32[]{:S(2)}) %collective-permute-start.1) | collective-permute-done | bytes 81952 | tf_op jit(solution)/shard_map/ppermute | solution.py:197
  10.0 1.3 %collective-permute-start.2 = (f32[4,2,40,128]{3,2,1,0:T(8,128)S(1)}, f32[4,2,40,128]{3,2,1,0:T(8,128)S(1)}, u32[]{:S(2)}, u32[]{:S(2)}) collective-permute-start(f32[4,2,40,128]{3,2,1,0:T(8,128)S(1)} %pad_maximum_fusion.2), channel_id=1, source_target_pairs={{0,1},{1,0},{2,3},{3,2},{4,5},{5,4},{6,7},{7,6},{8,9},{9,8},{10,11... | collective-permute-start | bytes 491528 | tf_op jit(solution)/shard_map/ppermute | solution.py:197
  11.3 3.0 %collective-permute-done.2 = f32[4,2,40,128]{3,2,1,0:T(8,128)S(1)} collective-permute-done((f32[4,2,40,128]{3,2,1,0:T(8,128)S(1)}, f32[4,2,40,128]{3,2,1,0:T(8,128)S(1)}, u32[]{:S(2)}, u32[]{:S(2)}) %collective-permute-start.2) | collective-permute-done | bytes 163872 | tf_op jit(solution)/shard_map/ppermute | solution.py:197
  14.3 8.6 %collective-permute-start.4 = (f32[8,2,40,128]{3,2,1,0:T(8,128)S(1)}, f32[8,2,40,128]{3,2,1,0:T(8,128)S(1)}, u32[]{:S(2)}, u32[]{:S(2)}) collective-permute-start(f32[8,2,40,128]{3,2,1,0:T(8,128)S(1)} %pad_maximum_fusion.mid), channel_id=1, source_target_pairs={{8,16},{16,8},{24,32},{32,24},{40,48},{48,40},{56,64},{64,56},{72,... | collective-permute-start | bytes 983048 | tf_op jit(solution)/shard_map/ppermute | solution.py:205
  24.9 0.6 pad_add_fusion.place
  25.5 3.8 %collective-permute-done.4.far = f32[8,2,40,128]{3,2,1,0:T(8,128)S(1)} collective-permute-done((f32[8,2,40,128]{3,2,1,0:T(8,128)S(1)}, f32[8,2,40,128]{3,2,1,0:T(8,128)S(1)}, u32[]{:S(2)}, u32[]{:S(2)}) %collective-permute-start.4) | collective-permute-done | bytes 327712 | tf_op jit(solution)/shard_map/ppermute | solution.py:205
  29.3 0.7 copy-done.5
  30.1 0.7 copy-done.6
  30.8 7.4 %window.1 = (f32[8,104,128]{2,1,0:T(8,128)}, f32[8,104,128]{2,1,0:T(8,128)}, f32[8,3,40,128]{3,2,1,0:T(8,128)}, f32[8,3,40,128]{3,2,1,0:T(8,128)}, f32[8,3,40,128]{3,2,1,0:T(8,128)}, /*index=5*/f32[8,128]{1,0:T(8,128)}) custom-call(s32[2]{0:T(128)} %pad_add_fusion.place, s32[1]{0:T(128)S(6)} %copy.10.row_ref, s32[1]{0:T(128)S(6)} %copy.11.col_ref, ...), custom_call_target="tpu_custom_call" | custom-call | tf_op jit(solution)/shard_map/window/pallas_call | solution.py:220
  38.2 2.0 %collective-permute-done.10 = f32[8,104,128]{2,1,0:T(8,128)S(1)} collective-permute-done((f32[8,104,128]{2,1,0:T(8,128)}, f32[8,104,128]{2,1,0:T(8,128)S(1)}, u32[]{:S(2)}, u32[]{:S(2)}) %collective-permute-start.10) | collective-permute-done | bytes 426016 | tf_op jit(solution)/shard_map/ppermute | solution.py:197
  40.2 1.2 slice_add_fusion.2
  41.3 1.3 %collective-permute-start.11 = (f32[4,104,128]{2,1,0:T(8,128)S(1)}, f32[4,104,128]{2,1,0:T(8,128)S(1)}, u32[]{:S(2)}, u32[]{:S(2)}) collective-permute-start(f32[4,104,128]{2,1,0:T(8,128)S(1)} %get-tuple-element.15), channel_id=1, source_target_pairs={{0,1},{1,0},{2,3},{3,2},{4,5},{5,4},{6,7},{7,6},{8,9},{9,8},{10,11... | collective-permute-start | bytes 638984 | tf_op jit(solution)/shard_map/ppermute | solution.py:197
  42.6 5.5 %collective-permute-done.11 = f32[4,104,128]{2,1,0:T(8,128)S(1)} collective-permute-done((f32[4,104,128]{2,1,0:T(8,128)S(1)}, f32[4,104,128]{2,1,0:T(8,128)S(1)}, u32[]{:S(2)}, u32[]{:S(2)}) %collective-permute-start.11) | collective-permute-done | bytes 213024 | tf_op jit(solution)/shard_map/ppermute | solution.py:197
  48.4 1.2 %collective-permute-start.5 = (f32[8,3,40,128]{3,2,1,0:T(8,128)S(1)}, f32[8,3,40,128]{3,2,1,0:T(8,128)S(1)}, u32[]{:S(2)}, u32[]{:S(2)}) collective-permute-start(f32[8,3,40,128]{3,2,1,0:T(8,128)S(1)} %copy-done.12), channel_id=1, source_target_pairs={{0,8},{8,0},{16,24},{24,16},{32,40},{40,32},{48,56},{56,48},{64,72... | collective-permute-start | bytes 1474568 | tf_op jit(solution)/shard_map/ppermute | solution.py:197
  49.6 5.9 %collective-permute-start.6 = (f32[8,3,40,128]{3,2,1,0:T(8,128)S(1)}, f32[8,3,40,128]{3,2,1,0:T(8,128)S(1)}, u32[]{:S(2)}, u32[]{:S(2)}) collective-permute-start(f32[8,3,40,128]{3,2,1,0:T(8,128)S(1)} %copy-done.11), channel_id=1, source_target_pairs={{8,16},{16,8},{24,32},{32,24},{40,48},{48,40},{56,64},{64,56},{72,... | collective-permute-start | bytes 1474568 | tf_op jit(solution)/shard_map/ppermute | solution.py:205
  55.5 2.6 %collective-permute-start.13 = (f32[1,104,128]{2,1,0:T(8,128)S(1)}, f32[1,104,128]{2,1,0:T(8,128)S(1)}, u32[]{:S(2)}, u32[]{:S(2)}) collective-permute-start(f32[1,104,128]{2,1,0:T(8,128)S(1)} %slice_add_fusion.6), channel_id=1, source_target_pairs={{0,6},{1,7},{2,4},{3,5},{4,2},{5,3},{6,0},{7,1},{8,14},{9,15},{10,... | collective-permute-start | bytes 159752 | tf_op jit(solution)/shard_map/ppermute | solution.py:197
  58.1 1.7 %collective-permute-done.13 = f32[1,104,128]{2,1,0:T(8,128)S(1)} collective-permute-done((f32[1,104,128]{2,1,0:T(8,128)S(1)}, f32[1,104,128]{2,1,0:T(8,128)S(1)}, u32[]{:S(2)}, u32[]{:S(2)}) %collective-permute-start.13) | collective-permute-done | bytes 53280 | tf_op jit(solution)/shard_map/ppermute | solution.py:197
  59.8 2.3 %collective-permute-start.14 = (f32[1,104,128]{2,1,0:T(8,128)S(1)}, f32[1,104,128]{2,1,0:T(8,128)S(1)}, u32[]{:S(2)}, u32[]{:S(2)}) collective-permute-start(f32[1,104,128]{2,1,0:T(8,128)S(1)} %fusion), channel_id=1, source_target_pairs={{0,16},{8,24},{16,0},{24,8},{32,48},{40,56},{48,32},{56,40},{64,80... | collective-permute-start | bytes 159752 | tf_op jit(solution)/shard_map/ppermute | solution.py:197
  62.1 5.5 %collective-permute-done.14 = f32[1,104,128]{2,1,0:T(8,128)S(1)} collective-permute-done((f32[1,104,128]{2,1,0:T(8,128)S(1)}, f32[1,104,128]{2,1,0:T(8,128)S(1)}, u32[]{:S(2)}, u32[]{:S(2)}) %collective-permute-start.14) | collective-permute-done | bytes 53280 | tf_op jit(solution)/shard_map/ppermute | solution.py:197
  67.7 1.6 %collective-permute-start.15 = (f32[1,104,128]{2,1,0:T(8,128)S(1)}, f32[1,104,128]{2,1,0:T(8,128)S(1)}, u32[]{:S(2)}, u32[]{:S(2)}) collective-permute-start(f32[1,104,128]{2,1,0:T(8,128)S(1)} %add.53), channel_id=1, source_target_pairs={{0,32},{8,40},{16,48},{24,56},{32,0},{40,8},{48,16},{56,24},{64,96... | collective-permute-start | bytes 159752 | tf_op jit(solution)/shard_map/ppermute | solution.py:197
  69.3 1.5 %collective-permute-done.15 = f32[1,104,128]{2,1,0:T(8,128)S(1)} collective-permute-done((f32[1,104,128]{2,1,0:T(8,128)S(1)}, f32[1,104,128]{2,1,0:T(8,128)S(1)}, u32[]{:S(2)}, u32[]{:S(2)}) %collective-permute-start.15) | collective-permute-done | bytes 53280 | tf_op jit(solution)/shard_map/ppermute | solution.py:197
  70.8 3.8 %collective-permute-start.16 = (f32[1,104,128]{2,1,0:T(8,128)S(1)}, f32[1,104,128]{2,1,0:T(8,128)S(1)}, u32[]{:S(2)}, u32[]{:S(2)}) collective-permute-start(f32[1,104,128]{2,1,0:T(8,128)S(1)} %add.54), channel_id=1, source_target_pairs={{0,64},{8,72},{16,80},{24,88},{32,96},{40,104},{48,112},{56,120},{... | collective-permute-start | bytes 159752 | tf_op jit(solution)/shard_map/ppermute | solution.py:197
  74.7 0.4 collective-permute-start.7
  75.1 1.0 collective-permute-done.16
  76.2 2.8 %collective-permute-start.17 = (f32[1,104,128]{2,1,0:T(8,128)S(1)}, f32[1,104,128]{2,1,0:T(8,128)S(1)}, u32[]{:S(2)}, u32[]{:S(2)}) collective-permute-start(f32[1,104,128]{2,1,0:T(8,128)S(1)} %add.55.one), channel_id=1, source_target_pairs={{0,224},{8,232},{16,240},{24,248},{32,192},{40,200},{48,208},{56,2... | collective-permute-start | bytes 159752 | tf_op jit(solution)/shard_map/ppermute | solution.py:197
  79.0 1.5 %collective-permute-done.17.two = f32[1,104,128]{2,1,0:T(8,128)S(1)} collective-permute-done((f32[1,104,128]{2,1,0:T(8,128)S(1)}, f32[1,104,128]{2,1,0:T(8,128)S(1)}, u32[]{:S(2)}, u32[]{:S(2)}) %collective-permute-start.17) | collective-permute-done | bytes 53280 | tf_op jit(solution)/shard_map/ppermute | solution.py:197
  80.5 0.6 copy-done.10
  81.1 1.9 %probe.4 = f32[1,64,128]{2,1,0:T(8,128)} custom-call(s32[2]{0:T(128)} %pad_add_fusion.place, f32[1,104,128]{2,1,0:T(8,128)} %copy-done.8, f32[1,104,128]{2,1,0:T(8,128)} %copy-done.10, f32[2,256,256]{2,1,0:T(8,128)} %probe.5), custom_call_target="tpu_custom_call" | custom-call | tf_op jit(solution)/shard_map/probe/pallas_call | solution.py:251
  83.0 2.5 %collective-permute-start.18 = (f32[1,64,128]{2,1,0:T(8,128)}, f32[1,64,128]{2,1,0:T(8,128)S(1)}, u32[]{:S(2)}, u32[]{:S(2)}) collective-permute-start(f32[1,64,128]{2,1,0:T(8,128)} %probe.4), channel_id=1, source_target_pairs={{0,6},{1,7},{2,4},{3,5},{4,2},{5,3},{6,0},{7,1},{8,14},{9,15},{10,... | collective-permute-start | bytes 98312 | tf_op jit(solution)/shard_map/ppermute | solution.py:197
  85.5 2.0 %collective-permute-done.18 = f32[1,64,128]{2,1,0:T(8,128)S(1)} collective-permute-done((f32[1,64,128]{2,1,0:T(8,128)}, f32[1,64,128]{2,1,0:T(8,128)S(1)}, u32[]{:S(2)}, u32[]{:S(2)}) %collective-permute-start.18) | collective-permute-done | bytes 32800 | tf_op jit(solution)/shard_map/ppermute | solution.py:197
  87.5 0.8 pad_maximum_fusion.5
  88.2 0.5 collective-permute-start.19
  88.8 1.0 collective-permute-start.8
  89.8 1.5 %collective-permute-done.19 = f32[2,64,128]{2,1,0:T(8,128)S(1)} collective-permute-done((f32[2,64,128]{2,1,0:T(8,128)S(1)}, f32[2,64,128]{2,1,0:T(8,128)S(1)}, u32[]{:S(2)}, u32[]{:S(2)}) %collective-permute-start.19) | collective-permute-done | bytes 65568 | tf_op jit(solution)/shard_map/ppermute | solution.py:197
  91.4 1.0 collective-permute-start.20
  92.3 0.3 collective-permute-done.8
  92.7 2.6 %collective-permute-done.20 = f32[4,64,128]{2,1,0:T(8,128)S(1)} collective-permute-done((f32[4,64,128]{2,1,0:T(8,128)S(1)}, f32[4,64,128]{2,1,0:T(8,128)S(1)}, u32[]{:S(2)}, u32[]{:S(2)}) %collective-permute-start.20) | collective-permute-done | bytes 131104 | tf_op jit(solution)/shard_map/ppermute | solution.py:197
  95.3 11.6 %collective-permute-start.21 = (f32[8,64,128]{2,1,0:T(8,128)S(1)}, f32[8,64,128]{2,1,0:T(8,128)S(1)}, u32[]{:S(2)}, u32[]{:S(2)}) collective-permute-start(f32[8,64,128]{2,1,0:T(8,128)S(1)} %pad_maximum_fusion.1.one), channel_id=1, source_target_pairs={{0,8},{8,0},{16,24},{24,16},{32,40},{40,32},{48,56},{56,48},{64,72... | collective-permute-start | bytes 786440 | tf_op jit(solution)/shard_map/ppermute | solution.py:197
  106.9 0.6 fusion.1
  107.5 2.5 %collective-permute-start.9 = (f32[1,3,40,128]{3,2,1,0:T(8,128)S(1)}, f32[1,3,40,128]{3,2,1,0:T(8,128)S(1)}, u32[]{:S(2)}, u32[]{:S(2)}) collective-permute-start(f32[1,3,40,128]{3,2,1,0:T(8,128)S(1)} %get-tuple-element.18), channel_id=1, source_target_pairs={{0,6},{1,7},{2,4},{3,5},{4,2},{5,3},{6,0},{7,1},{8,14},{9,15},{10,... | collective-permute-start | bytes 184328 | tf_op jit(solution)/shard_map/ppermute | solution.py:197
  110.0 2.4 %collective-permute-done.9.two = f32[1,3,40,128]{3,2,1,0:T(8,128)S(1)} collective-permute-done((f32[1,3,40,128]{3,2,1,0:T(8,128)S(1)}, f32[1,3,40,128]{3,2,1,0:T(8,128)S(1)}, u32[]{:S(2)}, u32[]{:S(2)}) %collective-permute-start.9) | collective-permute-done | bytes 61472 | tf_op jit(solution)/shard_map/ppermute | solution.py:197
  112.4 0.6 copy-done.9
  113.0 1.5 %object.1 = f32[2,40,128]{2,1,0:T(8,128)} custom-call(f32[1,3,40,128]{3,2,1,0:T(8,128)} %get-tuple-element.19.one, f32[1,3,40,128]{3,2,1,0:T(8,128)} %copy-done.9, f32[2,40,128]{2,1,0:T(8,128)} %old.1, f32[8,128]{1,0:T(8,128)} %get-tuple-element.11.peak), custom_call_target="tpu_custom_call" | custom-call | tf_op jit(solution)/shard_map/object/pallas_call | solution.py:264
  114.5 0.7 copy-done.7
  115.2 1.9 %gather.1 = f32[2,256,256]{2,1,0:T(8,128)} custom-call(s32[2]{0:T(128)} %pad_add_fusion.place, f32[8,64,128]{2,1,0:T(8,128)} %copy-done.1, f32[8,64,128]{2,1,0:T(8,128)} %copy-done.7), custom_call_target="tpu_custom_call" | custom-call | tf_op jit(solution)/shard_map/gather/pallas_call | solution.py:274
  (46 shorter events, 0.6 us)
Async XLA Ops:
  0.6 9.3 %copy-start.2 = (f32[2,40,128]{2,1,0:T(8,128)S(1)}, f32[2,40,128]{2,1,0:T(8,128)}, u32[]{:S(2)}) copy-start(f32[2,40,128]{2,1,0:T(8,128)} %old.1) | copy-start | bytes 122884
  0.6 5.3 %collective-permute-start = (f32[1,2,40,128]{3,2,1,0:T(8,128)}, f32[1,2,40,128]{3,2,1,0:T(8,128)S(1)}, u32[]{:S(2)}, u32[]{:S(2)}) collective-permute-start(f32[1,2,40,128]{3,2,1,0:T(8,128)} %bitcast.3), channel_id=1, source_target_pairs={{0,6},{1,7},{2,4},{3,5},{4,2},{5,3},{6,0},{7,1},{8,14},{9,15},{10,... | collective-permute-start | bytes 122888 | tf_op jit(solution)/shard_map/ppermute | solution.py:197
  6.7 3.3 %collective-permute-start.1 = (f32[2,2,40,128]{3,2,1,0:T(8,128)S(1)}, f32[2,2,40,128]{3,2,1,0:T(8,128)S(1)}, u32[]{:S(2)}, u32[]{:S(2)}) collective-permute-start(f32[2,2,40,128]{3,2,1,0:T(8,128)S(1)} %pad_maximum_fusion.4), channel_id=1, source_target_pairs={{0,2},{1,3},{2,0},{3,1},{4,6},{5,7},{6,4},{7,5},{8,10},{9,11},{10,... | collective-permute-start | bytes 245768 | tf_op jit(solution)/shard_map/ppermute | solution.py:197
  10.0 4.3 %collective-permute-start.2 = (f32[4,2,40,128]{3,2,1,0:T(8,128)S(1)}, f32[4,2,40,128]{3,2,1,0:T(8,128)S(1)}, u32[]{:S(2)}, u32[]{:S(2)}) collective-permute-start(f32[4,2,40,128]{3,2,1,0:T(8,128)S(1)} %pad_maximum_fusion.2), channel_id=1, source_target_pairs={{0,1},{1,0},{2,3},{3,2},{4,5},{5,4},{6,7},{7,6},{8,9},{9,8},{10,11... | collective-permute-start | bytes 491528 | tf_op jit(solution)/shard_map/ppermute | solution.py:197
  14.3 15.0 %copy-start = (f32[8,2,40,128]{3,2,1,0:T(8,128)}, f32[8,2,40,128]{3,2,1,0:T(8,128)S(1)}, u32[]{:S(2)}) copy-start(f32[8,2,40,128]{3,2,1,0:T(8,128)S(1)} %pad_maximum_fusion.mid) | copy-start | bytes 983044
  14.3 15.0 %collective-permute-start.4 = (f32[8,2,40,128]{3,2,1,0:T(8,128)S(1)}, f32[8,2,40,128]{3,2,1,0:T(8,128)S(1)}, u32[]{:S(2)}, u32[]{:S(2)}) collective-permute-start(f32[8,2,40,128]{3,2,1,0:T(8,128)S(1)} %pad_maximum_fusion.mid), channel_id=1, source_target_pairs={{8,16},{16,8},{24,32},{32,24},{40,48},{48,40},{56,64},{64,56},{72,... | collective-permute-start | bytes 983048 | tf_op jit(solution)/shard_map/ppermute | solution.py:205
  22.9 6.4 %collective-permute-start.3 = (f32[8,2,40,128]{3,2,1,0:T(8,128)S(1)}, f32[8,2,40,128]{3,2,1,0:T(8,128)S(1)}, u32[]{:S(2)}, u32[]{:S(2)}) collective-permute-start(f32[8,2,40,128]{3,2,1,0:T(8,128)S(1)} %pad_maximum_fusion.mid), channel_id=1, source_target_pairs={{0,8},{8,0},{16,24},{24,16},{32,40},{40,32},{48,56},{56,48},{64,72... | collective-permute-start | bytes 983048 | tf_op jit(solution)/shard_map/ppermute | solution.py:197
  29.3 0.7 copy-start.5
  30.1 0.7 copy-start.6
  38.2 2.0 %collective-permute-start.10 = (f32[8,104,128]{2,1,0:T(8,128)}, f32[8,104,128]{2,1,0:T(8,128)S(1)}, u32[]{:S(2)}, u32[]{:S(2)}) collective-permute-start(f32[8,104,128]{2,1,0:T(8,128)} %get-tuple-element.13), channel_id=1, source_target_pairs={{0,8},{8,0},{16,24},{24,16},{32,40},{40,32},{48,56},{56,48},{64,72... | collective-permute-start | bytes 1277960 | tf_op jit(solution)/shard_map/ppermute | solution.py:197
  40.2 8.2 %copy-start.12 = (f32[8,3,40,128]{3,2,1,0:T(8,128)S(1)}, f32[8,3,40,128]{3,2,1,0:T(8,128)}, u32[]{:S(2)}) copy-start(f32[8,3,40,128]{3,2,1,0:T(8,128)} %get-tuple-element.9) | copy-start | bytes 1474564
  41.3 8.3 %copy-start.11 = (f32[8,3,40,128]{3,2,1,0:T(8,128)S(1)}, f32[8,3,40,128]{3,2,1,0:T(8,128)}, u32[]{:S(2)}) copy-start(f32[8,3,40,128]{3,2,1,0:T(8,128)} %get-tuple-element.10) | copy-start | bytes 1474564
  41.3 6.8 %collective-permute-start.11 = (f32[4,104,128]{2,1,0:T(8,128)S(1)}, f32[4,104,128]{2,1,0:T(8,128)S(1)}, u32[]{:S(2)}, u32[]{:S(2)}) collective-permute-start(f32[4,104,128]{2,1,0:T(8,128)S(1)} %get-tuple-element.15), channel_id=1, source_target_pairs={{0,1},{1,0},{2,3},{3,2},{4,5},{5,4},{6,7},{7,6},{8,9},{9,8},{10,11... | collective-permute-start | bytes 638984 | tf_op jit(solution)/shard_map/ppermute | solution.py:197
  48.2 26.5 %copy-start.4 = (f32[8,3,40,128]{3,2,1,0:T(8,128)S(1)}, f32[8,3,40,128]{3,2,1,0:T(8,128)}, u32[]{:S(2)}) copy-start(f32[8,3,40,128]{3,2,1,0:T(8,128)} %get-tuple-element.8) | copy-start | bytes 1474564
  48.2 7.3 %collective-permute-start.12 = (f32[2,104,128]{2,1,0:T(8,128)S(1)}, f32[2,104,128]{2,1,0:T(8,128)S(1)}, u32[]{:S(2)}, u32[]{:S(2)}) collective-permute-start(f32[2,104,128]{2,1,0:T(8,128)S(1)} %get-tuple-element.17), channel_id=1, source_target_pairs={{0,2},{1,3},{2,0},{3,1},{4,6},{5,7},{6,4},{7,5},{8,10},{9,11},{10,... | collective-permute-start | bytes 319496 | tf_op jit(solution)/shard_map/ppermute | solution.py:197
  48.4 26.3 %collective-permute-start.5 = (f32[8,3,40,128]{3,2,1,0:T(8,128)S(1)}, f32[8,3,40,128]{3,2,1,0:T(8,128)S(1)}, u32[]{:S(2)}, u32[]{:S(2)}) collective-permute-start(f32[8,3,40,128]{3,2,1,0:T(8,128)S(1)} %copy-done.12), channel_id=1, source_target_pairs={{0,8},{8,0},{16,24},{24,16},{32,40},{40,32},{48,56},{56,48},{64,72... | collective-permute-start | bytes 1474568 | tf_op jit(solution)/shard_map/ppermute | solution.py:197
  49.6 25.0 %collective-permute-start.6 = (f32[8,3,40,128]{3,2,1,0:T(8,128)S(1)}, f32[8,3,40,128]{3,2,1,0:T(8,128)S(1)}, u32[]{:S(2)}, u32[]{:S(2)}) collective-permute-start(f32[8,3,40,128]{3,2,1,0:T(8,128)S(1)} %copy-done.11), channel_id=1, source_target_pairs={{8,16},{16,8},{24,32},{32,24},{40,48},{48,40},{56,64},{64,56},{72,... | collective-permute-start | bytes 1474568 | tf_op jit(solution)/shard_map/ppermute | solution.py:205
  55.5 4.3 %collective-permute-start.13 = (f32[1,104,128]{2,1,0:T(8,128)S(1)}, f32[1,104,128]{2,1,0:T(8,128)S(1)}, u32[]{:S(2)}, u32[]{:S(2)}) collective-permute-start(f32[1,104,128]{2,1,0:T(8,128)S(1)} %slice_add_fusion.6), channel_id=1, source_target_pairs={{0,6},{1,7},{2,4},{3,5},{4,2},{5,3},{6,0},{7,1},{8,14},{9,15},{10,... | collective-permute-start | bytes 159752 | tf_op jit(solution)/shard_map/ppermute | solution.py:197
  59.8 7.8 %collective-permute-start.14 = (f32[1,104,128]{2,1,0:T(8,128)S(1)}, f32[1,104,128]{2,1,0:T(8,128)S(1)}, u32[]{:S(2)}, u32[]{:S(2)}) collective-permute-start(f32[1,104,128]{2,1,0:T(8,128)S(1)} %fusion), channel_id=1, source_target_pairs={{0,16},{8,24},{16,0},{24,8},{32,48},{40,56},{48,32},{56,40},{64,80... | collective-permute-start | bytes 159752 | tf_op jit(solution)/shard_map/ppermute | solution.py:197
  67.7 3.2 %collective-permute-start.15 = (f32[1,104,128]{2,1,0:T(8,128)S(1)}, f32[1,104,128]{2,1,0:T(8,128)S(1)}, u32[]{:S(2)}, u32[]{:S(2)}) collective-permute-start(f32[1,104,128]{2,1,0:T(8,128)S(1)} %add.53), channel_id=1, source_target_pairs={{0,32},{8,40},{16,48},{24,56},{32,0},{40,8},{48,16},{56,24},{64,96... | collective-permute-start | bytes 159752 | tf_op jit(solution)/shard_map/ppermute | solution.py:197
  70.8 5.3 %collective-permute-start.16 = (f32[1,104,128]{2,1,0:T(8,128)S(1)}, f32[1,104,128]{2,1,0:T(8,128)S(1)}, u32[]{:S(2)}, u32[]{:S(2)}) collective-permute-start(f32[1,104,128]{2,1,0:T(8,128)S(1)} %add.54), channel_id=1, source_target_pairs={{0,64},{8,72},{16,80},{24,88},{32,96},{40,104},{48,112},{56,120},{... | collective-permute-start | bytes 159752 | tf_op jit(solution)/shard_map/ppermute | solution.py:197
  74.7 14.0 %collective-permute-start.7 = (f32[4,3,40,128]{3,2,1,0:T(8,128)S(1)}, f32[4,3,40,128]{3,2,1,0:T(8,128)S(1)}, u32[]{:S(2)}, u32[]{:S(2)}) collective-permute-start(f32[4,3,40,128]{3,2,1,0:T(8,128)S(1)} %slice.73), channel_id=1, source_target_pairs={{0,1},{1,0},{2,3},{3,2},{4,5},{5,4},{6,7},{7,6},{8,9},{9,8},{10,11... | collective-permute-start | bytes 737288 | tf_op jit(solution)/shard_map/ppermute | solution.py:197
  76.2 4.3 %copy-start.8 = (f32[1,104,128]{2,1,0:T(8,128)}, f32[1,104,128]{2,1,0:T(8,128)S(1)}, u32[]{:S(2)}) copy-start(f32[1,104,128]{2,1,0:T(8,128)S(1)} %add.55.one) | copy-start | bytes 159748
  76.2 4.3 %collective-permute-start.17 = (f32[1,104,128]{2,1,0:T(8,128)S(1)}, f32[1,104,128]{2,1,0:T(8,128)S(1)}, u32[]{:S(2)}, u32[]{:S(2)}) collective-permute-start(f32[1,104,128]{2,1,0:T(8,128)S(1)} %add.55.one), channel_id=1, source_target_pairs={{0,224},{8,232},{16,240},{24,248},{32,192},{40,200},{48,208},{56,2... | collective-permute-start | bytes 159752 | tf_op jit(solution)/shard_map/ppermute | solution.py:197
  80.5 0.6 copy-start.10
  83.0 4.5 %collective-permute-start.18 = (f32[1,64,128]{2,1,0:T(8,128)}, f32[1,64,128]{2,1,0:T(8,128)S(1)}, u32[]{:S(2)}, u32[]{:S(2)}) collective-permute-start(f32[1,64,128]{2,1,0:T(8,128)} %probe.4), channel_id=1, source_target_pairs={{0,6},{1,7},{2,4},{3,5},{4,2},{5,3},{6,0},{7,1},{8,14},{9,15},{10,... | collective-permute-start | bytes 98312 | tf_op jit(solution)/shard_map/ppermute | solution.py:197
  88.2 3.1 %collective-permute-start.19 = (f32[2,64,128]{2,1,0:T(8,128)S(1)}, f32[2,64,128]{2,1,0:T(8,128)S(1)}, u32[]{:S(2)}, u32[]{:S(2)}) collective-permute-start(f32[2,64,128]{2,1,0:T(8,128)S(1)} %pad_maximum_fusion.5), channel_id=1, source_target_pairs={{0,2},{1,3},{2,0},{3,1},{4,6},{5,7},{6,4},{7,5},{8,10},{9,11},{10,... | collective-permute-start | bytes 196616 | tf_op jit(solution)/shard_map/ppermute | solution.py:197
  88.8 2.5 %copy-start.3 = (f32[1,64,128]{2,1,0:T(8,128)S(1)}, f32[1,64,128]{2,1,0:T(8,128)}, u32[]{:S(2)}) copy-start(f32[1,64,128]{2,1,0:T(8,128)} %probe.4) | copy-start | bytes 98308
  88.8 3.8 %collective-permute-start.8 = (f32[2,3,40,128]{3,2,1,0:T(8,128)S(1)}, f32[2,3,40,128]{3,2,1,0:T(8,128)S(1)}, u32[]{:S(2)}, u32[]{:S(2)}) collective-permute-start(f32[2,3,40,128]{3,2,1,0:T(8,128)S(1)} %slice.75), channel_id=1, source_target_pairs={{0,2},{1,3},{2,0},{3,1},{4,6},{5,7},{6,4},{7,5},{8,10},{9,11},{10,... | collective-permute-start | bytes 368648 | tf_op jit(solution)/shard_map/ppermute | solution.py:197
  91.4 3.9 %collective-permute-start.20 = (f32[4,64,128]{2,1,0:T(8,128)S(1)}, f32[4,64,128]{2,1,0:T(8,128)S(1)}, u32[]{:S(2)}, u32[]{:S(2)}) collective-permute-start(f32[4,64,128]{2,1,0:T(8,128)S(1)} %pad_maximum_fusion.3), channel_id=1, source_target_pairs={{0,1},{1,0},{2,3},{3,2},{4,5},{5,4},{6,7},{7,6},{8,9},{9,8},{10,11... | collective-permute-start | bytes 393224 | tf_op jit(solution)/shard_map/ppermute | solution.py:197
  95.3 19.2 %copy-start.1 = (f32[8,64,128]{2,1,0:T(8,128)}, f32[8,64,128]{2,1,0:T(8,128)S(1)}, u32[]{:S(2)}) copy-start(f32[8,64,128]{2,1,0:T(8,128)S(1)} %pad_maximum_fusion.1.one) | copy-start | bytes 786436
  95.3 19.2 %collective-permute-start.21 = (f32[8,64,128]{2,1,0:T(8,128)S(1)}, f32[8,64,128]{2,1,0:T(8,128)S(1)}, u32[]{:S(2)}, u32[]{:S(2)}) collective-permute-start(f32[8,64,128]{2,1,0:T(8,128)S(1)} %pad_maximum_fusion.1.one), channel_id=1, source_target_pairs={{0,8},{8,0},{16,24},{24,16},{32,40},{40,32},{48,56},{56,48},{64,72... | collective-permute-start | bytes 786440 | tf_op jit(solution)/shard_map/ppermute | solution.py:197
  107.5 4.8 %collective-permute-start.9 = (f32[1,3,40,128]{3,2,1,0:T(8,128)S(1)}, f32[1,3,40,128]{3,2,1,0:T(8,128)S(1)}, u32[]{:S(2)}, u32[]{:S(2)}) collective-permute-start(f32[1,3,40,128]{3,2,1,0:T(8,128)S(1)} %get-tuple-element.18), channel_id=1, source_target_pairs={{0,6},{1,7},{2,4},{3,5},{4,2},{5,3},{6,0},{7,1},{8,14},{9,15},{10,... | collective-permute-start | bytes 184328 | tf_op jit(solution)/shard_map/ppermute | solution.py:197
  112.4 0.6 copy-start.9
  114.5 0.7 copy-start.7

commit v2 on v1

v2 whole, which is shorter than its diff:
```python
import jax
import jax.numpy as jnp
import ml_dtypes
import numpy as np
from jax import lax
from jax.experimental import pallas as pl
from jax.experimental.pallas import tpu as pltpu
from jax.sharding import PartitionSpec as P

WIN = 256
LANES = 128
PIECE = 104
SMEM = pltpu.MemorySpace.SMEM
VMEM = pltpu.MemorySpace.VMEM


def split_tables():
    counter = np.arange(WIN)
    angles = 2.0 * np.pi / WIN * (counter[:, None] * counter[None, :] % WIN)
    cos, sin = np.cos(angles) / np.sqrt(WIN), np.sin(angles) / np.sqrt(WIN)
    both = np.concatenate([cos, sin], axis=0)
    high = both.astype(ml_dtypes.bfloat16)
    low = (both - high.astype(np.float64)).astype(ml_dtypes.bfloat16)
    return high, low


def halves(value):
    high = value.astype(jnp.bfloat16)
    low = (value - high.astype(jnp.float32)).astype(jnp.bfloat16)
    return high, low


def product(left, right):
    def dot(a, b):
        return jnp.dot(a, b, preferred_element_type=jnp.float32)

    return dot(left[0], right[0]) + dot(left[0], right[1]) + dot(left[1], right[0])


def transform(real, imag, tall, wide, sign):
    cols = product(tall, halves(jnp.concatenate([real, imag], axis=1)))
    left_real = cols[:WIN, :WIN] - sign * cols[WIN:, WIN:]
    left_imag = cols[:WIN, WIN:] + sign * cols[WIN:, :WIN]
    rows = product(halves(jnp.concatenate([left_real, left_imag], axis=0)), wide)
    right_real = rows[:WIN, :WIN] - sign * rows[WIN:, WIN:]
    right_imag = rows[WIN:, :WIN] + sign * rows[:WIN, WIN:]
    return right_real, right_imag


def window_kernel(
    place, row_ref, col_ref, live_ref, stack, probe, amps, high, low,
    keep, send, far_out, peak, field, grads, sums,
):
    row, col = row_ref[0], col_ref[0]
    live = live_ref[0].astype(jnp.float32)
    odd = place[0] & 1
    for member in range(8):
        lines = slice(member * 40, member * 40 + 40)
        for part in range(2):
            for block, where in enumerate((1, 2 - 2 * odd, 2 * odd)):
                first_line = block * 80 + part * 40
                field[part, where, lines, :] = stack[member, first_line : first_line + 40, :]
    lane = lax.broadcasted_iota(jnp.int32, (WIN, LANES), 1)
    back = lax.rem(LANES - col, LANES)
    ahead = lax.rem(col, LANES)
    first = lane < LANES - col

    def cut(part):
        turned = [
            pltpu.roll(field[part, block, pl.ds(row, WIN), :], back, 1) for block in range(3)
        ]
        return jnp.concatenate(
            [jnp.where(first, turned[0], turned[1]), jnp.where(first, turned[1], turned[2])], axis=1
        )

    sample_real, sample_imag = cut(0), cut(1)
    probe_real, probe_imag = probe[0], probe[1]
    exit_real = probe_real * sample_real - probe_imag * sample_imag
    exit_imag = probe_real * sample_imag + probe_imag * sample_real
    tall = (high[...], low[...])
    wide = tuple(jnp.concatenate([table[:WIN], table[WIN:]], axis=1) for table in tall)
    far_real, far_imag = transform(exit_real, exit_imag, tall, wide, -1.0)
    power = far_real * far_real + far_imag * far_imag
    factor = 1.0 - amps[0] * lax.rsqrt(jnp.maximum(power, 0.0625))
    miss_real, miss_imag = transform(far_real * factor, far_imag * factor, tall, wide, 1.0)
    miss_real = miss_real * live
    miss_imag = miss_imag * live
    light = probe_real * probe_real + probe_imag * probe_imag
    peak[...] = jnp.full((8, LANES), jnp.max(light), jnp.float32)

    terms = (
        probe_real * miss_real + probe_imag * miss_imag,
        probe_real * miss_imag - probe_imag * miss_real,
        live * light,
    )
    wrapped = lane < col
    zero = jnp.zeros((WIN, LANES), jnp.float32)
    grads[...] = jnp.zeros_like(grads)
    for part in range(3):
        start = pltpu.roll(terms[part][:, :LANES], ahead, 1)
        end = pltpu.roll(terms[part][:, LANES:], ahead, 1)
        grads[part, 0, pl.ds(row, WIN), :] = jnp.where(wrapped, zero, start)
        grads[part, 1, pl.ds(row, WIN), :] = jnp.where(wrapped, start, end)
        grads[part, 2, pl.ds(row, WIN), :] = jnp.where(wrapped, end, zero)
    window_light = live * (sample_real * sample_real + sample_imag * sample_imag)
    sums[0] = sample_real * miss_real + sample_imag * miss_imag
    sums[1] = sample_real * miss_imag - sample_imag * miss_real
    sums[2] = window_light
    total = jnp.zeros((8, LANES), jnp.float32)
    for line in range(0, WIN, 8):
        total = total + window_light[line : line + 8, :LANES] + window_light[line : line + 8, LANES:]
    for member in range(8):
        lines = slice(member * 40, member * 40 + 40)
        for out, half, block in ((keep, odd, 1), (send, 1 - odd, 2 - 2 * odd)):
            top = pl.multiple_of(half * 128 + member * 16, 16)
            for part in range(3):
                for side in range(2):
                    put = part * 32 + side * 16
                    out[member, put : put + 16, :] = sums[
                        part, pl.ds(top, 16), side * LANES : (side + 1) * LANES
                    ]
                put = PIECE + part * 40
                out[member, put : put + 40, :] = grads[part, block, lines, :]
            out[member, 96:PIECE, :] = total
        for part in range(3):
            far_out[member, part * 40 : part * 40 + 40, :] = grads[part, 2 * odd, lines, :]


def probe_kernel(place, one, two, probe, out):
    piece = (place[0] & 1) * 8 + place[1]
    summed = one[...] + two[...]
    mean = jnp.sum(summed[96:PIECE]) * (1.0 / (WIN * WIN))
    for side in range(2):
        bottom = summed[64 + side * 16 : 80 + side * 16] + 0.25 * mean + 1e-05
        for part in range(2):
            lines = part * 32 + side * 16
            top = pl.multiple_of(piece * 16, 16)
            old = probe[part, pl.ds(top, 16), side * LANES : (side + 1) * LANES]
            out[lines : lines + 16, :] = old - summed[lines : lines + 16] / bottom


def gather_kernel(place, mine, other, out):
    odd = place[0] & 1
    for source, half in ((mine, odd), (other, 1 - odd)):
        for member in range(8):
            top = pl.multiple_of(half * 128 + member * 16, 16)
            for part in range(2):
                for side in range(2):
                    lines = part * 32 + side * 16
                    out[part, pl.ds(top, 16), side * LANES : (side + 1) * LANES] = source[
                        member, lines : lines + 16, :
                    ]


def object_kernel(pieces, old, peak, out):
    summed = pieces[0, 64:184, :]
    for member in range(1, 8):
        summed = summed + pieces[member, 64:184, :]
    bottom = summed[80:120] + 0.25 * (peak[0:1, :] + 1e-06)
    out[0] = old[0] - summed[0:40] / bottom
    out[1] = old[1] - summed[40:80] / bottom


def pair_up(axis, mask):
    return [(i, i ^ mask) for i in range(lax.axis_size(axis))]


def swap(value, axis, mask):
    return lax.ppermute(value, axis, pair_up(axis, mask))


def swap_far(value):
    count = lax.axis_size("tile")
    pairs = []
    for i in range(1, count - 1, 2):
        pairs += [(i, i + 1), (i + 1, i)]
    return lax.ppermute(value, "tile", pairs)


def on_chip(value):
    return pltpu.with_memory_space_constraint(value, pltpu.VMEM)


def sum_first(value):
    total = value[0]
    for index in range(1, value.shape[0]):
        total = total + value[index]
    return total


def local(object_field, probe_field, amplitudes, row_start, column_start, live_slots):
    smem, vmem = pl.BlockSpec(memory_space=SMEM), pl.BlockSpec(memory_space=VMEM)
    place = jnp.stack([lax.axis_index("tile"), lax.axis_index("group")]).astype(jnp.int32)
    high, low = (on_chip(jnp.asarray(table)) for table in split_tables())
    probe = on_chip(probe_field)

    def buffer(*dims):
        return pltpu.VMEM(dims, jnp.float32)

    own = object_field.reshape(80, LANES)
    rows = jnp.concatenate([own, swap(own, "tile", 1), swap_far(own)], axis=0)
    stack = lax.all_to_all(jnp.broadcast_to(rows, (8, 240, LANES)), "group", 0, 0)

    keep, send, far_out, peak = pl.pallas_call(
        window_kernel,
        out_shape=(
            buffer(8, PIECE + 120, LANES),
            buffer(8, PIECE + 120, LANES),
            buffer(8, 120, LANES),
            buffer(8, LANES),
        ),
        in_specs=[smem] * 4 + [vmem] * 5,
        out_specs=(vmem,) * 4,
        scratch_shapes=[buffer(2, 3, 320, LANES), buffer(3, 3, 320, LANES), buffer(3, WIN, WIN)],
        compiler_params=pltpu.CompilerParams(vmem_limit_bytes=24 << 20),
        name="window",
    )(
        place, row_start, column_start, live_slots, on_chip(stack), probe, on_chip(amplitudes),
        high, low,
    )

    both = keep + swap(send, "tile", 1)
    eighths = lax.all_to_all(both[:, :PIECE], "group", 0, 0)
    gradient = both[:, PIECE:] + swap_far(far_out)
    total = sum_first(eighths)
    for mask in (2, 4, 8):
        total = total + swap(total, "tile", mask)
    piece = pl.pallas_call(
        probe_kernel,
        out_shape=buffer(64, LANES),
        in_specs=[smem] + [vmem] * 3,
        out_specs=vmem,
        compiler_params=pltpu.CompilerParams(vmem_limit_bytes=4 << 20),
        name="probe",
    )(place, on_chip(total), on_chip(swap(total, "tile", 28)), probe)

    outgoing = jnp.concatenate([jnp.broadcast_to(piece, (8, 64, LANES)), gradient], axis=1)
    pieces = lax.all_to_all(outgoing, "group", 0, 0)
    mine = pieces[:, :64]
    new_object = pl.pallas_call(
        object_kernel,
        out_shape=jax.ShapeDtypeStruct((2, 40, LANES), jnp.float32),
        in_specs=[vmem] * 3,
        out_specs=vmem,
        compiler_params=pltpu.CompilerParams(vmem_limit_bytes=4 << 20),
        name="object",
    )(on_chip(pieces), on_chip(object_field), peak)
    new_probe = pl.pallas_call(
        gather_kernel,
        out_shape=jax.ShapeDtypeStruct((2, WIN, WIN), jnp.float32),
        in_specs=[smem] + [vmem] * 2,
        out_specs=vmem,
        compiler_params=pltpu.CompilerParams(vmem_limit_bytes=4 << 20),
        name="gather",
    )(place, on_chip(pieces), on_chip(swap(mine, "tile", 1)))
    return new_object, new_probe


def solution(mesh):
    return jax.shard_map(
        local,
        mesh=mesh,
        in_specs=(
            P(None, "group", "tile"),
            P(),
            P(("tile", "group"), None, None),
            P(("tile", "group")),
            P(("tile", "group")),
            P(("tile", "group")),
        ),
        out_specs=(P(None, "group", "tile"), P()),
        check_vma=False,
    )
```

time: 118 us -> 99.3 us (0.84)
  blocking collectives: 0 us -> 11.8 us
  starting transfers between devices: 54.9 us -> 44.3 us
  waiting for transfers between devices: 39.2 us -> 30 us
  Pallas kernels: 12.6 us -> 6.98 us
  other arithmetic: 3.55 us -> 1.18 us
  local copies, waits for them, and re-layouts: 4.09 us -> 1.87 us
    ppermute x20 -> x7, waiting for transfers between devices: 35.4 us -> 12.9 us  [swap(): return lax.ppermute(value, axis, pair_up(axis, mask))]
    ppermute x20 -> x7, starting transfers between devices: 40.4 us -> 23.5 us  [swap(): return lax.ppermute(value, axis, pair_up(axis, mask))]
    all_to_all x0 -> x2, waiting for transfers between devices: none -> 15.3 us  [the longest x1 13 us: local(): lax.all_to_all(jnp.broadcast_to(rows, (8, 240, LANES)), 'group', 0, 0)]
    all_to_all x0 -> x1, blocking collectives: none -> 11.8 us  [local(): pieces = lax.all_to_all(outgoing, 'group', 0, 0)]
    all_to_all x0 -> x2, starting transfers between devices: none -> 8.66 us  [the longest x1 5.2 us: local(): lax.all_to_all(jnp.broadcast_to(rows, (8, 240, LANES)), 'group', 0, 0)]
    pallas_call x4, Pallas kernels: 12.6 us -> 6.98 us  [the longest x1 4.29 us: local(): pl.pallas_call(window_kernel, out_shape=(buffer(8, PIECE + 120, LANES), b...]
    unnamed x26 -> x10, local copies, waits for them, and re-layouts: 3.43 us -> 0.02 us
    ppermute x2, starting transfers between devices: 14.5 us -> 12.2 us  [swap_far(): return lax.ppermute(value, 'tile', pairs)]
  transfers between devices with their start and end apart: 22 -> 11, of which waited for: 16 -> 9; matrix products, arithmetic and copies ran while one was open for 2% -> 0% of each run, Pallas kernels for 3% -> 1%
where the time goes in v2:
time: 99.3 us; the launch traced here: 98.8 us
  starting transfers between devices  44.3 us (45%)
  waiting for transfers between devices  30 us (30%)
  blocking collectives  11.8 us (12%)
  Pallas kernels  6.98 us (7%)
  between operations  2.68 us (3%)
  local copies, waits for them, and re-layouts  1.87 us (2%)
  other arithmetic  1.18 us (1%)
    ppermute x7, starting transfers between devices, swap(): return lax.ppermute(value, axis, pair_up(axis, mask))  23.5 us
    all_to_all x1, waiting for transfers between devices, local(): lax.all_to_all(jnp.broadcast_to(rows, (8, 240, LANES)), 'group', 0, 0)  13 us
    ppermute x7, waiting for transfers between devices, swap(): return lax.ppermute(value, axis, pair_up(axis, mask))  12.9 us
    ppermute x2, starting transfers between devices, swap_far(): return lax.ppermute(value, 'tile', pairs)  12.2 us
    all_to_all x1, blocking collectives, local(): pieces = lax.all_to_all(outgoing, 'group', 0, 0)  11.8 us
    all_to_all x1, starting transfers between devices, local(): lax.all_to_all(jnp.broadcast_to(rows, (8, 240, LANES)), 'group', 0, 0)  5.2 us
    pallas_call x1, Pallas kernels, local(): pl.pallas_call(window_kernel, out_shape=(buffer(8, PIECE + 120, LANES), b...  4.29 us
    all_to_all x1, starting transfers between devices, local(): eighths = lax.all_to_all(both[:, :PIECE], 'group', 0, 0)  3.46 us
  transfers between devices with their start and end apart: 11, of which 9 were waited for; matrix products, arithmetic and copies ran while one was open for 0% of the time, Pallas kernels for 1%

profile of v2, /device:TPU:1, one launch (start us, length us, event | category | flops | bytes accessed | tf_op | source)
XLA Modules:
  0.0 98.8 jit_solution(14586781142133471189)
XLA Ops:
  0.6 6.0 %collective-permute-start.1 = (f32[80,128]{1,0:T(8,128)}, f32[80,128]{1,0:T(8,128)S(1)}, u32[]{:S(2)}, u32[]{:S(2)}) collective-permute-start(f32[80,128]{1,0:T(8,128)} %bitcast.7), channel_id=1, source_target_pairs={{8,16},{16,8},{24,32},{32,24},{40,48},{48,40},{56,64},{64,56},{72,... | collective-permute-start | bytes 122888 | tf_op jit(solution)/shard_map/ppermute | solution.py:177
  6.7 0.1 collective-permute-start
  6.8 1.8 %collective-permute-done.1 = f32[80,128]{1,0:T(8,128)S(1)} collective-permute-done((f32[80,128]{1,0:T(8,128)}, f32[80,128]{1,0:T(8,128)S(1)}, u32[]{:S(2)}, u32[]{:S(2)}) %collective-permute-start.1) | collective-permute-done | bytes 40992 | tf_op jit(solution)/shard_map/ppermute | solution.py:177
  8.6 0.0 collective-permute-done
  8.6 0.8 pad_maximum_fusion.1
  9.4 1.0 %broadcast_in_dim.6 = f32[8,240,128]{2,1,0:T(8,128)} broadcast(f32[240,128]{1,0:T(8,128)S(1)} %pad_maximum_fusion.1), dimensions={1,2} | broadcast | bytes 1105920 | tf_op jit(solution)/shard_map/broadcast_in_dim | solution.py:202
  10.4 0.0 copy-start
  10.4 0.0 copy-start.1
  10.4 0.0 copy-start.2
  10.4 0.0 copy-start.3
  10.4 5.2 %all-to-all-start = ((f32[8,240,128]{2,1,0:T(8,128)}), f32[8,240,128]{2,1,0:T(8,128)S(1)}, u32[]{:S(2)}, u32[]{:S(2)}) async-start(f32[8,240,128]{2,1,0:T(8,128)} %broadcast_in_dim.6), calls=%async_computation | async-start | bytes 1966080 | tf_op jit(solution)/shard_map/all_to_all | solution.py:202
  17.5 0.1 pad_add_fusion.place
  17.6 13.0 %all-to-all-done.stack = f32[8,240,128]{2,1,0:T(8,128)S(1)} async-done(((f32[8,240,128]{2,1,0:T(8,128)}), f32[8,240,128]{2,1,0:T(8,128)S(1)}, u32[]{:S(2)}, u32[]{:S(2)}) %all-to-all-start) | async-done | bytes 983072 | tf_op jit(solution)/shard_map/all_to_all | solution.py:202
  30.6 0.0 copy-done
  30.6 0.0 copy-done.1
  30.6 0.0 copy-done.2
  30.6 0.0 copy-done.3
  30.6 4.3 %window.1 = (f32[8,224,128]{2,1,0:T(8,128)S(1)}, f32[8,224,128]{2,1,0:T(8,128)S(1)}, f32[8,120,128]{2,1,0:T(8,128)S(1)}, f32[8,128]{1,0:T(8,128)S(1)}) custom-call(s32[2]{0:T(128)S(1)} %pad_add_fusion.place, s32[1]{0:T(128)S(6)} %copy.10.row_ref, s32[1]{0:T(128)S(6)} %copy.11.col_ref, s32[1]{0:T(128)S(6)} %copy.12.live_ref, ...), custom_call_target="tpu_custom_call" | custom-call | tf_op jit(solution)/shard_map/window/pallas_call | solution.py:204
  34.9 0.5 collective-permute-start.2
  35.4 2.1 %collective-permute-done.2 = f32[8,224,128]{2,1,0:T(8,128)S(1)} collective-permute-done((f32[8,224,128]{2,1,0:T(8,128)S(1)}, f32[8,224,128]{2,1,0:T(8,128)S(1)}, u32[]{:S(2)}, u32[]{:S(2)}) %collective-permute-start.2) | collective-permute-done | bytes 917536 | tf_op jit(solution)/shard_map/ppermute | solution.py:169
  37.5 0.1 add.42
  37.6 0.8 slice.44
  38.4 3.5 %all-to-all-start.1 = ((f32[8,104,128]{2,1,0:T(8,128)}), f32[8,104,128]{2,1,0:T(8,128)S(1)}, u32[]{:S(2)}, u32[]{:S(2)}) async-start(f32[8,104,128]{2,1,0:T(8,128)} %slice.44), calls=%async_computation.1 | async-start | bytes 851968 | tf_op jit(solution)/shard_map/all_to_all | solution.py:223
  41.9 6.1 %collective-permute-start.7 = (f32[8,120,128]{2,1,0:T(8,128)S(1)}, f32[8,120,128]{2,1,0:T(8,128)S(1)}, u32[]{:S(2)}, u32[]{:S(2)}) collective-permute-start(f32[8,120,128]{2,1,0:T(8,128)S(1)} %get-tuple-element.8), channel_id=1, source_target_pairs={{8,16},{16,8},{24,32},{32,24},{40,48},{48,40},{56,64},{64,56},{72,... | collective-permute-start | bytes 1474568 | tf_op jit(solution)/shard_map/ppermute | solution.py:177
  48.0 2.3 %all-to-all-done.1 = f32[8,104,128]{2,1,0:T(8,128)S(1)} async-done(((f32[8,104,128]{2,1,0:T(8,128)}), f32[8,104,128]{2,1,0:T(8,128)S(1)}, u32[]{:S(2)}, u32[]{:S(2)}) %all-to-all-start.1) | async-done | bytes 426016 | tf_op jit(solution)/shard_map/all_to_all | solution.py:223
  50.3 4.0 %collective-permute-start.3 = (f32[104,128]{1,0:T(8,128)S(1)}, f32[104,128]{1,0:T(8,128)S(1)}, u32[]{:S(2)}, u32[]{:S(2)}) collective-permute-start(f32[104,128]{1,0:T(8,128)S(1)} %fusion), channel_id=1, source_target_pairs={{0,16},{8,24},{16,0},{24,8},{32,48},{40,56},{48,32},{56,40},{64,80... | collective-permute-start | bytes 159752 | tf_op jit(solution)/shard_map/ppermute | solution.py:169
  54.4 5.8 %collective-permute-done.3 = f32[104,128]{1,0:T(8,128)S(1)} collective-permute-done((f32[104,128]{1,0:T(8,128)S(1)}, f32[104,128]{1,0:T(8,128)S(1)}, u32[]{:S(2)}, u32[]{:S(2)}) %collective-permute-start.3) | collective-permute-done | bytes 53280 | tf_op jit(solution)/shard_map/ppermute | solution.py:169
  60.2 3.4 %collective-permute-start.4 = (f32[104,128]{1,0:T(8,128)S(1)}, f32[104,128]{1,0:T(8,128)S(1)}, u32[]{:S(2)}, u32[]{:S(2)}) collective-permute-start(f32[104,128]{1,0:T(8,128)S(1)} %fusion.1), channel_id=1, source_target_pairs={{0,32},{8,40},{16,48},{24,56},{32,0},{40,8},{48,16},{56,24},{64,96... | collective-permute-start | bytes 159752 | tf_op jit(solution)/shard_map/ppermute | solution.py:169
  63.5 1.5 %collective-permute-done.4 = f32[104,128]{1,0:T(8,128)S(1)} collective-permute-done((f32[104,128]{1,0:T(8,128)S(1)}, f32[104,128]{1,0:T(8,128)S(1)}, u32[]{:S(2)}, u32[]{:S(2)}) %collective-permute-start.4) | collective-permute-done | bytes 53280 | tf_op jit(solution)/shard_map/ppermute | solution.py:169
  65.1 3.6 %collective-permute-start.5 = (f32[104,128]{1,0:T(8,128)S(1)}, f32[104,128]{1,0:T(8,128)S(1)}, u32[]{:S(2)}, u32[]{:S(2)}) collective-permute-start(f32[104,128]{1,0:T(8,128)S(1)} %add.52), channel_id=1, source_target_pairs={{0,64},{8,72},{16,80},{24,88},{32,96},{40,104},{48,112},{56,120},{... | collective-permute-start | bytes 159752 | tf_op jit(solution)/shard_map/ppermute | solution.py:169
  68.7 1.5 %collective-permute-done.5 = f32[104,128]{1,0:T(8,128)S(1)} collective-permute-done((f32[104,128]{1,0:T(8,128)S(1)}, f32[104,128]{1,0:T(8,128)S(1)}, u32[]{:S(2)}, u32[]{:S(2)}) %collective-permute-start.5) | collective-permute-done | bytes 53280 | tf_op jit(solution)/shard_map/ppermute | solution.py:169
  70.2 3.6 %collective-permute-start.6 = (f32[104,128]{1,0:T(8,128)S(1)}, f32[104,128]{1,0:T(8,128)S(1)}, u32[]{:S(2)}, u32[]{:S(2)}) collective-permute-start(f32[104,128]{1,0:T(8,128)S(1)} %add.53.one), channel_id=1, source_target_pairs={{0,224},{8,232},{16,240},{24,248},{32,192},{40,200},{48,208},{56,2... | collective-permute-start | bytes 159752 | tf_op jit(solution)/shard_map/ppermute | solution.py:169
  73.8 0.0 collective-permute-done.7
  73.8 0.1 slice_add_fusion
  73.9 1.4 %collective-permute-done.6.two = f32[104,128]{1,0:T(8,128)S(1)} collective-permute-done((f32[104,128]{1,0:T(8,128)S(1)}, f32[104,128]{1,0:T(8,128)S(1)}, u32[]{:S(2)}, u32[]{:S(2)}) %collective-permute-start.6) | collective-permute-done | bytes 53280 | tf_op jit(solution)/shard_map/ppermute | solution.py:169
  75.3 0.7 probe.4
  76.0 0.1 pad_maximum_fusion
  76.1 11.8 %all_to_all.15.pieces.mine = f32[8,184,128]{2,1,0:T(8,128)S(1)} all-to-all(f32[8,184,128]{2,1,0:T(8,128)S(1)} %pad_maximum_fusion), channel_id=1, replica_groups=mesh['tile'=32,'group'=8] {'group'}, dimensions={0} | all-to-all | bytes 1507328 | tf_op jit(solution)/shard_map/all_to_all | solution.py:238
  87.9 0.0 copy-start.4
  87.9 8.3 %collective-permute-start.8 = (f32[8,64,128]{2,1,0:T(8,128)S(1)}, f32[8,64,128]{2,1,0:T(8,128)S(1)}, u32[]{:S(2)}, u32[]{:S(2)}) collective-permute-start(f32[8,64,128]{2,1,0:T(8,128)S(1)} %slice.54), channel_id=1, source_target_pairs={{0,8},{8,0},{16,24},{24,16},{32,40},{40,32},{48,56},{56,48},{64,72... | collective-permute-start | bytes 786440 | tf_op jit(solution)/shard_map/ppermute | solution.py:169
  96.2 0.0 copy-done.4
  96.3 0.6 object.1
  96.9 0.5 collective-permute-done.8.other
  97.4 1.4 %gather.1 = f32[2,256,256]{2,1,0:T(8,128)} custom-call(s32[2]{0:T(128)S(1)} %pad_add_fusion.place, f32[8,184,128]{2,1,0:T(8,128)S(1)} %all_to_all.15.pieces.mine, f32[8,64,128]{2,1,0:T(8,128)S(1)} %collective-permute-done.8.other), custom_call_target="tpu_custom_call" | custom-call | tf_op jit(solution)/shard_map/gather/pallas_call | solution.py:248
  (6 shorter events, 0.1 us)
Async XLA Ops:
  0.6 7.9 %collective-permute-start.1 = (f32[80,128]{1,0:T(8,128)}, f32[80,128]{1,0:T(8,128)S(1)}, u32[]{:S(2)}, u32[]{:S(2)}) collective-permute-start(f32[80,128]{1,0:T(8,128)} %bitcast.7), channel_id=1, source_target_pairs={{8,16},{16,8},{24,32},{32,24},{40,48},{48,40},{56,64},{64,56},{72,... | collective-permute-start | bytes 122888 | tf_op jit(solution)/shard_map/ppermute | solution.py:177
  6.7 1.9 %collective-permute-start = (f32[80,128]{1,0:T(8,128)}, f32[80,128]{1,0:T(8,128)S(1)}, u32[]{:S(2)}, u32[]{:S(2)}) collective-permute-start(f32[80,128]{1,0:T(8,128)} %bitcast.8), channel_id=1, source_target_pairs={{0,8},{8,0},{16,24},{24,16},{32,40},{40,32},{48,56},{56,48},{64,72... | collective-permute-start | bytes 122888 | tf_op jit(solution)/shard_map/ppermute | solution.py:169
  10.4 20.2 %copy-start = (f32[2,256,256]{2,1,0:T(8,128)S(1)}, f32[2,256,256]{2,1,0:T(8,128)}, u32[]{:S(2)}) copy-start(f32[2,256,256]{2,1,0:T(8,128)} %probe.5) | copy-start | bytes 1572868
  10.4 20.2 %copy-start.1 = (f32[1,256,256]{2,1,0:T(8,128)S(1)}, f32[1,256,256]{2,1,0:T(8,128)}, u32[]{:S(2)}) copy-start(f32[1,256,256]{2,1,0:T(8,128)} %amps.1) | copy-start | bytes 786436
  10.4 20.2 %copy-start.2 = (bf16[512,256]{1,0:T(8,128)(2,1)S(1)}, bf16[512,256]{1,0:T(8,128)(2,1)}, u32[]{:S(2)}) copy-start(bf16[512,256]{1,0:T(8,128)(2,1)} %constant.14.clone.low) | copy-start | bytes 786436
  10.4 20.2 %copy-start.3 = (bf16[512,256]{1,0:T(8,128)(2,1)S(1)}, bf16[512,256]{1,0:T(8,128)(2,1)}, u32[]{:S(2)}) copy-start(bf16[512,256]{1,0:T(8,128)(2,1)} %constant.13.clone.high) | copy-start | bytes 786436
  10.4 20.2 %all-to-all-start = ((f32[8,240,128]{2,1,0:T(8,128)}), f32[8,240,128]{2,1,0:T(8,128)S(1)}, u32[]{:S(2)}, u32[]{:S(2)}) async-start(f32[8,240,128]{2,1,0:T(8,128)} %broadcast_in_dim.6), calls=%async_computation | async-start | bytes 1966080 | tf_op jit(solution)/shard_map/all_to_all | solution.py:202
  34.9 2.6 %collective-permute-start.2 = (f32[8,224,128]{2,1,0:T(8,128)S(1)}, f32[8,224,128]{2,1,0:T(8,128)S(1)}, u32[]{:S(2)}, u32[]{:S(2)}) collective-permute-start(f32[8,224,128]{2,1,0:T(8,128)S(1)} %get-tuple-element.7), channel_id=1, source_target_pairs={{0,8},{8,0},{16,24},{24,16},{32,40},{40,32},{48,56},{56,48},{64,72... | collective-permute-start | bytes 2752520 | tf_op jit(solution)/shard_map/ppermute | solution.py:169
  38.4 11.9 %all-to-all-start.1 = ((f32[8,104,128]{2,1,0:T(8,128)}), f32[8,104,128]{2,1,0:T(8,128)S(1)}, u32[]{:S(2)}, u32[]{:S(2)}) async-start(f32[8,104,128]{2,1,0:T(8,128)} %slice.44), calls=%async_computation.1 | async-start | bytes 851968 | tf_op jit(solution)/shard_map/all_to_all | solution.py:223
  41.9 31.9 %collective-permute-start.7 = (f32[8,120,128]{2,1,0:T(8,128)S(1)}, f32[8,120,128]{2,1,0:T(8,128)S(1)}, u32[]{:S(2)}, u32[]{:S(2)}) collective-permute-start(f32[8,120,128]{2,1,0:T(8,128)S(1)} %get-tuple-element.8), channel_id=1, source_target_pairs={{8,16},{16,8},{24,32},{32,24},{40,48},{48,40},{56,64},{64,56},{72,... | collective-permute-start | bytes 1474568 | tf_op jit(solution)/shard_map/ppermute | solution.py:177
  50.3 9.8 %collective-permute-start.3 = (f32[104,128]{1,0:T(8,128)S(1)}, f32[104,128]{1,0:T(8,128)S(1)}, u32[]{:S(2)}, u32[]{:S(2)}) collective-permute-start(f32[104,128]{1,0:T(8,128)S(1)} %fusion), channel_id=1, source_target_pairs={{0,16},{8,24},{16,0},{24,8},{32,48},{40,56},{48,32},{56,40},{64,80... | collective-permute-start | bytes 159752 | tf_op jit(solution)/shard_map/ppermute | solution.py:169
  60.2 4.9 %collective-permute-start.4 = (f32[104,128]{1,0:T(8,128)S(1)}, f32[104,128]{1,0:T(8,128)S(1)}, u32[]{:S(2)}, u32[]{:S(2)}) collective-permute-start(f32[104,128]{1,0:T(8,128)S(1)} %fusion.1), channel_id=1, source_target_pairs={{0,32},{8,40},{16,48},{24,56},{32,0},{40,8},{48,16},{56,24},{64,96... | collective-permute-start | bytes 159752 | tf_op jit(solution)/shard_map/ppermute | solution.py:169
  65.1 5.1 %collective-permute-start.5 = (f32[104,128]{1,0:T(8,128)S(1)}, f32[104,128]{1,0:T(8,128)S(1)}, u32[]{:S(2)}, u32[]{:S(2)}) collective-permute-start(f32[104,128]{1,0:T(8,128)S(1)} %add.52), channel_id=1, source_target_pairs={{0,64},{8,72},{16,80},{24,88},{32,96},{40,104},{48,112},{56,120},{... | collective-permute-start | bytes 159752 | tf_op jit(solution)/shard_map/ppermute | solution.py:169
  70.2 5.1 %collective-permute-start.6 = (f32[104,128]{1,0:T(8,128)S(1)}, f32[104,128]{1,0:T(8,128)S(1)}, u32[]{:S(2)}, u32[]{:S(2)}) collective-permute-start(f32[104,128]{1,0:T(8,128)S(1)} %add.53.one), channel_id=1, source_target_pairs={{0,224},{8,232},{16,240},{24,248},{32,192},{40,200},{48,208},{56,2... | collective-permute-start | bytes 159752 | tf_op jit(solution)/shard_map/ppermute | solution.py:169
  87.9 8.4 %copy-start.4 = (f32[2,40,128]{2,1,0:T(8,128)S(1)}, f32[2,40,128]{2,1,0:T(8,128)}, u32[]{:S(2)}) copy-start(f32[2,40,128]{2,1,0:T(8,128)} %old.1) | copy-start | bytes 122884
  87.9 9.5 %collective-permute-start.8 = (f32[8,64,128]{2,1,0:T(8,128)S(1)}, f32[8,64,128]{2,1,0:T(8,128)S(1)}, u32[]{:S(2)}, u32[]{:S(2)}) collective-permute-start(f32[8,64,128]{2,1,0:T(8,128)S(1)} %slice.54), channel_id=1, source_target_pairs={{0,8},{8,0},{16,24},{24,16},{32,40},{40,32},{48,56},{56,48},{64,72... | collective-permute-start | bytes 786440 | tf_op jit(solution)/shard_map/ppermute | solution.py:169

commit v3 on v2

--- a/solution.py
+++ b/solution.py
@@ -198,8 +198,9 @@
         return pltpu.VMEM(dims, jnp.float32)
 
     own = object_field.reshape(80, LANES)
-    rows = jnp.concatenate([own, swap(own, "tile", 1), swap_far(own)], axis=0)
-    stack = lax.all_to_all(jnp.broadcast_to(rows, (8, 240, LANES)), "group", 0, 0)
+    rows = (own, swap(own, "tile", 1), swap_far(own))
+    rows = jnp.concatenate([jnp.broadcast_to(block, (8, 80, LANES)) for block in rows], axis=1)
+    stack = lax.all_to_all(rows, "group", 0, 0)
 
     keep, send, far_out, peak = pl.pallas_call(
         window_kernel,
@@ -219,11 +220,11 @@
         high, low,
     )
 
-    both = keep + swap(send, "tile", 1)
-    eighths = lax.all_to_all(both[:, :PIECE], "group", 0, 0)
-    gradient = both[:, PIECE:] + swap_far(far_out)
+    got = swap(send, "tile", 1)
+    eighths = lax.all_to_all(keep[:, :PIECE] + got[:, :PIECE], "group", 0, 0)
+    gradient = keep[:, PIECE:] + got[:, PIECE:] + swap_far(far_out)
     total = sum_first(eighths)
-    for mask in (2, 4, 8):
+    for mask in (4, 8, 28):
         total = total + swap(total, "tile", mask)
     piece = pl.pallas_call(
         probe_kernel,
@@ -232,7 +233,7 @@
         out_specs=vmem,
         compiler_params=pltpu.CompilerParams(vmem_limit_bytes=4 << 20),
         name="probe",
-    )(place, on_chip(total), on_chip(swap(total, "tile", 28)), probe)
+    )(place, on_chip(total), on_chip(swap(total, "tile", 2)), probe)
 
     outgoing = jnp.concatenate([jnp.broadcast_to(piece, (8, 64, LANES)), gradient], axis=1)
     pieces = lax.all_to_all(outgoing, "group", 0, 0)

time: 99.3 us -> 98.1 us (0.988); the launches traced: 98.8 us -> 96.5 us
  waiting for transfers between devices: 30 us -> 25.3 us
  other arithmetic: 1.18 us -> 3.13 us
  starting transfers between devices: 44.3 us -> 45.5 us
    ppermute x7, waiting for transfers between devices: 12.9 us -> 8.23 us  [swap(): return lax.ppermute(value, axis, pair_up(axis, mask))]
    add x2, other arithmetic: 0.2 us -> 1.92 us  [the longest x1 1.1 us: local(): gradient = keep[:, PIECE:] + got[:, PIECE:] + swap_far(far_out)]
    unnamed x10 -> x14, local copies, waits for them, and re-layouts: 0.02 us -> 1.53 us
    ppermute x7, starting transfers between devices: 23.5 us -> 24.6 us  [swap(): return lax.ppermute(value, axis, pair_up(axis, mask))]
  transfers between devices with their start and end apart: 11 -> 11, of which waited for: 9 -> 9; matrix products, arithmetic and copies ran while one was open for 0% -> 1% of each run, Pallas kernels for 1% -> 1%
where the time goes in v3:
time: 98.1 us; the launch traced here: 96.5 us
  starting transfers between devices  45.5 us (46%)
  waiting for transfers between devices  25.3 us (26%)
  blocking collectives  11.2 us (11%)
  Pallas kernels  7.01 us (7%)
  other arithmetic  3.13 us (3%)
  between operations  2.72 us (3%)
  local copies, waits for them, and re-layouts  1.64 us (2%)
    ppermute x7, starting transfers between devices, swap(): return lax.ppermute(value, axis, pair_up(axis, mask))  24.6 us
    all_to_all x1, waiting for transfers between devices, local(): stack = lax.all_to_all(rows, 'group', 0, 0)  13 us
    ppermute x2, starting transfers between devices, swap_far(): return lax.ppermute(value, 'tile', pairs)  12.2 us
    all_to_all x1, blocking collectives, local(): pieces = lax.all_to_all(outgoing, 'group', 0, 0)  11.2 us
    ppermute x7, waiting for transfers between devices, swap(): return lax.ppermute(value, axis, pair_up(axis, mask))  8.23 us
    all_to_all x1, starting transfers between devices, local(): stack = lax.all_to_all(rows, 'group', 0, 0)  5.2 us
    pallas_call x1, Pallas kernels, local(): pl.pallas_call(window_kernel, out_shape=(buffer(8, PIECE + 120, LANES), b...  4.32 us
    all_to_all x1, starting transfers between devices, local(): eighths = lax.all_to_all(keep[:, :PIECE] + got[:, :PIECE], 'group', 0, 0)  3.59 us
  transfers between devices with their start and end apart: 11, of which 9 were waited for; matrix products, arithmetic and copies ran while one was open for 1% of the time, Pallas kernels for 1%

profile of v3, /device:TPU:1, one launch (start us, length us, event | category | flops | bytes accessed | tf_op | source)
XLA Modules:
  0.0 96.5 jit_solution(2512102758515275346)
XLA Ops:
  0.6 6.0 %collective-permute-start.1 = (f32[80,128]{1,0:T(8,128)}, f32[80,128]{1,0:T(8,128)S(1)}, u32[]{:S(2)}, u32[]{:S(2)}) collective-permute-start(f32[80,128]{1,0:T(8,128)} %bitcast.7), channel_id=1, source_target_pairs={{8,16},{16,8},{24,32},{32,24},{40,48},{48,40},{56,64},{64,56},{72,... | collective-permute-start | bytes 122888 | tf_op jit(solution)/shard_map/ppermute | solution.py:177
  6.7 0.1 collective-permute-start
  6.8 1.8 %collective-permute-done.1 = f32[80,128]{1,0:T(8,128)S(1)} collective-permute-done((f32[80,128]{1,0:T(8,128)}, f32[80,128]{1,0:T(8,128)S(1)}, u32[]{:S(2)}, u32[]{:S(2)}) %collective-permute-start.1) | collective-permute-done | bytes 40992 | tf_op jit(solution)/shard_map/ppermute | solution.py:177
  8.6 0.0 collective-permute-done
  8.6 0.0 copy-start.4
  8.6 0.7 copy-done.4
  9.4 1.0 %pad_maximum_fusion = f32[8,240,128]{2,1,0:T(8,128)} fusion(f32[8,80,128]{2,1,0:T(8,128)S(1)} %broadcast_in_dim.14, f32[8,80,128]{2,1,0:T(8,128)S(1)} %broadcast_in_dim.13, f32[8,80,128]{2,1,0:T(8,128)S(1)} %broadcast_in_dim.12), kind=kLoop, calls=%fused_computation | loop fusion | flops 491520 | bytes 1966080 | tf_op jit(solution)/shard_map/concatenate | solution.py:202
  10.4 0.0 copy-start
  10.4 0.0 copy-start.1
  10.4 0.0 copy-start.2
  10.4 0.0 copy-start.3
  10.4 5.2 %all-to-all-start = ((f32[8,240,128]{2,1,0:T(8,128)}), f32[8,240,128]{2,1,0:T(8,128)S(1)}, u32[]{:S(2)}, u32[]{:S(2)}) async-start(f32[8,240,128]{2,1,0:T(8,128)} %pad_maximum_fusion), calls=%async_computation | async-start | bytes 1966080 | tf_op jit(solution)/shard_map/all_to_all | solution.py:203
  17.6 0.1 pad_add_fusion.place
  17.6 13.0 %all-to-all-done.stack = f32[8,240,128]{2,1,0:T(8,128)S(1)} async-done(((f32[8,240,128]{2,1,0:T(8,128)}), f32[8,240,128]{2,1,0:T(8,128)S(1)}, u32[]{:S(2)}, u32[]{:S(2)}) %all-to-all-start) | async-done | bytes 983072 | tf_op jit(solution)/shard_map/all_to_all | solution.py:203
  30.6 0.0 copy-done
  30.6 0.0 copy-done.1
  30.6 0.0 copy-done.2
  30.6 0.0 copy-done.3
  30.7 4.3 %window.1 = (f32[8,224,128]{2,1,0:T(8,128)S(1)}, f32[8,224,128]{2,1,0:T(8,128)S(1)}, f32[8,120,128]{2,1,0:T(8,128)S(1)}, f32[8,128]{1,0:T(8,128)S(1)}) custom-call(s32[2]{0:T(128)S(1)} %pad_add_fusion.place, s32[1]{0:T(128)S(6)} %copy.10.row_ref, s32[1]{0:T(128)S(6)} %copy.11.col_ref, s32[1]{0:T(128)S(6)} %copy.12.live_ref, ...), custom_call_target="tpu_custom_call" | custom-call | tf_op jit(solution)/shard_map/window/pallas_call | solution.py:205
  35.0 0.0 copy-start.5
  35.0 0.8 copy-done.5
  35.8 0.4 collective-permute-start.2
  36.1 2.1 %collective-permute-done.2 = f32[8,224,128]{2,1,0:T(8,128)S(1)} collective-permute-done((f32[8,224,128]{2,1,0:T(8,128)S(1)}, f32[8,224,128]{2,1,0:T(8,128)S(1)}, u32[]{:S(2)}, u32[]{:S(2)}) %collective-permute-start.2) | collective-permute-done | bytes 917536 | tf_op jit(solution)/shard_map/ppermute | solution.py:169
  38.2 0.8 slice_add_fusion.1
  39.1 0.0 copy-start.6
  39.1 3.6 %all-to-all-start.1 = ((f32[8,104,128]{2,1,0:T(8,128)}), f32[8,104,128]{2,1,0:T(8,128)S(1)}, u32[]{:S(2)}, u32[]{:S(2)}) async-start(f32[8,104,128]{2,1,0:T(8,128)} %slice_add_fusion.1), calls=%async_computation.1 | async-start | bytes 851968 | tf_op jit(solution)/shard_map/all_to_all | solution.py:224
  42.7 0.0 copy-done.6
  42.7 6.1 %collective-permute-start.7 = (f32[8,120,128]{2,1,0:T(8,128)S(1)}, f32[8,120,128]{2,1,0:T(8,128)}, u32[]{:S(2)}, u32[]{:S(2)}) collective-permute-start(f32[8,120,128]{2,1,0:T(8,128)S(1)} %copy-done.6), channel_id=1, source_target_pairs={{8,16},{16,8},{24,32},{32,24},{40,48},{48,40},{56,64},{64,56},{72,... | collective-permute-start | bytes 1474568 | tf_op jit(solution)/shard_map/ppermute | solution.py:177
  48.8 2.3 %all-to-all-done.1 = f32[8,104,128]{2,1,0:T(8,128)S(1)} async-done(((f32[8,104,128]{2,1,0:T(8,128)}), f32[8,104,128]{2,1,0:T(8,128)S(1)}, u32[]{:S(2)}, u32[]{:S(2)}) %all-to-all-start.1) | async-done | bytes 426016 | tf_op jit(solution)/shard_map/all_to_all | solution.py:224
  51.1 2.7 %collective-permute-start.3 = (f32[104,128]{1,0:T(8,128)S(1)}, f32[104,128]{1,0:T(8,128)S(1)}, u32[]{:S(2)}, u32[]{:S(2)}) collective-permute-start(f32[104,128]{1,0:T(8,128)S(1)} %fusion.1), channel_id=1, source_target_pairs={{0,32},{8,40},{16,48},{24,56},{32,0},{40,8},{48,16},{56,24},{64,96... | collective-permute-start | bytes 159752 | tf_op jit(solution)/shard_map/ppermute | solution.py:169
  53.8 2.2 %collective-permute-done.3 = f32[104,128]{1,0:T(8,128)S(1)} collective-permute-done((f32[104,128]{1,0:T(8,128)S(1)}, f32[104,128]{1,0:T(8,128)S(1)}, u32[]{:S(2)}, u32[]{:S(2)}) %collective-permute-start.3) | collective-permute-done | bytes 53280 | tf_op jit(solution)/shard_map/ppermute | solution.py:169
  56.0 3.1 %collective-permute-start.4 = (f32[104,128]{1,0:T(8,128)S(1)}, f32[104,128]{1,0:T(8,128)S(1)}, u32[]{:S(2)}, u32[]{:S(2)}) collective-permute-start(f32[104,128]{1,0:T(8,128)S(1)} %fusion.2), channel_id=1, source_target_pairs={{0,64},{8,72},{16,80},{24,88},{32,96},{40,104},{48,112},{56,120},{... | collective-permute-start | bytes 159752 | tf_op jit(solution)/shard_map/ppermute | solution.py:169
  59.1 1.5 %collective-permute-done.4 = f32[104,128]{1,0:T(8,128)S(1)} collective-permute-done((f32[104,128]{1,0:T(8,128)S(1)}, f32[104,128]{1,0:T(8,128)S(1)}, u32[]{:S(2)}, u32[]{:S(2)}) %collective-permute-start.4) | collective-permute-done | bytes 53280 | tf_op jit(solution)/shard_map/ppermute | solution.py:169
  60.6 4.6 %collective-permute-start.5 = (f32[104,128]{1,0:T(8,128)S(1)}, f32[104,128]{1,0:T(8,128)S(1)}, u32[]{:S(2)}, u32[]{:S(2)}) collective-permute-start(f32[104,128]{1,0:T(8,128)S(1)} %add.55), channel_id=1, source_target_pairs={{0,224},{8,232},{16,240},{24,248},{32,192},{40,200},{48,208},{56,2... | collective-permute-start | bytes 159752 | tf_op jit(solution)/shard_map/ppermute | solution.py:169
  65.3 1.5 %collective-permute-done.5 = f32[104,128]{1,0:T(8,128)S(1)} collective-permute-done((f32[104,128]{1,0:T(8,128)S(1)}, f32[104,128]{1,0:T(8,128)S(1)}, u32[]{:S(2)}, u32[]{:S(2)}) %collective-permute-start.5) | collective-permute-done | bytes 53280 | tf_op jit(solution)/shard_map/ppermute | solution.py:169
  66.8 7.2 %collective-permute-start.6 = (f32[104,128]{1,0:T(8,128)S(1)}, f32[104,128]{1,0:T(8,128)S(1)}, u32[]{:S(2)}, u32[]{:S(2)}) collective-permute-start(f32[104,128]{1,0:T(8,128)S(1)} %add.56.one), channel_id=1, source_target_pairs={{0,16},{8,24},{16,0},{24,8},{32,48},{40,56},{48,32},{56,40},{64,80... | collective-permute-start | bytes 159752 | tf_op jit(solution)/shard_map/ppermute | solution.py:169
  74.0 0.0 collective-permute-done.7
  74.0 1.1 %fusion = f32[8,120,128]{2,1,0:T(8,128)S(1)} fusion(f32[8,120,128]{2,1,0:T(8,128)} %collective-permute-done.7, f32[8,224,128]{2,1,0:T(8,128)S(1)} %collective-permute-done.2, f32[8,224,128]{2,1,0:T(8,128)S(1)} %get-tuple-element.6), kind=kLoop, calls=%fused_computation.3 | loop fusion | flops 245760 | bytes 1966080 | tf_op jit(solution)/shard_map/add | solution.py:225
  75.1 0.4 collective-permute-done.6.two
  75.5 0.7 probe.4
  76.2 0.1 pad_maximum_fusion.1
  76.2 11.2 %all_to_all.15.pieces.mine = f32[8,184,128]{2,1,0:T(8,128)S(1)} all-to-all(f32[8,184,128]{2,1,0:T(8,128)S(1)} %pad_maximum_fusion.1), channel_id=1, replica_groups=mesh['tile'=32,'group'=8] {'group'}, dimensions={0} | all-to-all | bytes 1507328 | tf_op jit(solution)/shard_map/all_to_all | solution.py:239
  87.5 6.5 %collective-permute-start.8 = (f32[8,64,128]{2,1,0:T(8,128)S(1)}, f32[8,64,128]{2,1,0:T(8,128)S(1)}, u32[]{:S(2)}, u32[]{:S(2)}) collective-permute-start(f32[8,64,128]{2,1,0:T(8,128)S(1)} %slice.62), channel_id=1, source_target_pairs={{0,8},{8,0},{16,24},{24,16},{32,40},{40,32},{48,56},{56,48},{64,72... | collective-permute-start | bytes 786440 | tf_op jit(solution)/shard_map/ppermute | solution.py:169
  94.0 0.6 object.1
  94.6 0.5 collective-permute-done.8.other
  95.1 1.4 %gather.1 = f32[2,256,256]{2,1,0:T(8,128)} custom-call(s32[2]{0:T(128)S(1)} %pad_add_fusion.place, f32[8,184,128]{2,1,0:T(8,128)S(1)} %all_to_all.15.pieces.mine, f32[8,64,128]{2,1,0:T(8,128)S(1)} %collective-permute-done.8.other), custom_call_target="tpu_custom_call" | custom-call | tf_op jit(solution)/shard_map/gather/pallas_call | solution.py:249
  (9 shorter events, 0.2 us)
Async XLA Ops:
  0.6 7.9 %collective-permute-start.1 = (f32[80,128]{1,0:T(8,128)}, f32[80,128]{1,0:T(8,128)S(1)}, u32[]{:S(2)}, u32[]{:S(2)}) collective-permute-start(f32[80,128]{1,0:T(8,128)} %bitcast.7), channel_id=1, source_target_pairs={{8,16},{16,8},{24,32},{32,24},{40,48},{48,40},{56,64},{64,56},{72,... | collective-permute-start | bytes 122888 | tf_op jit(solution)/shard_map/ppermute | solution.py:177
  6.7 1.9 %collective-permute-start = (f32[80,128]{1,0:T(8,128)}, f32[80,128]{1,0:T(8,128)S(1)}, u32[]{:S(2)}, u32[]{:S(2)}) collective-permute-start(f32[80,128]{1,0:T(8,128)} %bitcast.8), channel_id=1, source_target_pairs={{0,8},{8,0},{16,24},{24,16},{32,40},{40,32},{48,56},{56,48},{64,72... | collective-permute-start | bytes 122888 | tf_op jit(solution)/shard_map/ppermute | solution.py:169
  8.6 0.8 copy-start.4
  10.4 20.2 %copy-start = (f32[2,256,256]{2,1,0:T(8,128)S(1)}, f32[2,256,256]{2,1,0:T(8,128)}, u32[]{:S(2)}) copy-start(f32[2,256,256]{2,1,0:T(8,128)} %probe.5) | copy-start | bytes 1572868
  10.4 20.2 %copy-start.1 = (f32[1,256,256]{2,1,0:T(8,128)S(1)}, f32[1,256,256]{2,1,0:T(8,128)}, u32[]{:S(2)}) copy-start(f32[1,256,256]{2,1,0:T(8,128)} %amps.1) | copy-start | bytes 786436
  10.4 20.2 %copy-start.2 = (bf16[512,256]{1,0:T(8,128)(2,1)S(1)}, bf16[512,256]{1,0:T(8,128)(2,1)}, u32[]{:S(2)}) copy-start(bf16[512,256]{1,0:T(8,128)(2,1)} %constant.14.clone.low) | copy-start | bytes 786436
  10.4 20.2 %copy-start.3 = (bf16[512,256]{1,0:T(8,128)(2,1)S(1)}, bf16[512,256]{1,0:T(8,128)(2,1)}, u32[]{:S(2)}) copy-start(bf16[512,256]{1,0:T(8,128)(2,1)} %constant.13.clone.high) | copy-start | bytes 786436
  10.4 20.2 %all-to-all-start = ((f32[8,240,128]{2,1,0:T(8,128)}), f32[8,240,128]{2,1,0:T(8,128)S(1)}, u32[]{:S(2)}, u32[]{:S(2)}) async-start(f32[8,240,128]{2,1,0:T(8,128)} %pad_maximum_fusion), calls=%async_computation | async-start | bytes 1966080 | tf_op jit(solution)/shard_map/all_to_all | solution.py:203
  35.0 0.8 copy-start.5
  35.8 2.5 %collective-permute-start.2 = (f32[8,224,128]{2,1,0:T(8,128)S(1)}, f32[8,224,128]{2,1,0:T(8,128)S(1)}, u32[]{:S(2)}, u32[]{:S(2)}) collective-permute-start(f32[8,224,128]{2,1,0:T(8,128)S(1)} %get-tuple-element.7), channel_id=1, source_target_pairs={{0,8},{8,0},{16,24},{24,16},{32,40},{40,32},{48,56},{56,48},{64,72... | collective-permute-start | bytes 2752520 | tf_op jit(solution)/shard_map/ppermute | solution.py:169
  39.1 3.6 %copy-start.6 = (f32[8,120,128]{2,1,0:T(8,128)S(1)}, f32[8,120,128]{2,1,0:T(8,128)}, u32[]{:S(2)}) copy-start(f32[8,120,128]{2,1,0:T(8,128)} %copy-done.5) | copy-start | bytes 1474564
  39.1 12.0 %all-to-all-start.1 = ((f32[8,104,128]{2,1,0:T(8,128)}), f32[8,104,128]{2,1,0:T(8,128)S(1)}, u32[]{:S(2)}, u32[]{:S(2)}) async-start(f32[8,104,128]{2,1,0:T(8,128)} %slice_add_fusion.1), calls=%async_computation.1 | async-start | bytes 851968 | tf_op jit(solution)/shard_map/all_to_all | solution.py:224
  42.7 31.3 %collective-permute-start.7 = (f32[8,120,128]{2,1,0:T(8,128)S(1)}, f32[8,120,128]{2,1,0:T(8,128)}, u32[]{:S(2)}, u32[]{:S(2)}) collective-permute-start(f32[8,120,128]{2,1,0:T(8,128)S(1)} %copy-done.6), channel_id=1, source_target_pairs={{8,16},{16,8},{24,32},{32,24},{40,48},{48,40},{56,64},{64,56},{72,... | collective-permute-start | bytes 1474568 | tf_op jit(solution)/shard_map/ppermute | solution.py:177
  51.1 4.9 %collective-permute-start.3 = (f32[104,128]{1,0:T(8,128)S(1)}, f32[104,128]{1,0:T(8,128)S(1)}, u32[]{:S(2)}, u32[]{:S(2)}) collective-permute-start(f32[104,128]{1,0:T(8,128)S(1)} %fusion.1), channel_id=1, source_target_pairs={{0,32},{8,40},{16,48},{24,56},{32,0},{40,8},{48,16},{56,24},{64,96... | collective-permute-start | bytes 159752 | tf_op jit(solution)/shard_map/ppermute | solution.py:169
  56.0 4.6 %collective-permute-start.4 = (f32[104,128]{1,0:T(8,128)S(1)}, f32[104,128]{1,0:T(8,128)S(1)}, u32[]{:S(2)}, u32[]{:S(2)}) collective-permute-start(f32[104,128]{1,0:T(8,128)S(1)} %fusion.2), channel_id=1, source_target_pairs={{0,64},{8,72},{16,80},{24,88},{32,96},{40,104},{48,112},{56,120},{... | collective-permute-start | bytes 159752 | tf_op jit(solution)/shard_map/ppermute | solution.py:169
  60.6 6.1 %collective-permute-start.5 = (f32[104,128]{1,0:T(8,128)S(1)}, f32[104,128]{1,0:T(8,128)S(1)}, u32[]{:S(2)}, u32[]{:S(2)}) collective-permute-start(f32[104,128]{1,0:T(8,128)S(1)} %add.55), channel_id=1, source_target_pairs={{0,224},{8,232},{16,240},{24,248},{32,192},{40,200},{48,208},{56,2... | collective-permute-start | bytes 159752 | tf_op jit(solution)/shard_map/ppermute | solution.py:169
  66.8 8.7 %collective-permute-start.6 = (f32[104,128]{1,0:T(8,128)S(1)}, f32[104,128]{1,0:T(8,128)S(1)}, u32[]{:S(2)}, u32[]{:S(2)}) collective-permute-start(f32[104,128]{1,0:T(8,128)S(1)} %add.56.one), channel_id=1, source_target_pairs={{0,16},{8,24},{16,0},{24,8},{32,48},{40,56},{48,32},{56,40},{64,80... | collective-permute-start | bytes 159752 | tf_op jit(solution)/shard_map/ppermute | solution.py:169
  87.5 7.7 %collective-permute-start.8 = (f32[8,64,128]{2,1,0:T(8,128)S(1)}, f32[8,64,128]{2,1,0:T(8,128)S(1)}, u32[]{:S(2)}, u32[]{:S(2)}) collective-permute-start(f32[8,64,128]{2,1,0:T(8,128)S(1)} %slice.62), channel_id=1, source_target_pairs={{0,8},{8,0},{16,24},{24,16},{32,40},{40,32},{48,56},{56,48},{64,72... | collective-permute-start | bytes 786440 | tf_op jit(solution)/shard_map/ppermute | solution.py:169

commit v4 on v3

--- a/solution.py
+++ b/solution.py
@@ -9,7 +9,10 @@
 
 WIN = 256
 LANES = 128
+SPARE = 96
 PIECE = 104
+NEAR = 184
+ROWS = 264
 SMEM = pltpu.MemorySpace.SMEM
 VMEM = pltpu.MemorySpace.VMEM
 
@@ -49,7 +52,7 @@
 
 def window_kernel(
     place, row_ref, col_ref, live_ref, stack, probe, amps, high, low,
-    keep, send, far_out, peak, field, grads, sums,
+    keep, send, peak, field, grads, sums,
 ):
     row, col = row_ref[0], col_ref[0]
     live = live_ref[0].astype(jnp.float32)
@@ -91,12 +94,11 @@
     terms = (
         probe_real * miss_real + probe_imag * miss_imag,
         probe_real * miss_imag - probe_imag * miss_real,
-        live * light,
     )
     wrapped = lane < col
     zero = jnp.zeros((WIN, LANES), jnp.float32)
     grads[...] = jnp.zeros_like(grads)
-    for part in range(3):
+    for part in range(2):
         start = pltpu.roll(terms[part][:, :LANES], ahead, 1)
         end = pltpu.roll(terms[part][:, LANES:], ahead, 1)
         grads[part, 0, pl.ds(row, WIN), :] = jnp.where(wrapped, zero, start)
@@ -109,6 +111,18 @@
     total = jnp.zeros((8, LANES), jnp.float32)
     for line in range(0, WIN, 8):
         total = total + window_light[line : line + 8, :LANES] + window_light[line : line + 8, LANES:]
+    spare_line = lax.broadcasted_iota(jnp.int32, (8, LANES), 0)
+    spare_lane = lax.broadcasted_iota(jnp.int32, (8, LANES), 1)
+    where_mine = jnp.where(
+        spare_lane == 0,
+        row.astype(jnp.float32),
+        jnp.where(spare_lane == 1, col.astype(jnp.float32), jnp.where(spare_lane == 2, live, 0.0)),
+    )
+    spare = jnp.where(
+        spare_line == 0,
+        jnp.broadcast_to(jnp.sum(total, axis=0, keepdims=True), (8, LANES)),
+        jnp.where(spare_line == 1 + odd, where_mine, 0.0),
+    )
     for member in range(8):
         lines = slice(member * 40, member * 40 + 40)
         for out, half, block in ((keep, odd, 1), (send, 1 - odd, 2 - 2 * odd)):
@@ -119,24 +133,59 @@
                     out[member, put : put + 16, :] = sums[
                         part, pl.ds(top, 16), side * LANES : (side + 1) * LANES
                     ]
+            out[member, SPARE:PIECE, :] = spare
+            for part in range(2):
                 put = PIECE + part * 40
                 out[member, put : put + 40, :] = grads[part, block, lines, :]
-            out[member, 96:PIECE, :] = total
-        for part in range(3):
-            far_out[member, part * 40 : part * 40 + 40, :] = grads[part, 2 * odd, lines, :]
+        for part in range(2):
+            put = NEAR + part * 40
+            keep[member, put : put + 40, :] = grads[part, 2 * odd, lines, :]
+
+
+def pack_kernel(own, near, far, out):
+    for member in range(8):
+        out[member, 0:80, :] = own[...]
+        out[member, 80:160, :] = near[...]
+        out[member, 160:240, :] = far[...]
+
+
+def merge_kernel(keep, got, out):
+    out[:, :NEAR, :] = keep[:, :NEAR, :] + got[...]
+    out[:, NEAR:, :] = keep[:, NEAR:, :]
+
+
+def reduce_kernel(place, pieces, probe_sum, own_sum, far_sum):
+    def added(start, end):
+        total = pieces[0, start:end, :]
+        for member in range(1, 8):
+            total = total + pieces[member, start:end, :]
+        return total
+
+    probe_sum[...] = added(0, PIECE)
+    own_sum[...] = added(PIECE, NEAR)
+    far_sum[0:80, :] = added(NEAR, ROWS)
+    line = lax.broadcasted_iota(jnp.int32, (8, LANES), 0)
+    mine = jnp.zeros((8, LANES), jnp.float32)
+    for member in range(8):
+        spare = pieces[member, SPARE:PIECE, :]
+        place_row = jnp.where((place[0] & 1) == 1, spare[2:3], spare[1:2])
+        mine = jnp.where(line == member, place_row, mine)
+    far_sum[80:88, :] = mine
 
 
 def probe_kernel(place, one, two, probe, out):
     piece = (place[0] & 1) * 8 + place[1]
     summed = one[...] + two[...]
-    mean = jnp.sum(summed[96:PIECE]) * (1.0 / (WIN * WIN))
+    mean = jnp.sum(summed[SPARE : SPARE + 1]) * (1.0 / (WIN * WIN))
     for side in range(2):
         bottom = summed[64 + side * 16 : 80 + side * 16] + 0.25 * mean + 1e-05
         for part in range(2):
             lines = part * 32 + side * 16
             top = pl.multiple_of(piece * 16, 16)
             old = probe[part, pl.ds(top, 16), side * LANES : (side + 1) * LANES]
-            out[lines : lines + 16, :] = old - summed[lines : lines + 16] / bottom
+            new = old - summed[lines : lines + 16] / bottom
+            for member in range(8):
+                out[member, lines : lines + 16, :] = new
 
 
 def gather_kernel(place, mine, other, out):
@@ -152,13 +201,46 @@
                     ]
 
 
-def object_kernel(pieces, old, peak, out):
-    summed = pieces[0, 64:184, :]
-    for member in range(1, 8):
-        summed = summed + pieces[member, 64:184, :]
-    bottom = summed[80:120] + 0.25 * (peak[0:1, :] + 1e-06)
-    out[0] = old[0] - summed[0:40] / bottom
-    out[1] = old[1] - summed[40:80] / bottom
+def object_kernel(place, pieces, own_sum, far_sum, old, probe, peak, out, light, near_at, far_at, sems):
+    copies = [
+        pltpu.make_async_copy(pieces.at[:, SPARE:PIECE, :], near_at, sems.at[0]),
+        pltpu.make_async_copy(far_sum.at[80:88, :], far_at, sems.at[1]),
+    ]
+    for copy in copies:
+        copy.start()
+    odd = place[0] & 1
+    blank = jnp.zeros((64, LANES), jnp.float32)
+    for side in range(2):
+        cols = slice(side * LANES, (side + 1) * LANES)
+        light[1 + side, 64:320, :] = probe[0, :, cols] * probe[0, :, cols] + (
+            probe[1, :, cols] * probe[1, :, cols]
+        )
+        light[1 + side, 0:64, :] = blank
+        light[1 + side, 320:384, :] = blank
+        light[3 * side, :, :] = jnp.zeros((384, LANES), jnp.float32)
+    for copy in copies:
+        copy.wait()
+    lane = lax.broadcasted_iota(jnp.int32, (40, LANES), 1)
+
+    def shine(total, row, col, live, block):
+        row, col = row.astype(jnp.int32), col.astype(jnp.int32)
+        top = 64 + place[1] * 40 - row
+        turn = lax.rem(col, LANES)
+        before = pltpu.roll(light[block, pl.ds(top, 40), :], turn, 1)
+        after = pltpu.roll(light[block + 1, pl.ds(top, 40), :], turn, 1)
+        return total + live * jnp.where(lane < col, before, after)
+
+    total = jnp.zeros((40, LANES), jnp.float32)
+    for member in range(8):
+        for core in range(2):
+            block = 1 + core * (1 - odd) * -1 + (1 - core) * odd
+            at = [near_at[member, 1 + core, k] for k in range(3)]
+            total = shine(total, *at, block)
+        total = shine(total, *[far_at[member, k] for k in range(3)], 2 - 2 * odd)
+    bottom = total + 0.25 * (peak[0:1, :] + 1e-06)
+    for part in range(2):
+        lines = slice(part * 40, part * 40 + 40)
+        out[part] = old[part] - (own_sum[lines, :] + far_sum[lines, :]) / bottom
 
 
 def pair_up(axis, mask):
@@ -181,11 +263,16 @@
     return pltpu.with_memory_space_constraint(value, pltpu.VMEM)
 
 
-def sum_first(value):
-    total = value[0]
-    for index in range(1, value.shape[0]):
-        total = total + value[index]
-    return total
+def kernel_call(body, out_shape, in_specs, out_specs, megabytes, **kwargs):
+    return pl.pallas_call(
+        body,
+        out_shape=out_shape,
+        in_specs=in_specs,
+        out_specs=out_specs,
+        compiler_params=pltpu.CompilerParams(vmem_limit_bytes=megabytes << 20),
+        name=body.__name__.removesuffix("_kernel"),
+        **kwargs,
+    )
 
 
 def local(object_field, probe_field, amplitudes, row_start, column_start, live_slots):
@@ -198,62 +285,62 @@
         return pltpu.VMEM(dims, jnp.float32)
 
     own = object_field.reshape(80, LANES)
-    rows = (own, swap(own, "tile", 1), swap_far(own))
-    rows = jnp.concatenate([jnp.broadcast_to(block, (8, 80, LANES)) for block in rows], axis=1)
+    near, far = swap(own, "tile", 1), swap_far(own)
+    rows = kernel_call(pack_kernel, buffer(8, 240, LANES), [vmem] * 3, vmem, 4)(
+        *map(on_chip, (own, near, far))
+    )
     stack = lax.all_to_all(rows, "group", 0, 0)
-
-    keep, send, far_out, peak = pl.pallas_call(
+    keep, send, peak = kernel_call(
         window_kernel,
-        out_shape=(
-            buffer(8, PIECE + 120, LANES),
-            buffer(8, PIECE + 120, LANES),
-            buffer(8, 120, LANES),
-            buffer(8, LANES),
-        ),
-        in_specs=[smem] * 4 + [vmem] * 5,
-        out_specs=(vmem,) * 4,
-        scratch_shapes=[buffer(2, 3, 320, LANES), buffer(3, 3, 320, LANES), buffer(3, WIN, WIN)],
-        compiler_params=pltpu.CompilerParams(vmem_limit_bytes=24 << 20),
-        name="window",
+        (buffer(8, ROWS, LANES), buffer(8, NEAR, LANES), buffer(8, LANES)),
+        [smem] * 4 + [vmem] * 5,
+        (vmem,) * 3,
+        24,
+        scratch_shapes=[buffer(2, 3, 320, LANES), buffer(2, 3, 320, LANES), buffer(3, WIN, WIN)],
     )(
         place, row_start, column_start, live_slots, on_chip(stack), probe, on_chip(amplitudes),
         high, low,
     )
 
-    got = swap(send, "tile", 1)
-    eighths = lax.all_to_all(keep[:, :PIECE] + got[:, :PIECE], "group", 0, 0)
-    gradient = keep[:, PIECE:] + got[:, PIECE:] + swap_far(far_out)
-    total = sum_first(eighths)
+    merged = kernel_call(merge_kernel, buffer(8, ROWS, LANES), [vmem] * 2, vmem, 4)(
+        keep, on_chip(swap(send, "tile", 1))
+    )
+    pieces = on_chip(lax.all_to_all(merged, "group", 0, 0))
+    total, own_sum, far_sum = kernel_call(
+        reduce_kernel,
+        (buffer(PIECE, LANES), buffer(80, LANES), buffer(88, LANES)),
+        [smem, vmem],
+        (vmem,) * 3,
+        4,
+    )(place, pieces)
+    far_got = swap_far(far_sum)
     for mask in (4, 8, 28):
         total = total + swap(total, "tile", mask)
-    piece = pl.pallas_call(
-        probe_kernel,
-        out_shape=buffer(64, LANES),
-        in_specs=[smem] + [vmem] * 3,
-        out_specs=vmem,
-        compiler_params=pltpu.CompilerParams(vmem_limit_bytes=4 << 20),
-        name="probe",
-    )(place, on_chip(total), on_chip(swap(total, "tile", 2)), probe)
-
-    outgoing = jnp.concatenate([jnp.broadcast_to(piece, (8, 64, LANES)), gradient], axis=1)
-    pieces = lax.all_to_all(outgoing, "group", 0, 0)
-    mine = pieces[:, :64]
-    new_object = pl.pallas_call(
+    piece = kernel_call(probe_kernel, buffer(8, 64, LANES), [smem] + [vmem] * 3, vmem, 4)(
+        place, on_chip(total), on_chip(swap(total, "tile", 2)), probe
+    )
+    new_object = kernel_call(
         object_kernel,
-        out_shape=jax.ShapeDtypeStruct((2, 40, LANES), jnp.float32),
-        in_specs=[vmem] * 3,
-        out_specs=vmem,
-        compiler_params=pltpu.CompilerParams(vmem_limit_bytes=4 << 20),
-        name="object",
-    )(on_chip(pieces), on_chip(object_field), peak)
-    new_probe = pl.pallas_call(
+        jax.ShapeDtypeStruct((2, 40, LANES), jnp.float32),
+        [smem] + [vmem] * 6,
+        vmem,
+        8,
+        scratch_shapes=[
+            buffer(4, 384, LANES),
+            pltpu.SMEM((8, 8, LANES), jnp.float32),
+            pltpu.SMEM((8, LANES), jnp.float32),
+            pltpu.SemaphoreType.DMA((2,)),
+        ],
+    )(place, pieces, own_sum, on_chip(far_got), on_chip(object_field), probe, peak)
+
+    mine = lax.all_to_all(piece, "group", 0, 0)
+    new_probe = kernel_call(
         gather_kernel,
-        out_shape=jax.ShapeDtypeStruct((2, WIN, WIN), jnp.float32),
-        in_specs=[smem] + [vmem] * 2,
-        out_specs=vmem,
-        compiler_params=pltpu.CompilerParams(vmem_limit_bytes=4 << 20),
-        name="gather",
-    )(place, on_chip(pieces), on_chip(swap(mine, "tile", 1)))
+        jax.ShapeDtypeStruct((2, WIN, WIN), jnp.float32),
+        [smem] + [vmem] * 2,
+        vmem,
+        4,
+    )(place, on_chip(mine), on_chip(swap(mine, "tile", 1)))
     return new_object, new_probe
 
 

time: 98.1 us -> 104 us (1.060); the launches traced: 96.5 us -> 104 us
  blocking collectives: 11.2 us -> 26.6 us
  starting transfers between devices: 45.5 us -> 34.1 us
  Pallas kernels: 7.01 us -> 10.7 us
  waiting for transfers between devices: 25.3 us -> 28.7 us
  other arithmetic: 3.13 us -> 0.1 us
    all_to_all x1 -> x2, blocking collectives: 11.2 us -> 26.6 us  [the longest x1 18.1 us: local(): pieces = on_chip(lax.all_to_all(merged, 'group', 0, 0))]
    ppermute x7, starting transfers between devices: 24.6 us -> 19.9 us  [swap(): return lax.ppermute(value, axis, pair_up(axis, mask))]
    ppermute x2, waiting for transfers between devices: 1.78 us -> 5.61 us  [swap_far(): return lax.ppermute(value, 'tile', pairs)]
    pallas_call x4 -> x7, Pallas kernels: 7.01 us -> 10.7 us  [the longest x1 4.28 us: local(): kernel_call(window_kernel, (buffer(8, ROWS, LANES), buffer(8, NEAR, LANES...]
    all_to_all x1 -> x0, starting transfers between devices: 3.59 us -> none  [local(): eighths = lax.all_to_all(keep[:, :PIECE] + got[:, :PIECE], 'group', 0, 0)]
    ppermute x2, starting transfers between devices: 12.2 us -> 9.06 us  [swap_far(): return lax.ppermute(value, 'tile', pairs)]
    all_to_all x1 -> x0, waiting for transfers between devices: 2.29 us -> none  [local(): eighths = lax.all_to_all(keep[:, :PIECE] + got[:, :PIECE], 'group', 0, 0)]
    add x3 -> x0, other arithmetic: 1.94 us -> none  [the longest x1 1.1 us: local(): gradient = keep[:, PIECE:] + got[:, PIECE:] + swap_far(far_out)]
  transfers between devices with their start and end apart: 11 -> 10, of which waited for: 9 -> 8; matrix products, arithmetic and copies ran while one was open for 1% -> 0% of each run, Pallas kernels for 1% -> 3%
where the time goes in v4:
time: 104 us
  starting transfers between devices  34.1 us (33%)
  waiting for transfers between devices  28.7 us (28%)
  blocking collectives  26.6 us (26%)
  Pallas kernels  10.7 us (10%)
  between operations  2.68 us (3%)
    ppermute x7, starting transfers between devices, swap(): return lax.ppermute(value, axis, pair_up(axis, mask))  19.9 us
    all_to_all x1, blocking collectives, local(): pieces = on_chip(lax.all_to_all(merged, 'group', 0, 0))  18.1 us
    all_to_all x1, waiting for transfers between devices, local(): stack = lax.all_to_all(rows, 'group', 0, 0)  13 us
    ppermute x7, waiting for transfers between devices, swap(): return lax.ppermute(value, axis, pair_up(axis, mask))  10.1 us
    ppermute x2, starting transfers between devices, swap_far(): return lax.ppermute(value, 'tile', pairs)  9.06 us
    all_to_all x1, blocking collectives, local(): mine = lax.all_to_all(piece, 'group', 0, 0)  8.55 us
    ppermute x2, waiting for transfers between devices, swap_far(): return lax.ppermute(value, 'tile', pairs)  5.61 us
    all_to_all x1, starting transfers between devices, local(): stack = lax.all_to_all(rows, 'group', 0, 0)  5.2 us
  transfers between devices with their start and end apart: 10, of which 8 were waited for; matrix products, arithmetic and copies ran while one was open for 0% of the time, Pallas kernels for 3%

profile of v4, /device:TPU:1, one launch (start us, length us, event | category | flops | bytes accessed | tf_op | source)
XLA Modules:
  0.0 103.7 jit_solution(10417129599187324141)
XLA Ops:
  0.6 6.0 %collective-permute-start.1 = (f32[80,128]{1,0:T(8,128)}, f32[80,128]{1,0:T(8,128)S(1)}, u32[]{:S(2)}, u32[]{:S(2)}) collective-permute-start(f32[80,128]{1,0:T(8,128)} %bitcast.3), channel_id=1, source_target_pairs={{8,16},{16,8},{24,32},{32,24},{40,48},{48,40},{56,64},{64,56},{72,... | collective-permute-start | bytes 122888 | tf_op jit(solution)/shard_map/ppermute | solution.py:259
  6.7 0.1 collective-permute-start
  6.8 1.8 %collective-permute-done.1.far = f32[80,128]{1,0:T(8,128)S(1)} collective-permute-done((f32[80,128]{1,0:T(8,128)}, f32[80,128]{1,0:T(8,128)S(1)}, u32[]{:S(2)}, u32[]{:S(2)}) %collective-permute-start.1) | collective-permute-done | bytes 40992 | tf_op jit(solution)/shard_map/ppermute | solution.py:259
  8.6 0.0 collective-permute-done.near
  8.6 0.0 copy-start.4
  8.6 0.8 copy-done.4
  9.3 1.0 pack.1
  10.4 0.0 copy-start
  10.4 0.0 copy-start.1
  10.4 0.0 copy-start.2
  10.4 0.0 copy-start.3
  10.4 5.2 %all-to-all-start = ((f32[8,240,128]{2,1,0:T(8,128)}), f32[8,240,128]{2,1,0:T(8,128)S(1)}, u32[]{:S(2)}, u32[]{:S(2)}) async-start(f32[8,240,128]{2,1,0:T(8,128)} %pack.1), calls=%async_computation | async-start | bytes 1966080 | tf_op jit(solution)/shard_map/all_to_all | solution.py:292
  17.5 0.1 pad_add_fusion.place
  17.6 13.0 %all-to-all-done.stack = f32[8,240,128]{2,1,0:T(8,128)S(1)} async-done(((f32[8,240,128]{2,1,0:T(8,128)}), f32[8,240,128]{2,1,0:T(8,128)S(1)}, u32[]{:S(2)}, u32[]{:S(2)}) %all-to-all-start) | async-done | bytes 983072 | tf_op jit(solution)/shard_map/all_to_all | solution.py:292
  30.6 0.0 copy-done
  30.6 0.0 copy-done.1
  30.6 0.0 copy-done.2
  30.6 0.0 copy-done.3
  30.6 4.3 %window.1 = (f32[8,264,128]{2,1,0:T(8,128)S(1)}, f32[8,184,128]{2,1,0:T(8,128)S(1)}, f32[8,128]{1,0:T(8,128)S(1)}) custom-call(s32[2]{0:T(128)S(1)} %pad_add_fusion.place, s32[1]{0:T(128)S(6)} %copy.10.row_ref, s32[1]{0:T(128)S(6)} %copy.11.col_ref, s32[1]{0:T(128)S(6)} %copy.12.live_ref, f32[8,240,128]{2,1,0:T(8,128)S(1)} %all-to-all-done.stack, ...), custom_call_target="tpu_custom_call" | custom-call | tf_op jit(solution)/shard_map/window/pallas_call | solution.py:293
  34.9 0.5 collective-permute-start.2
  35.4 1.9 %collective-permute-done.2.got = f32[8,184,128]{2,1,0:T(8,128)S(1)} collective-permute-done((f32[8,184,128]{2,1,0:T(8,128)S(1)}, f32[8,184,128]{2,1,0:T(8,128)S(1)}, u32[]{:S(2)}, u32[]{:S(2)}) %collective-permute-start.2) | collective-permute-done | bytes 753696 | tf_op jit(solution)/shard_map/ppermute | solution.py:251
  37.2 0.1 merge.1
  37.3 18.1 %all_to_all.15.pieces = f32[8,264,128]{2,1,0:T(8,128)S(1)} all-to-all(f32[8,264,128]{2,1,0:T(8,128)S(1)} %merge.1), channel_id=1, replica_groups=mesh['tile'=32,'group'=8] {'group'}, dimensions={0} | all-to-all | bytes 2162688 | tf_op jit(solution)/shard_map/all_to_all | solution.py:308
  55.4 0.6 reduce.1
  56.0 0.0 copy-start.5
  56.0 2.4 %collective-permute-start.4 = (f32[104,128]{1,0:T(8,128)S(1)}, f32[104,128]{1,0:T(8,128)S(1)}, u32[]{:S(2)}, u32[]{:S(2)}) collective-permute-start(f32[104,128]{1,0:T(8,128)S(1)} %get-tuple-element.13), channel_id=1, source_target_pairs={{0,32},{8,40},{16,48},{24,56},{32,0},{40,8},{48,16},{56,24},{64,96... | collective-permute-start | bytes 159752 | tf_op jit(solution)/shard_map/ppermute | solution.py:251
  58.5 1.5 %collective-permute-done.4 = f32[104,128]{1,0:T(8,128)S(1)} collective-permute-done((f32[104,128]{1,0:T(8,128)S(1)}, f32[104,128]{1,0:T(8,128)S(1)}, u32[]{:S(2)}, u32[]{:S(2)}) %collective-permute-start.4) | collective-permute-done | bytes 53280 | tf_op jit(solution)/shard_map/ppermute | solution.py:251
  60.0 3.1 %collective-permute-start.5 = (f32[104,128]{1,0:T(8,128)S(1)}, f32[104,128]{1,0:T(8,128)S(1)}, u32[]{:S(2)}, u32[]{:S(2)}) collective-permute-start(f32[104,128]{1,0:T(8,128)S(1)} %add.9), channel_id=1, source_target_pairs={{0,64},{8,72},{16,80},{24,88},{32,96},{40,104},{48,112},{56,120},{... | collective-permute-start | bytes 159752 | tf_op jit(solution)/shard_map/ppermute | solution.py:251
  63.1 1.5 %collective-permute-done.5 = f32[104,128]{1,0:T(8,128)S(1)} collective-permute-done((f32[104,128]{1,0:T(8,128)S(1)}, f32[104,128]{1,0:T(8,128)S(1)}, u32[]{:S(2)}, u32[]{:S(2)}) %collective-permute-start.5) | collective-permute-done | bytes 53280 | tf_op jit(solution)/shard_map/ppermute | solution.py:251
  64.6 5.4 %collective-permute-start.6 = (f32[104,128]{1,0:T(8,128)S(1)}, f32[104,128]{1,0:T(8,128)S(1)}, u32[]{:S(2)}, u32[]{:S(2)}) collective-permute-start(f32[104,128]{1,0:T(8,128)S(1)} %add.10), channel_id=1, source_target_pairs={{0,224},{8,232},{16,240},{24,248},{32,192},{40,200},{48,208},{56,2... | collective-permute-start | bytes 159752 | tf_op jit(solution)/shard_map/ppermute | solution.py:251
  70.1 2.1 %collective-permute-done.6 = f32[104,128]{1,0:T(8,128)S(1)} collective-permute-done((f32[104,128]{1,0:T(8,128)S(1)}, f32[104,128]{1,0:T(8,128)S(1)}, u32[]{:S(2)}, u32[]{:S(2)}) %collective-permute-start.6) | collective-permute-done | bytes 53280 | tf_op jit(solution)/shard_map/ppermute | solution.py:251
  72.1 1.5 %collective-permute-start.7 = (f32[104,128]{1,0:T(8,128)S(1)}, f32[104,128]{1,0:T(8,128)S(1)}, u32[]{:S(2)}, u32[]{:S(2)}) collective-permute-start(f32[104,128]{1,0:T(8,128)S(1)} %add.11.one), channel_id=1, source_target_pairs={{0,16},{8,24},{16,0},{24,8},{32,48},{40,56},{48,32},{56,40},{64,80... | collective-permute-start | bytes 159752 | tf_op jit(solution)/shard_map/ppermute | solution.py:251
  73.7 3.1 %collective-permute-done.7.two = f32[104,128]{1,0:T(8,128)S(1)} collective-permute-done((f32[104,128]{1,0:T(8,128)S(1)}, f32[104,128]{1,0:T(8,128)S(1)}, u32[]{:S(2)}, u32[]{:S(2)}) %collective-permute-start.7) | collective-permute-done | bytes 53280 | tf_op jit(solution)/shard_map/ppermute | solution.py:251
  76.7 0.7 probe.6
  77.4 8.5 %all_to_all.16.mine = f32[8,64,128]{2,1,0:T(8,128)S(1)} all-to-all(f32[8,64,128]{2,1,0:T(8,128)S(1)} %probe.6), channel_id=1, replica_groups=mesh['tile'=32,'group'=8] {'group'}, dimensions={0} | all-to-all | bytes 524288 | tf_op jit(solution)/shard_map/all_to_all | solution.py:336
  86.0 6.9 %collective-permute-start.8 = (f32[8,64,128]{2,1,0:T(8,128)S(1)}, f32[8,64,128]{2,1,0:T(8,128)S(1)}, u32[]{:S(2)}, u32[]{:S(2)}) collective-permute-start(f32[8,64,128]{2,1,0:T(8,128)S(1)} %all_to_all.16.mine), channel_id=1, source_target_pairs={{0,8},{8,0},{16,24},{24,16},{32,40},{40,32},{48,56},{56,48},{64,72... | collective-permute-start | bytes 786440 | tf_op jit(solution)/shard_map/ppermute | solution.py:251
  92.8 3.0 %collective-permute-start.3 = (f32[88,128]{1,0:T(8,128)S(1)}, f32[88,128]{1,0:T(8,128)S(1)}, u32[]{:S(2)}, u32[]{:S(2)}) collective-permute-start(f32[88,128]{1,0:T(8,128)S(1)} %get-tuple-element.11), channel_id=1, source_target_pairs={{8,16},{16,8},{24,32},{32,24},{40,48},{48,40},{56,64},{64,56},{72,... | collective-permute-start | bytes 135176 | tf_op jit(solution)/shard_map/ppermute | solution.py:259
  95.9 3.8 %collective-permute-done.3.far_sum = f32[88,128]{1,0:T(8,128)S(1)} collective-permute-done((f32[88,128]{1,0:T(8,128)S(1)}, f32[88,128]{1,0:T(8,128)S(1)}, u32[]{:S(2)}, u32[]{:S(2)}) %collective-permute-start.3) | collective-permute-done | bytes 45088 | tf_op jit(solution)/shard_map/ppermute | solution.py:259
  99.7 0.0 copy-done.5
  99.7 2.6 %object.1 = f32[2,40,128]{2,1,0:T(8,128)} custom-call(s32[2]{0:T(128)S(1)} %pad_add_fusion.place, f32[8,264,128]{2,1,0:T(8,128)S(1)} %all_to_all.15.pieces, f32[80,128]{1,0:T(8,128)S(1)} %get-tuple-element.10.own_sum, f32[88,128]{1,0:T(8,128)S(1)} %collective-permute-done.3.far_sum, f32[2,40,128]{2,1,0:T(8,128)S(1)} %copy-done.5, ...), custom_call_target="tpu_custom_call" | custom-call | tf_op jit(solution)/shard_map/object/pallas_call | solution.py:322
  102.3 0.0 collective-permute-done.8.other
  102.4 1.4 %gather.1 = f32[2,256,256]{2,1,0:T(8,128)} custom-call(s32[2]{0:T(128)S(1)} %pad_add_fusion.place, f32[8,64,128]{2,1,0:T(8,128)S(1)} %all_to_all.16.mine, f32[8,64,128]{2,1,0:T(8,128)S(1)} %collective-permute-done.8.other), custom_call_target="tpu_custom_call" | custom-call | tf_op jit(solution)/shard_map/gather/pallas_call | solution.py:337
  (3 shorter events, 0.0 us)
Async XLA Ops:
  0.6 7.9 %collective-permute-start.1 = (f32[80,128]{1,0:T(8,128)}, f32[80,128]{1,0:T(8,128)S(1)}, u32[]{:S(2)}, u32[]{:S(2)}) collective-permute-start(f32[80,128]{1,0:T(8,128)} %bitcast.3), channel_id=1, source_target_pairs={{8,16},{16,8},{24,32},{32,24},{40,48},{48,40},{56,64},{64,56},{72,... | collective-permute-start | bytes 122888 | tf_op jit(solution)/shard_map/ppermute | solution.py:259
  6.7 1.9 %collective-permute-start = (f32[80,128]{1,0:T(8,128)}, f32[80,128]{1,0:T(8,128)S(1)}, u32[]{:S(2)}, u32[]{:S(2)}) collective-permute-start(f32[80,128]{1,0:T(8,128)} %bitcast.4), channel_id=1, source_target_pairs={{0,8},{8,0},{16,24},{24,16},{32,40},{40,32},{48,56},{56,48},{64,72... | collective-permute-start | bytes 122888 | tf_op jit(solution)/shard_map/ppermute | solution.py:251
  8.6 0.8 copy-start.4
  10.4 20.2 %copy-start = (f32[2,256,256]{2,1,0:T(8,128)S(1)}, f32[2,256,256]{2,1,0:T(8,128)}, u32[]{:S(2)}) copy-start(f32[2,256,256]{2,1,0:T(8,128)} %probe.7) | copy-start | bytes 1572868
  10.4 20.2 %copy-start.1 = (f32[1,256,256]{2,1,0:T(8,128)S(1)}, f32[1,256,256]{2,1,0:T(8,128)}, u32[]{:S(2)}) copy-start(f32[1,256,256]{2,1,0:T(8,128)} %amps.1) | copy-start | bytes 786436
  10.4 20.2 %copy-start.2 = (bf16[512,256]{1,0:T(8,128)(2,1)S(1)}, bf16[512,256]{1,0:T(8,128)(2,1)}, u32[]{:S(2)}) copy-start(bf16[512,256]{1,0:T(8,128)(2,1)} %constant.14.clone.low) | copy-start | bytes 786436
  10.4 20.2 %copy-start.3 = (bf16[512,256]{1,0:T(8,128)(2,1)S(1)}, bf16[512,256]{1,0:T(8,128)(2,1)}, u32[]{:S(2)}) copy-start(bf16[512,256]{1,0:T(8,128)(2,1)} %constant.13.clone.high) | copy-start | bytes 786436
  10.4 20.2 %all-to-all-start = ((f32[8,240,128]{2,1,0:T(8,128)}), f32[8,240,128]{2,1,0:T(8,128)S(1)}, u32[]{:S(2)}, u32[]{:S(2)}) async-start(f32[8,240,128]{2,1,0:T(8,128)} %pack.1), calls=%async_computation | async-start | bytes 1966080 | tf_op jit(solution)/shard_map/all_to_all | solution.py:292
  34.9 2.3 %collective-permute-start.2 = (f32[8,184,128]{2,1,0:T(8,128)S(1)}, f32[8,184,128]{2,1,0:T(8,128)S(1)}, u32[]{:S(2)}, u32[]{:S(2)}) collective-permute-start(f32[8,184,128]{2,1,0:T(8,128)S(1)} %get-tuple-element.9), channel_id=1, source_target_pairs={{0,8},{8,0},{16,24},{24,16},{32,40},{40,32},{48,56},{56,48},{64,72... | collective-permute-start | bytes 2261000 | tf_op jit(solution)/shard_map/ppermute | solution.py:251
  56.0 43.7 %copy-start.5 = (f32[2,40,128]{2,1,0:T(8,128)S(1)}, f32[2,40,128]{2,1,0:T(8,128)}, u32[]{:S(2)}) copy-start(f32[2,40,128]{2,1,0:T(8,128)} %old.1) | copy-start | bytes 122884
  56.0 4.0 %collective-permute-start.4 = (f32[104,128]{1,0:T(8,128)S(1)}, f32[104,128]{1,0:T(8,128)S(1)}, u32[]{:S(2)}, u32[]{:S(2)}) collective-permute-start(f32[104,128]{1,0:T(8,128)S(1)} %get-tuple-element.13), channel_id=1, source_target_pairs={{0,32},{8,40},{16,48},{24,56},{32,0},{40,8},{48,16},{56,24},{64,96... | collective-permute-start | bytes 159752 | tf_op jit(solution)/shard_map/ppermute | solution.py:251
  60.0 4.6 %collective-permute-start.5 = (f32[104,128]{1,0:T(8,128)S(1)}, f32[104,128]{1,0:T(8,128)S(1)}, u32[]{:S(2)}, u32[]{:S(2)}) collective-permute-start(f32[104,128]{1,0:T(8,128)S(1)} %add.9), channel_id=1, source_target_pairs={{0,64},{8,72},{16,80},{24,88},{32,96},{40,104},{48,112},{56,120},{... | collective-permute-start | bytes 159752 | tf_op jit(solution)/shard_map/ppermute | solution.py:251
  64.6 7.5 %collective-permute-start.6 = (f32[104,128]{1,0:T(8,128)S(1)}, f32[104,128]{1,0:T(8,128)S(1)}, u32[]{:S(2)}, u32[]{:S(2)}) collective-permute-start(f32[104,128]{1,0:T(8,128)S(1)} %add.10), channel_id=1, source_target_pairs={{0,224},{8,232},{16,240},{24,248},{32,192},{40,200},{48,208},{56,2... | collective-permute-start | bytes 159752 | tf_op jit(solution)/shard_map/ppermute | solution.py:251
  72.1 4.6 %collective-permute-start.7 = (f32[104,128]{1,0:T(8,128)S(1)}, f32[104,128]{1,0:T(8,128)S(1)}, u32[]{:S(2)}, u32[]{:S(2)}) collective-permute-start(f32[104,128]{1,0:T(8,128)S(1)} %add.11.one), channel_id=1, source_target_pairs={{0,16},{8,24},{16,0},{24,8},{32,48},{40,56},{48,32},{56,40},{64,80... | collective-permute-start | bytes 159752 | tf_op jit(solution)/shard_map/ppermute | solution.py:251
  86.0 16.4 %collective-permute-start.8 = (f32[8,64,128]{2,1,0:T(8,128)S(1)}, f32[8,64,128]{2,1,0:T(8,128)S(1)}, u32[]{:S(2)}, u32[]{:S(2)}) collective-permute-start(f32[8,64,128]{2,1,0:T(8,128)S(1)} %all_to_all.16.mine), channel_id=1, source_target_pairs={{0,8},{8,0},{16,24},{24,16},{32,40},{40,32},{48,56},{56,48},{64,72... | collective-permute-start | bytes 786440 | tf_op jit(solution)/shard_map/ppermute | solution.py:251
  92.8 6.9 %collective-permute-start.3 = (f32[88,128]{1,0:T(8,128)S(1)}, f32[88,128]{1,0:T(8,128)S(1)}, u32[]{:S(2)}, u32[]{:S(2)}) collective-permute-start(f32[88,128]{1,0:T(8,128)S(1)} %get-tuple-element.11), channel_id=1, source_target_pairs={{8,16},{16,8},{24,32},{32,24},{40,48},{48,40},{56,64},{64,56},{72,... | collective-permute-start | bytes 135176 | tf_op jit(solution)/shard_map/ppermute | solution.py:259

commit v5 on v4

--- a/solution.py
+++ b/solution.py
@@ -12,7 +12,7 @@
 SPARE = 96
 PIECE = 104
 NEAR = 184
-ROWS = 264
+LAST = 152
 SMEM = pltpu.MemorySpace.SMEM
 VMEM = pltpu.MemorySpace.VMEM
 
@@ -51,8 +51,8 @@
 
 
 def window_kernel(
-    place, row_ref, col_ref, live_ref, stack, probe, amps, high, low,
-    keep, send, peak, field, grads, sums,
+    place, row_ref, col_ref, live_ref, stack, near, probe, amps, high, low,
+    keep, send, far_out, peak, field, grads, sums,
 ):
     row, col = row_ref[0], col_ref[0]
     live = live_ref[0].astype(jnp.float32)
@@ -60,9 +60,9 @@
     for member in range(8):
         lines = slice(member * 40, member * 40 + 40)
         for part in range(2):
-            for block, where in enumerate((1, 2 - 2 * odd, 2 * odd)):
-                first_line = block * 80 + part * 40
-                field[part, where, lines, :] = stack[member, first_line : first_line + 40, :]
+            field[part, 1, lines, :] = stack[member, part * 40 : part * 40 + 40, :]
+            field[part, 2 * odd, lines, :] = stack[member, 80 + part * 40 : 120 + part * 40, :]
+            field[part, 2 - 2 * odd, lines, :] = near[member, part * 40 : part * 40 + 40, :]
     lane = lax.broadcasted_iota(jnp.int32, (WIN, LANES), 1)
     back = lax.rem(LANES - col, LANES)
     ahead = lax.rem(col, LANES)
@@ -138,42 +138,36 @@
                 put = PIECE + part * 40
                 out[member, put : put + 40, :] = grads[part, block, lines, :]
         for part in range(2):
-            put = NEAR + part * 40
-            keep[member, put : put + 40, :] = grads[part, 2 * odd, lines, :]
-
-
-def pack_kernel(own, near, far, out):
-    for member in range(8):
-        out[member, 0:80, :] = own[...]
-        out[member, 80:160, :] = near[...]
-        out[member, 160:240, :] = far[...]
-
-
-def merge_kernel(keep, got, out):
-    out[:, :NEAR, :] = keep[:, :NEAR, :] + got[...]
-    out[:, NEAR:, :] = keep[:, NEAR:, :]
-
-
-def reduce_kernel(place, pieces, probe_sum, own_sum, far_sum):
-    def added(start, end):
-        total = pieces[0, start:end, :]
-        for member in range(1, 8):
-            total = total + pieces[member, start:end, :]
-        return total
-
-    probe_sum[...] = added(0, PIECE)
-    own_sum[...] = added(PIECE, NEAR)
-    far_sum[0:80, :] = added(NEAR, ROWS)
-    line = lax.broadcasted_iota(jnp.int32, (8, LANES), 0)
-    mine = jnp.zeros((8, LANES), jnp.float32)
-    for member in range(8):
-        spare = pieces[member, SPARE:PIECE, :]
-        place_row = jnp.where((place[0] & 1) == 1, spare[2:3], spare[1:2])
-        mine = jnp.where(line == member, place_row, mine)
-    far_sum[80:88, :] = mine
-
-
-def probe_kernel(place, one, two, probe, out):
+            put = member * 80 + part * 40
+            far_out[put : put + 40, :] = grads[part, 2 * odd, lines, :]
+    far_out[640:648, :] = where_mine
+
+
+def pack_kernel(own, far, out, sems):
+    copies = [
+        pltpu.make_async_copy(own, out.at[member, 0:80, :], sems.at[member]) for member in range(8)
+    ]
+    for copy in copies:
+        copy.start()
+    for member in range(8):
+        out[member, 80:160, :] = far[...]
+    for copy in copies:
+        copy.wait()
+
+
+def merge_kernel(keep, got, sums, gradient):
+    sums[...] = keep[:, :PIECE, :] + got[:, :PIECE, :]
+    gradient[...] = keep[:, PIECE:, :] + got[:, PIECE:, :]
+
+
+def reduce_kernel(pieces, out):
+    total = pieces[0]
+    for member in range(1, 8):
+        total = total + pieces[member]
+    out[...] = total
+
+
+def probe_kernel(place, one, two, probe, gradient, far, out):
     piece = (place[0] & 1) * 8 + place[1]
     summed = one[...] + two[...]
     mean = jnp.sum(summed[SPARE : SPARE + 1]) * (1.0 / (WIN * WIN))
@@ -186,6 +180,9 @@
             new = old - summed[lines : lines + 16] / bottom
             for member in range(8):
                 out[member, lines : lines + 16, :] = new
+    for member in range(8):
+        out[member, 64:144, :] = gradient[member] + far[member * 80 : member * 80 + 80, :]
+        out[member, 144:LAST, :] = far[640:648, :]
 
 
 def gather_kernel(place, mine, other, out):
@@ -201,13 +198,19 @@
                     ]
 
 
-def object_kernel(place, pieces, own_sum, far_sum, old, probe, peak, out, light, near_at, far_at, sems):
-    copies = [
-        pltpu.make_async_copy(pieces.at[:, SPARE:PIECE, :], near_at, sems.at[0]),
-        pltpu.make_async_copy(far_sum.at[80:88, :], far_at, sems.at[1]),
-    ]
-    for copy in copies:
-        copy.start()
+def shine(light, group, total, at, block):
+    row, col = at[0].astype(jnp.int32), at[1].astype(jnp.int32)
+    top = 64 + group * 40 - row
+    turn = lax.rem(col, LANES)
+    lane = lax.broadcasted_iota(jnp.int32, (40, LANES), 1)
+    before = pltpu.roll(light[block, pl.ds(top, 40), :], turn, 1)
+    after = pltpu.roll(light[block + 1, pl.ds(top, 40), :], turn, 1)
+    return total + at[2] * jnp.where(lane < col, before, after)
+
+
+def light_kernel(place, pieces, probe, out, light, at, sem):
+    copy = pltpu.make_async_copy(pieces.at[:, SPARE:PIECE, :], at, sem)
+    copy.start()
     odd = place[0] & 1
     blank = jnp.zeros((64, LANES), jnp.float32)
     for side in range(2):
@@ -218,29 +221,29 @@
         light[1 + side, 0:64, :] = blank
         light[1 + side, 320:384, :] = blank
         light[3 * side, :, :] = jnp.zeros((384, LANES), jnp.float32)
-    for copy in copies:
-        copy.wait()
-    lane = lax.broadcasted_iota(jnp.int32, (40, LANES), 1)
-
-    def shine(total, row, col, live, block):
-        row, col = row.astype(jnp.int32), col.astype(jnp.int32)
-        top = 64 + place[1] * 40 - row
-        turn = lax.rem(col, LANES)
-        before = pltpu.roll(light[block, pl.ds(top, 40), :], turn, 1)
-        after = pltpu.roll(light[block + 1, pl.ds(top, 40), :], turn, 1)
-        return total + live * jnp.where(lane < col, before, after)
-
+    copy.wait()
     total = jnp.zeros((40, LANES), jnp.float32)
     for member in range(8):
         for core in range(2):
-            block = 1 + core * (1 - odd) * -1 + (1 - core) * odd
-            at = [near_at[member, 1 + core, k] for k in range(3)]
-            total = shine(total, *at, block)
-        total = shine(total, *[far_at[member, k] for k in range(3)], 2 - 2 * odd)
+            block = 1 - core * (1 - odd) + (1 - core) * odd
+            total = shine(light, place[1], total, [at[member, 1 + core, k] for k in range(3)], block)
+    out[...] = total
+
+
+def object_kernel(place, pieces, old, near_light, light, peak, out, at, sem):
+    copy = pltpu.make_async_copy(pieces.at[:, 144:LAST, :], at, sem)
+    copy.start()
+    summed = pieces[0, 64:144, :]
+    for member in range(1, 8):
+        summed = summed + pieces[member, 64:144, :]
+    copy.wait()
+    total = near_light[...]
+    block = 2 - 2 * (place[0] & 1)
+    for member in range(8):
+        total = shine(light, place[1], total, [at[member, 0, k] for k in range(3)], block)
     bottom = total + 0.25 * (peak[0:1, :] + 1e-06)
     for part in range(2):
-        lines = slice(part * 40, part * 40 + 40)
-        out[part] = old[part] - (own_sum[lines, :] + far_sum[lines, :]) / bottom
+        out[part] = old[part] - summed[part * 40 : part * 40 + 40, :] / bottom
 
 
 def pair_up(axis, mask):
@@ -285,62 +288,68 @@
         return pltpu.VMEM(dims, jnp.float32)
 
     own = object_field.reshape(80, LANES)
-    near, far = swap(own, "tile", 1), swap_far(own)
-    rows = kernel_call(pack_kernel, buffer(8, 240, LANES), [vmem] * 3, vmem, 4)(
-        *map(on_chip, (own, near, far))
-    )
+    rows = kernel_call(
+        pack_kernel,
+        buffer(8, 160, LANES),
+        [pl.BlockSpec(memory_space=pltpu.MemorySpace.HBM), vmem],
+        vmem,
+        4,
+        scratch_shapes=[pltpu.SemaphoreType.DMA((8,))],
+    )(own, on_chip(swap_far(own)))
     stack = lax.all_to_all(rows, "group", 0, 0)
-    keep, send, peak = kernel_call(
+    near = swap(stack[:, :80], "tile", 1)
+    keep, send, far_out, peak = kernel_call(
         window_kernel,
-        (buffer(8, ROWS, LANES), buffer(8, NEAR, LANES), buffer(8, LANES)),
-        [smem] * 4 + [vmem] * 5,
-        (vmem,) * 3,
+        (buffer(8, NEAR, LANES), buffer(8, NEAR, LANES), buffer(648, LANES), buffer(8, LANES)),
+        [smem] * 4 + [vmem] * 6,
+        (vmem,) * 4,
         24,
         scratch_shapes=[buffer(2, 3, 320, LANES), buffer(2, 3, 320, LANES), buffer(3, WIN, WIN)],
     )(
-        place, row_start, column_start, live_slots, on_chip(stack), probe, on_chip(amplitudes),
-        high, low,
-    )
-
-    merged = kernel_call(merge_kernel, buffer(8, ROWS, LANES), [vmem] * 2, vmem, 4)(
-        keep, on_chip(swap(send, "tile", 1))
-    )
-    pieces = on_chip(lax.all_to_all(merged, "group", 0, 0))
-    total, own_sum, far_sum = kernel_call(
-        reduce_kernel,
-        (buffer(PIECE, LANES), buffer(80, LANES), buffer(88, LANES)),
-        [smem, vmem],
-        (vmem,) * 3,
+        place, row_start, column_start, live_slots, on_chip(stack), on_chip(near), probe,
+        on_chip(amplitudes), high, low,
+    )
+
+    sums, gradient = kernel_call(
+        merge_kernel, (buffer(8, PIECE, LANES), buffer(8, 80, LANES)), [vmem] * 2, (vmem,) * 2, 4
+    )(keep, on_chip(swap(send, "tile", 1)))
+    pieces = lax.all_to_all(sums, "group", 0, 0)
+    pieces, far_out = lax.optimization_barrier((pieces, far_out))
+    far_got = swap_far(far_out)
+    total = kernel_call(reduce_kernel, buffer(PIECE, LANES), [vmem], vmem, 4)(on_chip(pieces))
+    near_light, light = kernel_call(
+        light_kernel,
+        (buffer(40, LANES), buffer(4, 384, LANES)),
+        [smem] + [vmem] * 2,
+        (vmem,) * 2,
         4,
-    )(place, pieces)
-    far_got = swap_far(far_sum)
+        scratch_shapes=[pltpu.SMEM((8, 8, LANES), jnp.float32), pltpu.SemaphoreType.DMA],
+        cost_estimate=pl.CostEstimate(flops=500000, bytes_accessed=1500000, transcendentals=0),
+    )(place, on_chip(pieces), probe)
     for mask in (4, 8, 28):
         total = total + swap(total, "tile", mask)
-    piece = kernel_call(probe_kernel, buffer(8, 64, LANES), [smem] + [vmem] * 3, vmem, 4)(
-        place, on_chip(total), on_chip(swap(total, "tile", 2)), probe
-    )
+    total, near_light = lax.optimization_barrier((total, near_light))
+    outgoing = kernel_call(probe_kernel, buffer(8, LAST, LANES), [smem] + [vmem] * 5, vmem, 8)(
+        place, on_chip(total), on_chip(swap(total, "tile", 2)), probe, gradient, on_chip(far_got)
+    )
+
+    arrived = lax.all_to_all(outgoing, "group", 0, 0)
+    other = swap(arrived[:, :64], "tile", 1)
     new_object = kernel_call(
         object_kernel,
         jax.ShapeDtypeStruct((2, 40, LANES), jnp.float32),
-        [smem] + [vmem] * 6,
+        [smem] + [vmem] * 5,
         vmem,
-        8,
-        scratch_shapes=[
-            buffer(4, 384, LANES),
-            pltpu.SMEM((8, 8, LANES), jnp.float32),
-            pltpu.SMEM((8, LANES), jnp.float32),
-            pltpu.SemaphoreType.DMA((2,)),
-        ],
-    )(place, pieces, own_sum, on_chip(far_got), on_chip(object_field), probe, peak)
-
-    mine = lax.all_to_all(piece, "group", 0, 0)
+        4,
+        scratch_shapes=[pltpu.SMEM((8, 8, LANES), jnp.float32), pltpu.SemaphoreType.DMA],
+    )(place, on_chip(arrived), on_chip(object_field), on_chip(near_light), light, peak)
     new_probe = kernel_call(
         gather_kernel,
         jax.ShapeDtypeStruct((2, WIN, WIN), jnp.float32),
         [smem] + [vmem] * 2,
         vmem,
         4,
-    )(place, on_chip(mine), on_chip(swap(mine, "tile", 1)))
+    )(place, on_chip(arrived), on_chip(other))
     return new_object, new_probe
 
 

time: 104 us -> 95.7 us (0.920)
  waiting for transfers between devices: 28.7 us -> 8.97 us
  blocking collectives: 26.6 us -> 35 us
  starting transfers between devices: 34.1 us -> 35.5 us
    all_to_all x1 -> x0, waiting for transfers between devices: 13 us -> none  [local(): stack = lax.all_to_all(rows, 'group', 0, 0)]
    all_to_all x2 -> x3, blocking collectives: 26.6 us -> 35 us  [the longest x1 13.3 us: local(): stack = lax.all_to_all(rows, 'group', 0, 0)]
    ppermute x2, starting transfers between devices: 9.06 us -> 16.6 us  [swap_far(): return lax.ppermute(value, 'tile', pairs)]
    all_to_all x1 -> x0, starting transfers between devices: 5.2 us -> none  [local(): stack = lax.all_to_all(rows, 'group', 0, 0)]
    ppermute x2, waiting for transfers between devices: 5.61 us -> 1.88 us  [swap_far(): return lax.ppermute(value, 'tile', pairs)]
    ppermute x7, waiting for transfers between devices: 10.1 us -> 7.08 us  [swap(): return lax.ppermute(value, axis, pair_up(axis, mask))]
    pallas_call x5 -> x6, Pallas kernels: 6.71 us -> 7.47 us  [the longest x1 4.28 us: local(): kernel_call(window_kernel, (buffer(8, NEAR, LANES), buffer(8, NEAR, LANES...]
  transfers between devices with their start and end apart: 10 -> 9, of which waited for: 8 -> 5; matrix products, arithmetic and copies ran while one was open for 0% -> 0% of each run, Pallas kernels for 3% -> 5%
where the time goes in v5:
time: 95.7 us; the launch traced here: 94.4 us
  starting transfers between devices  35.5 us (37%)
  blocking collectives  35 us (37%)
  Pallas kernels  11.3 us (12%)
  waiting for transfers between devices  8.97 us (9%)
  between operations  2.76 us (3%)
    ppermute x7, starting transfers between devices, swap(): return lax.ppermute(value, axis, pair_up(axis, mask))  18.9 us
    ppermute x2, starting transfers between devices, swap_far(): return lax.ppermute(value, 'tile', pairs)  16.6 us
    all_to_all x1, blocking collectives, local(): stack = lax.all_to_all(rows, 'group', 0, 0)  13.3 us
    all_to_all x1, blocking collectives, local(): pieces = lax.all_to_all(sums, 'group', 0, 0)  11.1 us
    all_to_all x1, blocking collectives, local(): arrived = lax.all_to_all(outgoing, 'group', 0, 0)  10.6 us
    ppermute x7, waiting for transfers between devices, swap(): return lax.ppermute(value, axis, pair_up(axis, mask))  7.08 us
    pallas_call x1, Pallas kernels, local(): kernel_call(window_kernel, (buffer(8, NEAR, LANES), buffer(8, NEAR, LANES...  4.28 us
    pallas_call x1, Pallas kernels, local(): kernel_call(object_kernel, jax.ShapeDtypeStruct((2, 40, LANES), jnp.float...  2.41 us
  transfers between devices with their start and end apart: 9, of which 5 were waited for; matrix products, arithmetic and copies ran while one was open for 0% of the time, Pallas kernels for 5%

profile of v5, /device:TPU:1, one launch (start us, length us, event | category | flops | bytes accessed | tf_op | source)
XLA Modules:
  0.0 94.4 jit_solution(11210969236561918802)
XLA Ops:
  0.6 6.0 %collective-permute-start = (f32[80,128]{1,0:T(8,128)}, f32[80,128]{1,0:T(8,128)S(1)}, u32[]{:S(2)}, u32[]{:S(2)}) collective-permute-start(f32[80,128]{1,0:T(8,128)} %bitcast.3), channel_id=1, source_target_pairs={{8,16},{16,8},{24,32},{32,24},{40,48},{48,40},{56,64},{64,56},{72,... | collective-permute-start | bytes 122888 | tf_op jit(solution)/shard_map/ppermute | solution.py:262
  6.7 1.9 %collective-permute-done.far = f32[80,128]{1,0:T(8,128)S(1)} collective-permute-done((f32[80,128]{1,0:T(8,128)}, f32[80,128]{1,0:T(8,128)S(1)}, u32[]{:S(2)}, u32[]{:S(2)}) %collective-permute-start) | collective-permute-done | bytes 40992 | tf_op jit(solution)/shard_map/ppermute | solution.py:262
  8.6 0.0 copy-start.4
  8.6 0.8 copy-done.4
  9.3 0.5 pack.1
  9.8 0.0 copy-start.1
  9.9 0.0 copy-start.2
  9.9 0.0 copy-start.3
  9.9 13.3 %all_to_all.15.stack = f32[8,160,128]{2,1,0:T(8,128)S(1)} all-to-all(f32[8,160,128]{2,1,0:T(8,128)S(1)} %pack.1), channel_id=1, replica_groups=mesh['tile'=32,'group'=8] {'group'}, dimensions={0} | all-to-all | bytes 1310720 | tf_op jit(solution)/shard_map/all_to_all | solution.py:299
  23.2 0.0 copy-start
  23.2 0.1 collective-permute-start.1
  25.3 0.1 pad_add_fusion.place
  25.4 0.0 collective-permute-done.1.near
  25.4 0.0 copy-done.1
  25.4 0.0 copy-done.2
  25.4 0.0 copy-done.3
  25.4 0.0 copy-done
  25.4 4.3 %window.1 = (f32[8,184,128]{2,1,0:T(8,128)S(1)}, f32[8,184,128]{2,1,0:T(8,128)S(1)}, f32[648,128]{1,0:T(8,128)S(1)}, f32[8,128]{1,0:T(8,128)S(1)}) custom-call(s32[2]{0:T(128)S(1)} %pad_add_fusion.place, s32[1]{0:T(128)S(6)} %copy.10.row_ref, s32[1]{0:T(128)S(6)} %copy.11.col_ref, s32[1]{0:T(128)S(6)} %copy.12.live_ref, ...), custom_call_target="tpu_custom_call" | custom-call | tf_op jit(solution)/shard_map/window/pallas_call | solution.py:301
  29.7 0.5 collective-permute-start.2
  30.3 1.9 %collective-permute-done.2.got = f32[8,184,128]{2,1,0:T(8,128)S(1)} collective-permute-done((f32[8,184,128]{2,1,0:T(8,128)S(1)}, f32[8,184,128]{2,1,0:T(8,128)S(1)}, u32[]{:S(2)}, u32[]{:S(2)}) %collective-permute-start.2) | collective-permute-done | bytes 753696 | tf_op jit(solution)/shard_map/ppermute | solution.py:254
  32.1 0.1 merge.1
  32.2 11.1 %all_to_all.16.pieces = f32[8,104,128]{2,1,0:T(8,128)S(1)} all-to-all(f32[8,104,128]{2,1,0:T(8,128)S(1)} %get-tuple-element.16), channel_id=1, replica_groups=mesh['tile'=32,'group'=8] {'group'}, dimensions={0} | all-to-all | bytes 851968 | tf_op jit(solution)/shard_map/all_to_all | solution.py:316
  43.3 10.6 %collective-permute-start.7 = (f32[648,128]{1,0:T(8,128)S(1)}, f32[648,128]{1,0:T(8,128)S(1)}, u32[]{:S(2)}, u32[]{:S(2)}) collective-permute-start(f32[648,128]{1,0:T(8,128)S(1)} %get-tuple-element.22), channel_id=1, source_target_pairs={{8,16},{16,8},{24,32},{32,24},{40,48},{48,40},{56,64},{64,56},{72,... | collective-permute-start | bytes 995336 | tf_op jit(solution)/shard_map/ppermute | solution.py:262
  53.9 1.7 %collective-permute-start.3 = (f32[104,128]{1,0:T(8,128)S(1)}, f32[104,128]{1,0:T(8,128)S(1)}, u32[]{:S(2)}, u32[]{:S(2)}) collective-permute-start(f32[104,128]{1,0:T(8,128)S(1)} %reduce.1), channel_id=1, source_target_pairs={{0,32},{8,40},{16,48},{24,56},{32,0},{40,8},{48,16},{56,24},{64,96... | collective-permute-start | bytes 159752 | tf_op jit(solution)/shard_map/ppermute | solution.py:254
  55.6 2.1 %collective-permute-done.3 = f32[104,128]{1,0:T(8,128)S(1)} collective-permute-done((f32[104,128]{1,0:T(8,128)S(1)}, f32[104,128]{1,0:T(8,128)S(1)}, u32[]{:S(2)}, u32[]{:S(2)}) %collective-permute-start.3) | collective-permute-done | bytes 53280 | tf_op jit(solution)/shard_map/ppermute | solution.py:254
  57.7 3.3 %collective-permute-start.4 = (f32[104,128]{1,0:T(8,128)S(1)}, f32[104,128]{1,0:T(8,128)S(1)}, u32[]{:S(2)}, u32[]{:S(2)}) collective-permute-start(f32[104,128]{1,0:T(8,128)S(1)} %add.9), channel_id=1, source_target_pairs={{0,64},{8,72},{16,80},{24,88},{32,96},{40,104},{48,112},{56,120},{... | collective-permute-start | bytes 159752 | tf_op jit(solution)/shard_map/ppermute | solution.py:254
  61.1 1.5 %collective-permute-done.4 = f32[104,128]{1,0:T(8,128)S(1)} collective-permute-done((f32[104,128]{1,0:T(8,128)S(1)}, f32[104,128]{1,0:T(8,128)S(1)}, u32[]{:S(2)}, u32[]{:S(2)}) %collective-permute-start.4) | collective-permute-done | bytes 53280 | tf_op jit(solution)/shard_map/ppermute | solution.py:254
  62.6 3.6 %collective-permute-start.5 = (f32[104,128]{1,0:T(8,128)S(1)}, f32[104,128]{1,0:T(8,128)S(1)}, u32[]{:S(2)}, u32[]{:S(2)}) collective-permute-start(f32[104,128]{1,0:T(8,128)S(1)} %add.10), channel_id=1, source_target_pairs={{0,224},{8,232},{16,240},{24,248},{32,192},{40,200},{48,208},{56,2... | collective-permute-start | bytes 159752 | tf_op jit(solution)/shard_map/ppermute | solution.py:254
  66.2 1.9 %light.1 = (f32[40,128]{1,0:T(8,128)S(1)}, f32[4,384,128]{2,1,0:T(8,128)S(1)}) custom-call(s32[2]{0:T(128)S(1)} %pad_add_fusion.place, f32[8,104,128]{2,1,0:T(8,128)S(1)} %all_to_all.16.pieces, f32[2,256,256]{2,1,0:T(8,128)S(1)} %copy-done), custom_call_target="tpu_custom_call" | custom-call | flops 500000 | bytes 1500000 | tf_op jit(solution)/shard_map/light/pallas_call | solution.py:320
  68.1 0.0 collective-permute-done.5
  68.1 4.7 %collective-permute-start.6 = (f32[104,128]{1,0:T(8,128)S(1)}, f32[104,128]{1,0:T(8,128)S(1)}, u32[]{:S(2)}, u32[]{:S(2)}) collective-permute-start(f32[104,128]{1,0:T(8,128)S(1)} %add.11.one), channel_id=1, source_target_pairs={{0,16},{8,24},{16,0},{24,8},{32,48},{40,56},{48,32},{56,40},{64,80... | collective-permute-start | bytes 159752 | tf_op jit(solution)/shard_map/ppermute | solution.py:254
  72.8 1.6 %collective-permute-done.6.two = f32[104,128]{1,0:T(8,128)S(1)} collective-permute-done((f32[104,128]{1,0:T(8,128)S(1)}, f32[104,128]{1,0:T(8,128)S(1)}, u32[]{:S(2)}, u32[]{:S(2)}) %collective-permute-start.6) | collective-permute-done | bytes 53280 | tf_op jit(solution)/shard_map/ppermute | solution.py:254
  74.4 0.0 collective-permute-done.7.far
  74.4 0.7 probe.6
  75.0 10.6 %all_to_all.17.pieces.mine = f32[8,152,128]{2,1,0:T(8,128)S(1)} all-to-all(f32[8,152,128]{2,1,0:T(8,128)S(1)} %probe.6), channel_id=1, replica_groups=mesh['tile'=32,'group'=8] {'group'}, dimensions={0} | all-to-all | bytes 1245184 | tf_op jit(solution)/shard_map/all_to_all | solution.py:336
  85.6 0.0 copy-start.5
  85.7 5.0 %collective-permute-start.8 = (f32[8,64,128]{2,1,0:T(8,128)S(1)}, f32[8,64,128]{2,1,0:T(8,128)S(1)}, u32[]{:S(2)}, u32[]{:S(2)}) collective-permute-start(f32[8,64,128]{2,1,0:T(8,128)S(1)} %slice.9), channel_id=1, source_target_pairs={{0,8},{8,0},{16,24},{24,16},{32,40},{40,32},{48,56},{56,48},{64,72... | collective-permute-start | bytes 786440 | tf_op jit(solution)/shard_map/ppermute | solution.py:254
  90.6 0.0 copy-done.5
  90.6 2.4 %object.1 = f32[2,40,128]{2,1,0:T(8,128)} custom-call(s32[2]{0:T(128)S(1)} %pad_add_fusion.place, f32[8,152,128]{2,1,0:T(8,128)S(1)} %all_to_all.17.pieces.mine, f32[2,40,128]{2,1,0:T(8,128)S(1)} %copy-done.5, f32[40,128]{1,0:T(8,128)S(1)} %get-tuple-element.23.near_light, f32[4,384,128]{2,1,0:T(8,128)S(1)} %get-tuple-element.24.light, ...), custom_call_target="tpu_custom_call" | custom-call | tf_op jit(solution)/shard_map/object/pallas_call | solution.py:338
  93.1 0.0 collective-permute-done.8.other
  93.1 1.4 %gather.1 = f32[2,256,256]{2,1,0:T(8,128)} custom-call(s32[2]{0:T(128)S(1)} %pad_add_fusion.place, f32[8,152,128]{2,1,0:T(8,128)S(1)} %all_to_all.17.pieces.mine, f32[8,64,128]{2,1,0:T(8,128)S(1)} %collective-permute-done.8.other), custom_call_target="tpu_custom_call" | custom-call | tf_op jit(solution)/shard_map/gather/pallas_call | solution.py:346
  (6 shorter events, 0.1 us)
Async XLA Ops:
  0.6 7.9 %collective-permute-start = (f32[80,128]{1,0:T(8,128)}, f32[80,128]{1,0:T(8,128)S(1)}, u32[]{:S(2)}, u32[]{:S(2)}) collective-permute-start(f32[80,128]{1,0:T(8,128)} %bitcast.3), channel_id=1, source_target_pairs={{8,16},{16,8},{24,32},{32,24},{40,48},{48,40},{56,64},{64,56},{72,... | collective-permute-start | bytes 122888 | tf_op jit(solution)/shard_map/ppermute | solution.py:262
  8.6 0.8 copy-start.4
  9.8 15.6 %copy-start.1 = (f32[1,256,256]{2,1,0:T(8,128)S(1)}, f32[1,256,256]{2,1,0:T(8,128)}, u32[]{:S(2)}) copy-start(f32[1,256,256]{2,1,0:T(8,128)} %amps.1) | copy-start | bytes 786436
  9.9 15.6 %copy-start.2 = (bf16[512,256]{1,0:T(8,128)(2,1)S(1)}, bf16[512,256]{1,0:T(8,128)(2,1)}, u32[]{:S(2)}) copy-start(bf16[512,256]{1,0:T(8,128)(2,1)} %constant.14.clone.low) | copy-start | bytes 786436
  9.9 15.5 %copy-start.3 = (bf16[512,256]{1,0:T(8,128)(2,1)S(1)}, bf16[512,256]{1,0:T(8,128)(2,1)}, u32[]{:S(2)}) copy-start(bf16[512,256]{1,0:T(8,128)(2,1)} %constant.13.clone.high) | copy-start | bytes 786436
  23.2 2.2 %copy-start = (f32[2,256,256]{2,1,0:T(8,128)S(1)}, f32[2,256,256]{2,1,0:T(8,128)}, u32[]{:S(2)}) copy-start(f32[2,256,256]{2,1,0:T(8,128)} %probe.7) | copy-start | bytes 1572868
  23.2 2.2 %collective-permute-start.1 = (f32[8,80,128]{2,1,0:T(8,128)S(1)}, f32[8,80,128]{2,1,0:T(8,128)S(1)}, u32[]{:S(2)}, u32[]{:S(2)}) collective-permute-start(f32[8,80,128]{2,1,0:T(8,128)S(1)} %slice.8), channel_id=1, source_target_pairs={{0,8},{8,0},{16,24},{24,16},{32,40},{40,32},{48,56},{56,48},{64,72... | collective-permute-start | bytes 983048 | tf_op jit(solution)/shard_map/ppermute | solution.py:254
  29.7 2.4 %collective-permute-start.2 = (f32[8,184,128]{2,1,0:T(8,128)S(1)}, f32[8,184,128]{2,1,0:T(8,128)S(1)}, u32[]{:S(2)}, u32[]{:S(2)}) collective-permute-start(f32[8,184,128]{2,1,0:T(8,128)S(1)} %get-tuple-element.15), channel_id=1, source_target_pairs={{0,8},{8,0},{16,24},{24,16},{32,40},{40,32},{48,56},{56,48},{64,72... | collective-permute-start | bytes 2261000 | tf_op jit(solution)/shard_map/ppermute | solution.py:254
  43.3 31.1 %collective-permute-start.7 = (f32[648,128]{1,0:T(8,128)S(1)}, f32[648,128]{1,0:T(8,128)S(1)}, u32[]{:S(2)}, u32[]{:S(2)}) collective-permute-start(f32[648,128]{1,0:T(8,128)S(1)} %get-tuple-element.22), channel_id=1, source_target_pairs={{8,16},{16,8},{24,32},{32,24},{40,48},{48,40},{56,64},{64,56},{72,... | collective-permute-start | bytes 995336 | tf_op jit(solution)/shard_map/ppermute | solution.py:262
  53.9 3.8 %collective-permute-start.3 = (f32[104,128]{1,0:T(8,128)S(1)}, f32[104,128]{1,0:T(8,128)S(1)}, u32[]{:S(2)}, u32[]{:S(2)}) collective-permute-start(f32[104,128]{1,0:T(8,128)S(1)} %reduce.1), channel_id=1, source_target_pairs={{0,32},{8,40},{16,48},{24,56},{32,0},{40,8},{48,16},{56,24},{64,96... | collective-permute-start | bytes 159752 | tf_op jit(solution)/shard_map/ppermute | solution.py:254
  57.7 4.8 %collective-permute-start.4 = (f32[104,128]{1,0:T(8,128)S(1)}, f32[104,128]{1,0:T(8,128)S(1)}, u32[]{:S(2)}, u32[]{:S(2)}) collective-permute-start(f32[104,128]{1,0:T(8,128)S(1)} %add.9), channel_id=1, source_target_pairs={{0,64},{8,72},{16,80},{24,88},{32,96},{40,104},{48,112},{56,120},{... | collective-permute-start | bytes 159752 | tf_op jit(solution)/shard_map/ppermute | solution.py:254
  62.6 5.5 %collective-permute-start.5 = (f32[104,128]{1,0:T(8,128)S(1)}, f32[104,128]{1,0:T(8,128)S(1)}, u32[]{:S(2)}, u32[]{:S(2)}) collective-permute-start(f32[104,128]{1,0:T(8,128)S(1)} %add.10), channel_id=1, source_target_pairs={{0,224},{8,232},{16,240},{24,248},{32,192},{40,200},{48,208},{56,2... | collective-permute-start | bytes 159752 | tf_op jit(solution)/shard_map/ppermute | solution.py:254
  68.1 6.2 %collective-permute-start.6 = (f32[104,128]{1,0:T(8,128)S(1)}, f32[104,128]{1,0:T(8,128)S(1)}, u32[]{:S(2)}, u32[]{:S(2)}) collective-permute-start(f32[104,128]{1,0:T(8,128)S(1)} %add.11.one), channel_id=1, source_target_pairs={{0,16},{8,24},{16,0},{24,8},{32,48},{40,56},{48,32},{56,40},{64,80... | collective-permute-start | bytes 159752 | tf_op jit(solution)/shard_map/ppermute | solution.py:254
  85.6 5.0 %copy-start.5 = (f32[2,40,128]{2,1,0:T(8,128)S(1)}, f32[2,40,128]{2,1,0:T(8,128)}, u32[]{:S(2)}) copy-start(f32[2,40,128]{2,1,0:T(8,128)} %old.1) | copy-start | bytes 122884
  85.7 7.4 %collective-permute-start.8 = (f32[8,64,128]{2,1,0:T(8,128)S(1)}, f32[8,64,128]{2,1,0:T(8,128)S(1)}, u32[]{:S(2)}, u32[]{:S(2)}) collective-permute-start(f32[8,64,128]{2,1,0:T(8,128)S(1)} %slice.9), channel_id=1, source_target_pairs={{0,8},{8,0},{16,24},{24,16},{32,40},{40,32},{48,56},{56,48},{64,72... | collective-permute-start | bytes 786440 | tf_op jit(solution)/shard_map/ppermute | solution.py:254

commit v6 on v5

v6 whole, which is shorter than its diff:
```python
import jax
import jax.numpy as jnp
import ml_dtypes
import numpy as np
from jax import lax
from jax.experimental import pallas as pl
from jax.experimental.pallas import tpu as pltpu
from jax.sharding import PartitionSpec as P

WIN = 256
LANES = 128
TILES = 32
SPARE = 48
PIECE = 56
LINES = 136
SMEM = pltpu.MemorySpace.SMEM
VMEM = pltpu.MemorySpace.VMEM


def split_tables():
    counter = np.arange(WIN)
    angles = 2.0 * np.pi / WIN * (counter[:, None] * counter[None, :] % WIN)
    cos, sin = np.cos(angles) / np.sqrt(WIN), np.sin(angles) / np.sqrt(WIN)
    both = np.concatenate([cos, sin], axis=0)
    high = both.astype(ml_dtypes.bfloat16)
    low = (both - high.astype(np.float64)).astype(ml_dtypes.bfloat16)
    return high, low


def halves(value):
    high = value.astype(jnp.bfloat16)
    low = (value - high.astype(jnp.float32)).astype(jnp.bfloat16)
    return high, low


def product(left, right):
    def dot(a, b):
        return jnp.dot(a, b, preferred_element_type=jnp.float32)

    return dot(left[0], right[0]) + dot(left[0], right[1]) + dot(left[1], right[0])


def transform(real, imag, tall, wide, sign):
    cols = product(tall, halves(jnp.concatenate([real, imag], axis=1)))
    left_real = cols[:WIN, :WIN] - sign * cols[WIN:, WIN:]
    left_imag = cols[:WIN, WIN:] + sign * cols[WIN:, :WIN]
    rows = product(halves(jnp.concatenate([left_real, left_imag], axis=0)), wide)
    right_real = rows[:WIN, :WIN] - sign * rows[WIN:, WIN:]
    right_imag = rows[WIN:, :WIN] + sign * rows[:WIN, WIN:]
    return right_real, right_imag


def window_kernel(
    place, row_ref, col_ref, live_ref, stack, near, probe, amps, high, low,
    keep, send, peak, field, grads, sums,
):
    row, col = row_ref[0], col_ref[0]
    live = live_ref[0].astype(jnp.float32)
    odd, half = place[0] & 1, half_of(place[0])
    inside = far_exists(place[0])
    for member in range(8):
        lines = slice(member * 40, member * 40 + 40)
        for part in range(2):
            rows = slice(part * 40, part * 40 + 40)
            field[part, 1, lines, :] = stack[8 - 8 * odd + member, rows, :]
            field[part, 2 * odd, lines, :] = jnp.where(inside, stack[8 * odd + member, rows, :], 0.0)
            field[part, 2 - 2 * odd, lines, :] = near[8 * odd + member, rows, :]
    lane = lax.broadcasted_iota(jnp.int32, (WIN, LANES), 1)
    back = lax.rem(LANES - col, LANES)
    ahead = lax.rem(col, LANES)
    first = lane < LANES - col

    def cut(part):
        turned = [
            pltpu.roll(field[part, block, pl.ds(row, WIN), :], back, 1) for block in range(3)
        ]
        return jnp.concatenate(
            [jnp.where(first, turned[0], turned[1]), jnp.where(first, turned[1], turned[2])], axis=1
        )

    sample_real, sample_imag = cut(0), cut(1)
    probe_real, probe_imag = probe[0], probe[1]
    exit_real = probe_real * sample_real - probe_imag * sample_imag
    exit_imag = probe_real * sample_imag + probe_imag * sample_real
    tall = (high[...], low[...])
    wide = tuple(jnp.concatenate([table[:WIN], table[WIN:]], axis=1) for table in tall)
    far_real, far_imag = transform(exit_real, exit_imag, tall, wide, -1.0)
    power = far_real * far_real + far_imag * far_imag
    factor = 1.0 - amps[0] * lax.rsqrt(jnp.maximum(power, 0.0625))
    miss_real, miss_imag = transform(far_real * factor, far_imag * factor, tall, wide, 1.0)
    miss_real = miss_real * live
    miss_imag = miss_imag * live
    light = probe_real * probe_real + probe_imag * probe_imag
    peak[...] = jnp.full((8, LANES), jnp.max(light), jnp.float32)

    terms = (
        probe_real * miss_real + probe_imag * miss_imag,
        probe_real * miss_imag - probe_imag * miss_real,
    )
    wrapped = lane < col
    zero = jnp.zeros((WIN, LANES), jnp.float32)
    grads[...] = jnp.zeros_like(grads)
    for part in range(2):
        start = pltpu.roll(terms[part][:, :LANES], ahead, 1)
        end = pltpu.roll(terms[part][:, LANES:], ahead, 1)
        grads[part, 0, pl.ds(row, WIN), :] = jnp.where(wrapped, zero, start)
        grads[part, 1, pl.ds(row, WIN), :] = jnp.where(wrapped, start, end)
        grads[part, 2, pl.ds(row, WIN), :] = jnp.where(wrapped, end, zero)
    window_light = live * (sample_real * sample_real + sample_imag * sample_imag)
    sums[0] = sample_real * miss_real + sample_imag * miss_imag
    sums[1] = sample_real * miss_imag - sample_imag * miss_real
    sums[2] = window_light
    total = jnp.zeros((8, LANES), jnp.float32)
    for line in range(0, WIN, 8):
        total = total + window_light[line : line + 8, :LANES] + window_light[line : line + 8, LANES:]
    spare_line = lax.broadcasted_iota(jnp.int32, (8, LANES), 0)
    spare_lane = lax.broadcasted_iota(jnp.int32, (8, LANES), 1)
    where_mine = jnp.where(
        spare_lane == 0,
        row.astype(jnp.float32),
        jnp.where(spare_lane == 1, col.astype(jnp.float32), jnp.where(spare_lane == 2, live, 0.0)),
    )
    spare = jnp.where(
        spare_line == 2,
        jnp.broadcast_to(jnp.sum(total, axis=0, keepdims=True), (8, LANES)),
        jnp.where(spare_line == odd, where_mine, 0.0),
    )
    for member in range(16):
        for kept, side_half in ((True, half), (False, 1 - half)):
            top = pl.multiple_of(side_half * 128 + member * 8, 8)
            for part in range(3):
                for side in range(2):
                    put = part * 16 + side * 8
                    value = sums[part, pl.ds(top, 8), side * LANES : (side + 1) * LANES]
                    if kept:
                        keep[member, put : put + 8, :] = value
                    else:
                        send[member * PIECE + put : member * PIECE + put + 8, :] = value
            if kept:
                keep[member, SPARE:PIECE, :] = spare
            else:
                send[member * PIECE + SPARE : member * PIECE + PIECE, :] = spare
    for member in range(8):
        lines = slice(member * 40, member * 40 + 40)
        for part in range(2):
            put = PIECE + part * 40
            keep[8 - 8 * odd + member, put : put + 40, :] = grads[part, 1, lines, :]
            keep[8 * odd + member, put : put + 40, :] = jnp.where(
                inside, grads[part, 2 * odd, lines, :], 0.0
            )
            put = 16 * PIECE + member * 80 + part * 40
            send[put : put + 40, :] = grads[part, 2 - 2 * odd, lines, :]


def merge_kernel(place, keep, got, out):
    mine = 8 - 8 * (place[0] & 1)
    for member in range(16):
        out[member, :PIECE, :] = keep[member, :PIECE, :] + got[member * PIECE : (member + 1) * PIECE, :]
    for member in range(8):
        put = 16 * PIECE + member * 80
        out[mine + member, PIECE:, :] = keep[mine + member, PIECE:, :] + got[put : put + 80, :]
        out[8 - mine + member, PIECE:, :] = keep[8 - mine + member, PIECE:, :]


def reduce_kernel(pieces, probe_sum, gradient):
    total = pieces[0]
    for member in range(1, 16):
        total = total + pieces[member]
    probe_sum[...] = total[:PIECE]
    gradient[...] = total[PIECE:]


def probe_kernel(place, one, two, probe, out):
    odd = place[0] & 1
    top = pl.multiple_of(half_of(place[0]) * 128 + (8 - 8 * odd + place[1]) * 8, 8)
    summed = one[...] + two[...]
    mean = jnp.sum(summed[SPARE + 2 : SPARE + 3]) * (1.0 / (WIN * WIN))
    for side in range(2):
        bottom = summed[32 + side * 8 : 40 + side * 8] + 0.25 * mean + 1e-05
        for part in range(2):
            lines = part * 16 + side * 8
            old = probe[part, pl.ds(top, 8), side * LANES : (side + 1) * LANES]
            new = old - summed[lines : lines + 8] / bottom
            for member in range(16):
                out[member, lines : lines + 8, :] = new


def gather_kernel(place, mine, other, out):
    half = half_of(place[0])
    for source, which in ((mine, half), (other, 1 - half)):
        for member in range(16):
            top = pl.multiple_of(which * 128 + member * 8, 8)
            for part in range(2):
                for side in range(2):
                    lines = part * 16 + side * 8
                    out[part, pl.ds(top, 8), side * LANES : (side + 1) * LANES] = source[
                        member, lines : lines + 8, :
                    ]


def shine(light, group, total, at, block):
    row, col = at[0].astype(jnp.int32), at[1].astype(jnp.int32)
    top = 64 + group * 40 - row
    turn = lax.rem(col, LANES)
    lane = lax.broadcasted_iota(jnp.int32, (40, LANES), 1)
    before = pltpu.roll(light[block, pl.ds(top, 40), :], turn, 1)
    after = pltpu.roll(light[block + 1, pl.ds(top, 40), :], turn, 1)
    return total + at[2] * jnp.where(lane < col, before, after)


def object_kernel(place, pieces, gradient, old, probe, peak, out, light, at, sem):
    copy = pltpu.make_async_copy(pieces.at[:, SPARE:PIECE, :], at, sem)
    copy.start()
    odd = place[0] & 1
    blank = jnp.zeros((64, LANES), jnp.float32)
    for side in range(2):
        cols = slice(side * LANES, (side + 1) * LANES)
        light[1 + side, 64:320, :] = probe[0, :, cols] * probe[0, :, cols] + (
            probe[1, :, cols] * probe[1, :, cols]
        )
        light[1 + side, 0:64, :] = blank
        light[1 + side, 320:384, :] = blank
        light[3 * side, :, :] = jnp.zeros((384, LANES), jnp.float32)
    copy.wait()
    mine = 8 - 8 * odd
    total = jnp.zeros((40, LANES), jnp.float32)
    outside = jnp.zeros((40, LANES), jnp.float32)
    for member in range(8):
        for core in range(2):
            block = 1 - core * (1 - odd) + (1 - core) * odd
            total = shine(light, place[1], total, [at[mine + member, core, k] for k in range(3)], block)
        outside = shine(
            light, place[1], outside, [at[8 - mine + member, 1 - odd, k] for k in range(3)], 2 - 2 * odd
        )
    total = total + jnp.where(far_exists(place[0]), outside, 0.0)
    bottom = total + 0.25 * (peak[0:1, :] + 1e-06)
    for part in range(2):
        out[part] = old[part] - gradient[part * 40 : part * 40 + 40, :] / bottom


def half_of(tile):
    return (tile ^ (tile >> 1)) & 1


def far_exists(tile):
    return jnp.logical_and(tile > 0, tile < TILES - 1)


def swap_cores(value):
    return lax.ppermute(value, "tile", [(i, i ^ 1) for i in range(TILES)])


def swap_z(value, mask):
    pairs = []
    for tile in range(TILES):
        layer, rest = divmod(tile, 4)
        ahead = 1 if rest == 0 else 0
        other = (((layer - ahead) % (TILES // 4)) ^ mask) + ahead
        pairs.append((tile, other % (TILES // 4) * 4 + rest))
    return lax.ppermute(value, "tile", pairs)


def exchange(value):
    groups = []
    for first in range(1, TILES, 2):
        second = (first + 1) % TILES
        groups.append([first * 8 + i for i in range(8)] + [second * 8 + i for i in range(8)])
    return lax.all_to_all(value, ("tile", "group"), 0, 0, axis_index_groups=groups)


def on_chip(value):
    return pltpu.with_memory_space_constraint(value, pltpu.VMEM)


def kernel_call(body, out_shape, in_specs, out_specs, megabytes, **kwargs):
    return pl.pallas_call(
        body,
        out_shape=out_shape,
        in_specs=in_specs,
        out_specs=out_specs,
        compiler_params=pltpu.CompilerParams(vmem_limit_bytes=megabytes << 20),
        name=body.__name__.removesuffix("_kernel"),
        **kwargs,
    )


def local(object_field, probe_field, amplitudes, row_start, column_start, live_slots):
    smem, vmem = pl.BlockSpec(memory_space=SMEM), pl.BlockSpec(memory_space=VMEM)
    place = jnp.stack([lax.axis_index("tile"), lax.axis_index("group")]).astype(jnp.int32)
    high, low = (on_chip(jnp.asarray(table)) for table in split_tables())
    probe = on_chip(probe_field)

    def buffer(*dims):
        return pltpu.VMEM(dims, jnp.float32)

    own = object_field.reshape(80, LANES)
    stack = exchange(jnp.broadcast_to(own, (16, 80, LANES)))
    keep, send, peak = kernel_call(
        window_kernel,
        (buffer(16, LINES, LANES), buffer(16 * PIECE + 640, LANES), buffer(8, LANES)),
        [smem] * 4 + [vmem] * 6,
        (vmem,) * 3,
        24,
        scratch_shapes=[buffer(2, 3, 320, LANES), buffer(2, 3, 320, LANES), buffer(3, WIN, WIN)],
    )(
        place, row_start, column_start, live_slots, on_chip(stack), on_chip(swap_cores(stack)),
        probe, on_chip(amplitudes), high, low,
    )

    merged = kernel_call(merge_kernel, buffer(16, LINES, LANES), [smem] + [vmem] * 2, vmem, 4)(
        place, keep, on_chip(swap_cores(send))
    )
    pieces = on_chip(exchange(merged))
    total, gradient = kernel_call(
        reduce_kernel, (buffer(PIECE, LANES), buffer(80, LANES)), [vmem], (vmem,) * 2, 4
    )(pieces)
    new_object = kernel_call(
        object_kernel,
        jax.ShapeDtypeStruct((2, 40, LANES), jnp.float32),
        [smem] + [vmem] * 5,
        vmem,
        8,
        scratch_shapes=[
            buffer(4, 384, LANES),
            pltpu.SMEM((16, 8, LANES), jnp.float32),
            pltpu.SemaphoreType.DMA,
        ],
        cost_estimate=pl.CostEstimate(flops=700000, bytes_accessed=2000000, transcendentals=0),
    )(place, pieces, gradient, on_chip(object_field), probe, peak)
    for mask in (1, 2):
        total = total + swap_z(total, mask)
    total, new_object = lax.optimization_barrier((total, new_object))
    piece = kernel_call(probe_kernel, buffer(16, 32, LANES), [smem] + [vmem] * 3, vmem, 4)(
        place, on_chip(total), on_chip(swap_z(total, 6)), probe
    )

    mine = exchange(piece)
    new_probe = kernel_call(
        gather_kernel,
        jax.ShapeDtypeStruct((2, WIN, WIN), jnp.float32),
        [smem] + [vmem] * 2,
        vmem,
        4,
    )(place, on_chip(mine), on_chip(swap_cores(mine)))
    return new_object, new_probe


def solution(mesh):
    return jax.shard_map(
        local,
        mesh=mesh,
        in_specs=(
            P(None, "group", "tile"),
            P(),
            P(("tile", "group"), None, None),
            P(("tile", "group")),
            P(("tile", "group")),
            P(("tile", "group")),
        ),
        out_specs=(P(None, "group", "tile"), P()),
        check_vma=False,
    )
```

time: 95.7 us -> 88.7 us (0.927); the launches traced: 94.4 us -> 88.5 us
  starting transfers between devices: 35.5 us -> 8.69 us
  blocking collectives: 35 us -> 58.6 us
  waiting for transfers between devices: 8.97 us -> 7.23 us
  Pallas kernels: 11.3 us -> 10.2 us
    ppermute x9 -> x6, starting transfers between devices: 35.5 us -> 8.69 us  [the longest x3 7.33 us: swap_z(): return lax.ppermute(value, 'tile', pairs)]
    all_to_all x3, blocking collectives: 35 us -> 58.6 us  [exchange(): lax.all_to_all(value, ('tile', 'group'), 0, 0, axis_index_groups=groups)]
    pallas_call x6 -> x4, Pallas kernels: 7.47 us -> 5.68 us  [the longest x1 4.29 us: local(): kernel_call(window_kernel, (buffer(16, LINES, LANES), buffer(16 * PIECE +...]
    ppermute x9 -> x6, waiting for transfers between devices: 8.97 us -> 7.23 us  [the longest x3 3.79 us: swap_z(): return lax.ppermute(value, 'tile', pairs)]
  transfers between devices with their start and end apart: 9 -> 6, of which waited for: 5 -> 4; matrix products, arithmetic and copies ran while one was open for 0% -> 0% of each run, Pallas kernels for 5% -> 4%
where the time goes in v6:
time: 88.7 us; the launch traced here: 88.5 us
  blocking collectives  58.6 us (66%)
  Pallas kernels  10.2 us (11%)
  starting transfers between devices  8.69 us (10%)
  waiting for transfers between devices  7.23 us (8%)
  between operations  2.68 us (3%)
  local copies, waits for them, and re-layouts  0.95 us (1%)
    all_to_all x3, blocking collectives, exchange(): lax.all_to_all(value, ('tile', 'group'), 0, 0, axis_index_groups=groups)  58.6 us
    ppermute x3, starting transfers between devices, swap_z(): return lax.ppermute(value, 'tile', pairs)  7.33 us
    pallas_call x1, Pallas kernels, local(): kernel_call(window_kernel, (buffer(16, LINES, LANES), buffer(16 * PIECE +...  4.29 us
    ppermute x3, waiting for transfers between devices, swap_z(): return lax.ppermute(value, 'tile', pairs)  3.79 us
    ppermute x3, waiting for transfers between devices, swap_cores(): return lax.ppermute(value, 'tile', [(i, i ^ 1) for i in range(TILES)])  3.44 us
    pallas_call x1, Pallas kernels, local(): kernel_call(object_kernel, jax.ShapeDtypeStruct((2, 40, LANES), jnp.float...  3.12 us
  transfers between devices with their start and end apart: 6, of which 4 were waited for; matrix products, arithmetic and copies ran while one was open for 0% of the time, Pallas kernels for 4%

profile of v6, /device:TPU:1, one launch (start us, length us, event | category | flops | bytes accessed | tf_op | source)
XLA Modules:
  0.0 88.5 jit_solution(16468361940545021576)
XLA Ops:
  0.6 0.0 copy-start.2
  0.6 0.0 copy-start.3
  0.7 0.0 copy-start
  0.7 0.0 copy-start.1
  0.7 0.9 %broadcast_in_dim.3 = f32[16,80,128]{2,1,0:T(8,128)S(1)} broadcast(f32[80,128]{1,0:T(8,128)} %bitcast.3), dimensions={1,2} | broadcast | bytes 696320 | tf_op jit(solution)/shard_map/broadcast_in_dim | solution.py:297
  1.6 21.5 %all_to_all.15.stack = f32[16,80,128]{2,1,0:T(8,128)S(1)} all-to-all(f32[16,80,128]{2,1,0:T(8,128)S(1)} %broadcast_in_dim.3), channel_id=1, replica_groups={{8,9,10,11,12,13,14,15,16,17,18,19,20,21,22,23},{24,25,26,27,28,29,30,3..., dimensions={0} | all-to-all | bytes 1310720 | tf_op jit(solution)/shard_map/all_to_all | solution.py:268
  23.1 0.9 %collective-permute-start = (f32[16,80,128]{2,1,0:T(8,128)S(1)}, f32[16,80,128]{2,1,0:T(8,128)S(1)}, u32[]{:S(2)}, u32[]{:S(2)}) collective-permute-start(f32[16,80,128]{2,1,0:T(8,128)S(1)} %all_to_all.15.stack), channel_id=1, source_target_pairs={{0,8},{8,0},{16,24},{24,16},{32,40},{40,32},{48,56},{56,48},{64,72... | collective-permute-start | bytes 1966088 | tf_op jit(solution)/shard_map/ppermute | solution.py:250
  25.9 0.1 pad_add_fusion.place
  26.0 0.0 collective-permute-done.near
  26.0 0.0 copy-done.2
  26.0 0.0 copy-done.3
  26.0 0.0 copy-done
  26.0 0.0 copy-done.1
  26.0 4.3 %window.1 = (f32[16,136,128]{2,1,0:T(8,128)S(1)}, f32[1536,128]{1,0:T(8,128)S(1)}, f32[8,128]{1,0:T(8,128)S(1)}) custom-call(s32[2]{0:T(128)S(1)} %pad_add_fusion.place, s32[1]{0:T(128)S(6)} %copy.10.row_ref, s32[1]{0:T(128)S(6)} %copy.11.col_ref, s32[1]{0:T(128)S(6)} %copy.12.live_ref, f32[16,80,128]{2,1,0:T(8,128)S(1)} %all_to_all.15.stack, ...), custom_call_target="tpu_custom_call" | custom-call | tf_op jit(solution)/shard_map/window/pallas_call | solution.py:298
  30.3 0.1 collective-permute-start.1
  30.5 2.2 %collective-permute-done.1.got = f32[1536,128]{1,0:T(8,128)S(1)} collective-permute-done((f32[1536,128]{1,0:T(8,128)S(1)}, f32[1536,128]{1,0:T(8,128)S(1)}, u32[]{:S(2)}, u32[]{:S(2)}) %collective-permute-start.1) | collective-permute-done | bytes 786464 | tf_op jit(solution)/shard_map/ppermute | solution.py:250
  32.7 0.6 merge.1
  33.4 21.1 %all_to_all.16.pieces = f32[16,136,128]{2,1,0:T(8,128)S(1)} all-to-all(f32[16,136,128]{2,1,0:T(8,128)S(1)} %merge.1), channel_id=1, replica_groups={{8,9,10,11,12,13,14,15,16,17,18,19,20,21,22,23},{24,25,26,27,28,29,30,3..., dimensions={0} | all-to-all | bytes 2228224 | tf_op jit(solution)/shard_map/all_to_all | solution.py:268
  54.5 0.0 copy-start.4
  54.5 0.1 reduce.1
  54.5 0.3 collective-permute-start.2
  54.8 2.5 %collective-permute-done.2 = f32[56,128]{1,0:T(8,128)S(1)} collective-permute-done((f32[56,128]{1,0:T(8,128)S(1)}, f32[56,128]{1,0:T(8,128)S(1)}, u32[]{:S(2)}, u32[]{:S(2)}) %collective-permute-start.2) | collective-permute-done | bytes 28704 | tf_op jit(solution)/shard_map/ppermute | solution.py:260
  57.3 3.1 %collective-permute-start.3 = (f32[56,128]{1,0:T(8,128)S(1)}, f32[56,128]{1,0:T(8,128)S(1)}, u32[]{:S(2)}, u32[]{:S(2)}) collective-permute-start(f32[56,128]{1,0:T(8,128)S(1)} %add.6), channel_id=1, source_target_pairs={{0,192},{8,72},{16,80},{24,88},{32,96},{40,104},{48,112},{56,120},... | collective-permute-start | bytes 86024 | tf_op jit(solution)/shard_map/ppermute | solution.py:260
  60.5 0.0 copy-done.4
  60.5 3.1 %object.1 = f32[2,40,128]{2,1,0:T(8,128)} custom-call(s32[2]{0:T(128)S(1)} %pad_add_fusion.place, f32[16,136,128]{2,1,0:T(8,128)S(1)} %all_to_all.16.pieces, f32[80,128]{1,0:T(8,128)S(1)} %get-tuple-element.12.gradient, f32[2,40,128]{2,1,0:T(8,128)S(1)} %copy-done.4, f32[2,256,256]{2,1,0:T(8,128)S(1)} %copy-done, f32[8,128]{1,0:T(8,128)S(1)} %get-tuple-element.13.peak), custom_call_target="tpu_custom_call" | custom-call | flops 700000 | bytes 2000000 | tf_op jit(solution)/shard_map/object/pallas_call | solution.py:317
  63.6 0.0 collective-permute-done.3
  63.6 3.9 %collective-permute-start.4 = (f32[56,128]{1,0:T(8,128)S(1)}, f32[56,128]{1,0:T(8,128)S(1)}, u32[]{:S(2)}, u32[]{:S(2)}) collective-permute-start(f32[56,128]{1,0:T(8,128)S(1)} %add.7.one), channel_id=1, source_target_pairs={{0,64},{8,200},{16,208},{24,216},{32,224},{40,232},{48,240},{56,24... | collective-permute-start | bytes 86024 | tf_op jit(solution)/shard_map/ppermute | solution.py:260
  67.5 1.3 %collective-permute-done.4.two = f32[56,128]{1,0:T(8,128)S(1)} collective-permute-done((f32[56,128]{1,0:T(8,128)S(1)}, f32[56,128]{1,0:T(8,128)S(1)}, u32[]{:S(2)}, u32[]{:S(2)}) %collective-permute-start.4) | collective-permute-done | bytes 28704 | tf_op jit(solution)/shard_map/ppermute | solution.py:260
  68.8 0.7 probe.6
  69.5 16.0 %all_to_all.17.mine = f32[16,32,128]{2,1,0:T(8,128)S(1)} all-to-all(f32[16,32,128]{2,1,0:T(8,128)S(1)} %probe.6), channel_id=1, replica_groups={{8,9,10,11,12,13,14,15,16,17,18,19,20,21,22,23},{24,25,26,27,28,29,30,3..., dimensions={0} | all-to-all | bytes 524288 | tf_op jit(solution)/shard_map/all_to_all | solution.py:268
  85.6 0.3 collective-permute-start.5
  85.9 1.2 %collective-permute-done.5.other = f32[16,32,128]{2,1,0:T(8,128)S(1)} collective-permute-done((f32[16,32,128]{2,1,0:T(8,128)S(1)}, f32[16,32,128]{2,1,0:T(8,128)S(1)}, u32[]{:S(2)}, u32[]{:S(2)}) %collective-permute-start.5) | collective-permute-done | bytes 262176 | tf_op jit(solution)/shard_map/ppermute | solution.py:250
  87.1 1.4 %gather.1 = f32[2,256,256]{2,1,0:T(8,128)} custom-call(s32[2]{0:T(128)S(1)} %pad_add_fusion.place, f32[16,32,128]{2,1,0:T(8,128)S(1)} %all_to_all.17.mine, f32[16,32,128]{2,1,0:T(8,128)S(1)} %collective-permute-done.5.other), custom_call_target="tpu_custom_call" | custom-call | tf_op jit(solution)/shard_map/gather/pallas_call | solution.py:338
  (2 shorter events, 0.0 us)
Async XLA Ops:
  0.6 25.4 %copy-start.2 = (bf16[512,256]{1,0:T(8,128)(2,1)S(1)}, bf16[512,256]{1,0:T(8,128)(2,1)}, u32[]{:S(2)}) copy-start(bf16[512,256]{1,0:T(8,128)(2,1)} %constant.14.clone.low) | copy-start | bytes 786436
  0.6 25.4 %copy-start.3 = (bf16[512,256]{1,0:T(8,128)(2,1)S(1)}, bf16[512,256]{1,0:T(8,128)(2,1)}, u32[]{:S(2)}) copy-start(bf16[512,256]{1,0:T(8,128)(2,1)} %constant.13.clone.high) | copy-start | bytes 786436
  0.7 25.4 %copy-start = (f32[2,256,256]{2,1,0:T(8,128)S(1)}, f32[2,256,256]{2,1,0:T(8,128)}, u32[]{:S(2)}) copy-start(f32[2,256,256]{2,1,0:T(8,128)} %probe.7) | copy-start | bytes 1572868
  0.7 25.4 %copy-start.1 = (f32[1,256,256]{2,1,0:T(8,128)S(1)}, f32[1,256,256]{2,1,0:T(8,128)}, u32[]{:S(2)}) copy-start(f32[1,256,256]{2,1,0:T(8,128)} %amps.1) | copy-start | bytes 786436
  23.1 2.9 %collective-permute-start = (f32[16,80,128]{2,1,0:T(8,128)S(1)}, f32[16,80,128]{2,1,0:T(8,128)S(1)}, u32[]{:S(2)}, u32[]{:S(2)}) collective-permute-start(f32[16,80,128]{2,1,0:T(8,128)S(1)} %all_to_all.15.stack), channel_id=1, source_target_pairs={{0,8},{8,0},{16,24},{24,16},{32,40},{40,32},{48,56},{56,48},{64,72... | collective-permute-start | bytes 1966088 | tf_op jit(solution)/shard_map/ppermute | solution.py:250
  30.3 2.4 %collective-permute-start.1 = (f32[1536,128]{1,0:T(8,128)S(1)}, f32[1536,128]{1,0:T(8,128)S(1)}, u32[]{:S(2)}, u32[]{:S(2)}) collective-permute-start(f32[1536,128]{1,0:T(8,128)S(1)} %get-tuple-element.10), channel_id=1, source_target_pairs={{0,8},{8,0},{16,24},{24,16},{32,40},{40,32},{48,56},{56,48},{64,72... | collective-permute-start | bytes 2359304 | tf_op jit(solution)/shard_map/ppermute | solution.py:250
  54.5 6.0 %copy-start.4 = (f32[2,40,128]{2,1,0:T(8,128)S(1)}, f32[2,40,128]{2,1,0:T(8,128)}, u32[]{:S(2)}) copy-start(f32[2,40,128]{2,1,0:T(8,128)} %old.1) | copy-start | bytes 122884
  54.5 2.8 %collective-permute-start.2 = (f32[56,128]{1,0:T(8,128)S(1)}, f32[56,128]{1,0:T(8,128)S(1)}, u32[]{:S(2)}, u32[]{:S(2)}) collective-permute-start(f32[56,128]{1,0:T(8,128)S(1)} %get-tuple-element.11), channel_id=1, source_target_pairs={{0,224},{8,40},{16,48},{24,56},{32,64},{40,8},{48,16},{56,24},{64,... | collective-permute-start | bytes 86024 | tf_op jit(solution)/shard_map/ppermute | solution.py:260
  57.3 6.3 %collective-permute-start.3 = (f32[56,128]{1,0:T(8,128)S(1)}, f32[56,128]{1,0:T(8,128)S(1)}, u32[]{:S(2)}, u32[]{:S(2)}) collective-permute-start(f32[56,128]{1,0:T(8,128)S(1)} %add.6), channel_id=1, source_target_pairs={{0,192},{8,72},{16,80},{24,88},{32,96},{40,104},{48,112},{56,120},... | collective-permute-start | bytes 86024 | tf_op jit(solution)/shard_map/ppermute | solution.py:260
  63.6 5.2 %collective-permute-start.4 = (f32[56,128]{1,0:T(8,128)S(1)}, f32[56,128]{1,0:T(8,128)S(1)}, u32[]{:S(2)}, u32[]{:S(2)}) collective-permute-start(f32[56,128]{1,0:T(8,128)S(1)} %add.7.one), channel_id=1, source_target_pairs={{0,64},{8,200},{16,208},{24,216},{32,224},{40,232},{48,240},{56,24... | collective-permute-start | bytes 86024 | tf_op jit(solution)/shard_map/ppermute | solution.py:260
  85.6 1.5 %collective-permute-start.5 = (f32[16,32,128]{2,1,0:T(8,128)S(1)}, f32[16,32,128]{2,1,0:T(8,128)S(1)}, u32[]{:S(2)}, u32[]{:S(2)}) collective-permute-start(f32[16,32,128]{2,1,0:T(8,128)S(1)} %all_to_all.17.mine), channel_id=1, source_target_pairs={{0,8},{8,0},{16,24},{24,16},{32,40},{40,32},{48,56},{56,48},{64,72... | collective-permute-start | bytes 786440 | tf_op jit(solution)/shard_map/ppermute | solution.py:250

commit v7 on v6

--- a/solution.py
+++ b/solution.py
@@ -12,7 +12,6 @@
 TILES = 32
 SPARE = 48
 PIECE = 56
-LINES = 136
 SMEM = pltpu.MemorySpace.SMEM
 VMEM = pltpu.MemorySpace.VMEM
 
@@ -51,11 +50,10 @@
 
 
 def window_kernel(
-    place, row_ref, col_ref, live_ref, stack, near, probe, amps, high, low,
-    keep, send, peak, field, grads, sums,
+    place, stack, near, probe, amps, high, low, keep, keep_grad, send, field, grads, sums
 ):
-    row, col = row_ref[0], col_ref[0]
-    live = live_ref[0].astype(jnp.float32)
+    row, col = place[2], place[3]
+    live = place[4].astype(jnp.float32)
     odd, half = place[0] & 1, half_of(place[0])
     inside = far_exists(place[0])
     for member in range(8):
@@ -90,9 +88,6 @@
     miss_real, miss_imag = transform(far_real * factor, far_imag * factor, tall, wide, 1.0)
     miss_real = miss_real * live
     miss_imag = miss_imag * live
-    light = probe_real * probe_real + probe_imag * probe_imag
-    peak[...] = jnp.full((8, LANES), jnp.max(light), jnp.float32)
-
     terms = (
         probe_real * miss_real + probe_imag * miss_imag,
         probe_real * miss_imag - probe_imag * miss_real,
@@ -115,16 +110,15 @@
         total = total + window_light[line : line + 8, :LANES] + window_light[line : line + 8, LANES:]
     spare_line = lax.broadcasted_iota(jnp.int32, (8, LANES), 0)
     spare_lane = lax.broadcasted_iota(jnp.int32, (8, LANES), 1)
-    where_mine = jnp.where(
-        spare_lane == 0,
-        row.astype(jnp.float32),
-        jnp.where(spare_lane == 1, col.astype(jnp.float32), jnp.where(spare_lane == 2, live, 0.0)),
-    )
+    first_lane = 8 * odd
     spare = jnp.where(
-        spare_line == 2,
+        spare_line == 1,
         jnp.broadcast_to(jnp.sum(total, axis=0, keepdims=True), (8, LANES)),
-        jnp.where(spare_line == odd, where_mine, 0.0),
-    )
+        0.0,
+    )
+    for lane_off, number in enumerate((row.astype(jnp.float32), col.astype(jnp.float32), live)):
+        here = jnp.logical_and(spare_line == 0, spare_lane == first_lane + lane_off)
+        spare = jnp.where(here, number, spare)
     for member in range(16):
         for kept, side_half in ((True, half), (False, 1 - half)):
             top = pl.multiple_of(side_half * 128 + member * 8, 8)
@@ -143,38 +137,37 @@
     for member in range(8):
         lines = slice(member * 40, member * 40 + 40)
         for part in range(2):
-            put = PIECE + part * 40
-            keep[8 - 8 * odd + member, put : put + 40, :] = grads[part, 1, lines, :]
-            keep[8 * odd + member, put : put + 40, :] = jnp.where(
+            put = part * 40
+            keep_grad[8 - 8 * odd + member, put : put + 40, :] = grads[part, 1, lines, :]
+            keep_grad[8 * odd + member, put : put + 40, :] = jnp.where(
                 inside, grads[part, 2 * odd, lines, :], 0.0
             )
             put = 16 * PIECE + member * 80 + part * 40
             send[put : put + 40, :] = grads[part, 2 - 2 * odd, lines, :]
 
 
-def merge_kernel(place, keep, got, out):
+def merge_kernel(place, keep, keep_grad, got, out, out_grad):
+    for member in range(16):
+        out[member] = keep[member] + got[member * PIECE : (member + 1) * PIECE, :]
     mine = 8 - 8 * (place[0] & 1)
-    for member in range(16):
-        out[member, :PIECE, :] = keep[member, :PIECE, :] + got[member * PIECE : (member + 1) * PIECE, :]
     for member in range(8):
         put = 16 * PIECE + member * 80
-        out[mine + member, PIECE:, :] = keep[mine + member, PIECE:, :] + got[put : put + 80, :]
-        out[8 - mine + member, PIECE:, :] = keep[8 - mine + member, PIECE:, :]
-
-
-def reduce_kernel(pieces, probe_sum, gradient):
+        out_grad[mine + member] = keep_grad[mine + member] + got[put : put + 80, :]
+        out_grad[8 - mine + member] = keep_grad[8 - mine + member]
+
+
+def reduce_kernel(pieces, out):
     total = pieces[0]
     for member in range(1, 16):
         total = total + pieces[member]
-    probe_sum[...] = total[:PIECE]
-    gradient[...] = total[PIECE:]
+    out[...] = total
 
 
 def probe_kernel(place, one, two, probe, out):
     odd = place[0] & 1
     top = pl.multiple_of(half_of(place[0]) * 128 + (8 - 8 * odd + place[1]) * 8, 8)
     summed = one[...] + two[...]
-    mean = jnp.sum(summed[SPARE + 2 : SPARE + 3]) * (1.0 / (WIN * WIN))
+    mean = jnp.sum(summed[SPARE + 1 : SPARE + 2]) * (1.0 / (WIN * WIN))
     for side in range(2):
         bottom = summed[32 + side * 8 : 40 + side * 8] + 0.25 * mean + 1e-05
         for part in range(2):
@@ -208,30 +201,38 @@
     return total + at[2] * jnp.where(lane < col, before, after)
 
 
-def object_kernel(place, pieces, gradient, old, probe, peak, out, light, at, sem):
-    copy = pltpu.make_async_copy(pieces.at[:, SPARE:PIECE, :], at, sem)
-    copy.start()
-    odd = place[0] & 1
+def prep_kernel(probe, light, peak):
     blank = jnp.zeros((64, LANES), jnp.float32)
+    most = jnp.zeros((WIN, LANES), jnp.float32)
     for side in range(2):
         cols = slice(side * LANES, (side + 1) * LANES)
-        light[1 + side, 64:320, :] = probe[0, :, cols] * probe[0, :, cols] + (
-            probe[1, :, cols] * probe[1, :, cols]
-        )
+        bright = probe[0, :, cols] * probe[0, :, cols] + probe[1, :, cols] * probe[1, :, cols]
+        most = jnp.maximum(most, bright)
+        light[1 + side, 64:320, :] = bright
         light[1 + side, 0:64, :] = blank
         light[1 + side, 320:384, :] = blank
         light[3 * side, :, :] = jnp.zeros((384, LANES), jnp.float32)
+    peak[...] = jnp.full((8, LANES), jnp.max(most), jnp.float32)
+
+
+def object_kernel(place, pieces, grads, old, light, peak, out, at, sem):
+    copy = pltpu.make_async_copy(pieces.at[:, SPARE : SPARE + 1, :], at, sem)
+    copy.start()
+    gradient = grads[0]
+    for member in range(1, 16):
+        gradient = gradient + grads[member]
     copy.wait()
+    odd = place[0] & 1
     mine = 8 - 8 * odd
     total = jnp.zeros((40, LANES), jnp.float32)
     outside = jnp.zeros((40, LANES), jnp.float32)
     for member in range(8):
         for core in range(2):
             block = 1 - core * (1 - odd) + (1 - core) * odd
-            total = shine(light, place[1], total, [at[mine + member, core, k] for k in range(3)], block)
-        outside = shine(
-            light, place[1], outside, [at[8 - mine + member, 1 - odd, k] for k in range(3)], 2 - 2 * odd
-        )
+            seen = [at[mine + member, 0, core * 8 + k] for k in range(3)]
+            total = shine(light, place[1], total, seen, block)
+        seen = [at[8 - mine + member, 0, (1 - odd) * 8 + k] for k in range(3)]
+        outside = shine(light, place[1], outside, seen, 2 - 2 * odd)
     total = total + jnp.where(far_exists(place[0]), outside, 0.0)
     bottom = total + 0.25 * (peak[0:1, :] + 1e-06)
     for part in range(2):
@@ -286,7 +287,6 @@
 
 def local(object_field, probe_field, amplitudes, row_start, column_start, live_slots):
     smem, vmem = pl.BlockSpec(memory_space=SMEM), pl.BlockSpec(memory_space=VMEM)
-    place = jnp.stack([lax.axis_index("tile"), lax.axis_index("group")]).astype(jnp.int32)
     high, low = (on_chip(jnp.asarray(table)) for table in split_tables())
     probe = on_chip(probe_field)
 
@@ -294,44 +294,55 @@
         return pltpu.VMEM(dims, jnp.float32)
 
     own = object_field.reshape(80, LANES)
-    stack = exchange(jnp.broadcast_to(own, (16, 80, LANES)))
-    keep, send, peak = kernel_call(
+    here = [lax.axis_index(axis)[None].astype(jnp.int32) for axis in ("tile", "group")]
+    place = jnp.concatenate([*here, row_start, column_start, live_slots])
+    stack, place = lax.optimization_barrier((exchange(jnp.broadcast_to(own, (16, 80, LANES))), place))
+    light, peak = kernel_call(
+        prep_kernel,
+        (buffer(4, 384, LANES), buffer(8, LANES)),
+        [vmem],
+        (vmem,) * 2,
+        4,
+        cost_estimate=pl.CostEstimate(flops=300000, bytes_accessed=2000000, transcendentals=0),
+    )(probe)
+    keep, keep_grad, send = kernel_call(
         window_kernel,
-        (buffer(16, LINES, LANES), buffer(16 * PIECE + 640, LANES), buffer(8, LANES)),
-        [smem] * 4 + [vmem] * 6,
+        (buffer(16, PIECE, LANES), buffer(16, 80, LANES), buffer(16 * PIECE + 640, LANES)),
+        [smem] + [vmem] * 6,
         (vmem,) * 3,
         24,
         scratch_shapes=[buffer(2, 3, 320, LANES), buffer(2, 3, 320, LANES), buffer(3, WIN, WIN)],
     )(
-        place, row_start, column_start, live_slots, on_chip(stack), on_chip(swap_cores(stack)),
-        probe, on_chip(amplitudes), high, low,
-    )
-
-    merged = kernel_call(merge_kernel, buffer(16, LINES, LANES), [smem] + [vmem] * 2, vmem, 4)(
-        place, keep, on_chip(swap_cores(send))
-    )
-    pieces = on_chip(exchange(merged))
-    total, gradient = kernel_call(
-        reduce_kernel, (buffer(PIECE, LANES), buffer(80, LANES)), [vmem], (vmem,) * 2, 4
-    )(pieces)
+        place, on_chip(stack), on_chip(swap_cores(stack)), probe, on_chip(amplitudes), high, low
+    )
+
+    got, light = lax.optimization_barrier((swap_cores(send), light))
+    sums, grads = kernel_call(
+        merge_kernel,
+        (buffer(16, PIECE, LANES), buffer(16, 80, LANES)),
+        [smem] + [vmem] * 3,
+        (vmem,) * 2,
+        4,
+    )(place, keep, keep_grad, on_chip(got))
+    pieces = exchange(sums)
+    total = kernel_call(reduce_kernel, buffer(PIECE, LANES), [vmem], vmem, 4)(on_chip(pieces))
+    total, grads = lax.optimization_barrier((total, grads))
+    grads = exchange(grads)
+    for mask in (1, 2):
+        total = total + swap_z(total, mask)
+    total, grads = lax.optimization_barrier((total, grads))
     new_object = kernel_call(
         object_kernel,
         jax.ShapeDtypeStruct((2, 40, LANES), jnp.float32),
         [smem] + [vmem] * 5,
         vmem,
         8,
-        scratch_shapes=[
-            buffer(4, 384, LANES),
-            pltpu.SMEM((16, 8, LANES), jnp.float32),
-            pltpu.SemaphoreType.DMA,
-        ],
+        scratch_shapes=[pltpu.SMEM((16, 1, LANES), jnp.float32), pltpu.SemaphoreType.DMA],
         cost_estimate=pl.CostEstimate(flops=700000, bytes_accessed=2000000, transcendentals=0),
-    )(place, pieces, gradient, on_chip(object_field), probe, peak)
-    for mask in (1, 2):
-        total = total + swap_z(total, mask)
-    total, new_object = lax.optimization_barrier((total, new_object))
+    )(place, on_chip(pieces), on_chip(grads), on_chip(object_field), on_chip(light), peak)
+    got, new_object = lax.optimization_barrier((swap_z(total, 6), new_object))
     piece = kernel_call(probe_kernel, buffer(16, 32, LANES), [smem] + [vmem] * 3, vmem, 4)(
-        place, on_chip(total), on_chip(swap_z(total, 6)), probe
+        place, on_chip(total), on_chip(got), probe
     )
 
     mine = exchange(piece)

time: 88.7 us -> 93.9 us (1.059); the launches traced: 88.5 us -> 92.1 us
  blocking collectives: 58.6 us -> 27.2 us
  starting transfers between devices: 8.69 us -> 27.9 us
  waiting for transfers between devices: 7.23 us -> 22.4 us
    all_to_all x3 -> x2, blocking collectives: 58.6 us -> 27.2 us  [exchange(): lax.all_to_all(value, ('tile', 'group'), 0, 0, axis_index_groups=groups)]
    all_to_all x0 -> x2, waiting for transfers between devices: none -> 14.6 us  [exchange(): lax.all_to_all(value, ('tile', 'group'), 0, 0, axis_index_groups=groups)]
    all_to_all x0 -> x2, starting transfers between devices: none -> 11.9 us  [exchange(): lax.all_to_all(value, ('tile', 'group'), 0, 0, axis_index_groups=groups)]
    ppermute x3, starting transfers between devices: 1.36 us -> 5.73 us  [swap_cores(): return lax.ppermute(value, 'tile', [(i, i ^ 1) for i in range(TILES)])]
    ppermute x3, starting transfers between devices: 7.33 us -> 10.3 us  [swap_z(): return lax.ppermute(value, 'tile', pairs)]
    ppermute x3, waiting for transfers between devices: 3.44 us -> 4.56 us  [swap_cores(): return lax.ppermute(value, 'tile', [(i, i ^ 1) for i in range(TILES)])]
    pallas_call x3 -> x4, Pallas kernels: 4.99 us -> 6 us  [the longest x1 4.26 us: local(): kernel_call(window_kernel, (buffer(16, PIECE, LANES), buffer(16, 80, LANE...]
  transfers between devices with their start and end apart: 6 -> 8, of which waited for: 4 -> 7; matrix products, arithmetic and copies ran while one was open for 0% -> 0% of each run, Pallas kernels for 4% -> 3%
where the time goes in v7:
time: 93.9 us; the launch traced here: 92.1 us
  starting transfers between devices  27.9 us (30%)
  blocking collectives  27.2 us (29%)
  waiting for transfers between devices  22.4 us (24%)
  Pallas kernels  10.2 us (11%)
  between operations  2.66 us (3%)
  local copies, waits for them, and re-layouts  1.77 us (2%)
    all_to_all x2, blocking collectives, exchange(): lax.all_to_all(value, ('tile', 'group'), 0, 0, axis_index_groups=groups)  27.2 us
    all_to_all x2, waiting for transfers between devices, exchange(): lax.all_to_all(value, ('tile', 'group'), 0, 0, axis_index_groups=groups)  14.6 us
    all_to_all x2, starting transfers between devices, exchange(): lax.all_to_all(value, ('tile', 'group'), 0, 0, axis_index_groups=groups)  11.9 us
    ppermute x3, starting transfers between devices, swap_z(): return lax.ppermute(value, 'tile', pairs)  10.3 us
    ppermute x3, starting transfers between devices, swap_cores(): return lax.ppermute(value, 'tile', [(i, i ^ 1) for i in range(TILES)])  5.73 us
    ppermute x3, waiting for transfers between devices, swap_cores(): return lax.ppermute(value, 'tile', [(i, i ^ 1) for i in range(TILES)])  4.56 us
    pallas_call x1, Pallas kernels, local(): kernel_call(window_kernel, (buffer(16, PIECE, LANES), buffer(16, 80, LANE...  4.26 us
    ppermute x3, waiting for transfers between devices, swap_z(): return lax.ppermute(value, 'tile', pairs)  3.19 us
  transfers between devices with their start and end apart: 8, of which 7 were waited for; matrix products, arithmetic and copies ran while one was open for 0% of the time, Pallas kernels for 3%

profile of v7, /device:TPU:1, one launch (start us, length us, event | category | flops | bytes accessed | tf_op | source)
XLA Modules:
  0.0 92.1 jit_solution(7609241834554072146)
XLA Ops:
  0.6 1.7 %broadcast_in_dim.9 = f32[16,80,128]{2,1,0:T(8,128)} broadcast(f32[80,128]{1,0:T(8,128)} %bitcast.3), dimensions={1,2} | broadcast | bytes 696320 | tf_op jit(solution)/shard_map/broadcast_in_dim | solution.py:299
  2.3 0.0 copy-start
  2.3 0.0 copy-start.1
  2.3 0.0 copy-start.2
  2.3 0.0 copy-start.3
  2.3 8.3 %all-to-all-start = ((f32[16,80,128]{2,1,0:T(8,128)}), f32[16,80,128]{2,1,0:T(8,128)S(1)}, u32[]{:S(2)}, u32[]{:S(2)}) async-start(f32[16,80,128]{2,1,0:T(8,128)} %broadcast_in_dim.9), calls=%async_computation | async-start | bytes 1310720 | tf_op jit(solution)/shard_map/all_to_all | solution.py:269
  12.5 0.1 concatenate.3.place
  12.6 10.5 %all-to-all-done.stack = f32[16,80,128]{2,1,0:T(8,128)S(1)} async-done(((f32[16,80,128]{2,1,0:T(8,128)}), f32[16,80,128]{2,1,0:T(8,128)S(1)}, u32[]{:S(2)}, u32[]{:S(2)}) %all-to-all-start) | async-done | bytes 655392 | tf_op jit(solution)/shard_map/all_to_all | solution.py:269
  23.1 1.8 %collective-permute-start = (f32[16,80,128]{2,1,0:T(8,128)S(1)}, f32[16,80,128]{2,1,0:T(8,128)S(1)}, u32[]{:S(2)}, u32[]{:S(2)}) collective-permute-start(f32[16,80,128]{2,1,0:T(8,128)S(1)} %all-to-all-done.stack), channel_id=1, source_target_pairs={{0,8},{8,0},{16,24},{24,16},{32,40},{40,32},{48,56},{56,48},{64,72... | collective-permute-start | bytes 1966088 | tf_op jit(solution)/shard_map/ppermute | solution.py:251
  24.9 1.7 %collective-permute-done.near = f32[16,80,128]{2,1,0:T(8,128)S(1)} collective-permute-done((f32[16,80,128]{2,1,0:T(8,128)S(1)}, f32[16,80,128]{2,1,0:T(8,128)S(1)}, u32[]{:S(2)}, u32[]{:S(2)}) %collective-permute-start) | collective-permute-done | bytes 655392 | tf_op jit(solution)/shard_map/ppermute | solution.py:251
  26.6 0.0 copy-done
  26.6 0.0 copy-done.1
  26.7 0.0 copy-done.2
  26.7 0.0 copy-done.3
  26.7 4.3 %window.1 = (f32[16,56,128]{2,1,0:T(8,128)S(1)}, f32[16,80,128]{2,1,0:T(8,128)S(1)}, f32[1536,128]{1,0:T(8,128)S(1)}) custom-call(s32[5]{0:T(128)S(1)} %concatenate.3.place, f32[16,80,128]{2,1,0:T(8,128)S(1)} %all-to-all-done.stack, f32[16,80,128]{2,1,0:T(8,128)S(1)} %collective-permute-done.near, f32[2,256,256]{2,1,0:T(8,128)S(1)} %copy-done, ...), custom_call_target="tpu_custom_call" | custom-call | tf_op jit(solution)/shard_map/window/pallas_call | solution.py:308
  30.9 0.5 collective-permute-start.1
  31.4 0.2 prep.1
  31.6 1.7 %collective-permute-done.1.got = f32[1536,128]{1,0:T(8,128)S(1)} collective-permute-done((f32[1536,128]{1,0:T(8,128)S(1)}, f32[1536,128]{1,0:T(8,128)S(1)}, u32[]{:S(2)}, u32[]{:S(2)}) %collective-permute-start.1) | collective-permute-done | bytes 786464 | tf_op jit(solution)/shard_map/ppermute | solution.py:251
  33.3 1.5 %merge.1 = (f32[16,56,128]{2,1,0:T(8,128)S(1)}, f32[16,80,128]{2,1,0:T(8,128)}) custom-call(s32[5]{0:T(128)S(1)} %concatenate.3.place, f32[16,56,128]{2,1,0:T(8,128)S(1)} %get-tuple-element.21.keep, f32[16,80,128]{2,1,0:T(8,128)S(1)} %get-tuple-element.22.keep_grad, f32[1536,128]{1,0:T(8,128)S(1)} %collective-permute-done.1.got), custom_call_target="tpu_custom_call" | custom-call | tf_op jit(solution)/shard_map/merge/pallas_call | solution.py:320
  34.8 13.6 %all_to_all.20.pieces = f32[16,56,128]{2,1,0:T(8,128)S(1)} all-to-all(f32[16,56,128]{2,1,0:T(8,128)S(1)} %get-tuple-element.26), channel_id=1, replica_groups={{8,9,10,11,12,13,14,15,16,17,18,19,20,21,22,23},{24,25,26,27,28,29,30,3..., dimensions={0} | all-to-all | bytes 917504 | tf_op jit(solution)/shard_map/all_to_all | solution.py:269
  48.4 3.6 %all-to-all-start.2 = ((f32[16,80,128]{2,1,0:T(8,128)}), f32[16,80,128]{2,1,0:T(8,128)S(1)}, u32[]{:S(2)}, u32[]{:S(2)}) async-start(f32[16,80,128]{2,1,0:T(8,128)} %get-tuple-element.29), calls=%async_computation.2 | async-start | bytes 1310720 | tf_op jit(solution)/shard_map/all_to_all | solution.py:269
  52.1 1.8 %collective-permute-start.2 = (f32[56,128]{1,0:T(8,128)S(1)}, f32[56,128]{1,0:T(8,128)S(1)}, u32[]{:S(2)}, u32[]{:S(2)}) collective-permute-start(f32[56,128]{1,0:T(8,128)S(1)} %reduce.1), channel_id=1, source_target_pairs={{0,224},{8,40},{16,48},{24,56},{32,64},{40,8},{48,16},{56,24},{64,... | collective-permute-start | bytes 86024 | tf_op jit(solution)/shard_map/ppermute | solution.py:261
  53.8 1.3 %collective-permute-done.2 = f32[56,128]{1,0:T(8,128)S(1)} collective-permute-done((f32[56,128]{1,0:T(8,128)S(1)}, f32[56,128]{1,0:T(8,128)S(1)}, u32[]{:S(2)}, u32[]{:S(2)}) %collective-permute-start.2) | collective-permute-done | bytes 28704 | tf_op jit(solution)/shard_map/ppermute | solution.py:261
  55.1 0.0 copy-start.4
  55.1 3.5 %collective-permute-start.3 = (f32[56,128]{1,0:T(8,128)S(1)}, f32[56,128]{1,0:T(8,128)S(1)}, u32[]{:S(2)}, u32[]{:S(2)}) collective-permute-start(f32[56,128]{1,0:T(8,128)S(1)} %add.6), channel_id=1, source_target_pairs={{0,192},{8,72},{16,80},{24,88},{32,96},{40,104},{48,112},{56,120},... | collective-permute-start | bytes 86024 | tf_op jit(solution)/shard_map/ppermute | solution.py:261
  58.6 1.9 %collective-permute-done.3 = f32[56,128]{1,0:T(8,128)S(1)} collective-permute-done((f32[56,128]{1,0:T(8,128)S(1)}, f32[56,128]{1,0:T(8,128)S(1)}, u32[]{:S(2)}, u32[]{:S(2)}) %collective-permute-start.3) | collective-permute-done | bytes 28704 | tf_op jit(solution)/shard_map/ppermute | solution.py:261
  60.5 4.1 %all-to-all-done.2.grads = f32[16,80,128]{2,1,0:T(8,128)S(1)} async-done(((f32[16,80,128]{2,1,0:T(8,128)}), f32[16,80,128]{2,1,0:T(8,128)S(1)}, u32[]{:S(2)}, u32[]{:S(2)}) %all-to-all-start.2) | async-done | bytes 655392 | tf_op jit(solution)/shard_map/all_to_all | solution.py:269
  64.6 5.1 %collective-permute-start.4 = (f32[56,128]{1,0:T(8,128)S(1)}, f32[56,128]{1,0:T(8,128)S(1)}, u32[]{:S(2)}, u32[]{:S(2)}) collective-permute-start(f32[56,128]{1,0:T(8,128)S(1)} %add.7.one), channel_id=1, source_target_pairs={{0,64},{8,200},{16,208},{24,216},{32,224},{40,232},{48,240},{56,24... | collective-permute-start | bytes 86024 | tf_op jit(solution)/shard_map/ppermute | solution.py:261
  69.7 0.0 copy-done.4
  69.7 2.2 %object.1 = f32[2,40,128]{2,1,0:T(8,128)} custom-call(s32[5]{0:T(128)S(1)} %concatenate.3.place, f32[16,56,128]{2,1,0:T(8,128)S(1)} %all_to_all.20.pieces, f32[16,80,128]{2,1,0:T(8,128)S(1)} %all-to-all-done.2.grads, f32[2,40,128]{2,1,0:T(8,128)S(1)} %copy-done.4, f32[4,384,128]{2,1,0:T(8,128)S(1)} %get-tuple-element.32.light, ...), custom_call_target="tpu_custom_call" | custom-call | flops 700000 | bytes 2000000 | tf_op jit(solution)/shard_map/object/pallas_call | solution.py:334
  71.9 0.0 collective-permute-done.4.two
  71.9 0.7 probe.6
  72.6 13.5 %all_to_all.21.mine = f32[16,32,128]{2,1,0:T(8,128)S(1)} all-to-all(f32[16,32,128]{2,1,0:T(8,128)S(1)} %probe.6), channel_id=1, replica_groups={{8,9,10,11,12,13,14,15,16,17,18,19,20,21,22,23},{24,25,26,27,28,29,30,3..., dimensions={0} | all-to-all | bytes 524288 | tf_op jit(solution)/shard_map/all_to_all | solution.py:269
  86.1 3.5 %collective-permute-start.5 = (f32[16,32,128]{2,1,0:T(8,128)S(1)}, f32[16,32,128]{2,1,0:T(8,128)S(1)}, u32[]{:S(2)}, u32[]{:S(2)}) collective-permute-start(f32[16,32,128]{2,1,0:T(8,128)S(1)} %all_to_all.21.mine), channel_id=1, source_target_pairs={{0,8},{8,0},{16,24},{24,16},{32,40},{40,32},{48,56},{56,48},{64,72... | collective-permute-start | bytes 786440 | tf_op jit(solution)/shard_map/ppermute | solution.py:251
  89.6 1.2 %collective-permute-done.5.other = f32[16,32,128]{2,1,0:T(8,128)S(1)} collective-permute-done((f32[16,32,128]{2,1,0:T(8,128)S(1)}, f32[16,32,128]{2,1,0:T(8,128)S(1)}, u32[]{:S(2)}, u32[]{:S(2)}) %collective-permute-start.5) | collective-permute-done | bytes 262176 | tf_op jit(solution)/shard_map/ppermute | solution.py:251
  90.8 1.4 %gather.1 = f32[2,256,256]{2,1,0:T(8,128)} custom-call(s32[5]{0:T(128)S(1)} %concatenate.3.place, f32[16,32,128]{2,1,0:T(8,128)S(1)} %all_to_all.21.mine, f32[16,32,128]{2,1,0:T(8,128)S(1)} %collective-permute-done.5.other), custom_call_target="tpu_custom_call" | custom-call | tf_op jit(solution)/shard_map/gather/pallas_call | solution.py:349
  (3 shorter events, 0.0 us)
Async XLA Ops:
  2.3 24.4 %copy-start = (f32[2,256,256]{2,1,0:T(8,128)S(1)}, f32[2,256,256]{2,1,0:T(8,128)}, u32[]{:S(2)}) copy-start(f32[2,256,256]{2,1,0:T(8,128)} %probe.7) | copy-start | bytes 1572868
  2.3 24.4 %copy-start.1 = (f32[1,256,256]{2,1,0:T(8,128)S(1)}, f32[1,256,256]{2,1,0:T(8,128)}, u32[]{:S(2)}) copy-start(f32[1,256,256]{2,1,0:T(8,128)} %amps.1) | copy-start | bytes 786436
  2.3 24.4 %copy-start.2 = (bf16[512,256]{1,0:T(8,128)(2,1)S(1)}, bf16[512,256]{1,0:T(8,128)(2,1)}, u32[]{:S(2)}) copy-start(bf16[512,256]{1,0:T(8,128)(2,1)} %constant.14.clone.low) | copy-start | bytes 786436
  2.3 24.4 %copy-start.3 = (bf16[512,256]{1,0:T(8,128)(2,1)S(1)}, bf16[512,256]{1,0:T(8,128)(2,1)}, u32[]{:S(2)}) copy-start(bf16[512,256]{1,0:T(8,128)(2,1)} %constant.13.clone.high) | copy-start | bytes 786436
  2.3 20.8 %all-to-all-start = ((f32[16,80,128]{2,1,0:T(8,128)}), f32[16,80,128]{2,1,0:T(8,128)S(1)}, u32[]{:S(2)}, u32[]{:S(2)}) async-start(f32[16,80,128]{2,1,0:T(8,128)} %broadcast_in_dim.9), calls=%async_computation | async-start | bytes 1310720 | tf_op jit(solution)/shard_map/all_to_all | solution.py:269
  23.1 3.5 %collective-permute-start = (f32[16,80,128]{2,1,0:T(8,128)S(1)}, f32[16,80,128]{2,1,0:T(8,128)S(1)}, u32[]{:S(2)}, u32[]{:S(2)}) collective-permute-start(f32[16,80,128]{2,1,0:T(8,128)S(1)} %all-to-all-done.stack), channel_id=1, source_target_pairs={{0,8},{8,0},{16,24},{24,16},{32,40},{40,32},{48,56},{56,48},{64,72... | collective-permute-start | bytes 1966088 | tf_op jit(solution)/shard_map/ppermute | solution.py:251
  30.9 2.4 %collective-permute-start.1 = (f32[1536,128]{1,0:T(8,128)S(1)}, f32[1536,128]{1,0:T(8,128)S(1)}, u32[]{:S(2)}, u32[]{:S(2)}) collective-permute-start(f32[1536,128]{1,0:T(8,128)S(1)} %get-tuple-element.23), channel_id=1, source_target_pairs={{0,8},{8,0},{16,24},{24,16},{32,40},{40,32},{48,56},{56,48},{64,72... | collective-permute-start | bytes 2359304 | tf_op jit(solution)/shard_map/ppermute | solution.py:251
  48.4 16.2 %all-to-all-start.2 = ((f32[16,80,128]{2,1,0:T(8,128)}), f32[16,80,128]{2,1,0:T(8,128)S(1)}, u32[]{:S(2)}, u32[]{:S(2)}) async-start(f32[16,80,128]{2,1,0:T(8,128)} %get-tuple-element.29), calls=%async_computation.2 | async-start | bytes 1310720 | tf_op jit(solution)/shard_map/all_to_all | solution.py:269
  52.1 3.0 %collective-permute-start.2 = (f32[56,128]{1,0:T(8,128)S(1)}, f32[56,128]{1,0:T(8,128)S(1)}, u32[]{:S(2)}, u32[]{:S(2)}) collective-permute-start(f32[56,128]{1,0:T(8,128)S(1)} %reduce.1), channel_id=1, source_target_pairs={{0,224},{8,40},{16,48},{24,56},{32,64},{40,8},{48,16},{56,24},{64,... | collective-permute-start | bytes 86024 | tf_op jit(solution)/shard_map/ppermute | solution.py:261
  55.1 14.6 %copy-start.4 = (f32[2,40,128]{2,1,0:T(8,128)S(1)}, f32[2,40,128]{2,1,0:T(8,128)}, u32[]{:S(2)}) copy-start(f32[2,40,128]{2,1,0:T(8,128)} %old.1) | copy-start | bytes 122884
  55.1 5.4 %collective-permute-start.3 = (f32[56,128]{1,0:T(8,128)S(1)}, f32[56,128]{1,0:T(8,128)S(1)}, u32[]{:S(2)}, u32[]{:S(2)}) collective-permute-start(f32[56,128]{1,0:T(8,128)S(1)} %add.6), channel_id=1, source_target_pairs={{0,192},{8,72},{16,80},{24,88},{32,96},{40,104},{48,112},{56,120},... | collective-permute-start | bytes 86024 | tf_op jit(solution)/shard_map/ppermute | solution.py:261
  64.6 7.3 %collective-permute-start.4 = (f32[56,128]{1,0:T(8,128)S(1)}, f32[56,128]{1,0:T(8,128)S(1)}, u32[]{:S(2)}, u32[]{:S(2)}) collective-permute-start(f32[56,128]{1,0:T(8,128)S(1)} %add.7.one), channel_id=1, source_target_pairs={{0,64},{8,200},{16,208},{24,216},{32,224},{40,232},{48,240},{56,24... | collective-permute-start | bytes 86024 | tf_op jit(solution)/shard_map/ppermute | solution.py:261
  86.1 4.6 %collective-permute-start.5 = (f32[16,32,128]{2,1,0:T(8,128)S(1)}, f32[16,32,128]{2,1,0:T(8,128)S(1)}, u32[]{:S(2)}, u32[]{:S(2)}) collective-permute-start(f32[16,32,128]{2,1,0:T(8,128)S(1)} %all_to_all.21.mine), channel_id=1, source_target_pairs={{0,8},{8,0},{16,24},{24,16},{32,40},{40,32},{48,56},{56,48},{64,72... | collective-permute-start | bytes 786440 | tf_op jit(solution)/shard_map/ppermute | solution.py:251

commit v8 on v7

--- a/solution.py
+++ b/solution.py
@@ -12,6 +12,7 @@
 TILES = 32
 SPARE = 48
 PIECE = 56
+LINES = 136
 SMEM = pltpu.MemorySpace.SMEM
 VMEM = pltpu.MemorySpace.VMEM
 
@@ -20,10 +21,13 @@
     counter = np.arange(WIN)
     angles = 2.0 * np.pi / WIN * (counter[:, None] * counter[None, :] % WIN)
     cos, sin = np.cos(angles) / np.sqrt(WIN), np.sin(angles) / np.sqrt(WIN)
-    both = np.concatenate([cos, sin], axis=0)
+    both = np.concatenate([cos[:LANES], cos[LANES : LANES + 1], sin[1:LANES]], axis=0)
+    order = np.concatenate([counter[: LANES + 1], counter[:LANES:-1]])
     high = both.astype(ml_dtypes.bfloat16)
     low = (both - high.astype(np.float64)).astype(ml_dtypes.bfloat16)
-    return high, low
+    select = (order[:, None] == counter[None, :]).astype(ml_dtypes.bfloat16)
+    rows = np.concatenate([high, low, select], axis=0)
+    return rows, np.concatenate([high.T, low.T, select.T], axis=0)
 
 
 def halves(value):
@@ -32,25 +36,67 @@
     return high, low
 
 
+def dot(left, right):
+    return jnp.dot(left, right, preferred_element_type=jnp.float32)
+
+
 def product(left, right):
-    def dot(a, b):
-        return jnp.dot(a, b, preferred_element_type=jnp.float32)
-
     return dot(left[0], right[0]) + dot(left[0], right[1]) + dot(left[1], right[0])
 
 
-def transform(real, imag, tall, wide, sign):
-    cols = product(tall, halves(jnp.concatenate([real, imag], axis=1)))
-    left_real = cols[:WIN, :WIN] - sign * cols[WIN:, WIN:]
-    left_imag = cols[:WIN, WIN:] + sign * cols[WIN:, :WIN]
-    rows = product(halves(jnp.concatenate([left_real, left_imag], axis=0)), wide)
-    right_real = rows[:WIN, :WIN] - sign * rows[WIN:, WIN:]
-    right_imag = rows[WIN:, :WIN] + sign * rows[:WIN, WIN:]
-    return right_real, right_imag
+def unfold(cos_real, cos_imag, sin_real, sin_imag, axis):
+    zeroth = lax.broadcasted_iota(jnp.int32, cos_real.shape, axis) == 0
+    odd_real, odd_imag = jnp.where(zeroth, 0.0, sin_imag), jnp.where(zeroth, 0.0, sin_real)
+    low = cos_real + odd_real, cos_imag - odd_imag
+    high = (
+        jnp.where(zeroth, sin_real, cos_real - odd_real),
+        jnp.where(zeroth, sin_imag, cos_imag + odd_imag),
+    )
+    return tuple(jnp.concatenate(pair, axis=axis) for pair in zip(low, high))
+
+
+def fold(real, imag, axis):
+    if axis == 0:
+        (low_r, high_r), (low_i, high_i) = ((v[:LANES], v[LANES:]) for v in (real, imag))
+    else:
+        (low_r, high_r), (low_i, high_i) = ((v[:, :LANES], v[:, LANES:]) for v in (real, imag))
+    zeroth = lax.broadcasted_iota(jnp.int32, low_r.shape, axis) == 0
+    even = (low_r + jnp.where(zeroth, 0.0, high_r), low_i + jnp.where(zeroth, 0.0, high_i))
+    odd = (jnp.where(zeroth, high_r, high_i - low_i), jnp.where(zeroth, high_i, low_r - high_r))
+    return tuple(jnp.concatenate(pair, axis=axis) for pair in zip(even, odd))
+
+
+def parts(table):
+    return table[0:WIN], table[WIN : 2 * WIN]
+
+
+def forward(real, imag, rows, cols):
+    along = product(parts(rows), halves(jnp.concatenate([real, imag], axis=1)))
+    real, imag = unfold(
+        along[:LANES, :WIN], along[:LANES, WIN:], along[LANES:, :WIN], along[LANES:, WIN:], 0
+    )
+    across = product(halves(jnp.concatenate([real, imag], axis=0)), parts(cols))
+    return unfold(
+        across[:WIN, :LANES], across[WIN:, :LANES], across[:WIN, LANES:], across[WIN:, LANES:], 1
+    )
+
+
+def inverse(real, imag, rows, cols):
+    real, imag = fold(real, imag, 0)
+    along = product(parts(cols), halves(jnp.concatenate([real, imag], axis=1)))
+    real, imag = fold(along[:, :WIN], along[:, WIN:], 1)
+    across = product(halves(jnp.concatenate([real, imag], axis=0)), parts(rows))
+    return across[:WIN], across[WIN:]
+
+
+def reordered(value, rows, cols):
+    taken = dot(rows[2 * WIN :], jnp.concatenate(halves(value), axis=1)).astype(jnp.bfloat16)
+    taken = dot(jnp.concatenate([taken[:, :WIN], taken[:, WIN:]], axis=0), cols[2 * WIN :])
+    return taken[:WIN] + taken[WIN:]
 
 
 def window_kernel(
-    place, stack, near, probe, amps, high, low, keep, keep_grad, send, field, grads, sums
+    place, stack, near, probe, amps, row_table, col_table, keep, send, field, grads, sums
 ):
     row, col = place[2], place[3]
     live = place[4].astype(jnp.float32)
@@ -59,10 +105,10 @@
     for member in range(8):
         lines = slice(member * 40, member * 40 + 40)
         for part in range(2):
-            rows = slice(part * 40, part * 40 + 40)
-            field[part, 1, lines, :] = stack[8 - 8 * odd + member, rows, :]
-            field[part, 2 * odd, lines, :] = jnp.where(inside, stack[8 * odd + member, rows, :], 0.0)
-            field[part, 2 - 2 * odd, lines, :] = near[8 * odd + member, rows, :]
+            held = slice(part * 40, part * 40 + 40)
+            field[part, 1, lines, :] = stack[8 - 8 * odd + member, held, :]
+            field[part, 2 * odd, lines, :] = jnp.where(inside, stack[8 * odd + member, held, :], 0.0)
+            field[part, 2 - 2 * odd, lines, :] = near[8 * odd + member, held, :]
     lane = lax.broadcasted_iota(jnp.int32, (WIN, LANES), 1)
     back = lax.rem(LANES - col, LANES)
     ahead = lax.rem(col, LANES)
@@ -80,12 +126,11 @@
     probe_real, probe_imag = probe[0], probe[1]
     exit_real = probe_real * sample_real - probe_imag * sample_imag
     exit_imag = probe_real * sample_imag + probe_imag * sample_real
-    tall = (high[...], low[...])
-    wide = tuple(jnp.concatenate([table[:WIN], table[WIN:]], axis=1) for table in tall)
-    far_real, far_imag = transform(exit_real, exit_imag, tall, wide, -1.0)
+    rows, cols = row_table[...], col_table[...]
+    far_real, far_imag = forward(exit_real, exit_imag, rows, cols)
     power = far_real * far_real + far_imag * far_imag
-    factor = 1.0 - amps[0] * lax.rsqrt(jnp.maximum(power, 0.0625))
-    miss_real, miss_imag = transform(far_real * factor, far_imag * factor, tall, wide, 1.0)
+    factor = 1.0 - reordered(amps[0], rows, cols) * lax.rsqrt(jnp.maximum(power, 0.0625))
+    miss_real, miss_imag = inverse(far_real * factor, far_imag * factor, rows, cols)
     miss_real = miss_real * live
     miss_imag = miss_imag * live
     terms = (
@@ -137,29 +182,29 @@
     for member in range(8):
         lines = slice(member * 40, member * 40 + 40)
         for part in range(2):
-            put = part * 40
-            keep_grad[8 - 8 * odd + member, put : put + 40, :] = grads[part, 1, lines, :]
-            keep_grad[8 * odd + member, put : put + 40, :] = jnp.where(
+            put = PIECE + part * 40
+            keep[8 - 8 * odd + member, put : put + 40, :] = grads[part, 1, lines, :]
+            keep[8 * odd + member, put : put + 40, :] = jnp.where(
                 inside, grads[part, 2 * odd, lines, :], 0.0
             )
             put = 16 * PIECE + member * 80 + part * 40
             send[put : put + 40, :] = grads[part, 2 - 2 * odd, lines, :]
 
 
-def merge_kernel(place, keep, keep_grad, got, out, out_grad):
+def merge_kernel(place, keep, got, out):
     for member in range(16):
-        out[member] = keep[member] + got[member * PIECE : (member + 1) * PIECE, :]
+        out[member, :PIECE, :] = keep[member, :PIECE, :] + got[member * PIECE : (member + 1) * PIECE, :]
     mine = 8 - 8 * (place[0] & 1)
     for member in range(8):
         put = 16 * PIECE + member * 80
-        out_grad[mine + member] = keep_grad[mine + member] + got[put : put + 80, :]
-        out_grad[8 - mine + member] = keep_grad[8 - mine + member]
+        out[mine + member, PIECE:, :] = keep[mine + member, PIECE:, :] + got[put : put + 80, :]
+        out[8 - mine + member, PIECE:, :] = keep[8 - mine + member, PIECE:, :]
 
 
 def reduce_kernel(pieces, out):
-    total = pieces[0]
+    total = pieces[0, :PIECE, :]
     for member in range(1, 16):
-        total = total + pieces[member]
+        total = total + pieces[member, :PIECE, :]
     out[...] = total
 
 
@@ -178,17 +223,20 @@
                 out[member, lines : lines + 8, :] = new
 
 
-def gather_kernel(place, mine, other, out):
-    half = half_of(place[0])
-    for source, which in ((mine, half), (other, 1 - half)):
-        for member in range(16):
-            top = pl.multiple_of(which * 128 + member * 8, 8)
-            for part in range(2):
-                for side in range(2):
-                    lines = part * 16 + side * 8
-                    out[part, pl.ds(top, 8), side * LANES : (side + 1) * LANES] = source[
-                        member, lines : lines + 8, :
-                    ]
+def gather_kernel(place, which, source, *refs):
+    out, block, sem = refs[-3:]
+    half = half_of(place[0]) ^ which
+    for member in range(16):
+        for part in range(2):
+            for side in range(2):
+                lines = part * 16 + side * 8
+                block[part, member * 8 : member * 8 + 8, side * LANES : (side + 1) * LANES] = source[
+                    member, lines : lines + 8, :
+                ]
+    rows = pl.ds(pl.multiple_of(half * 128, 128), 128)
+    copy = pltpu.make_async_copy(block, out.at[:, rows, :], sem)
+    copy.start()
+    copy.wait()
 
 
 def shine(light, group, total, at, block):
@@ -215,12 +263,12 @@
     peak[...] = jnp.full((8, LANES), jnp.max(most), jnp.float32)
 
 
-def object_kernel(place, pieces, grads, old, light, peak, out, at, sem):
+def object_kernel(place, pieces, old, light, peak, out, at, sem):
     copy = pltpu.make_async_copy(pieces.at[:, SPARE : SPARE + 1, :], at, sem)
     copy.start()
-    gradient = grads[0]
+    gradient = pieces[0, PIECE:, :]
     for member in range(1, 16):
-        gradient = gradient + grads[member]
+        gradient = gradient + pieces[member, PIECE:, :]
     copy.wait()
     odd = place[0] & 1
     mine = 8 - 8 * odd
@@ -287,7 +335,7 @@
 
 def local(object_field, probe_field, amplitudes, row_start, column_start, live_slots):
     smem, vmem = pl.BlockSpec(memory_space=SMEM), pl.BlockSpec(memory_space=VMEM)
-    high, low = (on_chip(jnp.asarray(table)) for table in split_tables())
+    row_table, col_table = (on_chip(jnp.asarray(table)) for table in split_tables())
     probe = on_chip(probe_field)
 
     def buffer(*dims):
@@ -296,7 +344,7 @@
     own = object_field.reshape(80, LANES)
     here = [lax.axis_index(axis)[None].astype(jnp.int32) for axis in ("tile", "group")]
     place = jnp.concatenate([*here, row_start, column_start, live_slots])
-    stack, place = lax.optimization_barrier((exchange(jnp.broadcast_to(own, (16, 80, LANES))), place))
+    stack = exchange(jnp.broadcast_to(own, (16, 80, LANES)))
     light, peak = kernel_call(
         prep_kernel,
         (buffer(4, 384, LANES), buffer(8, LANES)),
@@ -305,54 +353,62 @@
         4,
         cost_estimate=pl.CostEstimate(flops=300000, bytes_accessed=2000000, transcendentals=0),
     )(probe)
-    keep, keep_grad, send = kernel_call(
+    keep, send = kernel_call(
         window_kernel,
-        (buffer(16, PIECE, LANES), buffer(16, 80, LANES), buffer(16 * PIECE + 640, LANES)),
+        (buffer(16, LINES, LANES), buffer(16 * PIECE + 640, LANES)),
         [smem] + [vmem] * 6,
-        (vmem,) * 3,
+        (vmem,) * 2,
         24,
         scratch_shapes=[buffer(2, 3, 320, LANES), buffer(2, 3, 320, LANES), buffer(3, WIN, WIN)],
     )(
-        place, on_chip(stack), on_chip(swap_cores(stack)), probe, on_chip(amplitudes), high, low
+        place, on_chip(stack), on_chip(swap_cores(stack)), probe, on_chip(amplitudes),
+        row_table, col_table,
     )
 
     got, light = lax.optimization_barrier((swap_cores(send), light))
-    sums, grads = kernel_call(
-        merge_kernel,
-        (buffer(16, PIECE, LANES), buffer(16, 80, LANES)),
-        [smem] + [vmem] * 3,
-        (vmem,) * 2,
-        4,
-    )(place, keep, keep_grad, on_chip(got))
-    pieces = exchange(sums)
+    merged = kernel_call(merge_kernel, buffer(16, LINES, LANES), [smem] + [vmem] * 2, vmem, 4)(
+        place, keep, on_chip(got)
+    )
+    pieces = exchange(merged)
     total = kernel_call(reduce_kernel, buffer(PIECE, LANES), [vmem], vmem, 4)(on_chip(pieces))
-    total, grads = lax.optimization_barrier((total, grads))
-    grads = exchange(grads)
-    for mask in (1, 2):
-        total = total + swap_z(total, mask)
-    total, grads = lax.optimization_barrier((total, grads))
     new_object = kernel_call(
         object_kernel,
         jax.ShapeDtypeStruct((2, 40, LANES), jnp.float32),
-        [smem] + [vmem] * 5,
+        [smem] + [vmem] * 4,
         vmem,
-        8,
+        4,
         scratch_shapes=[pltpu.SMEM((16, 1, LANES), jnp.float32), pltpu.SemaphoreType.DMA],
         cost_estimate=pl.CostEstimate(flops=700000, bytes_accessed=2000000, transcendentals=0),
-    )(place, on_chip(pieces), on_chip(grads), on_chip(object_field), on_chip(light), peak)
+    )(place, on_chip(pieces), on_chip(object_field), on_chip(light), peak)
+    for mask in (1, 2):
+        total = total + swap_z(total, mask)
     got, new_object = lax.optimization_barrier((swap_z(total, 6), new_object))
     piece = kernel_call(probe_kernel, buffer(16, 32, LANES), [smem] + [vmem] * 3, vmem, 4)(
         place, on_chip(total), on_chip(got), probe
     )
 
     mine = exchange(piece)
-    new_probe = kernel_call(
-        gather_kernel,
-        jax.ShapeDtypeStruct((2, WIN, WIN), jnp.float32),
-        [smem] + [vmem] * 2,
-        vmem,
-        4,
-    )(place, on_chip(mine), on_chip(swap_cores(mine)))
+    other = swap_cores(mine)
+    hbm = pl.BlockSpec(memory_space=pltpu.MemorySpace.HBM)
+
+    def put(which, source, *before):
+        def gather_half_kernel(place, *refs):
+            gather_kernel(place, which, *refs)
+
+        return kernel_call(
+            gather_half_kernel,
+            pltpu.HBM((2, WIN, WIN), jnp.float32),
+            [smem, vmem] + [hbm] * len(before),
+            hbm,
+            4,
+            scratch_shapes=[buffer(2, WIN // 2, WIN), pltpu.SemaphoreType.DMA],
+            input_output_aliases={2: 0} if before else {},
+            cost_estimate=pl.CostEstimate(flops=0, bytes_accessed=1000000, transcendentals=0),
+        )(place, on_chip(source), *before)
+
+    first_half = put(0, mine)
+    other, first_half = lax.optimization_barrier((other, first_half))
+    new_probe = put(1, other, first_half)
     return new_object, new_probe
 
 

time: 93.9 us -> 87.1 us (0.928); the launches traced: 92.1 us -> 86.9 us
  blocking collectives: 27.2 us -> 58.6 us
  starting transfers between devices: 27.9 us -> 9.02 us
  waiting for transfers between devices: 22.4 us -> 5.78 us
    all_to_all x2 -> x3, blocking collectives: 27.2 us -> 58.6 us  [exchange(): lax.all_to_all(value, ('tile', 'group'), 0, 0, axis_index_groups=groups)]
    all_to_all x2 -> x0, waiting for transfers between devices: 14.6 us -> none  [exchange(): lax.all_to_all(value, ('tile', 'group'), 0, 0, axis_index_groups=groups)]
    all_to_all x2 -> x0, starting transfers between devices: 11.9 us -> none  [exchange(): lax.all_to_all(value, ('tile', 'group'), 0, 0, axis_index_groups=groups)]
    ppermute x3, starting transfers between devices: 5.73 us -> 1.55 us  [swap_cores(): return lax.ppermute(value, 'tile', [(i, i ^ 1) for i in range(TILES)])]
    ppermute x3, starting transfers between devices: 10.3 us -> 7.47 us  [swap_z(): return lax.ppermute(value, 'tile', pairs)]
    ppermute x3, waiting for transfers between devices: 4.56 us -> 2 us  [swap_cores(): return lax.ppermute(value, 'tile', [(i, i ^ 1) for i in range(TILES)])]
    pallas_call x3 -> x4, Pallas kernels: 7.12 us -> 6.58 us  [the longest x1 3.39 us: local(): kernel_call(window_kernel, (buffer(16, LINES, LANES), buffer(16 * PIECE +...]
  transfers between devices with their start and end apart: 8 -> 6, of which waited for: 7 -> 3; matrix products, arithmetic and copies ran while one was open for 0% -> 0% of each run, Pallas kernels for 3% -> 4%
where the time goes in v8:
time: 87.1 us; the launch traced here: 86.9 us
  blocking collectives  58.6 us (67%)
  Pallas kernels  9.71 us (11%)
  starting transfers between devices  9.02 us (10%)
  waiting for transfers between devices  5.78 us (7%)
  between operations  2.7 us (3%)
  local copies, waits for them, and re-layouts  1.04 us (1%)
    all_to_all x3, blocking collectives, exchange(): lax.all_to_all(value, ('tile', 'group'), 0, 0, axis_index_groups=groups)  58.6 us
    ppermute x3, starting transfers between devices, swap_z(): return lax.ppermute(value, 'tile', pairs)  7.47 us
    ppermute x3, waiting for transfers between devices, swap_z(): return lax.ppermute(value, 'tile', pairs)  3.78 us
    pallas_call x1, Pallas kernels, local(): kernel_call(window_kernel, (buffer(16, LINES, LANES), buffer(16 * PIECE +...  3.39 us
    pallas_call x2, Pallas kernels, put(): kernel_call(gather_half_kernel, pltpu.HBM((2, WIN, WIN), jnp.float32), [s...  2.54 us
    pallas_call x1, Pallas kernels, local(): kernel_call(object_kernel, jax.ShapeDtypeStruct((2, 40, LANES), jnp.float...  2.18 us
    ppermute x3, waiting for transfers between devices, swap_cores(): return lax.ppermute(value, 'tile', [(i, i ^ 1) for i in range(TILES)])  2 us
  transfers between devices with their start and end apart: 6, of which 3 were waited for; matrix products, arithmetic and copies ran while one was open for 0% of the time, Pallas kernels for 4%

profile of v8, /device:TPU:1, one launch (start us, length us, event | category | flops | bytes accessed | tf_op | source)
XLA Modules:
  0.0 86.9 jit_solution(1251270700131286741)
XLA Ops:
  0.6 0.0 copy-start.1
  0.6 0.0 copy-start.2
  0.7 0.0 copy-start
  0.7 0.0 copy-start.3
  0.7 0.9 %broadcast_in_dim.11 = f32[16,80,128]{2,1,0:T(8,128)S(1)} broadcast(f32[80,128]{1,0:T(8,128)} %bitcast.3), dimensions={1,2} | broadcast | bytes 696320 | tf_op jit(solution)/shard_map/broadcast_in_dim | solution.py:347
  1.6 21.5 %all_to_all.15.stack = f32[16,80,128]{2,1,0:T(8,128)S(1)} all-to-all(f32[16,80,128]{2,1,0:T(8,128)S(1)} %broadcast_in_dim.11), channel_id=1, replica_groups={{8,9,10,11,12,13,14,15,16,17,18,19,20,21,22,23},{24,25,26,27,28,29,30,3..., dimensions={0} | all-to-all | bytes 1310720 | tf_op jit(solution)/shard_map/all_to_all | solution.py:317
  23.1 0.9 %collective-permute-start = (f32[16,80,128]{2,1,0:T(8,128)S(1)}, f32[16,80,128]{2,1,0:T(8,128)S(1)}, u32[]{:S(2)}, u32[]{:S(2)}) collective-permute-start(f32[16,80,128]{2,1,0:T(8,128)S(1)} %all_to_all.15.stack), channel_id=1, source_target_pairs={{0,8},{8,0},{16,24},{24,16},{32,40},{40,32},{48,56},{56,48},{64,72... | collective-permute-start | bytes 1966088 | tf_op jit(solution)/shard_map/ppermute | solution.py:299
  26.0 0.1 concatenate.3.place
  26.0 0.0 collective-permute-done.near
  26.0 0.0 copy-done.1
  26.0 0.0 copy-done.2
  26.1 0.0 copy-done
  26.1 0.0 copy-done.3
  26.1 3.4 %window.1 = (f32[16,136,128]{2,1,0:T(8,128)S(1)}, f32[1536,128]{1,0:T(8,128)S(1)}) custom-call(s32[5]{0:T(128)S(1)} %concatenate.3.place, f32[16,80,128]{2,1,0:T(8,128)S(1)} %all_to_all.15.stack, f32[16,80,128]{2,1,0:T(8,128)S(1)} %collective-permute-done.near, f32[2,256,256]{2,1,0:T(8,128)S(1)} %copy-done, f32[1,256,256]{2,1,0:T(8,128)S(1)} %copy-done.3, ...), custom_call_target="tpu_custom_call" | custom-call | tf_op jit(solution)/shard_map/window/pallas_call | solution.py:356
  29.5 0.1 collective-permute-start.1
  29.6 0.2 prep.1
  29.8 2.0 %collective-permute-done.1.got = f32[1536,128]{1,0:T(8,128)S(1)} collective-permute-done((f32[1536,128]{1,0:T(8,128)S(1)}, f32[1536,128]{1,0:T(8,128)S(1)}, u32[]{:S(2)}, u32[]{:S(2)}) %collective-permute-start.1) | collective-permute-done | bytes 786464 | tf_op jit(solution)/shard_map/ppermute | solution.py:299
  31.8 0.6 merge.1
  32.5 21.1 %all_to_all.16.pieces = f32[16,136,128]{2,1,0:T(8,128)S(1)} all-to-all(f32[16,136,128]{2,1,0:T(8,128)S(1)} %merge.1), channel_id=1, replica_groups={{8,9,10,11,12,13,14,15,16,17,18,19,20,21,22,23},{24,25,26,27,28,29,30,3..., dimensions={0} | all-to-all | bytes 2228224 | tf_op jit(solution)/shard_map/all_to_all | solution.py:317
  53.6 0.0 copy-start.4
  53.6 0.3 collective-permute-start.2
  53.9 2.5 %collective-permute-done.2 = f32[56,128]{1,0:T(8,128)S(1)} collective-permute-done((f32[56,128]{1,0:T(8,128)S(1)}, f32[56,128]{1,0:T(8,128)S(1)}, u32[]{:S(2)}, u32[]{:S(2)}) %collective-permute-start.2) | collective-permute-done | bytes 28704 | tf_op jit(solution)/shard_map/ppermute | solution.py:309
  56.5 3.1 %collective-permute-start.3 = (f32[56,128]{1,0:T(8,128)S(1)}, f32[56,128]{1,0:T(8,128)S(1)}, u32[]{:S(2)}, u32[]{:S(2)}) collective-permute-start(f32[56,128]{1,0:T(8,128)S(1)} %add.6), channel_id=1, source_target_pairs={{0,192},{8,72},{16,80},{24,88},{32,96},{40,104},{48,112},{56,120},... | collective-permute-start | bytes 86024 | tf_op jit(solution)/shard_map/ppermute | solution.py:309
  59.6 1.3 %collective-permute-done.3 = f32[56,128]{1,0:T(8,128)S(1)} collective-permute-done((f32[56,128]{1,0:T(8,128)S(1)}, f32[56,128]{1,0:T(8,128)S(1)}, u32[]{:S(2)}, u32[]{:S(2)}) %collective-permute-start.3) | collective-permute-done | bytes 28704 | tf_op jit(solution)/shard_map/ppermute | solution.py:309
  60.8 4.1 %collective-permute-start.4 = (f32[56,128]{1,0:T(8,128)S(1)}, f32[56,128]{1,0:T(8,128)S(1)}, u32[]{:S(2)}, u32[]{:S(2)}) collective-permute-start(f32[56,128]{1,0:T(8,128)S(1)} %add.7.one), channel_id=1, source_target_pairs={{0,64},{8,200},{16,208},{24,216},{32,224},{40,232},{48,240},{56,24... | collective-permute-start | bytes 86024 | tf_op jit(solution)/shard_map/ppermute | solution.py:309
  64.9 0.0 copy-done.4
  64.9 2.2 %object.1 = f32[2,40,128]{2,1,0:T(8,128)} custom-call(s32[5]{0:T(128)S(1)} %concatenate.3.place, f32[16,136,128]{2,1,0:T(8,128)S(1)} %all_to_all.16.pieces, f32[2,40,128]{2,1,0:T(8,128)S(1)} %copy-done.4, f32[4,384,128]{2,1,0:T(8,128)S(1)} %get-tuple-element.16.light, f32[8,128]{1,0:T(8,128)S(1)} %get-tuple-element.17.peak), custom_call_target="tpu_custom_call" | custom-call | flops 700000 | bytes 2000000 | tf_op jit(solution)/shard_map/object/pallas_call | solution.py:374
  67.1 0.0 collective-permute-done.4.two
  67.1 0.7 probe.6
  67.8 16.0 %all_to_all.17.refs_0_ = f32[16,32,128]{2,1,0:T(8,128)S(1)} all-to-all(f32[16,32,128]{2,1,0:T(8,128)S(1)} %probe.6), channel_id=1, replica_groups={{8,9,10,11,12,13,14,15,16,17,18,19,20,21,22,23},{24,25,26,27,28,29,30,3..., dimensions={0} | all-to-all | bytes 524288 | tf_op jit(solution)/shard_map/all_to_all | solution.py:317
  83.8 0.5 collective-permute-start.5
  84.3 1.3 %gather_half.2.refs_1_ = f32[2,256,256]{2,1,0:T(8,128)} custom-call(s32[5]{0:T(128)S(1)} %concatenate.3.place, f32[16,32,128]{2,1,0:T(8,128)S(1)} %all_to_all.17.refs_0_), custom_call_target="tpu_custom_call" | custom-call | bytes 1000000 | tf_op jit(solution)/shard_map/gather_half/pallas_call | solution.py:398
  85.6 0.0 collective-permute-done.5.refs_0_
  85.6 1.3 %gather_half.3 = f32[2,256,256]{2,1,0:T(8,128)} custom-call(s32[5]{0:T(128)S(1)} %concatenate.3.place, f32[16,32,128]{2,1,0:T(8,128)S(1)} %collective-permute-done.5.refs_0_, f32[2,256,256]{2,1,0:T(8,128)} %gather_half.2.refs_1_), custom_call_target="tpu_custom_call", output_to_operand_aliasing={{}: (2, {})} | custom-call | bytes 1000000 | tf_op jit(solution)/shard_map/gather_half/pallas_call | solution.py:398
  (3 shorter events, 0.0 us)
Async XLA Ops:
  0.6 25.4 %copy-start.1 = (bf16[768,256]{1,0:T(8,128)(2,1)S(1)}, bf16[768,256]{1,0:T(8,128)(2,1)}, u32[]{:S(2)}) copy-start(bf16[768,256]{1,0:T(8,128)(2,1)} %constant.14.clone.col_table) | copy-start | bytes 1179652
  0.6 25.4 %copy-start.2 = (bf16[768,256]{1,0:T(8,128)(2,1)S(1)}, bf16[768,256]{1,0:T(8,128)(2,1)}, u32[]{:S(2)}) copy-start(bf16[768,256]{1,0:T(8,128)(2,1)} %constant.13.clone.row_table) | copy-start | bytes 1179652
  0.7 25.4 %copy-start = (f32[2,256,256]{2,1,0:T(8,128)S(1)}, f32[2,256,256]{2,1,0:T(8,128)}, u32[]{:S(2)}) copy-start(f32[2,256,256]{2,1,0:T(8,128)} %probe.7) | copy-start | bytes 1572868
  0.7 25.4 %copy-start.3 = (f32[1,256,256]{2,1,0:T(8,128)S(1)}, f32[1,256,256]{2,1,0:T(8,128)}, u32[]{:S(2)}) copy-start(f32[1,256,256]{2,1,0:T(8,128)} %amps.1) | copy-start | bytes 786436
  23.1 2.9 %collective-permute-start = (f32[16,80,128]{2,1,0:T(8,128)S(1)}, f32[16,80,128]{2,1,0:T(8,128)S(1)}, u32[]{:S(2)}, u32[]{:S(2)}) collective-permute-start(f32[16,80,128]{2,1,0:T(8,128)S(1)} %all_to_all.15.stack), channel_id=1, source_target_pairs={{0,8},{8,0},{16,24},{24,16},{32,40},{40,32},{48,56},{56,48},{64,72... | collective-permute-start | bytes 1966088 | tf_op jit(solution)/shard_map/ppermute | solution.py:299
  29.5 2.4 %collective-permute-start.1 = (f32[1536,128]{1,0:T(8,128)S(1)}, f32[1536,128]{1,0:T(8,128)S(1)}, u32[]{:S(2)}, u32[]{:S(2)}) collective-permute-start(f32[1536,128]{1,0:T(8,128)S(1)} %get-tuple-element.13), channel_id=1, source_target_pairs={{0,8},{8,0},{16,24},{24,16},{32,40},{40,32},{48,56},{56,48},{64,72... | collective-permute-start | bytes 2359304 | tf_op jit(solution)/shard_map/ppermute | solution.py:299
  53.6 11.3 %copy-start.4 = (f32[2,40,128]{2,1,0:T(8,128)S(1)}, f32[2,40,128]{2,1,0:T(8,128)}, u32[]{:S(2)}) copy-start(f32[2,40,128]{2,1,0:T(8,128)} %old.1) | copy-start | bytes 122884
  53.6 2.8 %collective-permute-start.2 = (f32[56,128]{1,0:T(8,128)S(1)}, f32[56,128]{1,0:T(8,128)S(1)}, u32[]{:S(2)}, u32[]{:S(2)}) collective-permute-start(f32[56,128]{1,0:T(8,128)S(1)} %reduce.1), channel_id=1, source_target_pairs={{0,224},{8,40},{16,48},{24,56},{32,64},{40,8},{48,16},{56,24},{64,... | collective-permute-start | bytes 86024 | tf_op jit(solution)/shard_map/ppermute | solution.py:309
  56.5 4.4 %collective-permute-start.3 = (f32[56,128]{1,0:T(8,128)S(1)}, f32[56,128]{1,0:T(8,128)S(1)}, u32[]{:S(2)}, u32[]{:S(2)}) collective-permute-start(f32[56,128]{1,0:T(8,128)S(1)} %add.6), channel_id=1, source_target_pairs={{0,192},{8,72},{16,80},{24,88},{32,96},{40,104},{48,112},{56,120},... | collective-permute-start | bytes 86024 | tf_op jit(solution)/shard_map/ppermute | solution.py:309
  60.8 6.3 %collective-permute-start.4 = (f32[56,128]{1,0:T(8,128)S(1)}, f32[56,128]{1,0:T(8,128)S(1)}, u32[]{:S(2)}, u32[]{:S(2)}) collective-permute-start(f32[56,128]{1,0:T(8,128)S(1)} %add.7.one), channel_id=1, source_target_pairs={{0,64},{8,200},{16,208},{24,216},{32,224},{40,232},{48,240},{56,24... | collective-permute-start | bytes 86024 | tf_op jit(solution)/shard_map/ppermute | solution.py:309
  83.8 1.8 %collective-permute-start.5 = (f32[16,32,128]{2,1,0:T(8,128)S(1)}, f32[16,32,128]{2,1,0:T(8,128)S(1)}, u32[]{:S(2)}, u32[]{:S(2)}) collective-permute-start(f32[16,32,128]{2,1,0:T(8,128)S(1)} %all_to_all.17.refs_0_), channel_id=1, source_target_pairs={{0,8},{8,0},{16,24},{24,16},{32,40},{40,32},{48,56},{56,48},{64,72... | collective-permute-start | bytes 786440 | tf_op jit(solution)/shard_map/ppermute | solution.py:299

commit v9 on v8

--- a/solution.py
+++ b/solution.py
@@ -96,12 +96,14 @@
 
 
 def window_kernel(
-    place, stack, near, probe, amps, row_table, col_table, keep, send, field, grads, sums
+    row_ref, col_ref, live_ref, stack, near, probe, amps, row_table, col_table,
+    keep, send, field, grads, sums,
 ):
-    row, col = place[2], place[3]
-    live = place[4].astype(jnp.float32)
-    odd, half = place[0] & 1, half_of(place[0])
-    inside = far_exists(place[0])
+    row, col = row_ref[0], col_ref[0]
+    live = live_ref[0].astype(jnp.float32)
+    tile, _ = my_place()
+    odd, half = tile & 1, half_of(tile)
+    inside = far_exists(tile)
     for member in range(8):
         lines = slice(member * 40, member * 40 + 40)
         for part in range(2):
@@ -191,10 +193,10 @@
             send[put : put + 40, :] = grads[part, 2 - 2 * odd, lines, :]
 
 
-def merge_kernel(place, keep, got, out):
+def merge_kernel(keep, got, out):
     for member in range(16):
         out[member, :PIECE, :] = keep[member, :PIECE, :] + got[member * PIECE : (member + 1) * PIECE, :]
-    mine = 8 - 8 * (place[0] & 1)
+    mine = 8 - 8 * (my_place()[0] & 1)
     for member in range(8):
         put = 16 * PIECE + member * 80
         out[mine + member, PIECE:, :] = keep[mine + member, PIECE:, :] + got[put : put + 80, :]
@@ -205,13 +207,16 @@
     total = pieces[0, :PIECE, :]
     for member in range(1, 16):
         total = total + pieces[member, :PIECE, :]
-    out[...] = total
-
-
-def probe_kernel(place, one, two, probe, out):
-    odd = place[0] & 1
-    top = pl.multiple_of(half_of(place[0]) * 128 + (8 - 8 * odd + place[1]) * 8, 8)
-    summed = one[...] + two[...]
+    for layer in range(8):
+        out[layer] = total
+
+
+def probe_kernel(layers, probe, out):
+    tile, group = my_place()
+    top = pl.multiple_of(half_of(tile) * 128 + (8 - 8 * (tile & 1) + group) * 8, 8)
+    summed = layers[0]
+    for layer in range(1, 8):
+        summed = summed + layers[layer]
     mean = jnp.sum(summed[SPARE + 1 : SPARE + 2]) * (1.0 / (WIN * WIN))
     for side in range(2):
         bottom = summed[32 + side * 8 : 40 + side * 8] + 0.25 * mean + 1e-05
@@ -223,20 +228,17 @@
                 out[member, lines : lines + 8, :] = new
 
 
-def gather_kernel(place, which, source, *refs):
-    out, block, sem = refs[-3:]
-    half = half_of(place[0]) ^ which
-    for member in range(16):
-        for part in range(2):
-            for side in range(2):
-                lines = part * 16 + side * 8
-                block[part, member * 8 : member * 8 + 8, side * LANES : (side + 1) * LANES] = source[
-                    member, lines : lines + 8, :
-                ]
-    rows = pl.ds(pl.multiple_of(half * 128, 128), 128)
-    copy = pltpu.make_async_copy(block, out.at[:, rows, :], sem)
-    copy.start()
-    copy.wait()
+def gather_kernel(mine, other, out):
+    half = half_of(my_place()[0])
+    for source, which in ((mine, half), (other, 1 - half)):
+        for member in range(16):
+            top = pl.multiple_of(which * 128 + member * 8, 8)
+            for part in range(2):
+                for side in range(2):
+                    lines = part * 16 + side * 8
+                    out[part, pl.ds(top, 8), side * LANES : (side + 1) * LANES] = source[
+                        member, lines : lines + 8, :
+                    ]
 
 
 def shine(light, group, total, at, block):
@@ -263,14 +265,15 @@
     peak[...] = jnp.full((8, LANES), jnp.max(most), jnp.float32)
 
 
-def object_kernel(place, pieces, old, light, peak, out, at, sem):
+def object_kernel(pieces, old, light, peak, out, at, sem):
     copy = pltpu.make_async_copy(pieces.at[:, SPARE : SPARE + 1, :], at, sem)
     copy.start()
     gradient = pieces[0, PIECE:, :]
     for member in range(1, 16):
         gradient = gradient + pieces[member, PIECE:, :]
     copy.wait()
-    odd = place[0] & 1
+    tile, group = my_place()
+    odd = tile & 1
     mine = 8 - 8 * odd
     total = jnp.zeros((40, LANES), jnp.float32)
     outside = jnp.zeros((40, LANES), jnp.float32)
@@ -278,15 +281,19 @@
         for core in range(2):
             block = 1 - core * (1 - odd) + (1 - core) * odd
             seen = [at[mine + member, 0, core * 8 + k] for k in range(3)]
-            total = shine(light, place[1], total, seen, block)
+            total = shine(light, group, total, seen, block)
         seen = [at[8 - mine + member, 0, (1 - odd) * 8 + k] for k in range(3)]
-        outside = shine(light, place[1], outside, seen, 2 - 2 * odd)
-    total = total + jnp.where(far_exists(place[0]), outside, 0.0)
+        outside = shine(light, group, outside, seen, 2 - 2 * odd)
+    total = total + jnp.where(far_exists(tile), outside, 0.0)
     bottom = total + 0.25 * (peak[0:1, :] + 1e-06)
     for part in range(2):
         out[part] = old[part] - gradient[part * 40 : part * 40 + 40, :] / bottom
 
 
+def my_place():
+    return lax.axis_index("tile"), lax.axis_index("group")
+
+
 def half_of(tile):
     return (tile ^ (tile >> 1)) & 1
 
@@ -299,14 +306,9 @@
     return lax.ppermute(value, "tile", [(i, i ^ 1) for i in range(TILES)])
 
 
-def swap_z(value, mask):
-    pairs = []
-    for tile in range(TILES):
-        layer, rest = divmod(tile, 4)
-        ahead = 1 if rest == 0 else 0
-        other = (((layer - ahead) % (TILES // 4)) ^ mask) + ahead
-        pairs.append((tile, other % (TILES // 4) * 4 + rest))
-    return lax.ppermute(value, "tile", pairs)
+def exchange_z(value):
+    groups = [[4 * layer + rest for layer in range(TILES // 4)] for rest in range(4)]
+    return lax.all_to_all(value, "tile", 0, 0, axis_index_groups=groups)
 
 
 def exchange(value):
@@ -342,8 +344,6 @@
         return pltpu.VMEM(dims, jnp.float32)
 
     own = object_field.reshape(80, LANES)
-    here = [lax.axis_index(axis)[None].astype(jnp.int32) for axis in ("tile", "group")]
-    place = jnp.concatenate([*here, row_start, column_start, live_slots])
     stack = exchange(jnp.broadcast_to(own, (16, 80, LANES)))
     light, peak = kernel_call(
         prep_kernel,
@@ -356,59 +356,38 @@
     keep, send = kernel_call(
         window_kernel,
         (buffer(16, LINES, LANES), buffer(16 * PIECE + 640, LANES)),
-        [smem] + [vmem] * 6,
+        [smem] * 3 + [vmem] * 6,
         (vmem,) * 2,
         24,
         scratch_shapes=[buffer(2, 3, 320, LANES), buffer(2, 3, 320, LANES), buffer(3, WIN, WIN)],
     )(
-        place, on_chip(stack), on_chip(swap_cores(stack)), probe, on_chip(amplitudes),
-        row_table, col_table,
+        row_start, column_start, live_slots, on_chip(stack), on_chip(swap_cores(stack)), probe,
+        on_chip(amplitudes), row_table, col_table,
     )
 
     got, light = lax.optimization_barrier((swap_cores(send), light))
-    merged = kernel_call(merge_kernel, buffer(16, LINES, LANES), [smem] + [vmem] * 2, vmem, 4)(
-        place, keep, on_chip(got)
+    merged = kernel_call(merge_kernel, buffer(16, LINES, LANES), [vmem] * 2, vmem, 4)(
+        keep, on_chip(got)
     )
     pieces = exchange(merged)
-    total = kernel_call(reduce_kernel, buffer(PIECE, LANES), [vmem], vmem, 4)(on_chip(pieces))
+    total = kernel_call(reduce_kernel, buffer(8, PIECE, LANES), [vmem], vmem, 4)(on_chip(pieces))
+    piece = kernel_call(probe_kernel, buffer(16, 32, LANES), [vmem] * 2, vmem, 4)(
+        on_chip(exchange_z(total)), probe
+    )
+
+    mine, pieces = lax.optimization_barrier((exchange(piece), pieces))
     new_object = kernel_call(
         object_kernel,
         jax.ShapeDtypeStruct((2, 40, LANES), jnp.float32),
-        [smem] + [vmem] * 4,
+        [vmem] * 4,
         vmem,
         4,
         scratch_shapes=[pltpu.SMEM((16, 1, LANES), jnp.float32), pltpu.SemaphoreType.DMA],
         cost_estimate=pl.CostEstimate(flops=700000, bytes_accessed=2000000, transcendentals=0),
-    )(place, on_chip(pieces), on_chip(object_field), on_chip(light), peak)
-    for mask in (1, 2):
-        total = total + swap_z(total, mask)
-    got, new_object = lax.optimization_barrier((swap_z(total, 6), new_object))
-    piece = kernel_call(probe_kernel, buffer(16, 32, LANES), [smem] + [vmem] * 3, vmem, 4)(
-        place, on_chip(total), on_chip(got), probe
-    )
-
-    mine = exchange(piece)
-    other = swap_cores(mine)
-    hbm = pl.BlockSpec(memory_space=pltpu.MemorySpace.HBM)
-
-    def put(which, source, *before):
-        def gather_half_kernel(place, *refs):
-            gather_kernel(place, which, *refs)
-
-        return kernel_call(
-            gather_half_kernel,
-            pltpu.HBM((2, WIN, WIN), jnp.float32),
-            [smem, vmem] + [hbm] * len(before),
-            hbm,
-            4,
-            scratch_shapes=[buffer(2, WIN // 2, WIN), pltpu.SemaphoreType.DMA],
-            input_output_aliases={2: 0} if before else {},
-            cost_estimate=pl.CostEstimate(flops=0, bytes_accessed=1000000, transcendentals=0),
-        )(place, on_chip(source), *before)
-
-    first_half = put(0, mine)
-    other, first_half = lax.optimization_barrier((other, first_half))
-    new_probe = put(1, other, first_half)
+    )(on_chip(pieces), on_chip(object_field), on_chip(light), peak)
+    new_probe = kernel_call(
+        gather_kernel, jax.ShapeDtypeStruct((2, WIN, WIN), jnp.float32), [vmem] * 2, vmem, 4
+    )(on_chip(mine), on_chip(swap_cores(mine)))
     return new_object, new_probe
 
 

time: 87.1 us -> 87.5 us (level)
  blocking collectives: 58.6 us -> 72.6 us
  starting transfers between devices: 9.02 us -> 3.08 us
  Pallas kernels: 9.71 us -> 5.85 us
  waiting for transfers between devices: 5.78 us -> 1.94 us
    all_to_all x0 -> x1, blocking collectives: none -> 17.2 us  [exchange_z(): return lax.all_to_all(value, 'tile', 0, 0, axis_index_groups=groups)]
    ppermute x3 -> x0, starting transfers between devices: 7.47 us -> none  [swap_z(): return lax.ppermute(value, 'tile', pairs)]
    ppermute x3 -> x0, waiting for transfers between devices: 3.78 us -> none  [swap_z(): return lax.ppermute(value, 'tile', pairs)]
    all_to_all x3, blocking collectives: 58.6 us -> 55.4 us  [exchange(): lax.all_to_all(value, ('tile', 'group'), 0, 0, axis_index_groups=groups)]
    pallas_call x5 -> x4, Pallas kernels: 3.9 us -> 1.13 us  [the longest x1 0.84 us: local(): kernel_call(gather_kernel, jax.ShapeDtypeStruct((2, WIN, WIN), jnp.float3...]
    ppermute x3, starting transfers between devices: 1.55 us -> 3.08 us  [swap_cores(): return lax.ppermute(value, 'tile', [(i, i ^ 1) for i in range(TILES)])]
  transfers between devices with their start and end apart: 6 -> 3, of which waited for: 3 -> 1; matrix products, arithmetic and copies ran while one was open for 0% -> 0% of each run, Pallas kernels for 4% -> 2%
where the time goes in v9:
time: 87.5 us; the launch traced here: 87.2 us
  blocking collectives  72.6 us (83%)
  Pallas kernels  5.85 us (7%)
  starting transfers between devices  3.08 us (4%)
  between operations  2.71 us (3%)
  waiting for transfers between devices  1.94 us (2%)
  local copies, waits for them, and re-layouts  0.96 us (1%)
    all_to_all x3, blocking collectives, exchange(): lax.all_to_all(value, ('tile', 'group'), 0, 0, axis_index_groups=groups)  55.4 us
    all_to_all x1, blocking collectives, exchange_z(): return lax.all_to_all(value, 'tile', 0, 0, axis_index_groups=groups)  17.2 us
    ppermute x3, starting transfers between devices, swap_cores(): return lax.ppermute(value, 'tile', [(i, i ^ 1) for i in range(TILES)])  3.08 us
    pallas_call x1, Pallas kernels, local(): kernel_call(window_kernel, (buffer(16, LINES, LANES), buffer(16 * PIECE +...  2.85 us
    ppermute x3, waiting for transfers between devices, swap_cores(): return lax.ppermute(value, 'tile', [(i, i ^ 1) for i in range(TILES)])  1.94 us
  transfers between devices with their start and end apart: 3, of which 1 were waited for; matrix products, arithmetic and copies ran while one was open for 0% of the time, Pallas kernels for 2%

profile of v9, /device:TPU:1, one launch (start us, length us, event | category | flops | bytes accessed | tf_op | source)
XLA Modules:
  0.0 87.2 jit_solution(12987836008701864642)
XLA Ops:
  0.6 0.0 copy-start.1
  0.6 0.0 copy-start.2
  0.7 0.0 copy-start
  0.7 0.0 copy-start.3
  0.7 0.9 %broadcast_in_dim.3 = f32[16,80,128]{2,1,0:T(8,128)S(1)} broadcast(f32[80,128]{1,0:T(8,128)} %bitcast.1), dimensions={1,2} | broadcast | bytes 696320 | tf_op jit(solution)/shard_map/broadcast_in_dim | solution.py:347
  1.6 21.5 %all_to_all.20.stack = f32[16,80,128]{2,1,0:T(8,128)S(1)} all-to-all(f32[16,80,128]{2,1,0:T(8,128)S(1)} %broadcast_in_dim.3), channel_id=1, replica_groups={{8,9,10,11,12,13,14,15,16,17,18,19,20,21,22,23},{24,25,26,27,28,29,30,3..., dimensions={0} | all-to-all | bytes 1310720 | tf_op jit(solution)/shard_map/all_to_all | solution.py:319
  23.1 0.9 %collective-permute-start = (f32[16,80,128]{2,1,0:T(8,128)S(1)}, f32[16,80,128]{2,1,0:T(8,128)S(1)}, u32[]{:S(2)}, u32[]{:S(2)}) collective-permute-start(f32[16,80,128]{2,1,0:T(8,128)S(1)} %all_to_all.20.stack), channel_id=1, source_target_pairs={{0,8},{8,0},{16,24},{24,16},{32,40},{40,32},{48,56},{56,48},{64,72... | collective-permute-start | bytes 1966088 | tf_op jit(solution)/shard_map/ppermute | solution.py:306
  26.0 0.0 collective-permute-done.near
  26.0 0.0 copy-done.1
  26.0 0.0 copy-done.2
  26.0 0.0 copy-done
  26.0 0.0 copy-done.3
  26.0 2.8 %window.1 = (f32[16,136,128]{2,1,0:T(8,128)S(1)}, f32[1536,128]{1,0:T(8,128)S(1)}) custom-call(s32[1]{0:T(128)S(6)} %copy.10.row_ref, s32[1]{0:T(128)S(6)} %copy.11.col_ref, s32[1]{0:T(128)S(6)} %copy.12.live_ref, f32[16,80,128]{2,1,0:T(8,128)S(1)} %all_to_all.20.stack, f32[16,80,128]{2,1,0:T(8,128)S(1)} %collective-permute-done.near, ...), custom_call_target="tpu_custom_call" | custom-call | tf_op jit(solution)/shard_map/window/pallas_call | solution.py:356
  28.9 0.2 collective-permute-start.1
  29.1 0.2 prep.1
  29.3 1.9 %collective-permute-done.1.got = f32[1536,128]{1,0:T(8,128)S(1)} collective-permute-done((f32[1536,128]{1,0:T(8,128)S(1)}, f32[1536,128]{1,0:T(8,128)S(1)}, u32[]{:S(2)}, u32[]{:S(2)}) %collective-permute-start.1) | collective-permute-done | bytes 786464 | tf_op jit(solution)/shard_map/ppermute | solution.py:306
  31.2 0.1 merge.1
  31.3 21.1 %all_to_all.21.pieces = f32[16,136,128]{2,1,0:T(8,128)S(1)} all-to-all(f32[16,136,128]{2,1,0:T(8,128)S(1)} %merge.1), channel_id=1, replica_groups={{8,9,10,11,12,13,14,15,16,17,18,19,20,21,22,23},{24,25,26,27,28,29,30,3..., dimensions={0} | all-to-all | bytes 2228224 | tf_op jit(solution)/shard_map/all_to_all | solution.py:319
  52.5 0.0 copy-start.4
  52.5 17.2 %all_to_all.22.layers = f32[8,56,128]{2,1,0:T(8,128)S(1)} all-to-all(f32[8,56,128]{2,1,0:T(8,128)S(1)} %reduce.1), channel_id=1, replica_groups={{0,32,64,96,128,160,192,224},{8,40,72,104,136,168,200,232},{16,48,80,11..., dimensions={0} | all-to-all | bytes 458752 | tf_op jit(solution)/shard_map/all_to_all | solution.py:311
  69.7 0.2 probe.6
  69.9 12.8 %all_to_all.23.mine = f32[16,32,128]{2,1,0:T(8,128)S(1)} all-to-all(f32[16,32,128]{2,1,0:T(8,128)S(1)} %probe.6), channel_id=1, replica_groups={{8,9,10,11,12,13,14,15,16,17,18,19,20,21,22,23},{24,25,26,27,28,29,30,3..., dimensions={0} | all-to-all | bytes 524288 | tf_op jit(solution)/shard_map/all_to_all | solution.py:319
  82.7 2.0 %collective-permute-start.2 = (f32[16,32,128]{2,1,0:T(8,128)S(1)}, f32[16,32,128]{2,1,0:T(8,128)S(1)}, u32[]{:S(2)}, u32[]{:S(2)}) collective-permute-start(f32[16,32,128]{2,1,0:T(8,128)S(1)} %all_to_all.23.mine), channel_id=1, source_target_pairs={{0,8},{8,0},{16,24},{24,16},{32,40},{40,32},{48,56},{56,48},{64,72... | collective-permute-start | bytes 786440 | tf_op jit(solution)/shard_map/ppermute | solution.py:306
  84.7 0.0 copy-done.4
  84.7 1.6 %object.1 = f32[2,40,128]{2,1,0:T(8,128)} custom-call(f32[16,136,128]{2,1,0:T(8,128)S(1)} %all_to_all.21.pieces, f32[2,40,128]{2,1,0:T(8,128)S(1)} %copy-done.4, f32[4,384,128]{2,1,0:T(8,128)S(1)} %get-tuple-element.15.light, f32[8,128]{1,0:T(8,128)S(1)} %get-tuple-element.16.peak), custom_call_target="tpu_custom_call" | custom-call | flops 700000 | bytes 2000000 | tf_op jit(solution)/shard_map/object/pallas_call | solution.py:379
  86.3 0.0 collective-permute-done.2.other
  86.3 0.8 gather.1
  (1 shorter events, 0.0 us)
Async XLA Ops:
  0.6 25.3 %copy-start.1 = (bf16[768,256]{1,0:T(8,128)(2,1)S(1)}, bf16[768,256]{1,0:T(8,128)(2,1)}, u32[]{:S(2)}) copy-start(bf16[768,256]{1,0:T(8,128)(2,1)} %constant.5.clone.col_table) | copy-start | bytes 1179652
  0.6 25.3 %copy-start.2 = (bf16[768,256]{1,0:T(8,128)(2,1)S(1)}, bf16[768,256]{1,0:T(8,128)(2,1)}, u32[]{:S(2)}) copy-start(bf16[768,256]{1,0:T(8,128)(2,1)} %constant.4.clone.row_table) | copy-start | bytes 1179652
  0.7 25.3 %copy-start = (f32[2,256,256]{2,1,0:T(8,128)S(1)}, f32[2,256,256]{2,1,0:T(8,128)}, u32[]{:S(2)}) copy-start(f32[2,256,256]{2,1,0:T(8,128)} %probe.7) | copy-start | bytes 1572868
  0.7 25.3 %copy-start.3 = (f32[1,256,256]{2,1,0:T(8,128)S(1)}, f32[1,256,256]{2,1,0:T(8,128)}, u32[]{:S(2)}) copy-start(f32[1,256,256]{2,1,0:T(8,128)} %amps.1) | copy-start | bytes 786436
  23.1 2.8 %collective-permute-start = (f32[16,80,128]{2,1,0:T(8,128)S(1)}, f32[16,80,128]{2,1,0:T(8,128)S(1)}, u32[]{:S(2)}, u32[]{:S(2)}) collective-permute-start(f32[16,80,128]{2,1,0:T(8,128)S(1)} %all_to_all.20.stack), channel_id=1, source_target_pairs={{0,8},{8,0},{16,24},{24,16},{32,40},{40,32},{48,56},{56,48},{64,72... | collective-permute-start | bytes 1966088 | tf_op jit(solution)/shard_map/ppermute | solution.py:306
  28.9 2.4 %collective-permute-start.1 = (f32[1536,128]{1,0:T(8,128)S(1)}, f32[1536,128]{1,0:T(8,128)S(1)}, u32[]{:S(2)}, u32[]{:S(2)}) collective-permute-start(f32[1536,128]{1,0:T(8,128)S(1)} %get-tuple-element.11), channel_id=1, source_target_pairs={{0,8},{8,0},{16,24},{24,16},{32,40},{40,32},{48,56},{56,48},{64,72... | collective-permute-start | bytes 2359304 | tf_op jit(solution)/shard_map/ppermute | solution.py:306
  52.5 32.2 %copy-start.4 = (f32[2,40,128]{2,1,0:T(8,128)S(1)}, f32[2,40,128]{2,1,0:T(8,128)}, u32[]{:S(2)}) copy-start(f32[2,40,128]{2,1,0:T(8,128)} %old.1) | copy-start | bytes 122884
  82.7 3.6 %collective-permute-start.2 = (f32[16,32,128]{2,1,0:T(8,128)S(1)}, f32[16,32,128]{2,1,0:T(8,128)S(1)}, u32[]{:S(2)}, u32[]{:S(2)}) collective-permute-start(f32[16,32,128]{2,1,0:T(8,128)S(1)} %all_to_all.23.mine), channel_id=1, source_target_pairs={{0,8},{8,0},{16,24},{24,16},{32,40},{40,32},{48,56},{56,48},{64,72... | collective-permute-start | bytes 786440 | tf_op jit(solution)/shard_map/ppermute | solution.py:306

commit v10 on v9

--- a/solution.py
+++ b/solution.py
@@ -207,16 +207,13 @@
     total = pieces[0, :PIECE, :]
     for member in range(1, 16):
         total = total + pieces[member, :PIECE, :]
-    for layer in range(8):
-        out[layer] = total
-
-
-def probe_kernel(layers, probe, out):
+    out[...] = total
+
+
+def probe_kernel(one, two, probe, out):
     tile, group = my_place()
     top = pl.multiple_of(half_of(tile) * 128 + (8 - 8 * (tile & 1) + group) * 8, 8)
-    summed = layers[0]
-    for layer in range(1, 8):
-        summed = summed + layers[layer]
+    summed = one[...] + two[...]
     mean = jnp.sum(summed[SPARE + 1 : SPARE + 2]) * (1.0 / (WIN * WIN))
     for side in range(2):
         bottom = summed[32 + side * 8 : 40 + side * 8] + 0.25 * mean + 1e-05
@@ -306,9 +303,14 @@
     return lax.ppermute(value, "tile", [(i, i ^ 1) for i in range(TILES)])
 
 
-def exchange_z(value):
-    groups = [[4 * layer + rest for layer in range(TILES // 4)] for rest in range(4)]
-    return lax.all_to_all(value, "tile", 0, 0, axis_index_groups=groups)
+def swap_z(value, mask):
+    pairs = []
+    for tile in range(TILES):
+        layer, rest = divmod(tile, 4)
+        ahead = 1 if rest == 0 else 0
+        other = (((layer - ahead) % (TILES // 4)) ^ mask) + ahead
+        pairs.append((tile, other % (TILES // 4) * 4 + rest))
+    return lax.ppermute(value, "tile", pairs)
 
 
 def exchange(value):
@@ -370,12 +372,7 @@
         keep, on_chip(got)
     )
     pieces = exchange(merged)
-    total = kernel_call(reduce_kernel, buffer(8, PIECE, LANES), [vmem], vmem, 4)(on_chip(pieces))
-    piece = kernel_call(probe_kernel, buffer(16, 32, LANES), [vmem] * 2, vmem, 4)(
-        on_chip(exchange_z(total)), probe
-    )
-
-    mine, pieces = lax.optimization_barrier((exchange(piece), pieces))
+    total = kernel_call(reduce_kernel, buffer(PIECE, LANES), [vmem], vmem, 4)(on_chip(pieces))
     new_object = kernel_call(
         object_kernel,
         jax.ShapeDtypeStruct((2, 40, LANES), jnp.float32),
@@ -385,6 +382,14 @@
         scratch_shapes=[pltpu.SMEM((16, 1, LANES), jnp.float32), pltpu.SemaphoreType.DMA],
         cost_estimate=pl.CostEstimate(flops=700000, bytes_accessed=2000000, transcendentals=0),
     )(on_chip(pieces), on_chip(object_field), on_chip(light), peak)
+    for mask in (1, 2):
+        total = total + swap_z(total, mask)
+    got, new_object = lax.optimization_barrier((swap_z(total, 6), new_object))
+    piece = kernel_call(probe_kernel, buffer(16, 32, LANES), [vmem] * 3, vmem, 4)(
+        on_chip(total), on_chip(got), probe
+    )
+
+    mine = exchange(piece)
     new_probe = kernel_call(
         gather_kernel, jax.ShapeDtypeStruct((2, WIN, WIN), jnp.float32), [vmem] * 2, vmem, 4
     )(on_chip(mine), on_chip(swap_cores(mine)))

time: 87.5 us -> 84.8 us (0.969)
  blocking collectives: 72.6 us -> 59.1 us
  starting transfers between devices: 3.08 us -> 9.07 us
  waiting for transfers between devices: 1.94 us -> 6.88 us
    all_to_all x1 -> x0, blocking collectives: 17.2 us -> none  [exchange_z(): return lax.all_to_all(value, 'tile', 0, 0, axis_index_groups=groups)]
    ppermute x0 -> x3, starting transfers between devices: none -> 7.46 us  [swap_z(): return lax.ppermute(value, 'tile', pairs)]
    ppermute x0 -> x3, waiting for transfers between devices: none -> 3.78 us  [swap_z(): return lax.ppermute(value, 'tile', pairs)]
    all_to_all x3, blocking collectives: 55.4 us -> 59.1 us  [exchange(): lax.all_to_all(value, ('tile', 'group'), 0, 0, axis_index_groups=groups)]
    ppermute x3, starting transfers between devices: 3.08 us -> 1.61 us  [swap_cores(): return lax.ppermute(value, 'tile', [(i, i ^ 1) for i in range(TILES)])]
    ppermute x3, waiting for transfers between devices: 1.94 us -> 3.1 us  [swap_cores(): return lax.ppermute(value, 'tile', [(i, i ^ 1) for i in range(TILES)])]
  transfers between devices with their start and end apart: 3 -> 6, of which waited for: 1 -> 4; matrix products, arithmetic and copies ran while one was open for 0% -> 0% of each run, Pallas kernels for 2% -> 2%
where the time goes in v10:
time: 84.8 us; the launch traced here: 84.6 us
  blocking collectives  59.1 us (70%)
  starting transfers between devices  9.07 us (11%)
  waiting for transfers between devices  6.88 us (8%)
  Pallas kernels  5.83 us (7%)
  between operations  2.7 us (3%)
  local copies, waits for them, and re-layouts  0.96 us (1%)
    all_to_all x3, blocking collectives, exchange(): lax.all_to_all(value, ('tile', 'group'), 0, 0, axis_index_groups=groups)  59.1 us
    ppermute x3, starting transfers between devices, swap_z(): return lax.ppermute(value, 'tile', pairs)  7.46 us
    ppermute x3, waiting for transfers between devices, swap_z(): return lax.ppermute(value, 'tile', pairs)  3.78 us
    ppermute x3, waiting for transfers between devices, swap_cores(): return lax.ppermute(value, 'tile', [(i, i ^ 1) for i in range(TILES)])  3.1 us
    pallas_call x1, Pallas kernels, local(): kernel_call(window_kernel, (buffer(16, LINES, LANES), buffer(16 * PIECE +...  2.84 us
  transfers between devices with their start and end apart: 6, of which 4 were waited for; matrix products, arithmetic and copies ran while one was open for 0% of the time, Pallas kernels for 2%

profile of v10, /device:TPU:1, one launch (start us, length us, event | category | flops | bytes accessed | tf_op | source)
XLA Modules:
  0.0 84.6 jit_solution(15572552067989760338)
XLA Ops:
  0.6 0.0 copy-start.1
  0.6 0.0 copy-start.2
  0.7 0.0 copy-start
  0.7 0.0 copy-start.3
  0.7 0.9 %broadcast_in_dim.3 = f32[16,80,128]{2,1,0:T(8,128)S(1)} broadcast(f32[80,128]{1,0:T(8,128)} %bitcast.1), dimensions={1,2} | broadcast | bytes 696320 | tf_op jit(solution)/shard_map/broadcast_in_dim | solution.py:349
  1.6 21.5 %all_to_all.15.stack = f32[16,80,128]{2,1,0:T(8,128)S(1)} all-to-all(f32[16,80,128]{2,1,0:T(8,128)S(1)} %broadcast_in_dim.3), channel_id=1, replica_groups={{8,9,10,11,12,13,14,15,16,17,18,19,20,21,22,23},{24,25,26,27,28,29,30,3..., dimensions={0} | all-to-all | bytes 1310720 | tf_op jit(solution)/shard_map/all_to_all | solution.py:321
  23.1 0.9 %collective-permute-start = (f32[16,80,128]{2,1,0:T(8,128)S(1)}, f32[16,80,128]{2,1,0:T(8,128)S(1)}, u32[]{:S(2)}, u32[]{:S(2)}) collective-permute-start(f32[16,80,128]{2,1,0:T(8,128)S(1)} %all_to_all.15.stack), channel_id=1, source_target_pairs={{0,8},{8,0},{16,24},{24,16},{32,40},{40,32},{48,56},{56,48},{64,72... | collective-permute-start | bytes 1966088 | tf_op jit(solution)/shard_map/ppermute | solution.py:303
  26.0 0.0 collective-permute-done.near
  26.0 0.0 copy-done.1
  26.0 0.0 copy-done.2
  26.0 0.0 copy-done
  26.0 0.0 copy-done.3
  26.0 2.8 %window.1 = (f32[16,136,128]{2,1,0:T(8,128)S(1)}, f32[1536,128]{1,0:T(8,128)S(1)}) custom-call(s32[1]{0:T(128)S(6)} %copy.10.row_ref, s32[1]{0:T(128)S(6)} %copy.11.col_ref, s32[1]{0:T(128)S(6)} %copy.12.live_ref, f32[16,80,128]{2,1,0:T(8,128)S(1)} %all_to_all.15.stack, f32[16,80,128]{2,1,0:T(8,128)S(1)} %collective-permute-done.near, ...), custom_call_target="tpu_custom_call" | custom-call | tf_op jit(solution)/shard_map/window/pallas_call | solution.py:358
  28.9 0.2 collective-permute-start.1
  29.1 0.2 prep.1
  29.3 1.9 %collective-permute-done.1.got = f32[1536,128]{1,0:T(8,128)S(1)} collective-permute-done((f32[1536,128]{1,0:T(8,128)S(1)}, f32[1536,128]{1,0:T(8,128)S(1)}, u32[]{:S(2)}, u32[]{:S(2)}) %collective-permute-start.1) | collective-permute-done | bytes 786464 | tf_op jit(solution)/shard_map/ppermute | solution.py:303
  31.2 0.1 merge.1
  31.3 21.1 %all_to_all.16.pieces = f32[16,136,128]{2,1,0:T(8,128)S(1)} all-to-all(f32[16,136,128]{2,1,0:T(8,128)S(1)} %merge.1), channel_id=1, replica_groups={{8,9,10,11,12,13,14,15,16,17,18,19,20,21,22,23},{24,25,26,27,28,29,30,3..., dimensions={0} | all-to-all | bytes 2228224 | tf_op jit(solution)/shard_map/all_to_all | solution.py:321
  52.4 0.0 copy-start.4
  52.5 0.3 collective-permute-start.2
  52.8 2.5 %collective-permute-done.2 = f32[56,128]{1,0:T(8,128)S(1)} collective-permute-done((f32[56,128]{1,0:T(8,128)S(1)}, f32[56,128]{1,0:T(8,128)S(1)}, u32[]{:S(2)}, u32[]{:S(2)}) %collective-permute-start.2) | collective-permute-done | bytes 28704 | tf_op jit(solution)/shard_map/ppermute | solution.py:313
  55.3 3.1 %collective-permute-start.3 = (f32[56,128]{1,0:T(8,128)S(1)}, f32[56,128]{1,0:T(8,128)S(1)}, u32[]{:S(2)}, u32[]{:S(2)}) collective-permute-start(f32[56,128]{1,0:T(8,128)S(1)} %add.6), channel_id=1, source_target_pairs={{0,192},{8,72},{16,80},{24,88},{32,96},{40,104},{48,112},{56,120},... | collective-permute-start | bytes 86024 | tf_op jit(solution)/shard_map/ppermute | solution.py:313
  58.4 1.3 %collective-permute-done.3 = f32[56,128]{1,0:T(8,128)S(1)} collective-permute-done((f32[56,128]{1,0:T(8,128)S(1)}, f32[56,128]{1,0:T(8,128)S(1)}, u32[]{:S(2)}, u32[]{:S(2)}) %collective-permute-start.3) | collective-permute-done | bytes 28704 | tf_op jit(solution)/shard_map/ppermute | solution.py:313
  59.7 4.1 %collective-permute-start.4 = (f32[56,128]{1,0:T(8,128)S(1)}, f32[56,128]{1,0:T(8,128)S(1)}, u32[]{:S(2)}, u32[]{:S(2)}) collective-permute-start(f32[56,128]{1,0:T(8,128)S(1)} %add.7.one), channel_id=1, source_target_pairs={{0,64},{8,200},{16,208},{24,216},{32,224},{40,232},{48,240},{56,24... | collective-permute-start | bytes 86024 | tf_op jit(solution)/shard_map/ppermute | solution.py:313
  63.7 0.0 copy-done.4
  63.7 1.6 %object.1 = f32[2,40,128]{2,1,0:T(8,128)} custom-call(f32[16,136,128]{2,1,0:T(8,128)S(1)} %all_to_all.16.pieces, f32[2,40,128]{2,1,0:T(8,128)S(1)} %copy-done.4, f32[4,384,128]{2,1,0:T(8,128)S(1)} %get-tuple-element.14.light, f32[8,128]{1,0:T(8,128)S(1)} %get-tuple-element.15.peak), custom_call_target="tpu_custom_call" | custom-call | flops 700000 | bytes 2000000 | tf_op jit(solution)/shard_map/object/pallas_call | solution.py:376
  65.4 0.0 collective-permute-done.4.two
  65.4 0.1 probe.6
  65.6 16.5 %all_to_all.17.mine = f32[16,32,128]{2,1,0:T(8,128)S(1)} all-to-all(f32[16,32,128]{2,1,0:T(8,128)S(1)} %probe.6), channel_id=1, replica_groups={{8,9,10,11,12,13,14,15,16,17,18,19,20,21,22,23},{24,25,26,27,28,29,30,3..., dimensions={0} | all-to-all | bytes 524288 | tf_op jit(solution)/shard_map/all_to_all | solution.py:321
  82.1 0.5 collective-permute-start.5
  82.6 1.2 %collective-permute-done.5.other = f32[16,32,128]{2,1,0:T(8,128)S(1)} collective-permute-done((f32[16,32,128]{2,1,0:T(8,128)S(1)}, f32[16,32,128]{2,1,0:T(8,128)S(1)}, u32[]{:S(2)}, u32[]{:S(2)}) %collective-permute-start.5) | collective-permute-done | bytes 262176 | tf_op jit(solution)/shard_map/ppermute | solution.py:303
  83.8 0.8 gather.1
  (3 shorter events, 0.0 us)
Async XLA Ops:
  0.6 25.3 %copy-start.1 = (bf16[768,256]{1,0:T(8,128)(2,1)S(1)}, bf16[768,256]{1,0:T(8,128)(2,1)}, u32[]{:S(2)}) copy-start(bf16[768,256]{1,0:T(8,128)(2,1)} %constant.5.clone.col_table) | copy-start | bytes 1179652
  0.6 25.3 %copy-start.2 = (bf16[768,256]{1,0:T(8,128)(2,1)S(1)}, bf16[768,256]{1,0:T(8,128)(2,1)}, u32[]{:S(2)}) copy-start(bf16[768,256]{1,0:T(8,128)(2,1)} %constant.4.clone.row_table) | copy-start | bytes 1179652
  0.7 25.3 %copy-start = (f32[2,256,256]{2,1,0:T(8,128)S(1)}, f32[2,256,256]{2,1,0:T(8,128)}, u32[]{:S(2)}) copy-start(f32[2,256,256]{2,1,0:T(8,128)} %probe.7) | copy-start | bytes 1572868
  0.7 25.3 %copy-start.3 = (f32[1,256,256]{2,1,0:T(8,128)S(1)}, f32[1,256,256]{2,1,0:T(8,128)}, u32[]{:S(2)}) copy-start(f32[1,256,256]{2,1,0:T(8,128)} %amps.1) | copy-start | bytes 786436
  23.1 2.8 %collective-permute-start = (f32[16,80,128]{2,1,0:T(8,128)S(1)}, f32[16,80,128]{2,1,0:T(8,128)S(1)}, u32[]{:S(2)}, u32[]{:S(2)}) collective-permute-start(f32[16,80,128]{2,1,0:T(8,128)S(1)} %all_to_all.15.stack), channel_id=1, source_target_pairs={{0,8},{8,0},{16,24},{24,16},{32,40},{40,32},{48,56},{56,48},{64,72... | collective-permute-start | bytes 1966088 | tf_op jit(solution)/shard_map/ppermute | solution.py:303
  28.9 2.4 %collective-permute-start.1 = (f32[1536,128]{1,0:T(8,128)S(1)}, f32[1536,128]{1,0:T(8,128)S(1)}, u32[]{:S(2)}, u32[]{:S(2)}) collective-permute-start(f32[1536,128]{1,0:T(8,128)S(1)} %get-tuple-element.11), channel_id=1, source_target_pairs={{0,8},{8,0},{16,24},{24,16},{32,40},{40,32},{48,56},{56,48},{64,72... | collective-permute-start | bytes 2359304 | tf_op jit(solution)/shard_map/ppermute | solution.py:303
  52.4 11.3 %copy-start.4 = (f32[2,40,128]{2,1,0:T(8,128)S(1)}, f32[2,40,128]{2,1,0:T(8,128)}, u32[]{:S(2)}) copy-start(f32[2,40,128]{2,1,0:T(8,128)} %old.1) | copy-start | bytes 122884
  52.5 2.8 %collective-permute-start.2 = (f32[56,128]{1,0:T(8,128)S(1)}, f32[56,128]{1,0:T(8,128)S(1)}, u32[]{:S(2)}, u32[]{:S(2)}) collective-permute-start(f32[56,128]{1,0:T(8,128)S(1)} %reduce.1), channel_id=1, source_target_pairs={{0,224},{8,40},{16,48},{24,56},{32,64},{40,8},{48,16},{56,24},{64,... | collective-permute-start | bytes 86024 | tf_op jit(solution)/shard_map/ppermute | solution.py:313
  55.3 4.4 %collective-permute-start.3 = (f32[56,128]{1,0:T(8,128)S(1)}, f32[56,128]{1,0:T(8,128)S(1)}, u32[]{:S(2)}, u32[]{:S(2)}) collective-permute-start(f32[56,128]{1,0:T(8,128)S(1)} %add.6), channel_id=1, source_target_pairs={{0,192},{8,72},{16,80},{24,88},{32,96},{40,104},{48,112},{56,120},... | collective-permute-start | bytes 86024 | tf_op jit(solution)/shard_map/ppermute | solution.py:313
  59.7 5.7 %collective-permute-start.4 = (f32[56,128]{1,0:T(8,128)S(1)}, f32[56,128]{1,0:T(8,128)S(1)}, u32[]{:S(2)}, u32[]{:S(2)}) collective-permute-start(f32[56,128]{1,0:T(8,128)S(1)} %add.7.one), channel_id=1, source_target_pairs={{0,64},{8,200},{16,208},{24,216},{32,224},{40,232},{48,240},{56,24... | collective-permute-start | bytes 86024 | tf_op jit(solution)/shard_map/ppermute | solution.py:313
  82.1 1.7 %collective-permute-start.5 = (f32[16,32,128]{2,1,0:T(8,128)S(1)}, f32[16,32,128]{2,1,0:T(8,128)S(1)}, u32[]{:S(2)}, u32[]{:S(2)}) collective-permute-start(f32[16,32,128]{2,1,0:T(8,128)S(1)} %all_to_all.17.mine), channel_id=1, source_target_pairs={{0,8},{8,0},{16,24},{24,16},{32,40},{40,32},{48,56},{56,48},{64,72... | collective-permute-start | bytes 786440 | tf_op jit(solution)/shard_map/ppermute | solution.py:303

commit v11 on v10

--- a/solution.py
+++ b/solution.py
@@ -97,7 +97,7 @@
 
 def window_kernel(
     row_ref, col_ref, live_ref, stack, near, probe, amps, row_table, col_table,
-    keep, send, field, grads, sums,
+    send, sums, grads, spare_out, field,
 ):
     row, col = row_ref[0], col_ref[0]
     live = live_ref[0].astype(jnp.float32)
@@ -166,41 +166,43 @@
     for lane_off, number in enumerate((row.astype(jnp.float32), col.astype(jnp.float32), live)):
         here = jnp.logical_and(spare_line == 0, spare_lane == first_lane + lane_off)
         spare = jnp.where(here, number, spare)
+    spare_out[...] = spare
     for member in range(16):
-        for kept, side_half in ((True, half), (False, 1 - half)):
-            top = pl.multiple_of(side_half * 128 + member * 8, 8)
-            for part in range(3):
-                for side in range(2):
-                    put = part * 16 + side * 8
-                    value = sums[part, pl.ds(top, 8), side * LANES : (side + 1) * LANES]
-                    if kept:
-                        keep[member, put : put + 8, :] = value
-                    else:
-                        send[member * PIECE + put : member * PIECE + put + 8, :] = value
-            if kept:
-                keep[member, SPARE:PIECE, :] = spare
-            else:
-                send[member * PIECE + SPARE : member * PIECE + PIECE, :] = spare
+        first_line = member * PIECE
+        top = pl.multiple_of((1 - half) * 128 + member * 8, 8)
+        for part in range(3):
+            for side in range(2):
+                put = first_line + part * 16 + side * 8
+                send[put : put + 8, :] = sums[part, pl.ds(top, 8), side * LANES : (side + 1) * LANES]
+        send[first_line + SPARE : first_line + PIECE, :] = spare
+    for member in range(8):
+        lines = slice(member * 40, member * 40 + 40)
+        for part in range(2):
+            put = 16 * PIECE + member * 80 + part * 40
+            send[put : put + 40, :] = grads[part, 2 - 2 * odd, lines, :]
+
+
+def merge_kernel(sums, grads, spare, got, out):
+    tile, _ = my_place()
+    odd, half, inside = tile & 1, half_of(tile), far_exists(tile)
+    for member in range(16):
+        top = pl.multiple_of(half * 128 + member * 8, 8)
+        for part in range(3):
+            for side in range(2):
+                put = part * 16 + side * 8
+                other = got[member * PIECE + put : member * PIECE + put + 8, :]
+                own = sums[part, pl.ds(top, 8), side * LANES : (side + 1) * LANES]
+                out[member, put : put + 8, :] = own + other
+        out[member, SPARE:PIECE, :] = spare[...] + got[member * PIECE + SPARE : (member + 1) * PIECE, :]
     for member in range(8):
         lines = slice(member * 40, member * 40 + 40)
         for part in range(2):
             put = PIECE + part * 40
-            keep[8 - 8 * odd + member, put : put + 40, :] = grads[part, 1, lines, :]
-            keep[8 * odd + member, put : put + 40, :] = jnp.where(
+            other = 16 * PIECE + member * 80 + part * 40
+            out[8 - 8 * odd + member, put : put + 40, :] = grads[part, 1, lines, :] + got[other : other + 40, :]
+            out[8 * odd + member, put : put + 40, :] = jnp.where(
                 inside, grads[part, 2 * odd, lines, :], 0.0
             )
-            put = 16 * PIECE + member * 80 + part * 40
-            send[put : put + 40, :] = grads[part, 2 - 2 * odd, lines, :]
-
-
-def merge_kernel(keep, got, out):
-    for member in range(16):
-        out[member, :PIECE, :] = keep[member, :PIECE, :] + got[member * PIECE : (member + 1) * PIECE, :]
-    mine = 8 - 8 * (my_place()[0] & 1)
-    for member in range(8):
-        put = 16 * PIECE + member * 80
-        out[mine + member, PIECE:, :] = keep[mine + member, PIECE:, :] + got[put : put + 80, :]
-        out[8 - mine + member, PIECE:, :] = keep[8 - mine + member, PIECE:, :]
 
 
 def reduce_kernel(pieces, out):
@@ -226,10 +228,11 @@
 
 
 def gather_kernel(mine, other, out):
-    half = half_of(my_place()[0])
-    for source, which in ((mine, half), (other, 1 - half)):
+    core = my_place()[0] & 1
+    for source, which in ((mine, core), (other, 1 - core)):
         for member in range(16):
-            top = pl.multiple_of(which * 128 + member * 8, 8)
+            x_hi, group = (member >> 1) & 1, (member >> 2) * 2 + (member & 1)
+            top = pl.multiple_of((which ^ x_hi) * 128 + (8 - 8 * which + group) * 8, 8)
             for part in range(2):
                 for side in range(2):
                     lines = part * 16 + side * 8
@@ -321,6 +324,21 @@
     return lax.all_to_all(value, ("tile", "group"), 0, 0, axis_index_groups=groups)
 
 
+def exchange_plane(value):
+    groups = []
+    for layer in range(TILES // 4):
+        for core in range(2):
+            groups.append(
+                [
+                    (layer * 4 + x_hi * 2 + core) * 8 + y * 2 + x_lo
+                    for y in range(4)
+                    for x_hi in range(2)
+                    for x_lo in range(2)
+                ]
+            )
+    return lax.all_to_all(value, ("tile", "group"), 0, 0, axis_index_groups=groups)
+
+
 def on_chip(value):
     return pltpu.with_memory_space_constraint(value, pltpu.VMEM)
 
@@ -355,21 +373,26 @@
         4,
         cost_estimate=pl.CostEstimate(flops=300000, bytes_accessed=2000000, transcendentals=0),
     )(probe)
-    keep, send = kernel_call(
+    send, sums, grads, spare = kernel_call(
         window_kernel,
-        (buffer(16, LINES, LANES), buffer(16 * PIECE + 640, LANES)),
+        (
+            buffer(16 * PIECE + 640, LANES),
+            buffer(3, WIN, WIN),
+            buffer(2, 3, 320, LANES),
+            buffer(8, LANES),
+        ),
         [smem] * 3 + [vmem] * 6,
-        (vmem,) * 2,
+        (vmem,) * 4,
         24,
-        scratch_shapes=[buffer(2, 3, 320, LANES), buffer(2, 3, 320, LANES), buffer(3, WIN, WIN)],
+        scratch_shapes=[buffer(2, 3, 320, LANES)],
     )(
         row_start, column_start, live_slots, on_chip(stack), on_chip(swap_cores(stack)), probe,
         on_chip(amplitudes), row_table, col_table,
     )
 
     got, light = lax.optimization_barrier((swap_cores(send), light))
-    merged = kernel_call(merge_kernel, buffer(16, LINES, LANES), [vmem] * 2, vmem, 4)(
-        keep, on_chip(got)
+    merged = kernel_call(merge_kernel, buffer(16, LINES, LANES), [vmem] * 4, vmem, 4)(
+        sums, grads, spare, on_chip(got)
     )
     pieces = exchange(merged)
     total = kernel_call(reduce_kernel, buffer(PIECE, LANES), [vmem], vmem, 4)(on_chip(pieces))
@@ -389,7 +412,7 @@
         on_chip(total), on_chip(got), probe
     )
 
-    mine = exchange(piece)
+    mine = exchange_plane(piece)
     new_probe = kernel_call(
         gather_kernel, jax.ShapeDtypeStruct((2, WIN, WIN), jnp.float32), [vmem] * 2, vmem, 4
     )(on_chip(mine), on_chip(swap_cores(mine)))

time: 84.8 us -> 84.4 us (level)
  blocking collectives: 59.1 us -> 52.8 us
  starting transfers between devices: 9.07 us -> 15.1 us
    all_to_all x3 -> x2, blocking collectives: 59.1 us -> 42.6 us  [exchange(): lax.all_to_all(value, ('tile', 'group'), 0, 0, axis_index_groups=groups)]
    all_to_all x0 -> x1, blocking collectives: none -> 10.2 us  [exchange_plane(): lax.all_to_all(value, ('tile', 'group'), 0, 0, axis_index_groups=groups)]
    ppermute x3, starting transfers between devices: 1.61 us -> 7.58 us  [swap_cores(): return lax.ppermute(value, 'tile', [(i, i ^ 1) for i in range(TILES)])]
where the time goes in v11:
time: 84.4 us; the launch traced here: 84.2 us
  blocking collectives  52.8 us (63%)
  starting transfers between devices  15.1 us (18%)
  waiting for transfers between devices  6.83 us (8%)
  Pallas kernels  5.74 us (7%)
  between operations  2.7 us (3%)
  local copies, waits for them, and re-layouts  0.96 us (1%)
    all_to_all x2, blocking collectives, exchange(): lax.all_to_all(value, ('tile', 'group'), 0, 0, axis_index_groups=groups)  42.6 us
    all_to_all x1, blocking collectives, exchange_plane(): lax.all_to_all(value, ('tile', 'group'), 0, 0, axis_index_groups=groups)  10.2 us
    ppermute x3, starting transfers between devices, swap_cores(): return lax.ppermute(value, 'tile', [(i, i ^ 1) for i in range(TILES)])  7.58 us
    ppermute x3, starting transfers between devices, swap_z(): return lax.ppermute(value, 'tile', pairs)  7.51 us
    ppermute x3, waiting for transfers between devices, swap_z(): return lax.ppermute(value, 'tile', pairs)  3.75 us
    ppermute x3, waiting for transfers between devices, swap_cores(): return lax.ppermute(value, 'tile', [(i, i ^ 1) for i in range(TILES)])  3.08 us
    pallas_call x1, Pallas kernels, local(): kernel_call(window_kernel, (buffer(16 * PIECE + 640, LANES), buffer(3, WI...  2.71 us
  transfers between devices with their start and end apart: 6, of which 4 were waited for; matrix products, arithmetic and copies ran while one was open for 0% of the time, Pallas kernels for 2%

profile of v11, /device:TPU:1, one launch (start us, length us, event | category | flops | bytes accessed | tf_op | source)
XLA Modules:
  0.0 84.2 jit_solution(7129081446248218174)
XLA Ops:
  0.6 0.0 copy-start.1
  0.6 0.0 copy-start.2
  0.7 0.0 copy-start.3
  0.7 0.0 copy-start
  0.7 0.9 %broadcast_in_dim.3 = f32[16,80,128]{2,1,0:T(8,128)S(1)} broadcast(f32[80,128]{1,0:T(8,128)} %bitcast.1), dimensions={1,2} | broadcast | bytes 696320 | tf_op jit(solution)/shard_map/broadcast_in_dim | solution.py:367
  1.6 21.5 %all_to_all.15.stack = f32[16,80,128]{2,1,0:T(8,128)S(1)} all-to-all(f32[16,80,128]{2,1,0:T(8,128)S(1)} %broadcast_in_dim.3), channel_id=1, replica_groups={{8,9,10,11,12,13,14,15,16,17,18,19,20,21,22,23},{24,25,26,27,28,29,30,3..., dimensions={0} | all-to-all | bytes 1310720 | tf_op jit(solution)/shard_map/all_to_all | solution.py:324
  23.1 0.9 %collective-permute-start = (f32[16,80,128]{2,1,0:T(8,128)S(1)}, f32[16,80,128]{2,1,0:T(8,128)S(1)}, u32[]{:S(2)}, u32[]{:S(2)}) collective-permute-start(f32[16,80,128]{2,1,0:T(8,128)S(1)} %all_to_all.15.stack), channel_id=1, source_target_pairs={{0,8},{8,0},{16,24},{24,16},{32,40},{40,32},{48,56},{56,48},{64,72... | collective-permute-start | bytes 1966088 | tf_op jit(solution)/shard_map/ppermute | solution.py:306
  26.0 0.0 collective-permute-done.near
  26.0 0.0 copy-done.1
  26.0 0.0 copy-done.2
  26.0 0.0 copy-done.3
  26.0 0.0 copy-done
  26.0 2.7 %window.1 = (f32[1536,128]{1,0:T(8,128)S(1)}, f32[3,256,256]{2,1,0:T(8,128)S(1)}, f32[2,3,320,128]{3,2,1,0:T(8,128)S(1)}, f32[8,128]{1,0:T(8,128)S(1)}) custom-call(s32[1]{0:T(128)S(6)} %copy.10.row_ref, s32[1]{0:T(128)S(6)} %copy.11.col_ref, s32[1]{0:T(128)S(6)} %copy.12.live_ref, f32[16,80,128]{2,1,0:T(8,128)S(1)} %all_to_all.15.stack, ...), custom_call_target="tpu_custom_call" | custom-call | tf_op jit(solution)/shard_map/window/pallas_call | solution.py:376
  28.7 0.2 collective-permute-start.1
  28.9 0.2 prep.1
  29.2 1.9 %collective-permute-done.1.got = f32[1536,128]{1,0:T(8,128)S(1)} collective-permute-done((f32[1536,128]{1,0:T(8,128)S(1)}, f32[1536,128]{1,0:T(8,128)S(1)}, u32[]{:S(2)}, u32[]{:S(2)}) %collective-permute-start.1) | collective-permute-done | bytes 786464 | tf_op jit(solution)/shard_map/ppermute | solution.py:306
  31.1 0.1 merge.1
  31.2 21.1 %all_to_all.16.pieces = f32[16,136,128]{2,1,0:T(8,128)S(1)} all-to-all(f32[16,136,128]{2,1,0:T(8,128)S(1)} %merge.1), channel_id=1, replica_groups={{8,9,10,11,12,13,14,15,16,17,18,19,20,21,22,23},{24,25,26,27,28,29,30,3..., dimensions={0} | all-to-all | bytes 2228224 | tf_op jit(solution)/shard_map/all_to_all | solution.py:324
  52.3 0.0 copy-start.4
  52.4 0.3 collective-permute-start.2
  52.7 2.5 %collective-permute-done.2 = f32[56,128]{1,0:T(8,128)S(1)} collective-permute-done((f32[56,128]{1,0:T(8,128)S(1)}, f32[56,128]{1,0:T(8,128)S(1)}, u32[]{:S(2)}, u32[]{:S(2)}) %collective-permute-start.2) | collective-permute-done | bytes 28704 | tf_op jit(solution)/shard_map/ppermute | solution.py:316
  55.2 3.1 %collective-permute-start.3 = (f32[56,128]{1,0:T(8,128)S(1)}, f32[56,128]{1,0:T(8,128)S(1)}, u32[]{:S(2)}, u32[]{:S(2)}) collective-permute-start(f32[56,128]{1,0:T(8,128)S(1)} %add.6), channel_id=1, source_target_pairs={{0,192},{8,72},{16,80},{24,88},{32,96},{40,104},{48,112},{56,120},... | collective-permute-start | bytes 86024 | tf_op jit(solution)/shard_map/ppermute | solution.py:316
  58.3 1.3 %collective-permute-done.3 = f32[56,128]{1,0:T(8,128)S(1)} collective-permute-done((f32[56,128]{1,0:T(8,128)S(1)}, f32[56,128]{1,0:T(8,128)S(1)}, u32[]{:S(2)}, u32[]{:S(2)}) %collective-permute-start.3) | collective-permute-done | bytes 28704 | tf_op jit(solution)/shard_map/ppermute | solution.py:316
  59.6 4.1 %collective-permute-start.4 = (f32[56,128]{1,0:T(8,128)S(1)}, f32[56,128]{1,0:T(8,128)S(1)}, u32[]{:S(2)}, u32[]{:S(2)}) collective-permute-start(f32[56,128]{1,0:T(8,128)S(1)} %add.7.one), channel_id=1, source_target_pairs={{0,64},{8,200},{16,208},{24,216},{32,224},{40,232},{48,240},{56,24... | collective-permute-start | bytes 86024 | tf_op jit(solution)/shard_map/ppermute | solution.py:316
  63.6 0.0 copy-done.4
  63.6 1.6 %object.1 = f32[2,40,128]{2,1,0:T(8,128)} custom-call(f32[16,136,128]{2,1,0:T(8,128)S(1)} %all_to_all.16.pieces, f32[2,40,128]{2,1,0:T(8,128)S(1)} %copy-done.4, f32[4,384,128]{2,1,0:T(8,128)S(1)} %get-tuple-element.18.light, f32[8,128]{1,0:T(8,128)S(1)} %get-tuple-element.19.peak), custom_call_target="tpu_custom_call" | custom-call | flops 700000 | bytes 2000000 | tf_op jit(solution)/shard_map/object/pallas_call | solution.py:399
  65.3 0.0 collective-permute-done.4.two
  65.3 0.1 probe.6
  65.5 10.2 %all_to_all.17.mine = f32[16,32,128]{2,1,0:T(8,128)S(1)} all-to-all(f32[16,32,128]{2,1,0:T(8,128)S(1)} %probe.6), channel_id=1, replica_groups={{0,1,16,17,2,3,18,19,4,5,20,21,6,7,22,23},{8,9,24,25,10,11,26,27,12,13,..., dimensions={0} | all-to-all | bytes 524288 | tf_op jit(solution)/shard_map/all_to_all | solution.py:339
  75.7 6.5 %collective-permute-start.5 = (f32[16,32,128]{2,1,0:T(8,128)S(1)}, f32[16,32,128]{2,1,0:T(8,128)S(1)}, u32[]{:S(2)}, u32[]{:S(2)}) collective-permute-start(f32[16,32,128]{2,1,0:T(8,128)S(1)} %all_to_all.17.mine), channel_id=1, source_target_pairs={{0,8},{8,0},{16,24},{24,16},{32,40},{40,32},{48,56},{56,48},{64,72... | collective-permute-start | bytes 786440 | tf_op jit(solution)/shard_map/ppermute | solution.py:306
  82.1 1.2 %collective-permute-done.5.other = f32[16,32,128]{2,1,0:T(8,128)S(1)} collective-permute-done((f32[16,32,128]{2,1,0:T(8,128)S(1)}, f32[16,32,128]{2,1,0:T(8,128)S(1)}, u32[]{:S(2)}, u32[]{:S(2)}) %collective-permute-start.5) | collective-permute-done | bytes 262176 | tf_op jit(solution)/shard_map/ppermute | solution.py:306
  83.3 0.9 %gather.1 = f32[2,256,256]{2,1,0:T(8,128)} custom-call(f32[16,32,128]{2,1,0:T(8,128)S(1)} %all_to_all.17.mine, f32[16,32,128]{2,1,0:T(8,128)S(1)} %collective-permute-done.5.other), custom_call_target="tpu_custom_call" | custom-call | tf_op jit(solution)/shard_map/gather/pallas_call | solution.py:416
  (3 shorter events, 0.0 us)
Async XLA Ops:
  0.6 25.3 %copy-start.1 = (bf16[768,256]{1,0:T(8,128)(2,1)S(1)}, bf16[768,256]{1,0:T(8,128)(2,1)}, u32[]{:S(2)}) copy-start(bf16[768,256]{1,0:T(8,128)(2,1)} %constant.4.clone.row_table) | copy-start | bytes 1179652
  0.6 25.3 %copy-start.2 = (bf16[768,256]{1,0:T(8,128)(2,1)S(1)}, bf16[768,256]{1,0:T(8,128)(2,1)}, u32[]{:S(2)}) copy-start(bf16[768,256]{1,0:T(8,128)(2,1)} %constant.5.clone.col_table) | copy-start | bytes 1179652
  0.7 25.3 %copy-start.3 = (f32[1,256,256]{2,1,0:T(8,128)S(1)}, f32[1,256,256]{2,1,0:T(8,128)}, u32[]{:S(2)}) copy-start(f32[1,256,256]{2,1,0:T(8,128)} %amps.1) | copy-start | bytes 786436
  0.7 25.3 %copy-start = (f32[2,256,256]{2,1,0:T(8,128)S(1)}, f32[2,256,256]{2,1,0:T(8,128)}, u32[]{:S(2)}) copy-start(f32[2,256,256]{2,1,0:T(8,128)} %probe.7) | copy-start | bytes 1572868
  23.1 2.8 %collective-permute-start = (f32[16,80,128]{2,1,0:T(8,128)S(1)}, f32[16,80,128]{2,1,0:T(8,128)S(1)}, u32[]{:S(2)}, u32[]{:S(2)}) collective-permute-start(f32[16,80,128]{2,1,0:T(8,128)S(1)} %all_to_all.15.stack), channel_id=1, source_target_pairs={{0,8},{8,0},{16,24},{24,16},{32,40},{40,32},{48,56},{56,48},{64,72... | collective-permute-start | bytes 1966088 | tf_op jit(solution)/shard_map/ppermute | solution.py:306
  28.7 2.4 %collective-permute-start.1 = (f32[1536,128]{1,0:T(8,128)S(1)}, f32[1536,128]{1,0:T(8,128)S(1)}, u32[]{:S(2)}, u32[]{:S(2)}) collective-permute-start(f32[1536,128]{1,0:T(8,128)S(1)} %get-tuple-element.15), channel_id=1, source_target_pairs={{0,8},{8,0},{16,24},{24,16},{32,40},{40,32},{48,56},{56,48},{64,72... | collective-permute-start | bytes 2359304 | tf_op jit(solution)/shard_map/ppermute | solution.py:306
  52.3 11.3 %copy-start.4 = (f32[2,40,128]{2,1,0:T(8,128)S(1)}, f32[2,40,128]{2,1,0:T(8,128)}, u32[]{:S(2)}) copy-start(f32[2,40,128]{2,1,0:T(8,128)} %old.1) | copy-start | bytes 122884
  52.4 2.8 %collective-permute-start.2 = (f32[56,128]{1,0:T(8,128)S(1)}, f32[56,128]{1,0:T(8,128)S(1)}, u32[]{:S(2)}, u32[]{:S(2)}) collective-permute-start(f32[56,128]{1,0:T(8,128)S(1)} %reduce.1), channel_id=1, source_target_pairs={{0,224},{8,40},{16,48},{24,56},{32,64},{40,8},{48,16},{56,24},{64,... | collective-permute-start | bytes 86024 | tf_op jit(solution)/shard_map/ppermute | solution.py:316
  55.2 4.4 %collective-permute-start.3 = (f32[56,128]{1,0:T(8,128)S(1)}, f32[56,128]{1,0:T(8,128)S(1)}, u32[]{:S(2)}, u32[]{:S(2)}) collective-permute-start(f32[56,128]{1,0:T(8,128)S(1)} %add.6), channel_id=1, source_target_pairs={{0,192},{8,72},{16,80},{24,88},{32,96},{40,104},{48,112},{56,120},... | collective-permute-start | bytes 86024 | tf_op jit(solution)/shard_map/ppermute | solution.py:316
  59.6 5.7 %collective-permute-start.4 = (f32[56,128]{1,0:T(8,128)S(1)}, f32[56,128]{1,0:T(8,128)S(1)}, u32[]{:S(2)}, u32[]{:S(2)}) collective-permute-start(f32[56,128]{1,0:T(8,128)S(1)} %add.7.one), channel_id=1, source_target_pairs={{0,64},{8,200},{16,208},{24,216},{32,224},{40,232},{48,240},{56,24... | collective-permute-start | bytes 86024 | tf_op jit(solution)/shard_map/ppermute | solution.py:316
  75.7 7.6 %collective-permute-start.5 = (f32[16,32,128]{2,1,0:T(8,128)S(1)}, f32[16,32,128]{2,1,0:T(8,128)S(1)}, u32[]{:S(2)}, u32[]{:S(2)}) collective-permute-start(f32[16,32,128]{2,1,0:T(8,128)S(1)} %all_to_all.17.mine), channel_id=1, source_target_pairs={{0,8},{8,0},{16,24},{24,16},{32,40},{40,32},{48,56},{56,48},{64,72... | collective-permute-start | bytes 786440 | tf_op jit(solution)/shard_map/ppermute | solution.py:306

commit v12 on v11

--- a/solution.py
+++ b/solution.py
@@ -214,31 +214,34 @@
 
 def probe_kernel(one, two, probe, out):
     tile, group = my_place()
-    top = pl.multiple_of(half_of(tile) * 128 + (8 - 8 * (tile & 1) + group) * 8, 8)
-    summed = one[...] + two[...]
-    mean = jnp.sum(summed[SPARE + 1 : SPARE + 2]) * (1.0 / (WIN * WIN))
-    for side in range(2):
-        bottom = summed[32 + side * 8 : 40 + side * 8] + 0.25 * mean + 1e-05
-        for part in range(2):
-            lines = part * 16 + side * 8
-            old = probe[part, pl.ds(top, 8), side * LANES : (side + 1) * LANES]
-            new = old - summed[lines : lines + 8] / bottom
-            for member in range(16):
-                out[member, lines : lines + 8, :] = new
+    own_half = half_of(tile)
+    for piece, half in enumerate((own_half, 1 - own_half)):
+        top = pl.multiple_of(half * 128 + (piece * 8 + group) * 8, 8)
+        lines = slice(piece * PIECE, (piece + 1) * PIECE)
+        summed = one[lines, :] + two[lines, :]
+        mean = jnp.sum(summed[SPARE + 1 : SPARE + 2]) * (1.0 / (WIN * WIN))
+        for side in range(2):
+            bottom = summed[32 + side * 8 : 40 + side * 8] + 0.25 * mean + 1e-05
+            for part in range(2):
+                line = part * 16 + side * 8
+                old = probe[part, pl.ds(top, 8), side * LANES : (side + 1) * LANES]
+                new = old - summed[line : line + 8] / bottom
+                for member in range(16):
+                    out[member, piece * 32 + line : piece * 32 + line + 8, :] = new
 
 
 def gather_kernel(mine, other, out):
-    core = my_place()[0] & 1
-    for source, which in ((mine, core), (other, 1 - core)):
-        for member in range(16):
-            x_hi, group = (member >> 1) & 1, (member >> 2) * 2 + (member & 1)
-            top = pl.multiple_of((which ^ x_hi) * 128 + (8 - 8 * which + group) * 8, 8)
+    ahead = (my_place()[0] & 1) == 1
+    for member in range(16):
+        x_hi, group = (member >> 1) & 1, (member >> 2) * 2 + (member & 1)
+        for piece, half in enumerate((1 - x_hi, x_hi)):
+            top = half * 128 + (piece * 8 + group) * 8
             for part in range(2):
                 for side in range(2):
-                    lines = part * 16 + side * 8
-                    out[part, pl.ds(top, 8), side * LANES : (side + 1) * LANES] = source[
-                        member, lines : lines + 8, :
-                    ]
+                    line = piece * 32 + part * 16 + side * 8
+                    out[part, top : top + 8, side * LANES : (side + 1) * LANES] = jnp.where(
+                        ahead, mine[member, line : line + 8, :], other[member, line : line + 8, :]
+                    )
 
 
 def shine(light, group, total, at, block):
@@ -307,12 +310,7 @@
 
 
 def swap_z(value, mask):
-    pairs = []
-    for tile in range(TILES):
-        layer, rest = divmod(tile, 4)
-        ahead = 1 if rest == 0 else 0
-        other = (((layer - ahead) % (TILES // 4)) ^ mask) + ahead
-        pairs.append((tile, other % (TILES // 4) * 4 + rest))
+    pairs = [(tile, tile ^ (4 * mask)) for tile in range(1, TILES, 2)]
     return lax.ppermute(value, "tile", pairs)
 
 
@@ -396,6 +394,7 @@
     )
     pieces = exchange(merged)
     total = kernel_call(reduce_kernel, buffer(PIECE, LANES), [vmem], vmem, 4)(on_chip(pieces))
+    total = jnp.concatenate([total, swap_cores(total)], axis=0)
     new_object = kernel_call(
         object_kernel,
         jax.ShapeDtypeStruct((2, 40, LANES), jnp.float32),
@@ -408,7 +407,7 @@
     for mask in (1, 2):
         total = total + swap_z(total, mask)
     got, new_object = lax.optimization_barrier((swap_z(total, 6), new_object))
-    piece = kernel_call(probe_kernel, buffer(16, 32, LANES), [vmem] * 3, vmem, 4)(
+    piece = kernel_call(probe_kernel, buffer(16, 64, LANES), [vmem] * 3, vmem, 4)(
         on_chip(total), on_chip(got), probe
     )
 

time: 84.4 us -> 90.1 us (1.068)
  blocking collectives: 52.8 us -> 56.8 us
  waiting for transfers between devices: 6.83 us -> 9.37 us
  starting transfers between devices: 15.1 us -> 14.1 us
    ppermute x3 -> x4, starting transfers between devices: 7.58 us -> 1.22 us  [swap_cores(): return lax.ppermute(value, 'tile', [(i, i ^ 1) for i in range(TILES)])]
    ppermute x3, starting transfers between devices: 7.51 us -> 12.9 us  [swap_z(): return lax.ppermute(value, 'tile', pairs)]
    all_to_all x1, blocking collectives: 10.2 us -> 14.2 us  [exchange_plane(): lax.all_to_all(value, ('tile', 'group'), 0, 0, axis_index_groups=groups)]
    ppermute x3 -> x4, waiting for transfers between devices: 3.08 us -> 5.01 us  [swap_cores(): return lax.ppermute(value, 'tile', [(i, i ^ 1) for i in range(TILES)])]
  transfers between devices with their start and end apart: 6 -> 7, of which waited for: 4 -> 5; matrix products, arithmetic and copies ran while one was open for 0% -> 0% of each run, Pallas kernels for 2% -> 2%
where the time goes in v12:
time: 90.1 us; the launch traced here: 89.8 us
  blocking collectives  56.8 us (63%)
  starting transfers between devices  14.1 us (16%)
  waiting for transfers between devices  9.37 us (10%)
  Pallas kernels  5.76 us (6%)
  between operations  2.74 us (3%)
  local copies, waits for them, and re-layouts  0.96 us (1%)
    all_to_all x2, blocking collectives, exchange(): lax.all_to_all(value, ('tile', 'group'), 0, 0, axis_index_groups=groups)  42.6 us
    all_to_all x1, blocking collectives, exchange_plane(): lax.all_to_all(value, ('tile', 'group'), 0, 0, axis_index_groups=groups)  14.2 us
    ppermute x3, starting transfers between devices, swap_z(): return lax.ppermute(value, 'tile', pairs)  12.9 us
    ppermute x4, waiting for transfers between devices, swap_cores(): return lax.ppermute(value, 'tile', [(i, i ^ 1) for i in range(TILES)])  5.01 us
    ppermute x3, waiting for transfers between devices, swap_z(): return lax.ppermute(value, 'tile', pairs)  4.36 us
    pallas_call x1, Pallas kernels, local(): kernel_call(window_kernel, (buffer(16 * PIECE + 640, LANES), buffer(3, WI...  2.7 us
  transfers between devices with their start and end apart: 7, of which 5 were waited for; matrix products, arithmetic and copies ran while one was open for 0% of the time, Pallas kernels for 2%

profile of v12, /device:TPU:1, one launch (start us, length us, event | category | flops | bytes accessed | tf_op | source)
XLA Modules:
  0.0 89.8 jit_solution(12308846341193263008)
XLA Ops:
  0.6 0.0 copy-start.1
  0.6 0.0 copy-start.2
  0.7 0.0 copy-start.3
  0.7 0.0 copy-start
  0.7 0.9 %broadcast_in_dim.3 = f32[16,80,128]{2,1,0:T(8,128)S(1)} broadcast(f32[80,128]{1,0:T(8,128)} %bitcast.1), dimensions={1,2} | broadcast | bytes 696320 | tf_op jit(solution)/shard_map/broadcast_in_dim | solution.py:365
  1.6 21.5 %all_to_all.15.stack = f32[16,80,128]{2,1,0:T(8,128)S(1)} all-to-all(f32[16,80,128]{2,1,0:T(8,128)S(1)} %broadcast_in_dim.3), channel_id=1, replica_groups={{8,9,10,11,12,13,14,15,16,17,18,19,20,21,22,23},{24,25,26,27,28,29,30,3..., dimensions={0} | all-to-all | bytes 1310720 | tf_op jit(solution)/shard_map/all_to_all | solution.py:322
  23.1 0.9 %collective-permute-start = (f32[16,80,128]{2,1,0:T(8,128)S(1)}, f32[16,80,128]{2,1,0:T(8,128)S(1)}, u32[]{:S(2)}, u32[]{:S(2)}) collective-permute-start(f32[16,80,128]{2,1,0:T(8,128)S(1)} %all_to_all.15.stack), channel_id=1, source_target_pairs={{0,8},{8,0},{16,24},{24,16},{32,40},{40,32},{48,56},{56,48},{64,72... | collective-permute-start | bytes 1966088 | tf_op jit(solution)/shard_map/ppermute | solution.py:309
  26.0 0.0 collective-permute-done.near
  26.0 0.0 copy-done.1
  26.0 0.0 copy-done.2
  26.0 0.0 copy-done.3
  26.0 0.0 copy-done
  26.0 2.7 %window.1 = (f32[1536,128]{1,0:T(8,128)S(1)}, f32[3,256,256]{2,1,0:T(8,128)S(1)}, f32[2,3,320,128]{3,2,1,0:T(8,128)S(1)}, f32[8,128]{1,0:T(8,128)S(1)}) custom-call(s32[1]{0:T(128)S(6)} %copy.10.row_ref, s32[1]{0:T(128)S(6)} %copy.11.col_ref, s32[1]{0:T(128)S(6)} %copy.12.live_ref, f32[16,80,128]{2,1,0:T(8,128)S(1)} %all_to_all.15.stack, ...), custom_call_target="tpu_custom_call" | custom-call | tf_op jit(solution)/shard_map/window/pallas_call | solution.py:374
  28.7 0.2 collective-permute-start.1
  28.9 0.2 prep.1
  29.2 1.9 %collective-permute-done.1.got = f32[1536,128]{1,0:T(8,128)S(1)} collective-permute-done((f32[1536,128]{1,0:T(8,128)S(1)}, f32[1536,128]{1,0:T(8,128)S(1)}, u32[]{:S(2)}, u32[]{:S(2)}) %collective-permute-start.1) | collective-permute-done | bytes 786464 | tf_op jit(solution)/shard_map/ppermute | solution.py:309
  31.1 0.1 merge.1
  31.2 21.1 %all_to_all.16.pieces = f32[16,136,128]{2,1,0:T(8,128)S(1)} all-to-all(f32[16,136,128]{2,1,0:T(8,128)S(1)} %merge.1), channel_id=1, replica_groups={{8,9,10,11,12,13,14,15,16,17,18,19,20,21,22,23},{24,25,26,27,28,29,30,3..., dimensions={0} | all-to-all | bytes 2228224 | tf_op jit(solution)/shard_map/all_to_all | solution.py:322
  52.3 0.0 copy-start.4
  52.4 0.1 collective-permute-start.2
  52.5 1.2 %collective-permute-done.2 = f32[56,128]{1,0:T(8,128)S(1)} collective-permute-done((f32[56,128]{1,0:T(8,128)S(1)}, f32[56,128]{1,0:T(8,128)S(1)}, u32[]{:S(2)}, u32[]{:S(2)}) %collective-permute-start.2) | collective-permute-done | bytes 28704 | tf_op jit(solution)/shard_map/ppermute | solution.py:309
  53.7 2.1 %collective-permute-start.3 = (f32[112,128]{1,0:T(8,128)S(1)}, f32[112,128]{1,0:T(8,128)S(1)}, u32[]{:S(2)}, u32[]{:S(2)}) collective-permute-start(f32[112,128]{1,0:T(8,128)S(1)} %pad_maximum_fusion), channel_id=1, source_target_pairs={{8,40},{24,56},{40,8},{56,24},{72,104},{88,120},{104,72},{120,88},... | collective-permute-start | bytes 172040 | tf_op jit(solution)/shard_map/ppermute | solution.py:314
  55.8 2.8 %collective-permute-done.3 = f32[112,128]{1,0:T(8,128)S(1)} collective-permute-done((f32[112,128]{1,0:T(8,128)S(1)}, f32[112,128]{1,0:T(8,128)S(1)}, u32[]{:S(2)}, u32[]{:S(2)}) %collective-permute-start.3) | collective-permute-done | bytes 57376 | tf_op jit(solution)/shard_map/ppermute | solution.py:314
  58.6 5.1 %collective-permute-start.4 = (f32[112,128]{1,0:T(8,128)S(1)}, f32[112,128]{1,0:T(8,128)S(1)}, u32[]{:S(2)}, u32[]{:S(2)}) collective-permute-start(f32[112,128]{1,0:T(8,128)S(1)} %fusion), channel_id=1, source_target_pairs={{8,72},{24,88},{40,104},{56,120},{72,8},{88,24},{104,40},{120,56},... | collective-permute-start | bytes 172040 | tf_op jit(solution)/shard_map/ppermute | solution.py:314
  63.6 1.6 %collective-permute-done.4 = f32[112,128]{1,0:T(8,128)S(1)} collective-permute-done((f32[112,128]{1,0:T(8,128)S(1)}, f32[112,128]{1,0:T(8,128)S(1)}, u32[]{:S(2)}, u32[]{:S(2)}) %collective-permute-start.4) | collective-permute-done | bytes 57376 | tf_op jit(solution)/shard_map/ppermute | solution.py:314
  65.2 5.7 %collective-permute-start.5 = (f32[112,128]{1,0:T(8,128)S(1)}, f32[112,128]{1,0:T(8,128)S(1)}, u32[]{:S(2)}, u32[]{:S(2)}) collective-permute-start(f32[112,128]{1,0:T(8,128)S(1)} %add.7.one), channel_id=1, source_target_pairs={{8,200},{24,216},{40,232},{56,248},{72,136},{88,152},{104,168},{12... | collective-permute-start | bytes 172040 | tf_op jit(solution)/shard_map/ppermute | solution.py:314
  70.9 0.0 copy-done.4
  70.9 1.7 %object.1 = f32[2,40,128]{2,1,0:T(8,128)} custom-call(f32[16,136,128]{2,1,0:T(8,128)S(1)} %all_to_all.16.pieces, f32[2,40,128]{2,1,0:T(8,128)S(1)} %copy-done.4, f32[4,384,128]{2,1,0:T(8,128)S(1)} %get-tuple-element.18.light, f32[8,128]{1,0:T(8,128)S(1)} %get-tuple-element.19.peak), custom_call_target="tpu_custom_call" | custom-call | flops 700000 | bytes 2000000 | tf_op jit(solution)/shard_map/object/pallas_call | solution.py:398
  72.6 0.0 collective-permute-done.5.two
  72.6 0.2 probe.6
  72.8 14.2 %all_to_all.17.mine = f32[16,64,128]{2,1,0:T(8,128)S(1)} all-to-all(f32[16,64,128]{2,1,0:T(8,128)S(1)} %probe.6), channel_id=1, replica_groups={{0,1,16,17,2,3,18,19,4,5,20,21,6,7,22,23},{8,9,24,25,10,11,26,27,12,13,..., dimensions={0} | all-to-all | bytes 1048576 | tf_op jit(solution)/shard_map/all_to_all | solution.py:337
  87.0 0.0 collective-permute-start.6
  87.0 1.9 %collective-permute-done.6.other = f32[16,64,128]{2,1,0:T(8,128)S(1)} collective-permute-done((f32[16,64,128]{2,1,0:T(8,128)S(1)}, f32[16,64,128]{2,1,0:T(8,128)S(1)}, u32[]{:S(2)}, u32[]{:S(2)}) %collective-permute-start.6) | collective-permute-done | bytes 524320 | tf_op jit(solution)/shard_map/ppermute | solution.py:309
  88.9 0.8 gather.1
  (4 shorter events, 0.1 us)
Async XLA Ops:
  0.6 25.3 %copy-start.1 = (bf16[768,256]{1,0:T(8,128)(2,1)S(1)}, bf16[768,256]{1,0:T(8,128)(2,1)}, u32[]{:S(2)}) copy-start(bf16[768,256]{1,0:T(8,128)(2,1)} %constant.4.clone.row_table) | copy-start | bytes 1179652
  0.6 25.3 %copy-start.2 = (bf16[768,256]{1,0:T(8,128)(2,1)S(1)}, bf16[768,256]{1,0:T(8,128)(2,1)}, u32[]{:S(2)}) copy-start(bf16[768,256]{1,0:T(8,128)(2,1)} %constant.5.clone.col_table) | copy-start | bytes 1179652
  0.7 25.3 %copy-start.3 = (f32[1,256,256]{2,1,0:T(8,128)S(1)}, f32[1,256,256]{2,1,0:T(8,128)}, u32[]{:S(2)}) copy-start(f32[1,256,256]{2,1,0:T(8,128)} %amps.1) | copy-start | bytes 786436
  0.7 25.3 %copy-start = (f32[2,256,256]{2,1,0:T(8,128)S(1)}, f32[2,256,256]{2,1,0:T(8,128)}, u32[]{:S(2)}) copy-start(f32[2,256,256]{2,1,0:T(8,128)} %probe.7) | copy-start | bytes 1572868
  23.1 2.8 %collective-permute-start = (f32[16,80,128]{2,1,0:T(8,128)S(1)}, f32[16,80,128]{2,1,0:T(8,128)S(1)}, u32[]{:S(2)}, u32[]{:S(2)}) collective-permute-start(f32[16,80,128]{2,1,0:T(8,128)S(1)} %all_to_all.15.stack), channel_id=1, source_target_pairs={{0,8},{8,0},{16,24},{24,16},{32,40},{40,32},{48,56},{56,48},{64,72... | collective-permute-start | bytes 1966088 | tf_op jit(solution)/shard_map/ppermute | solution.py:309
  28.7 2.4 %collective-permute-start.1 = (f32[1536,128]{1,0:T(8,128)S(1)}, f32[1536,128]{1,0:T(8,128)S(1)}, u32[]{:S(2)}, u32[]{:S(2)}) collective-permute-start(f32[1536,128]{1,0:T(8,128)S(1)} %get-tuple-element.15), channel_id=1, source_target_pairs={{0,8},{8,0},{16,24},{24,16},{32,40},{40,32},{48,56},{56,48},{64,72... | collective-permute-start | bytes 2359304 | tf_op jit(solution)/shard_map/ppermute | solution.py:309
  52.3 18.6 %copy-start.4 = (f32[2,40,128]{2,1,0:T(8,128)S(1)}, f32[2,40,128]{2,1,0:T(8,128)}, u32[]{:S(2)}) copy-start(f32[2,40,128]{2,1,0:T(8,128)} %old.1) | copy-start | bytes 122884
  52.4 1.3 %collective-permute-start.2 = (f32[56,128]{1,0:T(8,128)S(1)}, f32[56,128]{1,0:T(8,128)S(1)}, u32[]{:S(2)}, u32[]{:S(2)}) collective-permute-start(f32[56,128]{1,0:T(8,128)S(1)} %reduce.1), channel_id=1, source_target_pairs={{0,8},{8,0},{16,24},{24,16},{32,40},{40,32},{48,56},{56,48},{64,72... | collective-permute-start | bytes 86024 | tf_op jit(solution)/shard_map/ppermute | solution.py:309
  53.7 4.9 %collective-permute-start.3 = (f32[112,128]{1,0:T(8,128)S(1)}, f32[112,128]{1,0:T(8,128)S(1)}, u32[]{:S(2)}, u32[]{:S(2)}) collective-permute-start(f32[112,128]{1,0:T(8,128)S(1)} %pad_maximum_fusion), channel_id=1, source_target_pairs={{8,40},{24,56},{40,8},{56,24},{72,104},{88,120},{104,72},{120,88},... | collective-permute-start | bytes 172040 | tf_op jit(solution)/shard_map/ppermute | solution.py:314
  58.6 6.6 %collective-permute-start.4 = (f32[112,128]{1,0:T(8,128)S(1)}, f32[112,128]{1,0:T(8,128)S(1)}, u32[]{:S(2)}, u32[]{:S(2)}) collective-permute-start(f32[112,128]{1,0:T(8,128)S(1)} %fusion), channel_id=1, source_target_pairs={{8,72},{24,88},{40,104},{56,120},{72,8},{88,24},{104,40},{120,56},... | collective-permute-start | bytes 172040 | tf_op jit(solution)/shard_map/ppermute | solution.py:314
  65.2 7.4 %collective-permute-start.5 = (f32[112,128]{1,0:T(8,128)S(1)}, f32[112,128]{1,0:T(8,128)S(1)}, u32[]{:S(2)}, u32[]{:S(2)}) collective-permute-start(f32[112,128]{1,0:T(8,128)S(1)} %add.7.one), channel_id=1, source_target_pairs={{8,200},{24,216},{40,232},{56,248},{72,136},{88,152},{104,168},{12... | collective-permute-start | bytes 172040 | tf_op jit(solution)/shard_map/ppermute | solution.py:314
  87.0 1.9 %collective-permute-start.6 = (f32[16,64,128]{2,1,0:T(8,128)S(1)}, f32[16,64,128]{2,1,0:T(8,128)S(1)}, u32[]{:S(2)}, u32[]{:S(2)}) collective-permute-start(f32[16,64,128]{2,1,0:T(8,128)S(1)} %all_to_all.17.mine), channel_id=1, source_target_pairs={{0,8},{8,0},{16,24},{24,16},{32,40},{40,32},{48,56},{56,48},{64,72... | collective-permute-start | bytes 1572872 | tf_op jit(solution)/shard_map/ppermute | solution.py:309

commit v13 on v11

--- a/solution.py
+++ b/solution.py
@@ -41,7 +41,9 @@
 
 
 def product(left, right):
-    return dot(left[0], right[0]) + dot(left[0], right[1]) + dot(left[1], right[0])
+    height = left[0].shape[0]
+    tall = dot(jnp.concatenate(left, axis=0), right[0])
+    return tall[:height] + tall[height:] + dot(left[0], right[1])
 
 
 def unfold(cos_real, cos_imag, sin_real, sin_imag, axis):
@@ -93,6 +95,10 @@
     taken = dot(rows[2 * WIN :], jnp.concatenate(halves(value), axis=1)).astype(jnp.bfloat16)
     taken = dot(jnp.concatenate([taken[:, :WIN], taken[:, WIN:]], axis=0), cols[2 * WIN :])
     return taken[:WIN] + taken[WIN:]
+
+
+def own_kernel(stack, out):
+    out[...] = stack[pl.ds(8 - 8 * (my_place()[0] & 1), 8)]
 
 
 def window_kernel(
@@ -110,7 +116,7 @@
             held = slice(part * 40, part * 40 + 40)
             field[part, 1, lines, :] = stack[8 - 8 * odd + member, held, :]
             field[part, 2 * odd, lines, :] = jnp.where(inside, stack[8 * odd + member, held, :], 0.0)
-            field[part, 2 - 2 * odd, lines, :] = near[8 * odd + member, held, :]
+            field[part, 2 - 2 * odd, lines, :] = near[member, held, :]
     lane = lax.broadcasted_iota(jnp.int32, (WIN, LANES), 1)
     back = lax.rem(LANES - col, LANES)
     ahead = lax.rem(col, LANES)
@@ -365,6 +371,7 @@
 
     own = object_field.reshape(80, LANES)
     stack = exchange(jnp.broadcast_to(own, (16, 80, LANES)))
+    near = swap_cores(kernel_call(own_kernel, buffer(8, 80, LANES), [vmem], vmem, 4)(on_chip(stack)))
     light, peak = kernel_call(
         prep_kernel,
         (buffer(4, 384, LANES), buffer(8, LANES)),
@@ -386,7 +393,7 @@
         24,
         scratch_shapes=[buffer(2, 3, 320, LANES)],
     )(
-        row_start, column_start, live_slots, on_chip(stack), on_chip(swap_cores(stack)), probe,
+        row_start, column_start, live_slots, on_chip(stack), on_chip(near), probe,
         on_chip(amplitudes), row_table, col_table,
     )
 

time: 84.4 us -> 84.4 us (level)
  no operation moved by 1% of the time
where the time goes in v13:
time: 84.4 us; the launch traced here: 84.1 us
  blocking collectives  52.9 us (63%)
  starting transfers between devices  15.1 us (18%)
  waiting for transfers between devices  6.95 us (8%)
  Pallas kernels  5.59 us (7%)
  between operations  2.71 us (3%)
  local copies, waits for them, and re-layouts  0.85 us (1%)
    all_to_all x2, blocking collectives, exchange(): lax.all_to_all(value, ('tile', 'group'), 0, 0, axis_index_groups=groups)  42.7 us
    all_to_all x1, blocking collectives, exchange_plane(): lax.all_to_all(value, ('tile', 'group'), 0, 0, axis_index_groups=groups)  10.2 us
    ppermute x3, starting transfers between devices, swap_cores(): return lax.ppermute(value, 'tile', [(i, i ^ 1) for i in range(TILES)])  7.55 us
    ppermute x3, starting transfers between devices, swap_z(): return lax.ppermute(value, 'tile', pairs)  7.51 us
    ppermute x3, waiting for transfers between devices, swap_z(): return lax.ppermute(value, 'tile', pairs)  3.76 us
    ppermute x3, waiting for transfers between devices, swap_cores(): return lax.ppermute(value, 'tile', [(i, i ^ 1) for i in range(TILES)])  3.2 us
    pallas_call x1, Pallas kernels, local(): kernel_call(window_kernel, (buffer(16 * PIECE + 640, LANES), buffer(3, WI...  2.53 us
  transfers between devices with their start and end apart: 6, of which 4 were waited for; matrix products, arithmetic and copies ran while one was open for 0% of the time, Pallas kernels for 2%

profile of v13, /device:TPU:1, one launch (start us, length us, event | category | flops | bytes accessed | tf_op | source)
XLA Modules:
  0.0 84.1 jit_solution(3748995477397451604)
XLA Ops:
  0.6 0.8 broadcast_in_dim.3
  1.5 0.0 copy-start
  1.5 0.0 copy-start.1
  1.5 0.0 copy-start.2
  1.5 0.0 copy-start.3
  1.5 21.6 %all_to_all.15.stack = f32[16,80,128]{2,1,0:T(8,128)S(1)} all-to-all(f32[16,80,128]{2,1,0:T(8,128)S(1)} %broadcast_in_dim.3), channel_id=1, replica_groups={{8,9,10,11,12,13,14,15,16,17,18,19,20,21,22,23},{24,25,26,27,28,29,30,3..., dimensions={0} | all-to-all | bytes 1310720 | tf_op jit(solution)/shard_map/all_to_all | solution.py:330
  23.2 1.0 %collective-permute-start = (f32[8,80,128]{2,1,0:T(8,128)S(1)}, f32[8,80,128]{2,1,0:T(8,128)S(1)}, u32[]{:S(2)}, u32[]{:S(2)}) collective-permute-start(f32[8,80,128]{2,1,0:T(8,128)S(1)} %own.1), channel_id=1, source_target_pairs={{0,8},{8,0},{16,24},{24,16},{32,40},{40,32},{48,56},{56,48},{64,72... | collective-permute-start | bytes 983048 | tf_op jit(solution)/shard_map/ppermute | solution.py:312
  26.1 0.0 collective-permute-done.near
  26.1 0.0 copy-done
  26.1 0.0 copy-done.1
  26.1 0.0 copy-done.2
  26.1 0.0 copy-done.3
  26.1 2.5 %window.1 = (f32[1536,128]{1,0:T(8,128)S(1)}, f32[3,256,256]{2,1,0:T(8,128)S(1)}, f32[2,3,320,128]{3,2,1,0:T(8,128)S(1)}, f32[8,128]{1,0:T(8,128)S(1)}) custom-call(s32[1]{0:T(128)S(6)} %copy.10.row_ref, s32[1]{0:T(128)S(6)} %copy.11.col_ref, s32[1]{0:T(128)S(6)} %copy.12.live_ref, f32[16,80,128]{2,1,0:T(8,128)S(1)} %all_to_all.15.stack, ...), custom_call_target="tpu_custom_call" | custom-call | tf_op jit(solution)/shard_map/window/pallas_call | solution.py:383
  28.7 0.1 collective-permute-start.1
  28.8 0.2 prep.1
  29.0 2.0 %collective-permute-done.1.got = f32[1536,128]{1,0:T(8,128)S(1)} collective-permute-done((f32[1536,128]{1,0:T(8,128)S(1)}, f32[1536,128]{1,0:T(8,128)S(1)}, u32[]{:S(2)}, u32[]{:S(2)}) %collective-permute-start.1) | collective-permute-done | bytes 786464 | tf_op jit(solution)/shard_map/ppermute | solution.py:312
  31.1 0.1 merge.1
  31.2 21.1 %all_to_all.16.pieces = f32[16,136,128]{2,1,0:T(8,128)S(1)} all-to-all(f32[16,136,128]{2,1,0:T(8,128)S(1)} %merge.1), channel_id=1, replica_groups={{8,9,10,11,12,13,14,15,16,17,18,19,20,21,22,23},{24,25,26,27,28,29,30,3..., dimensions={0} | all-to-all | bytes 2228224 | tf_op jit(solution)/shard_map/all_to_all | solution.py:330
  52.3 0.0 copy-start.4
  52.3 0.3 collective-permute-start.2
  52.6 2.5 %collective-permute-done.2 = f32[56,128]{1,0:T(8,128)S(1)} collective-permute-done((f32[56,128]{1,0:T(8,128)S(1)}, f32[56,128]{1,0:T(8,128)S(1)}, u32[]{:S(2)}, u32[]{:S(2)}) %collective-permute-start.2) | collective-permute-done | bytes 28704 | tf_op jit(solution)/shard_map/ppermute | solution.py:322
  55.1 3.1 %collective-permute-start.3 = (f32[56,128]{1,0:T(8,128)S(1)}, f32[56,128]{1,0:T(8,128)S(1)}, u32[]{:S(2)}, u32[]{:S(2)}) collective-permute-start(f32[56,128]{1,0:T(8,128)S(1)} %add.6), channel_id=1, source_target_pairs={{0,192},{8,72},{16,80},{24,88},{32,96},{40,104},{48,112},{56,120},... | collective-permute-start | bytes 86024 | tf_op jit(solution)/shard_map/ppermute | solution.py:322
  58.3 1.3 %collective-permute-done.3 = f32[56,128]{1,0:T(8,128)S(1)} collective-permute-done((f32[56,128]{1,0:T(8,128)S(1)}, f32[56,128]{1,0:T(8,128)S(1)}, u32[]{:S(2)}, u32[]{:S(2)}) %collective-permute-start.3) | collective-permute-done | bytes 28704 | tf_op jit(solution)/shard_map/ppermute | solution.py:322
  59.5 4.1 %collective-permute-start.4 = (f32[56,128]{1,0:T(8,128)S(1)}, f32[56,128]{1,0:T(8,128)S(1)}, u32[]{:S(2)}, u32[]{:S(2)}) collective-permute-start(f32[56,128]{1,0:T(8,128)S(1)} %add.7.one), channel_id=1, source_target_pairs={{0,64},{8,200},{16,208},{24,216},{32,224},{40,232},{48,240},{56,24... | collective-permute-start | bytes 86024 | tf_op jit(solution)/shard_map/ppermute | solution.py:322
  63.6 0.0 copy-done.4
  63.6 1.6 %object.1 = f32[2,40,128]{2,1,0:T(8,128)} custom-call(f32[16,136,128]{2,1,0:T(8,128)S(1)} %all_to_all.16.pieces, f32[2,40,128]{2,1,0:T(8,128)S(1)} %copy-done.4, f32[4,384,128]{2,1,0:T(8,128)S(1)} %get-tuple-element.18.light, f32[8,128]{1,0:T(8,128)S(1)} %get-tuple-element.19.peak), custom_call_target="tpu_custom_call" | custom-call | flops 700000 | bytes 2000000 | tf_op jit(solution)/shard_map/object/pallas_call | solution.py:406
  65.3 0.0 collective-permute-done.4.two
  65.3 0.1 probe.6
  65.4 10.2 %all_to_all.17.mine = f32[16,32,128]{2,1,0:T(8,128)S(1)} all-to-all(f32[16,32,128]{2,1,0:T(8,128)S(1)} %probe.6), channel_id=1, replica_groups={{0,1,16,17,2,3,18,19,4,5,20,21,6,7,22,23},{8,9,24,25,10,11,26,27,12,13,..., dimensions={0} | all-to-all | bytes 524288 | tf_op jit(solution)/shard_map/all_to_all | solution.py:345
  75.6 6.5 %collective-permute-start.5 = (f32[16,32,128]{2,1,0:T(8,128)S(1)}, f32[16,32,128]{2,1,0:T(8,128)S(1)}, u32[]{:S(2)}, u32[]{:S(2)}) collective-permute-start(f32[16,32,128]{2,1,0:T(8,128)S(1)} %all_to_all.17.mine), channel_id=1, source_target_pairs={{0,8},{8,0},{16,24},{24,16},{32,40},{40,32},{48,56},{56,48},{64,72... | collective-permute-start | bytes 786440 | tf_op jit(solution)/shard_map/ppermute | solution.py:312
  82.1 1.2 %collective-permute-done.5.other = f32[16,32,128]{2,1,0:T(8,128)S(1)} collective-permute-done((f32[16,32,128]{2,1,0:T(8,128)S(1)}, f32[16,32,128]{2,1,0:T(8,128)S(1)}, u32[]{:S(2)}, u32[]{:S(2)}) %collective-permute-start.5) | collective-permute-done | bytes 262176 | tf_op jit(solution)/shard_map/ppermute | solution.py:312
  83.3 0.9 %gather.1 = f32[2,256,256]{2,1,0:T(8,128)} custom-call(f32[16,32,128]{2,1,0:T(8,128)S(1)} %all_to_all.17.mine, f32[16,32,128]{2,1,0:T(8,128)S(1)} %collective-permute-done.5.other), custom_call_target="tpu_custom_call" | custom-call | tf_op jit(solution)/shard_map/gather/pallas_call | solution.py:423
  (4 shorter events, 0.1 us)
Async XLA Ops:
  1.5 24.6 %copy-start = (f32[2,256,256]{2,1,0:T(8,128)S(1)}, f32[2,256,256]{2,1,0:T(8,128)}, u32[]{:S(2)}) copy-start(f32[2,256,256]{2,1,0:T(8,128)} %probe.7) | copy-start | bytes 1572868
  1.5 24.6 %copy-start.1 = (bf16[768,256]{1,0:T(8,128)(2,1)S(1)}, bf16[768,256]{1,0:T(8,128)(2,1)}, u32[]{:S(2)}) copy-start(bf16[768,256]{1,0:T(8,128)(2,1)} %constant.5.clone.col_table) | copy-start | bytes 1179652
  1.5 24.6 %copy-start.2 = (bf16[768,256]{1,0:T(8,128)(2,1)S(1)}, bf16[768,256]{1,0:T(8,128)(2,1)}, u32[]{:S(2)}) copy-start(bf16[768,256]{1,0:T(8,128)(2,1)} %constant.4.clone.row_table) | copy-start | bytes 1179652
  1.5 24.6 %copy-start.3 = (f32[1,256,256]{2,1,0:T(8,128)S(1)}, f32[1,256,256]{2,1,0:T(8,128)}, u32[]{:S(2)}) copy-start(f32[1,256,256]{2,1,0:T(8,128)} %amps.1) | copy-start | bytes 786436
  23.2 2.9 %collective-permute-start = (f32[8,80,128]{2,1,0:T(8,128)S(1)}, f32[8,80,128]{2,1,0:T(8,128)S(1)}, u32[]{:S(2)}, u32[]{:S(2)}) collective-permute-start(f32[8,80,128]{2,1,0:T(8,128)S(1)} %own.1), channel_id=1, source_target_pairs={{0,8},{8,0},{16,24},{24,16},{32,40},{40,32},{48,56},{56,48},{64,72... | collective-permute-start | bytes 983048 | tf_op jit(solution)/shard_map/ppermute | solution.py:312
  28.7 2.4 %collective-permute-start.1 = (f32[1536,128]{1,0:T(8,128)S(1)}, f32[1536,128]{1,0:T(8,128)S(1)}, u32[]{:S(2)}, u32[]{:S(2)}) collective-permute-start(f32[1536,128]{1,0:T(8,128)S(1)} %get-tuple-element.15), channel_id=1, source_target_pairs={{0,8},{8,0},{16,24},{24,16},{32,40},{40,32},{48,56},{56,48},{64,72... | collective-permute-start | bytes 2359304 | tf_op jit(solution)/shard_map/ppermute | solution.py:312
  52.3 11.3 %copy-start.4 = (f32[2,40,128]{2,1,0:T(8,128)S(1)}, f32[2,40,128]{2,1,0:T(8,128)}, u32[]{:S(2)}) copy-start(f32[2,40,128]{2,1,0:T(8,128)} %old.1) | copy-start | bytes 122884
  52.3 2.8 %collective-permute-start.2 = (f32[56,128]{1,0:T(8,128)S(1)}, f32[56,128]{1,0:T(8,128)S(1)}, u32[]{:S(2)}, u32[]{:S(2)}) collective-permute-start(f32[56,128]{1,0:T(8,128)S(1)} %reduce.1), channel_id=1, source_target_pairs={{0,224},{8,40},{16,48},{24,56},{32,64},{40,8},{48,16},{56,24},{64,... | collective-permute-start | bytes 86024 | tf_op jit(solution)/shard_map/ppermute | solution.py:322
  55.1 4.4 %collective-permute-start.3 = (f32[56,128]{1,0:T(8,128)S(1)}, f32[56,128]{1,0:T(8,128)S(1)}, u32[]{:S(2)}, u32[]{:S(2)}) collective-permute-start(f32[56,128]{1,0:T(8,128)S(1)} %add.6), channel_id=1, source_target_pairs={{0,192},{8,72},{16,80},{24,88},{32,96},{40,104},{48,112},{56,120},... | collective-permute-start | bytes 86024 | tf_op jit(solution)/shard_map/ppermute | solution.py:322
  59.5 5.7 %collective-permute-start.4 = (f32[56,128]{1,0:T(8,128)S(1)}, f32[56,128]{1,0:T(8,128)S(1)}, u32[]{:S(2)}, u32[]{:S(2)}) collective-permute-start(f32[56,128]{1,0:T(8,128)S(1)} %add.7.one), channel_id=1, source_target_pairs={{0,64},{8,200},{16,208},{24,216},{32,224},{40,232},{48,240},{56,24... | collective-permute-start | bytes 86024 | tf_op jit(solution)/shard_map/ppermute | solution.py:322
  75.6 7.6 %collective-permute-start.5 = (f32[16,32,128]{2,1,0:T(8,128)S(1)}, f32[16,32,128]{2,1,0:T(8,128)S(1)}, u32[]{:S(2)}, u32[]{:S(2)}) collective-permute-start(f32[16,32,128]{2,1,0:T(8,128)S(1)} %all_to_all.17.mine), channel_id=1, source_target_pairs={{0,8},{8,0},{16,24},{24,16},{32,40},{40,32},{48,56},{56,48},{64,72... | collective-permute-start | bytes 786440 | tf_op jit(solution)/shard_map/ppermute | solution.py:312

commit v14 on v11

--- a/solution.py
+++ b/solution.py
@@ -41,7 +41,9 @@
 
 
 def product(left, right):
-    return dot(left[0], right[0]) + dot(left[0], right[1]) + dot(left[1], right[0])
+    height = left[0].shape[0]
+    tall = dot(jnp.concatenate(left, axis=0), right[0])
+    return tall[:height] + tall[height:] + dot(left[0], right[1])
 
 
 def unfold(cos_real, cos_imag, sin_real, sin_imag, axis):

time: 84.4 us -> 84.2 us (level)
  no operation moved by 1% of the time
where the time goes in v14:
time: 84.2 us; the launch traced here: 84 us
  blocking collectives  52.8 us (63%)
  starting transfers between devices  15.1 us (18%)
  waiting for transfers between devices  6.83 us (8%)
  Pallas kernels  5.57 us (7%)
  between operations  2.7 us (3%)
  local copies, waits for them, and re-layouts  0.96 us (1%)
    all_to_all x2, blocking collectives, exchange(): lax.all_to_all(value, ('tile', 'group'), 0, 0, axis_index_groups=groups)  42.6 us
    all_to_all x1, blocking collectives, exchange_plane(): lax.all_to_all(value, ('tile', 'group'), 0, 0, axis_index_groups=groups)  10.2 us
    ppermute x3, starting transfers between devices, swap_cores(): return lax.ppermute(value, 'tile', [(i, i ^ 1) for i in range(TILES)])  7.59 us
    ppermute x3, starting transfers between devices, swap_z(): return lax.ppermute(value, 'tile', pairs)  7.51 us
    ppermute x3, waiting for transfers between devices, swap_z(): return lax.ppermute(value, 'tile', pairs)  3.75 us
    ppermute x3, waiting for transfers between devices, swap_cores(): return lax.ppermute(value, 'tile', [(i, i ^ 1) for i in range(TILES)])  3.08 us
    pallas_call x1, Pallas kernels, local(): kernel_call(window_kernel, (buffer(16 * PIECE + 640, LANES), buffer(3, WI...  2.54 us
  transfers between devices with their start and end apart: 6, of which 4 were waited for; matrix products, arithmetic and copies ran while one was open for 0% of the time, Pallas kernels for 2%

profile of v14, /device:TPU:1, one launch (start us, length us, event | category | flops | bytes accessed | tf_op | source)
XLA Modules:
  0.0 84.0 jit_solution(1636991518454535549)
XLA Ops:
  0.6 0.0 copy-start.1
  0.6 0.0 copy-start.2
  0.7 0.0 copy-start.3
  0.7 0.0 copy-start
  0.7 0.9 %broadcast_in_dim.3 = f32[16,80,128]{2,1,0:T(8,128)S(1)} broadcast(f32[80,128]{1,0:T(8,128)} %bitcast.1), dimensions={1,2} | broadcast | bytes 696320 | tf_op jit(solution)/shard_map/broadcast_in_dim | solution.py:369
  1.6 21.5 %all_to_all.15.stack = f32[16,80,128]{2,1,0:T(8,128)S(1)} all-to-all(f32[16,80,128]{2,1,0:T(8,128)S(1)} %broadcast_in_dim.3), channel_id=1, replica_groups={{8,9,10,11,12,13,14,15,16,17,18,19,20,21,22,23},{24,25,26,27,28,29,30,3..., dimensions={0} | all-to-all | bytes 1310720 | tf_op jit(solution)/shard_map/all_to_all | solution.py:326
  23.1 0.9 %collective-permute-start = (f32[16,80,128]{2,1,0:T(8,128)S(1)}, f32[16,80,128]{2,1,0:T(8,128)S(1)}, u32[]{:S(2)}, u32[]{:S(2)}) collective-permute-start(f32[16,80,128]{2,1,0:T(8,128)S(1)} %all_to_all.15.stack), channel_id=1, source_target_pairs={{0,8},{8,0},{16,24},{24,16},{32,40},{40,32},{48,56},{56,48},{64,72... | collective-permute-start | bytes 1966088 | tf_op jit(solution)/shard_map/ppermute | solution.py:308
  26.0 0.0 collective-permute-done.near
  26.0 0.0 copy-done.1
  26.0 0.0 copy-done.2
  26.0 0.0 copy-done.3
  26.0 0.0 copy-done
  26.0 2.5 %window.1 = (f32[1536,128]{1,0:T(8,128)S(1)}, f32[3,256,256]{2,1,0:T(8,128)S(1)}, f32[2,3,320,128]{3,2,1,0:T(8,128)S(1)}, f32[8,128]{1,0:T(8,128)S(1)}) custom-call(s32[1]{0:T(128)S(6)} %copy.10.row_ref, s32[1]{0:T(128)S(6)} %copy.11.col_ref, s32[1]{0:T(128)S(6)} %copy.12.live_ref, f32[16,80,128]{2,1,0:T(8,128)S(1)} %all_to_all.15.stack, ...), custom_call_target="tpu_custom_call" | custom-call | tf_op jit(solution)/shard_map/window/pallas_call | solution.py:378
  28.5 0.2 collective-permute-start.1
  28.8 0.2 prep.1
  29.0 1.9 %collective-permute-done.1.got = f32[1536,128]{1,0:T(8,128)S(1)} collective-permute-done((f32[1536,128]{1,0:T(8,128)S(1)}, f32[1536,128]{1,0:T(8,128)S(1)}, u32[]{:S(2)}, u32[]{:S(2)}) %collective-permute-start.1) | collective-permute-done | bytes 786464 | tf_op jit(solution)/shard_map/ppermute | solution.py:308
  30.9 0.1 merge.1
  31.1 21.1 %all_to_all.16.pieces = f32[16,136,128]{2,1,0:T(8,128)S(1)} all-to-all(f32[16,136,128]{2,1,0:T(8,128)S(1)} %merge.1), channel_id=1, replica_groups={{8,9,10,11,12,13,14,15,16,17,18,19,20,21,22,23},{24,25,26,27,28,29,30,3..., dimensions={0} | all-to-all | bytes 2228224 | tf_op jit(solution)/shard_map/all_to_all | solution.py:326
  52.2 0.0 copy-start.4
  52.2 0.3 collective-permute-start.2
  52.5 2.5 %collective-permute-done.2 = f32[56,128]{1,0:T(8,128)S(1)} collective-permute-done((f32[56,128]{1,0:T(8,128)S(1)}, f32[56,128]{1,0:T(8,128)S(1)}, u32[]{:S(2)}, u32[]{:S(2)}) %collective-permute-start.2) | collective-permute-done | bytes 28704 | tf_op jit(solution)/shard_map/ppermute | solution.py:318
  55.0 3.1 %collective-permute-start.3 = (f32[56,128]{1,0:T(8,128)S(1)}, f32[56,128]{1,0:T(8,128)S(1)}, u32[]{:S(2)}, u32[]{:S(2)}) collective-permute-start(f32[56,128]{1,0:T(8,128)S(1)} %add.6), channel_id=1, source_target_pairs={{0,192},{8,72},{16,80},{24,88},{32,96},{40,104},{48,112},{56,120},... | collective-permute-start | bytes 86024 | tf_op jit(solution)/shard_map/ppermute | solution.py:318
  58.1 1.3 %collective-permute-done.3 = f32[56,128]{1,0:T(8,128)S(1)} collective-permute-done((f32[56,128]{1,0:T(8,128)S(1)}, f32[56,128]{1,0:T(8,128)S(1)}, u32[]{:S(2)}, u32[]{:S(2)}) %collective-permute-start.3) | collective-permute-done | bytes 28704 | tf_op jit(solution)/shard_map/ppermute | solution.py:318
  59.4 4.1 %collective-permute-start.4 = (f32[56,128]{1,0:T(8,128)S(1)}, f32[56,128]{1,0:T(8,128)S(1)}, u32[]{:S(2)}, u32[]{:S(2)}) collective-permute-start(f32[56,128]{1,0:T(8,128)S(1)} %add.7.one), channel_id=1, source_target_pairs={{0,64},{8,200},{16,208},{24,216},{32,224},{40,232},{48,240},{56,24... | collective-permute-start | bytes 86024 | tf_op jit(solution)/shard_map/ppermute | solution.py:318
  63.5 0.0 copy-done.4
  63.5 1.6 %object.1 = f32[2,40,128]{2,1,0:T(8,128)} custom-call(f32[16,136,128]{2,1,0:T(8,128)S(1)} %all_to_all.16.pieces, f32[2,40,128]{2,1,0:T(8,128)S(1)} %copy-done.4, f32[4,384,128]{2,1,0:T(8,128)S(1)} %get-tuple-element.18.light, f32[8,128]{1,0:T(8,128)S(1)} %get-tuple-element.19.peak), custom_call_target="tpu_custom_call" | custom-call | flops 700000 | bytes 2000000 | tf_op jit(solution)/shard_map/object/pallas_call | solution.py:401
  65.1 0.0 collective-permute-done.4.two
  65.1 0.1 probe.6
  65.3 10.2 %all_to_all.17.mine = f32[16,32,128]{2,1,0:T(8,128)S(1)} all-to-all(f32[16,32,128]{2,1,0:T(8,128)S(1)} %probe.6), channel_id=1, replica_groups={{0,1,16,17,2,3,18,19,4,5,20,21,6,7,22,23},{8,9,24,25,10,11,26,27,12,13,..., dimensions={0} | all-to-all | bytes 524288 | tf_op jit(solution)/shard_map/all_to_all | solution.py:341
  75.5 6.5 %collective-permute-start.5 = (f32[16,32,128]{2,1,0:T(8,128)S(1)}, f32[16,32,128]{2,1,0:T(8,128)S(1)}, u32[]{:S(2)}, u32[]{:S(2)}) collective-permute-start(f32[16,32,128]{2,1,0:T(8,128)S(1)} %all_to_all.17.mine), channel_id=1, source_target_pairs={{0,8},{8,0},{16,24},{24,16},{32,40},{40,32},{48,56},{56,48},{64,72... | collective-permute-start | bytes 786440 | tf_op jit(solution)/shard_map/ppermute | solution.py:308
  82.0 1.2 %collective-permute-done.5.other = f32[16,32,128]{2,1,0:T(8,128)S(1)} collective-permute-done((f32[16,32,128]{2,1,0:T(8,128)S(1)}, f32[16,32,128]{2,1,0:T(8,128)S(1)}, u32[]{:S(2)}, u32[]{:S(2)}) %collective-permute-start.5) | collective-permute-done | bytes 262176 | tf_op jit(solution)/shard_map/ppermute | solution.py:308
  83.1 0.9 %gather.1 = f32[2,256,256]{2,1,0:T(8,128)} custom-call(f32[16,32,128]{2,1,0:T(8,128)S(1)} %all_to_all.17.mine, f32[16,32,128]{2,1,0:T(8,128)S(1)} %collective-permute-done.5.other), custom_call_target="tpu_custom_call" | custom-call | tf_op jit(solution)/shard_map/gather/pallas_call | solution.py:418
  (3 shorter events, 0.0 us)
Async XLA Ops:
  0.6 25.3 %copy-start.1 = (bf16[768,256]{1,0:T(8,128)(2,1)S(1)}, bf16[768,256]{1,0:T(8,128)(2,1)}, u32[]{:S(2)}) copy-start(bf16[768,256]{1,0:T(8,128)(2,1)} %constant.4.clone.row_table) | copy-start | bytes 1179652
  0.6 25.3 %copy-start.2 = (bf16[768,256]{1,0:T(8,128)(2,1)S(1)}, bf16[768,256]{1,0:T(8,128)(2,1)}, u32[]{:S(2)}) copy-start(bf16[768,256]{1,0:T(8,128)(2,1)} %constant.5.clone.col_table) | copy-start | bytes 1179652
  0.7 25.3 %copy-start.3 = (f32[1,256,256]{2,1,0:T(8,128)S(1)}, f32[1,256,256]{2,1,0:T(8,128)}, u32[]{:S(2)}) copy-start(f32[1,256,256]{2,1,0:T(8,128)} %amps.1) | copy-start | bytes 786436
  0.7 25.3 %copy-start = (f32[2,256,256]{2,1,0:T(8,128)S(1)}, f32[2,256,256]{2,1,0:T(8,128)}, u32[]{:S(2)}) copy-start(f32[2,256,256]{2,1,0:T(8,128)} %probe.7) | copy-start | bytes 1572868
  23.1 2.8 %collective-permute-start = (f32[16,80,128]{2,1,0:T(8,128)S(1)}, f32[16,80,128]{2,1,0:T(8,128)S(1)}, u32[]{:S(2)}, u32[]{:S(2)}) collective-permute-start(f32[16,80,128]{2,1,0:T(8,128)S(1)} %all_to_all.15.stack), channel_id=1, source_target_pairs={{0,8},{8,0},{16,24},{24,16},{32,40},{40,32},{48,56},{56,48},{64,72... | collective-permute-start | bytes 1966088 | tf_op jit(solution)/shard_map/ppermute | solution.py:308
  28.5 2.4 %collective-permute-start.1 = (f32[1536,128]{1,0:T(8,128)S(1)}, f32[1536,128]{1,0:T(8,128)S(1)}, u32[]{:S(2)}, u32[]{:S(2)}) collective-permute-start(f32[1536,128]{1,0:T(8,128)S(1)} %get-tuple-element.15), channel_id=1, source_target_pairs={{0,8},{8,0},{16,24},{24,16},{32,40},{40,32},{48,56},{56,48},{64,72... | collective-permute-start | bytes 2359304 | tf_op jit(solution)/shard_map/ppermute | solution.py:308
  52.2 11.3 %copy-start.4 = (f32[2,40,128]{2,1,0:T(8,128)S(1)}, f32[2,40,128]{2,1,0:T(8,128)}, u32[]{:S(2)}) copy-start(f32[2,40,128]{2,1,0:T(8,128)} %old.1) | copy-start | bytes 122884
  52.2 2.8 %collective-permute-start.2 = (f32[56,128]{1,0:T(8,128)S(1)}, f32[56,128]{1,0:T(8,128)S(1)}, u32[]{:S(2)}, u32[]{:S(2)}) collective-permute-start(f32[56,128]{1,0:T(8,128)S(1)} %reduce.1), channel_id=1, source_target_pairs={{0,224},{8,40},{16,48},{24,56},{32,64},{40,8},{48,16},{56,24},{64,... | collective-permute-start | bytes 86024 | tf_op jit(solution)/shard_map/ppermute | solution.py:318
  55.0 4.4 %collective-permute-start.3 = (f32[56,128]{1,0:T(8,128)S(1)}, f32[56,128]{1,0:T(8,128)S(1)}, u32[]{:S(2)}, u32[]{:S(2)}) collective-permute-start(f32[56,128]{1,0:T(8,128)S(1)} %add.6), channel_id=1, source_target_pairs={{0,192},{8,72},{16,80},{24,88},{32,96},{40,104},{48,112},{56,120},... | collective-permute-start | bytes 86024 | tf_op jit(solution)/shard_map/ppermute | solution.py:318
  59.4 5.7 %collective-permute-start.4 = (f32[56,128]{1,0:T(8,128)S(1)}, f32[56,128]{1,0:T(8,128)S(1)}, u32[]{:S(2)}, u32[]{:S(2)}) collective-permute-start(f32[56,128]{1,0:T(8,128)S(1)} %add.7.one), channel_id=1, source_target_pairs={{0,64},{8,200},{16,208},{24,216},{32,224},{40,232},{48,240},{56,24... | collective-permute-start | bytes 86024 | tf_op jit(solution)/shard_map/ppermute | solution.py:318
  75.5 7.6 %collective-permute-start.5 = (f32[16,32,128]{2,1,0:T(8,128)S(1)}, f32[16,32,128]{2,1,0:T(8,128)S(1)}, u32[]{:S(2)}, u32[]{:S(2)}) collective-permute-start(f32[16,32,128]{2,1,0:T(8,128)S(1)} %all_to_all.17.mine), channel_id=1, source_target_pairs={{0,8},{8,0},{16,24},{24,16},{32,40},{40,32},{48,56},{56,48},{64,72... | collective-permute-start | bytes 786440 | tf_op jit(solution)/shard_map/ppermute | solution.py:308

commit v15 on v14

--- a/solution.py
+++ b/solution.py
@@ -309,13 +309,7 @@
 
 
 def swap_z(value, mask):
-    pairs = []
-    for tile in range(TILES):
-        layer, rest = divmod(tile, 4)
-        ahead = 1 if rest == 0 else 0
-        other = (((layer - ahead) % (TILES // 4)) ^ mask) + ahead
-        pairs.append((tile, other % (TILES // 4) * 4 + rest))
-    return lax.ppermute(value, "tile", pairs)
+    return lax.ppermute(value, "tile", [(tile, tile ^ (4 * mask)) for tile in range(TILES)])
 
 
 def exchange(value):

time: 84.2 us -> 84.2 us (level)
  starting transfers between devices: 15.1 us -> 14 us
where the time goes in v15:
time: 84.2 us; the launch traced here: 84 us
  blocking collectives  53.3 us (63%)
  starting transfers between devices  14 us (17%)
  waiting for transfers between devices  7.42 us (9%)
  Pallas kernels  5.57 us (7%)
  between operations  2.7 us (3%)
  local copies, waits for them, and re-layouts  0.96 us (1%)
    all_to_all x2, blocking collectives, exchange(): lax.all_to_all(value, ('tile', 'group'), 0, 0, axis_index_groups=groups)  42.6 us
    all_to_all x1, blocking collectives, exchange_plane(): lax.all_to_all(value, ('tile', 'group'), 0, 0, axis_index_groups=groups)  10.7 us
    ppermute x3, starting transfers between devices, swap_cores(): return lax.ppermute(value, 'tile', [(i, i ^ 1) for i in range(TILES)])  7.32 us
    ppermute x3, starting transfers between devices, swap_z(): lax.ppermute(value, 'tile', [(tile, tile ^ 4 * mask) for tile in range(TI...  6.69 us
    ppermute x3, waiting for transfers between devices, swap_z(): lax.ppermute(value, 'tile', [(tile, tile ^ 4 * mask) for tile in range(TI...  4.34 us
    ppermute x3, waiting for transfers between devices, swap_cores(): return lax.ppermute(value, 'tile', [(i, i ^ 1) for i in range(TILES)])  3.08 us
    pallas_call x1, Pallas kernels, local(): kernel_call(window_kernel, (buffer(16 * PIECE + 640, LANES), buffer(3, WI...  2.53 us
  transfers between devices with their start and end apart: 6, of which 4 were waited for; matrix products, arithmetic and copies ran while one was open for 0% of the time, Pallas kernels for 2%

profile of v15, /device:TPU:1, one launch (start us, length us, event | category | flops | bytes accessed | tf_op | source)
XLA Modules:
  0.0 84.0 jit_solution(3709936246256230465)
XLA Ops:
  0.6 0.0 copy-start.1
  0.6 0.0 copy-start.2
  0.7 0.0 copy-start.3
  0.7 0.0 copy-start
  0.7 0.9 %broadcast_in_dim.3 = f32[16,80,128]{2,1,0:T(8,128)S(1)} broadcast(f32[80,128]{1,0:T(8,128)} %bitcast.1), dimensions={1,2} | broadcast | bytes 696320 | tf_op jit(solution)/shard_map/broadcast_in_dim | solution.py:363
  1.6 21.5 %all_to_all.15.stack = f32[16,80,128]{2,1,0:T(8,128)S(1)} all-to-all(f32[16,80,128]{2,1,0:T(8,128)S(1)} %broadcast_in_dim.3), channel_id=1, replica_groups={{8,9,10,11,12,13,14,15,16,17,18,19,20,21,22,23},{24,25,26,27,28,29,30,3..., dimensions={0} | all-to-all | bytes 1310720 | tf_op jit(solution)/shard_map/all_to_all | solution.py:320
  23.1 0.9 %collective-permute-start = (f32[16,80,128]{2,1,0:T(8,128)S(1)}, f32[16,80,128]{2,1,0:T(8,128)S(1)}, u32[]{:S(2)}, u32[]{:S(2)}) collective-permute-start(f32[16,80,128]{2,1,0:T(8,128)S(1)} %all_to_all.15.stack), channel_id=1, source_target_pairs={{0,8},{8,0},{16,24},{24,16},{32,40},{40,32},{48,56},{56,48},{64,72... | collective-permute-start | bytes 1966088 | tf_op jit(solution)/shard_map/ppermute | solution.py:308
  26.0 0.0 collective-permute-done.near
  26.0 0.0 copy-done.1
  26.0 0.0 copy-done.2
  26.0 0.0 copy-done.3
  26.0 0.0 copy-done
  26.0 2.5 %window.1 = (f32[1536,128]{1,0:T(8,128)S(1)}, f32[3,256,256]{2,1,0:T(8,128)S(1)}, f32[2,3,320,128]{3,2,1,0:T(8,128)S(1)}, f32[8,128]{1,0:T(8,128)S(1)}) custom-call(s32[1]{0:T(128)S(6)} %copy.10.row_ref, s32[1]{0:T(128)S(6)} %copy.11.col_ref, s32[1]{0:T(128)S(6)} %copy.12.live_ref, f32[16,80,128]{2,1,0:T(8,128)S(1)} %all_to_all.15.stack, ...), custom_call_target="tpu_custom_call" | custom-call | tf_op jit(solution)/shard_map/window/pallas_call | solution.py:372
  28.5 0.2 collective-permute-start.1
  28.8 0.2 prep.1
  29.0 1.9 %collective-permute-done.1.got = f32[1536,128]{1,0:T(8,128)S(1)} collective-permute-done((f32[1536,128]{1,0:T(8,128)S(1)}, f32[1536,128]{1,0:T(8,128)S(1)}, u32[]{:S(2)}, u32[]{:S(2)}) %collective-permute-start.1) | collective-permute-done | bytes 786464 | tf_op jit(solution)/shard_map/ppermute | solution.py:308
  30.9 0.1 merge.1
  31.0 21.1 %all_to_all.16.pieces = f32[16,136,128]{2,1,0:T(8,128)S(1)} all-to-all(f32[16,136,128]{2,1,0:T(8,128)S(1)} %merge.1), channel_id=1, replica_groups={{8,9,10,11,12,13,14,15,16,17,18,19,20,21,22,23},{24,25,26,27,28,29,30,3..., dimensions={0} | all-to-all | bytes 2228224 | tf_op jit(solution)/shard_map/all_to_all | solution.py:320
  52.2 0.0 copy-start.4
  52.2 0.3 collective-permute-start.2
  52.5 3.1 %collective-permute-done.2 = f32[56,128]{1,0:T(8,128)S(1)} collective-permute-done((f32[56,128]{1,0:T(8,128)S(1)}, f32[56,128]{1,0:T(8,128)S(1)}, u32[]{:S(2)}, u32[]{:S(2)}) %collective-permute-start.2) | collective-permute-done | bytes 28704 | tf_op jit(solution)/shard_map/ppermute | solution.py:312
  55.6 2.6 %collective-permute-start.3 = (f32[56,128]{1,0:T(8,128)S(1)}, f32[56,128]{1,0:T(8,128)S(1)}, u32[]{:S(2)}, u32[]{:S(2)}) collective-permute-start(f32[56,128]{1,0:T(8,128)S(1)} %add.6), channel_id=1, source_target_pairs={{0,64},{8,72},{16,80},{24,88},{32,96},{40,104},{48,112},{56,120},{... | collective-permute-start | bytes 86024 | tf_op jit(solution)/shard_map/ppermute | solution.py:312
  58.1 1.3 %collective-permute-done.3 = f32[56,128]{1,0:T(8,128)S(1)} collective-permute-done((f32[56,128]{1,0:T(8,128)S(1)}, f32[56,128]{1,0:T(8,128)S(1)}, u32[]{:S(2)}, u32[]{:S(2)}) %collective-permute-start.3) | collective-permute-done | bytes 28704 | tf_op jit(solution)/shard_map/ppermute | solution.py:312
  59.4 3.8 %collective-permute-start.4 = (f32[56,128]{1,0:T(8,128)S(1)}, f32[56,128]{1,0:T(8,128)S(1)}, u32[]{:S(2)}, u32[]{:S(2)}) collective-permute-start(f32[56,128]{1,0:T(8,128)S(1)} %add.7.one), channel_id=1, source_target_pairs={{0,192},{8,200},{16,208},{24,216},{32,224},{40,232},{48,240},{56,2... | collective-permute-start | bytes 86024 | tf_op jit(solution)/shard_map/ppermute | solution.py:312
  63.2 0.0 copy-done.4
  63.2 1.6 %object.1 = f32[2,40,128]{2,1,0:T(8,128)} custom-call(f32[16,136,128]{2,1,0:T(8,128)S(1)} %all_to_all.16.pieces, f32[2,40,128]{2,1,0:T(8,128)S(1)} %copy-done.4, f32[4,384,128]{2,1,0:T(8,128)S(1)} %get-tuple-element.18.light, f32[8,128]{1,0:T(8,128)S(1)} %get-tuple-element.19.peak), custom_call_target="tpu_custom_call" | custom-call | flops 700000 | bytes 2000000 | tf_op jit(solution)/shard_map/object/pallas_call | solution.py:395
  64.9 0.0 collective-permute-done.4.two
  64.9 0.1 probe.6
  65.1 10.7 %all_to_all.17.mine = f32[16,32,128]{2,1,0:T(8,128)S(1)} all-to-all(f32[16,32,128]{2,1,0:T(8,128)S(1)} %probe.6), channel_id=1, replica_groups={{0,1,16,17,2,3,18,19,4,5,20,21,6,7,22,23},{8,9,24,25,10,11,26,27,12,13,..., dimensions={0} | all-to-all | bytes 524288 | tf_op jit(solution)/shard_map/all_to_all | solution.py:335
  75.8 6.2 %collective-permute-start.5 = (f32[16,32,128]{2,1,0:T(8,128)S(1)}, f32[16,32,128]{2,1,0:T(8,128)S(1)}, u32[]{:S(2)}, u32[]{:S(2)}) collective-permute-start(f32[16,32,128]{2,1,0:T(8,128)S(1)} %all_to_all.17.mine), channel_id=1, source_target_pairs={{0,8},{8,0},{16,24},{24,16},{32,40},{40,32},{48,56},{56,48},{64,72... | collective-permute-start | bytes 786440 | tf_op jit(solution)/shard_map/ppermute | solution.py:308
  82.0 1.2 %collective-permute-done.5.other = f32[16,32,128]{2,1,0:T(8,128)S(1)} collective-permute-done((f32[16,32,128]{2,1,0:T(8,128)S(1)}, f32[16,32,128]{2,1,0:T(8,128)S(1)}, u32[]{:S(2)}, u32[]{:S(2)}) %collective-permute-start.5) | collective-permute-done | bytes 262176 | tf_op jit(solution)/shard_map/ppermute | solution.py:308
  83.1 0.9 %gather.1 = f32[2,256,256]{2,1,0:T(8,128)} custom-call(f32[16,32,128]{2,1,0:T(8,128)S(1)} %all_to_all.17.mine, f32[16,32,128]{2,1,0:T(8,128)S(1)} %collective-permute-done.5.other), custom_call_target="tpu_custom_call" | custom-call | tf_op jit(solution)/shard_map/gather/pallas_call | solution.py:412
  (3 shorter events, 0.0 us)
Async XLA Ops:
  0.6 25.3 %copy-start.1 = (bf16[768,256]{1,0:T(8,128)(2,1)S(1)}, bf16[768,256]{1,0:T(8,128)(2,1)}, u32[]{:S(2)}) copy-start(bf16[768,256]{1,0:T(8,128)(2,1)} %constant.4.clone.row_table) | copy-start | bytes 1179652
  0.6 25.3 %copy-start.2 = (bf16[768,256]{1,0:T(8,128)(2,1)S(1)}, bf16[768,256]{1,0:T(8,128)(2,1)}, u32[]{:S(2)}) copy-start(bf16[768,256]{1,0:T(8,128)(2,1)} %constant.5.clone.col_table) | copy-start | bytes 1179652
  0.7 25.3 %copy-start.3 = (f32[1,256,256]{2,1,0:T(8,128)S(1)}, f32[1,256,256]{2,1,0:T(8,128)}, u32[]{:S(2)}) copy-start(f32[1,256,256]{2,1,0:T(8,128)} %amps.1) | copy-start | bytes 786436
  0.7 25.3 %copy-start = (f32[2,256,256]{2,1,0:T(8,128)S(1)}, f32[2,256,256]{2,1,0:T(8,128)}, u32[]{:S(2)}) copy-start(f32[2,256,256]{2,1,0:T(8,128)} %probe.7) | copy-start | bytes 1572868
  23.1 2.8 %collective-permute-start = (f32[16,80,128]{2,1,0:T(8,128)S(1)}, f32[16,80,128]{2,1,0:T(8,128)S(1)}, u32[]{:S(2)}, u32[]{:S(2)}) collective-permute-start(f32[16,80,128]{2,1,0:T(8,128)S(1)} %all_to_all.15.stack), channel_id=1, source_target_pairs={{0,8},{8,0},{16,24},{24,16},{32,40},{40,32},{48,56},{56,48},{64,72... | collective-permute-start | bytes 1966088 | tf_op jit(solution)/shard_map/ppermute | solution.py:308
  28.5 2.4 %collective-permute-start.1 = (f32[1536,128]{1,0:T(8,128)S(1)}, f32[1536,128]{1,0:T(8,128)S(1)}, u32[]{:S(2)}, u32[]{:S(2)}) collective-permute-start(f32[1536,128]{1,0:T(8,128)S(1)} %get-tuple-element.15), channel_id=1, source_target_pairs={{0,8},{8,0},{16,24},{24,16},{32,40},{40,32},{48,56},{56,48},{64,72... | collective-permute-start | bytes 2359304 | tf_op jit(solution)/shard_map/ppermute | solution.py:308
  52.2 11.1 %copy-start.4 = (f32[2,40,128]{2,1,0:T(8,128)S(1)}, f32[2,40,128]{2,1,0:T(8,128)}, u32[]{:S(2)}) copy-start(f32[2,40,128]{2,1,0:T(8,128)} %old.1) | copy-start | bytes 122884
  52.2 3.4 %collective-permute-start.2 = (f32[56,128]{1,0:T(8,128)S(1)}, f32[56,128]{1,0:T(8,128)S(1)}, u32[]{:S(2)}, u32[]{:S(2)}) collective-permute-start(f32[56,128]{1,0:T(8,128)S(1)} %reduce.1), channel_id=1, source_target_pairs={{0,32},{8,40},{16,48},{24,56},{32,0},{40,8},{48,16},{56,24},{64,96... | collective-permute-start | bytes 86024 | tf_op jit(solution)/shard_map/ppermute | solution.py:312
  55.6 3.8 %collective-permute-start.3 = (f32[56,128]{1,0:T(8,128)S(1)}, f32[56,128]{1,0:T(8,128)S(1)}, u32[]{:S(2)}, u32[]{:S(2)}) collective-permute-start(f32[56,128]{1,0:T(8,128)S(1)} %add.6), channel_id=1, source_target_pairs={{0,64},{8,72},{16,80},{24,88},{32,96},{40,104},{48,112},{56,120},{... | collective-permute-start | bytes 86024 | tf_op jit(solution)/shard_map/ppermute | solution.py:312
  59.4 5.5 %collective-permute-start.4 = (f32[56,128]{1,0:T(8,128)S(1)}, f32[56,128]{1,0:T(8,128)S(1)}, u32[]{:S(2)}, u32[]{:S(2)}) collective-permute-start(f32[56,128]{1,0:T(8,128)S(1)} %add.7.one), channel_id=1, source_target_pairs={{0,192},{8,200},{16,208},{24,216},{32,224},{40,232},{48,240},{56,2... | collective-permute-start | bytes 86024 | tf_op jit(solution)/shard_map/ppermute | solution.py:312
  75.8 7.4 %collective-permute-start.5 = (f32[16,32,128]{2,1,0:T(8,128)S(1)}, f32[16,32,128]{2,1,0:T(8,128)S(1)}, u32[]{:S(2)}, u32[]{:S(2)}) collective-permute-start(f32[16,32,128]{2,1,0:T(8,128)S(1)} %all_to_all.17.mine), channel_id=1, source_target_pairs={{0,8},{8,0},{16,24},{24,16},{32,40},{40,32},{48,56},{56,48},{64,72... | collective-permute-start | bytes 786440 | tf_op jit(solution)/shard_map/ppermute | solution.py:308

commit v16 on v15

--- a/solution.py
+++ b/solution.py
@@ -169,18 +169,18 @@
         here = jnp.logical_and(spare_line == 0, spare_lane == first_lane + lane_off)
         spare = jnp.where(here, number, spare)
     spare_out[...] = spare
+    send[16 * SPARE : 16 * SPARE + 8, :] = spare
     for member in range(16):
-        first_line = member * PIECE
+        first_line = member * SPARE
         top = pl.multiple_of((1 - half) * 128 + member * 8, 8)
         for part in range(3):
             for side in range(2):
                 put = first_line + part * 16 + side * 8
                 send[put : put + 8, :] = sums[part, pl.ds(top, 8), side * LANES : (side + 1) * LANES]
-        send[first_line + SPARE : first_line + PIECE, :] = spare
     for member in range(8):
         lines = slice(member * 40, member * 40 + 40)
         for part in range(2):
-            put = 16 * PIECE + member * 80 + part * 40
+            put = 16 * SPARE + 8 + member * 80 + part * 40
             send[put : put + 40, :] = grads[part, 2 - 2 * odd, lines, :]
 
 
@@ -192,15 +192,15 @@
         for part in range(3):
             for side in range(2):
                 put = part * 16 + side * 8
-                other = got[member * PIECE + put : member * PIECE + put + 8, :]
+                other = got[member * SPARE + put : member * SPARE + put + 8, :]
                 own = sums[part, pl.ds(top, 8), side * LANES : (side + 1) * LANES]
                 out[member, put : put + 8, :] = own + other
-        out[member, SPARE:PIECE, :] = spare[...] + got[member * PIECE + SPARE : (member + 1) * PIECE, :]
+        out[member, SPARE:PIECE, :] = spare[...] + got[16 * SPARE : 16 * SPARE + 8, :]
     for member in range(8):
         lines = slice(member * 40, member * 40 + 40)
         for part in range(2):
             put = PIECE + part * 40
-            other = 16 * PIECE + member * 80 + part * 40
+            other = 16 * SPARE + 8 + member * 80 + part * 40
             out[8 - 8 * odd + member, put : put + 40, :] = grads[part, 1, lines, :] + got[other : other + 40, :]
             out[8 * odd + member, put : put + 40, :] = jnp.where(
                 inside, grads[part, 2 * odd, lines, :], 0.0
@@ -372,7 +372,7 @@
     send, sums, grads, spare = kernel_call(
         window_kernel,
         (
-            buffer(16 * PIECE + 640, LANES),
+            buffer(16 * SPARE + 648, LANES),
             buffer(3, WIN, WIN),
             buffer(2, 3, 320, LANES),
             buffer(8, LANES),

time: 84.2 us -> 84.1 us (level)
  no operation moved by 1% of the time
where the time goes in v16:
time: 84.1 us; the launch traced here: 83.9 us
  blocking collectives  53.1 us (63%)
  starting transfers between devices  14.2 us (17%)
  waiting for transfers between devices  7.33 us (9%)
  Pallas kernels  5.58 us (7%)
  between operations  2.7 us (3%)
  local copies, waits for them, and re-layouts  0.96 us (1%)
    all_to_all x2, blocking collectives, exchange(): lax.all_to_all(value, ('tile', 'group'), 0, 0, axis_index_groups=groups)  42.6 us
    all_to_all x1, blocking collectives, exchange_plane(): lax.all_to_all(value, ('tile', 'group'), 0, 0, axis_index_groups=groups)  10.5 us
    ppermute x3, starting transfers between devices, swap_cores(): return lax.ppermute(value, 'tile', [(i, i ^ 1) for i in range(TILES)])  7.54 us
    ppermute x3, starting transfers between devices, swap_z(): lax.ppermute(value, 'tile', [(tile, tile ^ 4 * mask) for tile in range(TI...  6.69 us
    ppermute x3, waiting for transfers between devices, swap_z(): lax.ppermute(value, 'tile', [(tile, tile ^ 4 * mask) for tile in range(TI...  4.33 us
    ppermute x3, waiting for transfers between devices, swap_cores(): return lax.ppermute(value, 'tile', [(i, i ^ 1) for i in range(TILES)])  2.99 us
    pallas_call x1, Pallas kernels, local(): kernel_call(window_kernel, (buffer(16 * SPARE + 648, LANES), buffer(3, WI...  2.53 us
  transfers between devices with their start and end apart: 6, of which 4 were waited for; matrix products, arithmetic and copies ran while one was open for 0% of the time, Pallas kernels for 2%

profile of v16, /device:TPU:1, one launch (start us, length us, event | category | flops | bytes accessed | tf_op | source)
XLA Modules:
  0.0 83.9 jit_solution(10968467110626764362)
XLA Ops:
  0.6 0.0 copy-start.1
  0.6 0.0 copy-start.2
  0.7 0.0 copy-start.3
  0.7 0.0 copy-start
  0.7 0.9 %broadcast_in_dim.3 = f32[16,80,128]{2,1,0:T(8,128)S(1)} broadcast(f32[80,128]{1,0:T(8,128)} %bitcast.1), dimensions={1,2} | broadcast | bytes 696320 | tf_op jit(solution)/shard_map/broadcast_in_dim | solution.py:363
  1.6 21.5 %all_to_all.15.stack = f32[16,80,128]{2,1,0:T(8,128)S(1)} all-to-all(f32[16,80,128]{2,1,0:T(8,128)S(1)} %broadcast_in_dim.3), channel_id=1, replica_groups={{8,9,10,11,12,13,14,15,16,17,18,19,20,21,22,23},{24,25,26,27,28,29,30,3..., dimensions={0} | all-to-all | bytes 1310720 | tf_op jit(solution)/shard_map/all_to_all | solution.py:320
  23.1 0.9 %collective-permute-start = (f32[16,80,128]{2,1,0:T(8,128)S(1)}, f32[16,80,128]{2,1,0:T(8,128)S(1)}, u32[]{:S(2)}, u32[]{:S(2)}) collective-permute-start(f32[16,80,128]{2,1,0:T(8,128)S(1)} %all_to_all.15.stack), channel_id=1, source_target_pairs={{0,8},{8,0},{16,24},{24,16},{32,40},{40,32},{48,56},{56,48},{64,72... | collective-permute-start | bytes 1966088 | tf_op jit(solution)/shard_map/ppermute | solution.py:308
  26.0 0.0 collective-permute-done.near
  26.0 0.0 copy-done.1
  26.0 0.0 copy-done.2
  26.0 0.0 copy-done.3
  26.0 0.0 copy-done
  26.0 2.5 %window.1 = (f32[1416,128]{1,0:T(8,128)S(1)}, f32[3,256,256]{2,1,0:T(8,128)S(1)}, f32[2,3,320,128]{3,2,1,0:T(8,128)S(1)}, f32[8,128]{1,0:T(8,128)S(1)}) custom-call(s32[1]{0:T(128)S(6)} %copy.10.row_ref, s32[1]{0:T(128)S(6)} %copy.11.col_ref, s32[1]{0:T(128)S(6)} %copy.12.live_ref, f32[16,80,128]{2,1,0:T(8,128)S(1)} %all_to_all.15.stack, ...), custom_call_target="tpu_custom_call" | custom-call | tf_op jit(solution)/shard_map/window/pallas_call | solution.py:372
  28.5 0.2 collective-permute-start.1
  28.8 0.2 prep.1
  29.0 1.8 %collective-permute-done.1.got = f32[1416,128]{1,0:T(8,128)S(1)} collective-permute-done((f32[1416,128]{1,0:T(8,128)S(1)}, f32[1416,128]{1,0:T(8,128)S(1)}, u32[]{:S(2)}, u32[]{:S(2)}) %collective-permute-start.1) | collective-permute-done | bytes 725024 | tf_op jit(solution)/shard_map/ppermute | solution.py:308
  30.8 0.1 merge.1
  31.0 21.1 %all_to_all.16.pieces = f32[16,136,128]{2,1,0:T(8,128)S(1)} all-to-all(f32[16,136,128]{2,1,0:T(8,128)S(1)} %merge.1), channel_id=1, replica_groups={{8,9,10,11,12,13,14,15,16,17,18,19,20,21,22,23},{24,25,26,27,28,29,30,3..., dimensions={0} | all-to-all | bytes 2228224 | tf_op jit(solution)/shard_map/all_to_all | solution.py:320
  52.1 0.0 copy-start.4
  52.1 0.3 collective-permute-start.2
  52.4 3.1 %collective-permute-done.2 = f32[56,128]{1,0:T(8,128)S(1)} collective-permute-done((f32[56,128]{1,0:T(8,128)S(1)}, f32[56,128]{1,0:T(8,128)S(1)}, u32[]{:S(2)}, u32[]{:S(2)}) %collective-permute-start.2) | collective-permute-done | bytes 28704 | tf_op jit(solution)/shard_map/ppermute | solution.py:312
  55.5 2.6 %collective-permute-start.3 = (f32[56,128]{1,0:T(8,128)S(1)}, f32[56,128]{1,0:T(8,128)S(1)}, u32[]{:S(2)}, u32[]{:S(2)}) collective-permute-start(f32[56,128]{1,0:T(8,128)S(1)} %add.6), channel_id=1, source_target_pairs={{0,64},{8,72},{16,80},{24,88},{32,96},{40,104},{48,112},{56,120},{... | collective-permute-start | bytes 86024 | tf_op jit(solution)/shard_map/ppermute | solution.py:312
  58.1 1.3 %collective-permute-done.3 = f32[56,128]{1,0:T(8,128)S(1)} collective-permute-done((f32[56,128]{1,0:T(8,128)S(1)}, f32[56,128]{1,0:T(8,128)S(1)}, u32[]{:S(2)}, u32[]{:S(2)}) %collective-permute-start.3) | collective-permute-done | bytes 28704 | tf_op jit(solution)/shard_map/ppermute | solution.py:312
  59.3 3.8 %collective-permute-start.4 = (f32[56,128]{1,0:T(8,128)S(1)}, f32[56,128]{1,0:T(8,128)S(1)}, u32[]{:S(2)}, u32[]{:S(2)}) collective-permute-start(f32[56,128]{1,0:T(8,128)S(1)} %add.7.one), channel_id=1, source_target_pairs={{0,192},{8,200},{16,208},{24,216},{32,224},{40,232},{48,240},{56,2... | collective-permute-start | bytes 86024 | tf_op jit(solution)/shard_map/ppermute | solution.py:312
  63.1 0.0 copy-done.4
  63.2 1.6 %object.1 = f32[2,40,128]{2,1,0:T(8,128)} custom-call(f32[16,136,128]{2,1,0:T(8,128)S(1)} %all_to_all.16.pieces, f32[2,40,128]{2,1,0:T(8,128)S(1)} %copy-done.4, f32[4,384,128]{2,1,0:T(8,128)S(1)} %get-tuple-element.18.light, f32[8,128]{1,0:T(8,128)S(1)} %get-tuple-element.19.peak), custom_call_target="tpu_custom_call" | custom-call | flops 700000 | bytes 2000000 | tf_op jit(solution)/shard_map/object/pallas_call | solution.py:395
  64.8 0.0 collective-permute-done.4.two
  64.8 0.1 probe.6
  65.0 10.5 %all_to_all.17.mine = f32[16,32,128]{2,1,0:T(8,128)S(1)} all-to-all(f32[16,32,128]{2,1,0:T(8,128)S(1)} %probe.6), channel_id=1, replica_groups={{0,1,16,17,2,3,18,19,4,5,20,21,6,7,22,23},{8,9,24,25,10,11,26,27,12,13,..., dimensions={0} | all-to-all | bytes 524288 | tf_op jit(solution)/shard_map/all_to_all | solution.py:335
  75.5 6.4 %collective-permute-start.5 = (f32[16,32,128]{2,1,0:T(8,128)S(1)}, f32[16,32,128]{2,1,0:T(8,128)S(1)}, u32[]{:S(2)}, u32[]{:S(2)}) collective-permute-start(f32[16,32,128]{2,1,0:T(8,128)S(1)} %all_to_all.17.mine), channel_id=1, source_target_pairs={{0,8},{8,0},{16,24},{24,16},{32,40},{40,32},{48,56},{56,48},{64,72... | collective-permute-start | bytes 786440 | tf_op jit(solution)/shard_map/ppermute | solution.py:308
  81.9 1.2 %collective-permute-done.5.other = f32[16,32,128]{2,1,0:T(8,128)S(1)} collective-permute-done((f32[16,32,128]{2,1,0:T(8,128)S(1)}, f32[16,32,128]{2,1,0:T(8,128)S(1)}, u32[]{:S(2)}, u32[]{:S(2)}) %collective-permute-start.5) | collective-permute-done | bytes 262176 | tf_op jit(solution)/shard_map/ppermute | solution.py:308
  83.0 0.9 %gather.1 = f32[2,256,256]{2,1,0:T(8,128)} custom-call(f32[16,32,128]{2,1,0:T(8,128)S(1)} %all_to_all.17.mine, f32[16,32,128]{2,1,0:T(8,128)S(1)} %collective-permute-done.5.other), custom_call_target="tpu_custom_call" | custom-call | tf_op jit(solution)/shard_map/gather/pallas_call | solution.py:412
  (3 shorter events, 0.0 us)
Async XLA Ops:
  0.6 25.3 %copy-start.1 = (bf16[768,256]{1,0:T(8,128)(2,1)S(1)}, bf16[768,256]{1,0:T(8,128)(2,1)}, u32[]{:S(2)}) copy-start(bf16[768,256]{1,0:T(8,128)(2,1)} %constant.4.clone.row_table) | copy-start | bytes 1179652
  0.6 25.3 %copy-start.2 = (bf16[768,256]{1,0:T(8,128)(2,1)S(1)}, bf16[768,256]{1,0:T(8,128)(2,1)}, u32[]{:S(2)}) copy-start(bf16[768,256]{1,0:T(8,128)(2,1)} %constant.5.clone.col_table) | copy-start | bytes 1179652
  0.7 25.3 %copy-start.3 = (f32[1,256,256]{2,1,0:T(8,128)S(1)}, f32[1,256,256]{2,1,0:T(8,128)}, u32[]{:S(2)}) copy-start(f32[1,256,256]{2,1,0:T(8,128)} %amps.1) | copy-start | bytes 786436
  0.7 25.3 %copy-start = (f32[2,256,256]{2,1,0:T(8,128)S(1)}, f32[2,256,256]{2,1,0:T(8,128)}, u32[]{:S(2)}) copy-start(f32[2,256,256]{2,1,0:T(8,128)} %probe.7) | copy-start | bytes 1572868
  23.1 2.8 %collective-permute-start = (f32[16,80,128]{2,1,0:T(8,128)S(1)}, f32[16,80,128]{2,1,0:T(8,128)S(1)}, u32[]{:S(2)}, u32[]{:S(2)}) collective-permute-start(f32[16,80,128]{2,1,0:T(8,128)S(1)} %all_to_all.15.stack), channel_id=1, source_target_pairs={{0,8},{8,0},{16,24},{24,16},{32,40},{40,32},{48,56},{56,48},{64,72... | collective-permute-start | bytes 1966088 | tf_op jit(solution)/shard_map/ppermute | solution.py:308
  28.5 2.3 %collective-permute-start.1 = (f32[1416,128]{1,0:T(8,128)S(1)}, f32[1416,128]{1,0:T(8,128)S(1)}, u32[]{:S(2)}, u32[]{:S(2)}) collective-permute-start(f32[1416,128]{1,0:T(8,128)S(1)} %get-tuple-element.15), channel_id=1, source_target_pairs={{0,8},{8,0},{16,24},{24,16},{32,40},{40,32},{48,56},{56,48},{64,72... | collective-permute-start | bytes 2174984 | tf_op jit(solution)/shard_map/ppermute | solution.py:308
  52.1 11.1 %copy-start.4 = (f32[2,40,128]{2,1,0:T(8,128)S(1)}, f32[2,40,128]{2,1,0:T(8,128)}, u32[]{:S(2)}) copy-start(f32[2,40,128]{2,1,0:T(8,128)} %old.1) | copy-start | bytes 122884
  52.1 3.4 %collective-permute-start.2 = (f32[56,128]{1,0:T(8,128)S(1)}, f32[56,128]{1,0:T(8,128)S(1)}, u32[]{:S(2)}, u32[]{:S(2)}) collective-permute-start(f32[56,128]{1,0:T(8,128)S(1)} %reduce.1), channel_id=1, source_target_pairs={{0,32},{8,40},{16,48},{24,56},{32,0},{40,8},{48,16},{56,24},{64,96... | collective-permute-start | bytes 86024 | tf_op jit(solution)/shard_map/ppermute | solution.py:312
  55.5 3.8 %collective-permute-start.3 = (f32[56,128]{1,0:T(8,128)S(1)}, f32[56,128]{1,0:T(8,128)S(1)}, u32[]{:S(2)}, u32[]{:S(2)}) collective-permute-start(f32[56,128]{1,0:T(8,128)S(1)} %add.6), channel_id=1, source_target_pairs={{0,64},{8,72},{16,80},{24,88},{32,96},{40,104},{48,112},{56,120},{... | collective-permute-start | bytes 86024 | tf_op jit(solution)/shard_map/ppermute | solution.py:312
  59.3 5.5 %collective-permute-start.4 = (f32[56,128]{1,0:T(8,128)S(1)}, f32[56,128]{1,0:T(8,128)S(1)}, u32[]{:S(2)}, u32[]{:S(2)}) collective-permute-start(f32[56,128]{1,0:T(8,128)S(1)} %add.7.one), channel_id=1, source_target_pairs={{0,192},{8,200},{16,208},{24,216},{32,224},{40,232},{48,240},{56,2... | collective-permute-start | bytes 86024 | tf_op jit(solution)/shard_map/ppermute | solution.py:312
  75.5 7.6 %collective-permute-start.5 = (f32[16,32,128]{2,1,0:T(8,128)S(1)}, f32[16,32,128]{2,1,0:T(8,128)S(1)}, u32[]{:S(2)}, u32[]{:S(2)}) collective-permute-start(f32[16,32,128]{2,1,0:T(8,128)S(1)} %all_to_all.17.mine), channel_id=1, source_target_pairs={{0,8},{8,0},{16,24},{24,16},{32,40},{40,32},{48,56},{56,48},{64,72... | collective-permute-start | bytes 786440 | tf_op jit(solution)/shard_map/ppermute | solution.py:308
